TPU v7x, 256 devices: a whole 4x4x8 slice. The times are simulated.
256 devices in a mesh: img: 32 (over z_hi, x, core), fou: 8 (over z_lo, y).
Axes of the slice: x: 4, y: 4, z: 8 (z_hi: 4, z_lo: 2; z = z_hi * 2 + z_lo), core: 2. Of those that a mesh axis runs over, the one named last changes fastest.
Arguments:
- sky_estimate: float32 [4, 2048, 2048], P(None, 'img', 'fou'), may hold values from 0 to 2
- dual_coeffs: bfloat16 [4, 9, 2048, 2048], P(None, None, 'img', 'fou'), may hold values from -2 to 2
- dirty_image: float32 [4, 2048, 2048], P(None, 'img', 'fou'), may hold values from -4 to 4
- filters: float32 [8, 17], replicated, may hold values from -1.5 to 1.5
- thresholds: float32 [9], replicated, may hold values from 0.2 to 1.2
- facet_rows: int32 [32], P('img'), may hold values from 16 to 64, as said below
- tile_slots: int32 [4, 32, 6], P(None, 'img'), may hold values from 0 to 31, as said below
- tile_count: int32 [4, 32], P(None, 'img'), may hold values from 1 to 6, as said below
- gram_tiles: bfloat16 [4, 32, 6, 64, 64], P(None, 'img'), may hold values from -4 to 4
Outputs:
- image_next: float32 [4, 2048, 2048], P(None, 'img', 'fou')
- dual_next: bfloat16 [4, 9, 2048, 2048], P(None, None, 'img', 'fou')
Inputs may be any that keep to these rules, and one draw needn't show every extreme that they name: `facet_rows`: facet f covers image rows f * 64 to (f + 1) * 64 - 1; some facet is full. `tile_slots`: the 6 entries of one channel and v-tile are distinct. `tile_count`: slots at or beyond the count hold no tile; in each channel some v-tile uses all 6 slots.
All inputs are finite; a program needn't handle non-finite values.
Results may differ from a plain program's by a relative error of at most 0.005.
Values may be sent and summed in bfloat16 or wider, within the bound.
No kernel may reach another device: no remote copies, remote signals or barrier semaphores. Data moves between devices by JAX's collectives and lax.ppermute only.
A program may use at most 64 MiB of HBM per device.

v0:
```python
import math

import jax
import jax.numpy as jnp
import numpy as np
from jax import lax
from jax.experimental import pallas as pl
from jax.experimental.pallas import tpu as pltpu
from jax.sharding import PartitionSpec as P

PIXELS = 2048
RADIUS = 8
SLOTS = 6
ROWS = 64
COLS = 256
FRAMES = 8
PEERS_IMG = 32
STEP_PRIMAL = 0.5
STEP_DUAL = 0.5
BF = jnp.bfloat16
F32 = jnp.float32
VMEM_LIMIT = 48 << 20


def two_terms_np(table):
    high = table.astype(jnp.bfloat16)
    low = (table - high.astype(np.float64)).astype(jnp.bfloat16)
    return high, low


def two_terms(table):
    high = table.astype(BF)
    return high, (table - high.astype(F32)).astype(BF)


def dot(a, b, dims=((1,), (0,))):
    return lax.dot_general(a, b, (dims, ((), ())), preferred_element_type=F32)


def angle_np(a, b, period):
    return 2.0 * np.pi * ((a[:, None] * b[None, :]) % period) / period


def line_table():
    ang = angle_np(np.arange(256), np.arange(256), 256)
    return np.concatenate([-np.sin(ang), np.cos(ang), np.sin(ang)], axis=1)


def block_table():
    ang = angle_np(np.arange(32), np.arange(32), 32)
    c, s = np.cos(ang), np.sin(ang)
    return np.block([[c, s], [-s, c]])


def turn_table():
    ang = angle_np(np.arange(64), np.arange(64), 2048)
    ang = np.concatenate([ang, ang], axis=1)
    return np.stack([np.cos(ang), np.sin(ang)]).astype(np.float32)


def fold_tables(parity, scale):
    cls = jnp.arange(4, dtype=jnp.int32)
    freq = parity + 2 * cls
    pos = jnp.arange(4 * COLS, dtype=jnp.int32).reshape(4, COLS)
    ang = (freq[:, None, None] * pos[None] % PIXELS).astype(F32) * (2.0 * math.pi / PIXELS)
    return jnp.stack([jnp.cos(ang), jnp.sin(ang)]) * scale


def forward_kernel(x_ref, fold_ref, sign_ref, whi_ref, wlo_ref, o_ref):
    sign = sign_ref[0:1, :]
    xe = [x_ref[f].astype(F32) + sign * x_ref[f + 4].astype(F32) for f in range(4)]
    whi = whi_ref[:, 256:768]
    wlo = wlo_ref[:, 256:768]
    parts = [[], []]
    for chi in range(2):
        rows_re, rows_im = [], []
        for clo in range(2):
            cls = 2 * chi + clo
            yr = xe[0] * fold_ref[0, cls, 0:1, :]
            yi = xe[0] * fold_ref[1, cls, 0:1, :]
            for f in range(1, 4):
                yr = yr + xe[f] * fold_ref[0, cls, f : f + 1, :]
                yi = yi + xe[f] * fold_ref[1, cls, f : f + 1, :]
            yi = -yi
            rows_re.append(jnp.concatenate([yr, yi], axis=1))
            rows_im.append(jnp.concatenate([yi, -yr], axis=1))
        for part, rows in enumerate((rows_re, rows_im)):
            r = jnp.concatenate(rows, axis=0).astype(BF)
            out = dot(whi, r, ((1,), (1,))) + dot(wlo, r, ((1,), (1,)))
            parts[part].append(out.reshape(32, 8, 128))
    for part in range(2):
        both = jnp.concatenate(parts[part], axis=1)
        o_ref[:, part * 16 : (part + 1) * 16, :] = both.astype(BF)


def inverse_kernel(t_ref, fold_ref, sign_ref, whi_ref, wlo_ref, o_ref):
    sign = sign_ref[0:1, :]
    re = t_ref[:, 0:16, :].astype(F32)
    im = t_ref[:, 16:32, :].astype(F32)
    total = [None] * 4
    for chi in range(2):
        a = re[:, chi * 8 : chi * 8 + 8, :].reshape(256, 128).astype(BF)
        b = im[:, chi * 8 : chi * 8 + 8, :].reshape(256, 128).astype(BF)
        u = None
        for ref in (whi_ref, wlo_ref):
            term = dot(a, ref[:, 256:768], ((0,), (0,))) + dot(b, ref[:, 0:512], ((0,), (0,)))
            u = term if u is None else u + term
        for clo in range(2):
            cls = 2 * chi + clo
            ur = u[clo * 64 : clo * 64 + 64, 0:256]
            ui = u[clo * 64 : clo * 64 + 64, 256:512]
            for f in range(4):
                g = ur * fold_ref[0, cls, f : f + 1, :] - ui * fold_ref[1, cls, f : f + 1, :]
                total[f] = g if total[f] is None else total[f] + g
    for f in range(4):
        o_ref[f] = total[f].astype(BF)
        o_ref[f + 4] = (sign * total[f]).astype(BF)


def gram_kernel(
    d_ref, turn_ref, chi_ref, clo_ref, ehi_ref, elo_ref, gram_ref, o_ref, rows, rhs, mid
):
    rows[...] = d_ref[...].reshape(1024, 128).astype(F32)
    for vp in range(16):
        lanes = slice(vp * 128, vp * 128 + 128)
        rhs[0:32, lanes] = rows[pl.ds(vp, 32, stride=32), :].astype(BF)
        rhs[32:64, lanes] = rows[pl.ds(16 + vp, 32, stride=32), :].astype(BF)
    first = dot(chi_ref[...], rhs[...]) + dot(clo_ref[...], rhs[...])
    tc = turn_ref[0]
    ts = turn_ref[1]
    for vp in range(16):
        g = first[:, vp * 128 : vp * 128 + 128]
        gr = jnp.concatenate([g[0:32], g[0:32]], axis=0)
        gi = jnp.concatenate([g[32:64], g[32:64]], axis=0)
        mid[:, vp * 256 : vp * 256 + 128] = (gr * tc + gi * ts).astype(BF)
        mid[:, vp * 256 + 128 : vp * 256 + 256] = (gi * tc - gr * ts).astype(BF)
    pieces = []
    for g in range(4):
        m = mid[:, g * 1024 : (g + 1) * 1024]
        pieces.append((dot(m, ehi_ref[...]) + dot(m, elo_ref[...])).astype(BF))
    spec = jnp.concatenate(pieces, axis=1)
    mixed = dot(gram_ref[...], spec)
    lane_slot = (lax.broadcasted_iota(jnp.int32, (64, 512), 1) % 32) // 4
    weighted = jnp.where(lane_slot == 0, mixed[0:64], 0.0)
    for k in range(1, SLOTS):
        weighted = jnp.where(lane_slot == k, mixed[k * 64 : k * 64 + 64], weighted)
    weighted = weighted.astype(BF)
    for g in range(4):
        w = weighted[:, g * 128 : g * 128 + 128]
        z = dot(w, ehi_ref[...], ((1,), (1,))) + dot(w, elo_ref[...], ((1,), (1,)))
        for v in range(4):
            vp = g * 4 + v
            zr = z[:, v * 256 : v * 256 + 128]
            zi = z[:, v * 256 + 128 : v * 256 + 256]
            hr = zr * tc - zi * ts
            hi = zi * tc + zr * ts
            rhs[0:32, vp * 128 : vp * 128 + 128] = (hr[0:32] + hr[32:64]).astype(BF)
            rhs[32:64, vp * 128 : vp * 128 + 128] = (hi[0:32] + hi[32:64]).astype(BF)
    last = dot(chi_ref[...], rhs[...], ((0,), (0,))) + dot(clo_ref[...], rhs[...], ((0,), (0,)))
    for vp in range(16):
        lanes = slice(vp * 128, vp * 128 + 128)
        rows[pl.ds(vp, 32, stride=32), :] = last[0:32, lanes]
        rows[pl.ds(16 + vp, 32, stride=32), :] = last[32:64, lanes]
    o_ref[...] = rows[...].reshape(32, 32, 128).astype(BF)


def synth_kernel(dual_ref, strip_ref, o_ref, across):
    channels = o_ref.shape[0]
    for k in range(FRAMES):
        p = dual_ref[:, k].reshape(channels * ROWS, COLS)
        both = jnp.concatenate([p[:, 0:128], p[:, 128:256]], axis=0)
        a = dot(both, strip_ref[0, k]) + dot(both, strip_ref[1, k])
        a0 = a[0 : channels * ROWS]
        a1 = a[channels * ROWS :]
        out = jnp.concatenate([a0[:, 0:128], a0[:, 128:256] + a1[:, 0:128], a1[:, 128:256]], axis=1)
        for c in range(channels):
            across[c, k * ROWS : (k + 1) * ROWS, :] = out[c * ROWS : (c + 1) * ROWS].astype(BF)
    for c in range(channels):
        total = None
        for t in range(2):
            for k in range(FRAMES):
                term = dot(
                    strip_ref[t, k][0:64, 0:128],
                    across[c, k * ROWS : (k + 1) * ROWS, :],
                    ((0,), (0,)),
                )
                total = term if total is None else total + term
        o_ref[c] = total[0:80, 0:272]


def frames_kernel(bound_ref, probe_ref, dual_ref, strip_ref, o_ref, wide):
    step = pl.program_id(0)
    channels = probe_ref.shape[0]
    bound = bound_ref[step]

    @pl.when(step == 0)
    def _():
        wide[...] = jnp.zeros_like(wide)
        for c in range(channels):
            wide[c * 80 : c * 80 + 80, 0:272] = probe_ref[c].astype(BF)

    def finish(analysis):
        cand = [dual_ref[c, 0].astype(F32) + STEP_DUAL * analysis(c) for c in range(channels)]
        square = cand[0] * cand[0]
        for c in range(1, channels):
            square = square + cand[c] * cand[c]
        magnitude = jnp.sqrt(square)
        factor = bound / jnp.maximum(magnitude, bound)
        for c in range(channels):
            o_ref[c, 0] = (cand[c] * factor).astype(BF)

    @pl.when(step == 0)
    def _():
        finish(lambda c: probe_ref[c, 8:72, 8:264])

    @pl.when(step > 0)
    def _():
        down = []
        for c in range(channels):
            w = wide[c * 80 : c * 80 + 80, :]
            term = dot(strip_ref[0, 0][0:64, 0:80], w) + dot(strip_ref[1, 0][0:64, 0:80], w)
            down.append(term.astype(BF))
        down = jnp.concatenate(down, axis=0)
        both = jnp.concatenate([down[:, 0:256], down[:, 128:384]], axis=0)
        dims = ((1,), (1,))
        a = dot(both, strip_ref[0, 0], dims) + dot(both, strip_ref[1, 0], dims)
        rows = channels * ROWS
        finish(
            lambda c: jnp.concatenate(
                [a[c * ROWS : c * ROWS + ROWS], a[rows + c * ROWS : rows + c * ROWS + ROWS]], axis=1
            )
        )


def call(kernel, out_shape, scratch, flops, moved, *args):
    return pl.pallas_call(
        kernel,
        out_shape=out_shape,
        in_specs=[pl.BlockSpec(memory_space=pltpu.VMEM)] * len(args),
        out_specs=pl.BlockSpec(memory_space=pltpu.VMEM),
        scratch_shapes=scratch,
        compiler_params=pltpu.CompilerParams(vmem_limit_bytes=VMEM_LIMIT),
        cost_estimate=pl.CostEstimate(flops=flops, bytes_accessed=moved, transcendentals=0),
    )(*args)


def padded_2(cells, sides, width):
    for axis, dim in sides:
        count = lax.axis_size(axis)
        ends = count - 1
        head = lax.slice_in_dim(cells, 0, width, axis=dim)
        tail = lax.slice_in_dim(cells, cells.shape[dim] - width, cells.shape[dim], axis=dim)
        cells = jnp.concatenate(
            [
                lax.ppermute(tail, axis, [(i, (i + 1) % count) for i in range(ends)]),
                cells,
                lax.ppermute(head, axis, [((i + 1) % count, i) for i in range(ends)]),
            ],
            axis=dim,
        )
    return cells


def body(
    sky_estimate,
    dual_coeffs,
    dirty_image,
    filters,
    thresholds,
    facet_rows,
    tile_slots,
    tile_count,
    gram_tiles,
):
    channels, tile_rows, tile_cols = sky_estimate.shape
    place = lax.axis_index("fou")
    channel = place // 2
    parity = place % 2

    sent = jnp.repeat(sky_estimate.astype(BF), 2, axis=0)
    lines = lax.all_to_all(sent, "fou", split_axis=0, concat_axis=0, tiled=True)

    line_hi, line_lo = two_terms_np(line_table())
    fold = fold_tables(parity, 1.0)
    fold_back = fold_tables(parity, 1.0 / (PIXELS * PIXELS))
    sign = jnp.full((8, COLS), 1.0, F32) * (1 - 2 * parity).astype(F32)
    slab = jax.ShapeDtypeStruct((PEERS_IMG, 32, 128), BF)
    packed = call(
        forward_kernel, slab, [], 1 << 29, 1 << 20, lines, fold, sign, line_hi, line_lo
    )
    received = lax.all_to_all(packed, "img", split_axis=0, concat_axis=0, tiled=True)

    slots = lax.dynamic_index_in_dim(tile_slots[:, 0], channel, 0, keepdims=False)
    count = lax.dynamic_index_in_dim(tile_count[:, 0], channel, 0, keepdims=False)
    tiles = lax.dynamic_index_in_dim(gram_tiles[:, 0], channel, 0, keepdims=False)
    live_slot = (jnp.arange(SLOTS, dtype=jnp.int32) < count).astype(F32)
    r1 = jnp.arange(64, dtype=jnp.int32)
    ang = (r1[:, None] * slots[None, :] % 32).astype(F32) * (2.0 * math.pi / 32.0)
    ec = jnp.cos(ang) * live_slot
    es = jnp.sin(ang) * live_slot
    pad = ((0, 0), (0, 2))
    ec, es = jnp.pad(ec, pad), jnp.pad(es, pad)
    quad = jnp.stack([jnp.stack([ec, -es], -1), jnp.stack([es, ec], -1)])
    eye2 = jnp.eye(2, dtype=F32)
    one = quad[:, None, :, :, None, :] * eye2[None, :, None, None, :, None]
    one = one.reshape(256, 32)
    eye4 = jnp.eye(4, dtype=F32)
    four = (eye4[:, None, :, None] * one[None, :, None, :]).reshape(1024, 128)
    ehi, elo = two_terms(four)
    gram = jnp.swapaxes(tiles, 1, 2).reshape(SLOTS * 64, 64)

    block_hi, block_lo = two_terms_np(block_table())
    scratch = [
        pltpu.VMEM((1024, 128), F32),
        pltpu.VMEM((64, 2048), BF),
        pltpu.VMEM((64, 4096), BF),
    ]
    weighted = call(
        gram_kernel,
        slab,
        scratch,
        1 << 29,
        1 << 20,
        received,
        turn_table(),
        block_hi,
        block_lo,
        ehi,
        elo,
        gram,
    )
    returned = lax.all_to_all(weighted, "img", split_axis=0, concat_axis=0, tiled=True)
    blocks = call(
        inverse_kernel,
        jax.ShapeDtypeStruct((8, tile_rows, tile_cols), BF),
        [],
        1 << 29,
        1 << 20,
        returned,
        fold_back,
        sign,
        line_hi,
        line_lo,
    )
    halves = lax.all_to_all(blocks, "fou", split_axis=0, concat_axis=0, tiled=True)
    halves = halves.reshape(channels, 2, tile_rows, tile_cols).astype(F32)
    gram_image = halves[:, 0] + halves[:, 1]

    diff = (
        jnp.arange(256, dtype=jnp.int32)[None, :] - jnp.arange(128, dtype=jnp.int32)[:, None]
    )[None]
    strip = jnp.zeros((FRAMES, 128, 256), F32)
    for tap in range(2 * RADIUS + 1):
        strip = jnp.where(diff == tap, filters[:, tap][:, None, None], strip)
    strip = jnp.stack(two_terms(strip))

    spilled = call(
        synth_kernel,
        jax.ShapeDtypeStruct((channels, tile_rows + 16, tile_cols + 16), F32),
        [pltpu.VMEM((channels, FRAMES * ROWS, 384), BF)],
        1 << 31,
        4 << 20,
        dual_coeffs[:, 1:],
        strip,
    )
    double_rad = 2 * RADIUS
    edged = padded_2(spilled, (("img", 1), ("fou", 2)), RADIUS)
    upper_portion = jnp.pad(edged[:, :RADIUS, :], ((0, 0), (0, tile_rows - RADIUS), (0, 0)))
    lower_part = jnp.pad(
        edged[:, tile_rows + 3 * RADIUS :, :], ((0, 0), (tile_rows - RADIUS, 0), (0, 0))
    )
    row_folded = edged[:, double_rad : double_rad + tile_rows, :] + upper_portion + lower_part
    left_part = jnp.pad(row_folded[:, :, :RADIUS], ((0, 0), (0, 0), (0, tile_cols - RADIUS)))
    right_part = jnp.pad(
        row_folded[:, :, tile_cols + 3 * RADIUS :], ((0, 0), (0, 0), (tile_cols - RADIUS, 0))
    )
    folded = row_folded[:, :, double_rad : double_rad + tile_cols] + left_part + right_part
    synthesis = dual_coeffs[:, 0].astype(F32) + folded

    live_rows = (jnp.arange(tile_rows, dtype=jnp.int32) < facet_rows[0]).astype(F32)
    image_next = (
        jnp.maximum(sky_estimate - STEP_PRIMAL * (gram_image - dirty_image + synthesis), 0.0)
        * live_rows[None, :, None]
    )
    probe = 2.0 * image_next - sky_estimate
    beside_all = padded_2(probe, (("img", 1), ("fou", 2)), RADIUS)

    dual_spec = pl.BlockSpec((channels, 1, tile_rows, tile_cols), lambda f: (0, f, 0, 0))
    dual_next = pl.pallas_call(
        frames_kernel,
        out_shape=jax.ShapeDtypeStruct(dual_coeffs.shape, BF),
        grid=(FRAMES + 1,),
        in_specs=[
            pl.BlockSpec(memory_space=pltpu.SMEM),
            pl.BlockSpec(beside_all.shape, lambda f: (0, 0, 0)),
            dual_spec,
            pl.BlockSpec((2, 1, 128, 256), lambda f: (0, jnp.maximum(f - 1, 0), 0, 0)),
        ],
        out_specs=dual_spec,
        scratch_shapes=[pltpu.VMEM((channels * 80, 384), BF)],
        compiler_params=pltpu.CompilerParams(vmem_limit_bytes=VMEM_LIMIT),
        cost_estimate=pl.CostEstimate(flops=1 << 31, bytes_accessed=3 << 20, transcendentals=0),
    )(thresholds, beside_all, dual_coeffs, strip)
    return (image_next, dual_next)


def solution(mesh):
    in_specs = (
        P(None, "img", "fou"),
        P(None, None, "img", "fou"),
        P(None, "img", "fou"),
        P(),
        P(),
        P("img"),
        P(None, "img", None),
        P(None, "img"),
        P(None, "img", None, None, None),
    )
    out_specs = (P(None, "img", "fou"), P(None, None, "img", "fou"))
    return jax.shard_map(body, mesh=mesh, in_specs=in_specs, out_specs=out_specs, check_vma=False)
```

profile of v0, /device:TPU:160, one launch (start us, length us, event | category | flops | bytes accessed | tf_op | source)
XLA Modules:
  0.0 125.5 jit_solution(12958083688211768154)
XLA Ops:
  0.7 1.0 convert_element_type.118
  1.7 0.7 broadcast_in_dim.229
  2.4 5.9 %all-to-all-start = ((bf16[8,64,256]{2,1,0:T(8,128)(2,1)}), bf16[8,64,256]{2,1,0:T(8,128)(2,1)S(1)}, u32[]{:S(2)}, u32[]{:S(2)}) async-start(bf16[8,64,256]{2,1,0:T(8,128)(2,1)} %bitcast), calls=%async_computation | async-start | bytes 524288 | tf_op jit(solution)/shard_map/all_to_all | solution.py:281
  8.7 0.5 slice_reduce_fusion.16
  9.2 0.6 constant_dynamic-slice_fusion
  9.8 0.6 compare_convert_fusion.2
  10.5 0.7 fusion.47
  11.5 0.2 fusion.39
  11.8 4.6 %subtract_convert_fusion = (bf16[1,8,128,256]{3,2,1,0:T(8,128)(2,1)S(1)}, bf16[1,8,128,256]{3,2,1,0:T(8,128)(2,1)}) fusion(f32[8]{0:T(128)S(1)} %get-tuple-element.17, pred[128,256]{1,0:T(8,128)(4,1)S(1)} %get-tuple-element.43, f32[8]{0:T(128)S(1)} %get-tuple-element.18, pred[128,256]{1,0:T(8,128)(4,1)S(1)} %get-tuple-element.44, f32[8]{0:T(128)S(1)} %get-tuple-element.3, ...), kind=kLoop, calls=%fused_computation.1 | loop fusion | flops 9699328 | bytes 1606176 | tf_op jit(solution)/shard_map/convert_element_type | solution.py:33
  16.4 1.5 %shard_map.149 = bf16[32,32,128]{2,1,0:T(8,128)(2,1)} custom-call(bf16[8,64,256]{2,1,0:T(8,128)(2,1)S(1)} %all-to-all-done.x_ref, f32[2,4,4,256]{3,2,1,0:T(4,128)S(1)} %get-tuple-element.34.fold_ref, f32[8,256]{1,0:T(8,128)S(1)} %mul.164.sign_ref, bf16[256,768]{1,0:T(8,128)(2,1)S(1)} %copy-done.5, bf16[256,768]{1,0:T(8,128)(2,1)S(1)} %copy-done.7), custom_call_target="tpu_custom_call" | custom-call | flops 536870912 | bytes 1048576 | tf_op jit(solution)/shard_map/pallas_call | solution.py:236
  17.9 9.8 %all-to-all-start.1 = ((bf16[32,32,128]{2,1,0:T(8,128)(2,1)}), bf16[32,32,128]{2,1,0:T(8,128)(2,1)S(1)}, u32[]{:S(2)}, u32[]{:S(2)}) async-start(bf16[32,32,128]{2,1,0:T(8,128)(2,1)} %shard_map.149), calls=%async_computation.1 | async-start | bytes 524288 | tf_op jit(solution)/shard_map/all_to_all | solution.py:291
  27.7 0.1 broadcast_multiply_fusion
  27.9 1.0 slice.110.dual_ref
  29.0 1.0 copy.19
  30.2 1.2 pad_maximum_fusion.strip_ref
  31.5 4.9 %all-to-all-done.1.d_ref = bf16[32,32,128]{2,1,0:T(8,128)(2,1)S(1)} async-done(((bf16[32,32,128]{2,1,0:T(8,128)(2,1)}), bf16[32,32,128]{2,1,0:T(8,128)(2,1)S(1)}, u32[]{:S(2)}, u32[]{:S(2)}) %all-to-all-start.1) | async-done | bytes 262176 | tf_op jit(solution)/shard_map/all_to_all | solution.py:291
  36.4 0.8 copy-done.9
  37.2 0.7 copy-done.10
  37.9 0.7 copy-done.11
  38.6 3.0 %shard_map.150 = bf16[32,32,128]{2,1,0:T(8,128)(2,1)} custom-call(bf16[32,32,128]{2,1,0:T(8,128)(2,1)S(1)} %all-to-all-done.1.d_ref, f32[2,64,128]{2,1,0:T(8,128)S(1)} %copy-done.9, bf16[64,64]{1,0:T(8,128)(2,1)S(1)} %copy-done.10, bf16[64,64]{1,0:T(8,128)(2,1)S(1)} %copy-done.11, bf16[1024,128]{1,0:T(8,128)(2,1)S(1)} %get-tuple-element.22.ehi_ref, ...), custom_call_target="tpu_custom_call" | custom-call | flops 536870912 | bytes 1048576 | tf_op jit(solution)/shard_map/pallas_call | solution.py:236
  41.7 8.0 %all-to-all-start.2 = ((bf16[32,32,128]{2,1,0:T(8,128)(2,1)}), bf16[32,32,128]{2,1,0:T(8,128)(2,1)S(1)}, u32[]{:S(2)}, u32[]{:S(2)}) async-start(bf16[32,32,128]{2,1,0:T(8,128)(2,1)} %shard_map.150), calls=%async_computation.2 | async-start | bytes 524288 | tf_op jit(solution)/shard_map/all_to_all | solution.py:332
  49.7 1.2 copy-done.2
  50.9 3.4 %shard_map.152 = f32[4,80,272]{2,1,0:T(8,128)S(1)} custom-call(bf16[4,8,64,256]{3,2,1,0:T(8,128)(2,1)S(1)} %copy-done.2, bf16[2,8,128,256]{3,2,1,0:T(8,128)(2,1)S(1)} %pad_maximum_fusion.strip_ref), custom_call_target="tpu_custom_call" | custom-call | flops 2147483648 | bytes 4194304 | tf_op jit(solution)/shard_map/pallas_call | solution.py:236
  54.4 4.5 %collective-permute-start.1 = (f32[4,8,272]{2,1,0:T(8,128)S(1)}, f32[4,8,272]{2,1,0:T(8,128)S(1)}, u32[]{:S(2)}, u32[]{:S(2)}) collective-permute-start(f32[4,8,272]{2,1,0:T(8,128)S(1)} %get-tuple-element.28), channel_id=1, source_target_pairs={{8,0},{16,8},{24,16},{32,24},{40,32},{48,40},{56,48},{64,56},{72,6... | collective-permute-start | bytes 104456 | tf_op jit(solution)/shard_map/ppermute | solution.py:257
  58.9 1.9 %collective-permute-start = (f32[4,8,272]{2,1,0:T(8,128)S(1)}, f32[4,8,272]{2,1,0:T(8,128)S(1)}, u32[]{:S(2)}, u32[]{:S(2)}) collective-permute-start(f32[4,8,272]{2,1,0:T(8,128)S(1)} %get-tuple-element.27), channel_id=1, source_target_pairs={{0,8},{8,16},{16,24},{24,32},{32,40},{40,48},{48,56},{56,64},{64,7... | collective-permute-start | bytes 104456 | tf_op jit(solution)/shard_map/ppermute | solution.py:255
  61.5 7.5 %collective-permute-done = f32[4,8,272]{2,1,0:T(8,128)S(1)} collective-permute-done((f32[4,8,272]{2,1,0:T(8,128)S(1)}, f32[4,8,272]{2,1,0:T(8,128)S(1)}, u32[]{:S(2)}, u32[]{:S(2)}) %collective-permute-start) | collective-permute-done | bytes 34848 | tf_op jit(solution)/shard_map/ppermute | solution.py:255
  68.9 0.8 pad_maximum_fusion.6
  69.7 4.7 %collective-permute-start.3 = (f32[4,96,8]{2,1,0:T(8,128)}, f32[4,96,8]{2,1,0:T(8,128)}, u32[]{:S(2)}, u32[]{:S(2)}) collective-permute-start(f32[4,96,8]{2,1,0:T(8,128)} %get-tuple-element.26), channel_id=1, source_target_pairs={{1,0},{2,1},{3,2},{4,3},{5,4},{6,5},{7,6},{9,8},{10,9},{11,10},{12... | collective-permute-start | bytes 36872 | tf_op jit(solution)/shard_map/ppermute | solution.py:257
  74.5 1.9 %collective-permute-start.2 = (f32[4,96,8]{2,1,0:T(8,128)}, f32[4,96,8]{2,1,0:T(8,128)}, u32[]{:S(2)}, u32[]{:S(2)}) collective-permute-start(f32[4,96,8]{2,1,0:T(8,128)} %get-tuple-element.25), channel_id=1, source_target_pairs={{0,1},{1,2},{2,3},{3,4},{4,5},{5,6},{6,7},{8,9},{9,10},{10,11},{11... | collective-permute-start | bytes 36872 | tf_op jit(solution)/shard_map/ppermute | solution.py:255
  76.4 1.0 copy-done.6
  77.4 1.0 copy-done.8
  78.4 0.6 shard_map.151
  79.0 0.7 copy-done.3
  79.7 6.1 %all-to-all-start.3 = ((bf16[8,64,256]{2,1,0:T(8,128)(2,1)}), bf16[8,64,256]{2,1,0:T(8,128)(2,1)}, u32[]{:S(2)}, u32[]{:S(2)}) async-start(bf16[8,64,256]{2,1,0:T(8,128)(2,1)} %copy-done.3), calls=%async_computation.3 | async-start | bytes 524288 | tf_op jit(solution)/shard_map/all_to_all | solution.py:345
  85.8 1.3 %pad_maximum_fusion.1 = f32[4,96,288]{2,1,0:T(8,128)S(1)} fusion(f32[4,96,8]{2,1,0:T(8,128)} %collective-permute-done.3, f32[4,8,272]{2,1,0:T(8,128)S(1)} %collective-permute-done.1, f32[4,80,272]{2,1,0:T(8,128)S(1)} %shard_map.152, f32[4,8,272]{2,1,0:T(8,128)S(1)} %collective-permute-done, f32[4,96,8]{2,1,0:T(8,128)} %collective-permute-done.2), kind=kLoop, calls=%fused_computation.3 | loop fusion | flops 442368 | bytes 884736 | tf_op jit(solution)/shard_map/concatenate | solution.py:253
  87.1 1.1 fusion
  88.3 3.4 %all-to-all-done.3 = bf16[8,64,256]{2,1,0:T(8,128)(2,1)} async-done(((bf16[8,64,256]{2,1,0:T(8,128)(2,1)}), bf16[8,64,256]{2,1,0:T(8,128)(2,1)}, u32[]{:S(2)}, u32[]{:S(2)}) %all-to-all-start.3) | async-done | bytes 262176 | tf_op jit(solution)/shard_map/all_to_all | solution.py:345
  91.7 1.0 convert.2
  92.7 2.0 %multiply_subtract_fusion = (f32[4,64,256]{2,1,0:T(8,128)S(1)}, f32[4,64,256]{2,1,0:T(8,128)}) fusion(f32[4,64,256]{2,1,0:T(8,128)} %param.14, f32[64]{0:T(128)S(1)} %compare_convert_fusion, f32[4,64,8]{2,1,0:T(8,128)S(1)} %slice.150, f32[4,64,288]{2,1,0:T(8,128)S(1)} %fusion, pred[256]{0:T(512)(128)(4,1)S(1)} %copy-done.17, ...), kind=kLoop, calls=%fused_computation.32 | loop fusion | flops 917504 | bytes 2236928 | tf_op jit(solution)/shard_map/sub | solution.py:385
  94.7 1.9 %collective-permute-start.5 = (f32[4,8,256]{2,1,0:T(8,128)S(1)}, f32[4,8,256]{2,1,0:T(8,128)S(1)}, u32[]{:S(2)}, u32[]{:S(2)}) collective-permute-start(f32[4,8,256]{2,1,0:T(8,128)S(1)} %get-tuple-element.32), channel_id=1, source_target_pairs={{8,0},{16,8},{24,16},{32,24},{40,32},{48,40},{56,48},{64,56},{72,6... | collective-permute-start | bytes 98312 | tf_op jit(solution)/shard_map/ppermute | solution.py:257
  96.6 2.4 %collective-permute-start.4 = (f32[4,8,256]{2,1,0:T(8,128)S(1)}, f32[4,8,256]{2,1,0:T(8,128)S(1)}, u32[]{:S(2)}, u32[]{:S(2)}) collective-permute-start(f32[4,8,256]{2,1,0:T(8,128)S(1)} %get-tuple-element.31), channel_id=1, source_target_pairs={{0,8},{8,16},{16,24},{24,32},{32,40},{40,48},{48,56},{56,64},{64,7... | collective-permute-start | bytes 98312 | tf_op jit(solution)/shard_map/ppermute | solution.py:255
  99.0 7.0 %collective-permute-done.4 = f32[4,8,256]{2,1,0:T(8,128)S(1)} collective-permute-done((f32[4,8,256]{2,1,0:T(8,128)S(1)}, f32[4,8,256]{2,1,0:T(8,128)S(1)}, u32[]{:S(2)}, u32[]{:S(2)}) %collective-permute-start.4) | collective-permute-done | bytes 32800 | tf_op jit(solution)/shard_map/ppermute | solution.py:255
  106.2 3.7 %collective-permute-start.7 = (f32[4,80,8]{2,1,0:T(8,128)S(1)}, f32[4,80,8]{2,1,0:T(8,128)S(1)}, u32[]{:S(2)}, u32[]{:S(2)}) collective-permute-start(f32[4,80,8]{2,1,0:T(8,128)S(1)} %get-tuple-element.30), channel_id=1, source_target_pairs={{1,0},{2,1},{3,2},{4,3},{5,4},{6,5},{7,6},{9,8},{10,9},{11,10},{12... | collective-permute-start | bytes 30728 | tf_op jit(solution)/shard_map/ppermute | solution.py:257
  109.8 2.2 %collective-permute-start.6 = (f32[4,80,8]{2,1,0:T(8,128)S(1)}, f32[4,80,8]{2,1,0:T(8,128)S(1)}, u32[]{:S(2)}, u32[]{:S(2)}) collective-permute-start(f32[4,80,8]{2,1,0:T(8,128)S(1)} %get-tuple-element.29), channel_id=1, source_target_pairs={{0,1},{1,2},{2,3},{3,4},{4,5},{5,6},{6,7},{8,9},{9,10},{10,11},{11... | collective-permute-start | bytes 30728 | tf_op jit(solution)/shard_map/ppermute | solution.py:255
  112.0 1.4 %collective-permute-done.7 = f32[4,80,8]{2,1,0:T(8,128)S(1)} collective-permute-done((f32[4,80,8]{2,1,0:T(8,128)S(1)}, f32[4,80,8]{2,1,0:T(8,128)S(1)}, u32[]{:S(2)}, u32[]{:S(2)}) %collective-permute-start.7) | collective-permute-done | bytes 10272 | tf_op jit(solution)/shard_map/ppermute | solution.py:257
  113.4 5.8 %collective-permute-done.6 = f32[4,80,8]{2,1,0:T(8,128)S(1)} collective-permute-done((f32[4,80,8]{2,1,0:T(8,128)S(1)}, f32[4,80,8]{2,1,0:T(8,128)S(1)}, u32[]{:S(2)}, u32[]{:S(2)}) %collective-permute-start.6) | collective-permute-done | bytes 10272 | tf_op jit(solution)/shard_map/ppermute | solution.py:255
  119.2 0.2 pad_maximum_fusion.2.probe_ref
  119.4 6.1 %shard_map.153 = bf16[4,9,64,256]{3,2,1,0:T(8,128)(2,1)} custom-call(f32[9]{0:T(128)S(1)} %copy-done.4, f32[4,80,272]{2,1,0:T(8,128)S(1)} %pad_maximum_fusion.2.probe_ref, bf16[4,9,64,256]{3,2,1,0:T(8,128)(2,1)S(1)} %copy-done.1, bf16[2,8,128,256]{3,2,1,0:T(8,128)(2,1)S(1)} %pad_maximum_fusion.strip_ref), custom_call_target="tpu_custom_call" | custom-call | flops 2147483648 | bytes 3145728 | tf_op jit(solution)/shard_map/pallas_call | solution.py:389
  (69 shorter events, 1.3 us)
Async XLA Ops:
  0.6 29.4 %copy-start = (bf16[4,1,6,64,64]{4,3,2,1,0:T(8,128)(2,1)S(1)}, bf16[4,1,6,64,64]{4,3,2,1,0:T(8,128)(2,1)}, u32[]{:S(2)}) copy-start(bf16[4,1,6,64,64]{4,3,2,1,0:T(8,128)(2,1)} %param.22) | copy-start | bytes 589828
  0.6 8.1 %copy-start.13 = (f32[8,17]{1,0:T(8,128)S(1)}, f32[8,17]{1,0:T(8,128)}, u32[]{:S(2)}) copy-start(f32[8,17]{1,0:T(8,128)} %param.17) | copy-start | bytes 1636
  0.7 8.6 %copy-start.18 = (s32[4,1]{0,1:T(1,128)S(1)}, s32[4,1]{0,1:T(1,128)}, u32[]{:S(2)}) copy-start(s32[4,1]{0,1:T(1,128)} %param.21) | copy-start | bytes 52
  2.4 14.0 %all-to-all-start = ((bf16[8,64,256]{2,1,0:T(8,128)(2,1)}), bf16[8,64,256]{2,1,0:T(8,128)(2,1)S(1)}, u32[]{:S(2)}, u32[]{:S(2)}) async-start(bf16[8,64,256]{2,1,0:T(8,128)(2,1)} %bitcast), calls=%async_computation | async-start | bytes 524288 | tf_op jit(solution)/shard_map/all_to_all | solution.py:281
  8.6 7.8 %copy-start.5 = (bf16[256,768]{1,0:T(8,128)(2,1)S(1)}, bf16[256,768]{1,0:T(8,128)(2,1)}, u32[]{:S(2)}) copy-start(bf16[256,768]{1,0:T(8,128)(2,1)} %constant.138.clone.whi_ref) | copy-start | bytes 1179652
  8.6 7.8 %copy-start.7 = (bf16[256,768]{1,0:T(8,128)(2,1)S(1)}, bf16[256,768]{1,0:T(8,128)(2,1)}, u32[]{:S(2)}) copy-start(bf16[256,768]{1,0:T(8,128)(2,1)} %constant.139.clone.wlo_ref) | copy-start | bytes 1179652
  16.4 11.5 %copy-start.1 = (bf16[4,9,64,256]{3,2,1,0:T(8,128)(2,1)S(1)}, bf16[4,9,64,256]{3,2,1,0:T(8,128)(2,1)}, u32[]{:S(2)}) copy-start(bf16[4,9,64,256]{3,2,1,0:T(8,128)(2,1)} %dual_ref.1) | copy-start | bytes 3538948
  17.9 18.4 %all-to-all-start.1 = ((bf16[32,32,128]{2,1,0:T(8,128)(2,1)}), bf16[32,32,128]{2,1,0:T(8,128)(2,1)S(1)}, u32[]{:S(2)}, u32[]{:S(2)}) async-start(bf16[32,32,128]{2,1,0:T(8,128)(2,1)} %shard_map.149), calls=%async_computation.1 | async-start | bytes 524288 | tf_op jit(solution)/shard_map/all_to_all | solution.py:291
  30.2 1.2 copy-start.12
  36.4 0.8 copy-start.9
  37.2 0.7 copy-start.10
  37.9 0.7 copy-start.11
  41.7 34.7 %all-to-all-start.2 = ((bf16[32,32,128]{2,1,0:T(8,128)(2,1)}), bf16[32,32,128]{2,1,0:T(8,128)(2,1)S(1)}, u32[]{:S(2)}, u32[]{:S(2)}) async-start(bf16[32,32,128]{2,1,0:T(8,128)(2,1)} %shard_map.150), calls=%async_computation.2 | async-start | bytes 524288 | tf_op jit(solution)/shard_map/all_to_all | solution.py:332
  49.7 1.2 copy-start.2
  54.4 7.1 %collective-permute-start.1 = (f32[4,8,272]{2,1,0:T(8,128)S(1)}, f32[4,8,272]{2,1,0:T(8,128)S(1)}, u32[]{:S(2)}, u32[]{:S(2)}) collective-permute-start(f32[4,8,272]{2,1,0:T(8,128)S(1)} %get-tuple-element.28), channel_id=1, source_target_pairs={{8,0},{16,8},{24,16},{32,24},{40,32},{48,40},{56,48},{64,56},{72,6... | collective-permute-start | bytes 104456 | tf_op jit(solution)/shard_map/ppermute | solution.py:257
  58.9 10.1 %collective-permute-start = (f32[4,8,272]{2,1,0:T(8,128)S(1)}, f32[4,8,272]{2,1,0:T(8,128)S(1)}, u32[]{:S(2)}, u32[]{:S(2)}) collective-permute-start(f32[4,8,272]{2,1,0:T(8,128)S(1)} %get-tuple-element.27), channel_id=1, source_target_pairs={{0,8},{8,16},{16,24},{24,32},{32,40},{40,48},{48,56},{56,64},{64,7... | collective-permute-start | bytes 104456 | tf_op jit(solution)/shard_map/ppermute | solution.py:255
  61.5 24.3 %copy-start.14 = (f32[4,8,272]{2,1,0:T(8,128)}, f32[4,8,272]{2,1,0:T(8,128)S(1)}, u32[]{:S(2)}) copy-start(f32[4,8,272]{2,1,0:T(8,128)S(1)} %collective-permute-done.1) | copy-start | bytes 104452
  68.9 16.9 %copy-start.15 = (f32[4,8,272]{2,1,0:T(8,128)}, f32[4,8,272]{2,1,0:T(8,128)S(1)}, u32[]{:S(2)}) copy-start(f32[4,8,272]{2,1,0:T(8,128)S(1)} %collective-permute-done) | copy-start | bytes 104452
  69.7 16.0 %collective-permute-start.3 = (f32[4,96,8]{2,1,0:T(8,128)}, f32[4,96,8]{2,1,0:T(8,128)}, u32[]{:S(2)}, u32[]{:S(2)}) collective-permute-start(f32[4,96,8]{2,1,0:T(8,128)} %get-tuple-element.26), channel_id=1, source_target_pairs={{1,0},{2,1},{3,2},{4,3},{5,4},{6,5},{7,6},{9,8},{10,9},{11,10},{12... | collective-permute-start | bytes 36872 | tf_op jit(solution)/shard_map/ppermute | solution.py:257
  74.5 11.3 %collective-permute-start.2 = (f32[4,96,8]{2,1,0:T(8,128)}, f32[4,96,8]{2,1,0:T(8,128)}, u32[]{:S(2)}, u32[]{:S(2)}) collective-permute-start(f32[4,96,8]{2,1,0:T(8,128)} %get-tuple-element.25), channel_id=1, source_target_pairs={{0,1},{1,2},{2,3},{3,4},{4,5},{5,6},{6,7},{8,9},{9,10},{10,11},{11... | collective-permute-start | bytes 36872 | tf_op jit(solution)/shard_map/ppermute | solution.py:255
  76.4 1.0 copy-start.6
  77.4 1.0 copy-start.8
  79.0 0.7 copy-start.3
  79.7 7.4 %copy-start.16 = (pred[64]{0:T(512)(128)(4,1)S(1)}, pred[64]{0:T(512)(128)(4,1)}, u32[]{:S(2)}) copy-start(pred[64]{0:T(512)(128)(4,1)} %constant.134.clone.1) | copy-start | bytes 196
  79.7 12.0 %all-to-all-start.3 = ((bf16[8,64,256]{2,1,0:T(8,128)(2,1)}), bf16[8,64,256]{2,1,0:T(8,128)(2,1)}, u32[]{:S(2)}, u32[]{:S(2)}) async-start(bf16[8,64,256]{2,1,0:T(8,128)(2,1)} %copy-done.3), calls=%async_computation.3 | async-start | bytes 524288 | tf_op jit(solution)/shard_map/all_to_all | solution.py:345
  87.1 5.6 %copy-start.17 = (pred[256]{0:T(512)(128)(4,1)S(1)}, pred[256]{0:T(512)(128)(4,1)}, u32[]{:S(2)}) copy-start(pred[256]{0:T(512)(128)(4,1)} %constant.135.clone.1) | copy-start | bytes 772
  94.7 4.3 %collective-permute-start.5 = (f32[4,8,256]{2,1,0:T(8,128)S(1)}, f32[4,8,256]{2,1,0:T(8,128)S(1)}, u32[]{:S(2)}, u32[]{:S(2)}) collective-permute-start(f32[4,8,256]{2,1,0:T(8,128)S(1)} %get-tuple-element.32), channel_id=1, source_target_pairs={{8,0},{16,8},{24,16},{32,24},{40,32},{48,40},{56,48},{64,56},{72,6... | collective-permute-start | bytes 98312 | tf_op jit(solution)/shard_map/ppermute | solution.py:257
  96.6 22.8 %copy-start.4 = (f32[9]{0:T(128)S(1)}, f32[9]{0:T(128)}, u32[]{:S(2)}) copy-start(f32[9]{0:T(128)} %bound_ref.1) | copy-start | bytes 112
  96.6 9.5 %collective-permute-start.4 = (f32[4,8,256]{2,1,0:T(8,128)S(1)}, f32[4,8,256]{2,1,0:T(8,128)S(1)}, u32[]{:S(2)}, u32[]{:S(2)}) collective-permute-start(f32[4,8,256]{2,1,0:T(8,128)S(1)} %get-tuple-element.31), channel_id=1, source_target_pairs={{0,8},{8,16},{16,24},{24,32},{32,40},{40,48},{48,56},{56,64},{64,7... | collective-permute-start | bytes 98312 | tf_op jit(solution)/shard_map/ppermute | solution.py:255
  106.2 7.2 %collective-permute-start.7 = (f32[4,80,8]{2,1,0:T(8,128)S(1)}, f32[4,80,8]{2,1,0:T(8,128)S(1)}, u32[]{:S(2)}, u32[]{:S(2)}) collective-permute-start(f32[4,80,8]{2,1,0:T(8,128)S(1)} %get-tuple-element.30), channel_id=1, source_target_pairs={{1,0},{2,1},{3,2},{4,3},{5,4},{6,5},{7,6},{9,8},{10,9},{11,10},{12... | collective-permute-start | bytes 30728 | tf_op jit(solution)/shard_map/ppermute | solution.py:257
  109.8 9.3 %collective-permute-start.6 = (f32[4,80,8]{2,1,0:T(8,128)S(1)}, f32[4,80,8]{2,1,0:T(8,128)S(1)}, u32[]{:S(2)}, u32[]{:S(2)}) collective-permute-start(f32[4,80,8]{2,1,0:T(8,128)S(1)} %get-tuple-element.29), channel_id=1, source_target_pairs={{0,1},{1,2},{2,3},{3,4},{4,5},{5,6},{6,7},{8,9},{9,10},{10,11},{11... | collective-permute-start | bytes 30728 | tf_op jit(solution)/shard_map/ppermute | solution.py:255
where the time goes:
time: 127 us; the launch traced here: 126 us
  starting transfers between devices  53.1 us (42%)
  waiting for transfers between devices  29.9 us (24%)
  other arithmetic  14.8 us (12%)
  Pallas kernels  14.6 us (11%)
  local copies, waits for them, and re-layouts  11.3 us (9%)
  between operations  1.86 us (1%)
    ppermute x4, waiting for transfers between devices, padded_2(): lax.ppermute(tail, axis, [(i, (i + 1) % count) for i in range(ends)])  20.3 us
    ppermute x4, starting transfers between devices, padded_2(): lax.ppermute(head, axis, [((i + 1) % count, i) for i in range(ends)])  14.8 us
    all_to_all x1, starting transfers between devices, body(): lax.all_to_all(packed, 'img', split_axis=0, concat_axis=0, tiled=True)  9.83 us
    pallas_call x4, Pallas kernels, call(): pl.pallas_call(kernel, out_shape=out_shape, in_specs=[pl.BlockSpec(memory...  8.52 us
    ppermute x4, starting transfers between devices, padded_2(): lax.ppermute(tail, axis, [(i, (i + 1) % count) for i in range(ends)])  8.42 us
    all_to_all x1, starting transfers between devices, body(): lax.all_to_all(weighted, 'img', split_axis=0, concat_axis=0, tiled=True)  8 us
    unnamed x39, local copies, waits for them, and re-layouts  6.34 us
    pallas_call x1, Pallas kernels, body(): pl.pallas_call(frames_kernel, out_shape=jax.ShapeDtypeStruct(dual_coeffs....  6.1 us
  transfers between devices with their start and end apart: 12, of which 6 were waited for; matrix products, arithmetic and copies ran while one was open for 12% of the time, Pallas kernels for 3%

commit v1 on v0

v1 whole, which is shorter than its diff:
```python
import math

import jax
import jax.numpy as jnp
import numpy as np
from jax import lax
from jax.experimental import pallas as pl
from jax.experimental.pallas import tpu as pltpu
from jax.sharding import PartitionSpec as P

PIXELS = 2048
RADIUS = 8
SLOTS = 6
ROWS = 64
COLS = 256
FRAMES = 8
PEERS_IMG = 32
STEP_PRIMAL = 0.5
STEP_DUAL = 0.5
BF = jnp.bfloat16
F32 = jnp.float32
VMEM_LIMIT = 48 << 20
OUTSIDE = -1.0e30
LAST = ((1,), (1,))
FIRST = ((0,), (0,))


def two_terms_np(table):
    high = table.astype(jnp.bfloat16)
    low = (table - high.astype(np.float64)).astype(jnp.bfloat16)
    return high, low


def two_terms(table):
    high = table.astype(BF)
    return high, (table - high.astype(F32)).astype(BF)


def dot(a, b, dims=((1,), (0,))):
    return lax.dot_general(a, b, (dims, ((), ())), preferred_element_type=F32)


def angle_np(a, b, period):
    return 2.0 * np.pi * ((a[:, None] * b[None, :]) % period) / period


def line_table():
    ang = angle_np(np.arange(256), np.arange(256), 256)
    return two_terms_np(np.concatenate([-np.sin(ang), np.cos(ang), np.sin(ang)], axis=1))


def block_table():
    ang = angle_np(np.arange(32), np.arange(32), 32)
    c, s = np.cos(ang), np.sin(ang)
    return two_terms_np(np.block([[c, s], [-s, c]]))


HALO = np.concatenate([np.arange(-8, 0), np.arange(64, 72)])


def turn_table():
    main = np.tile(np.arange(64), 2)
    halo = np.tile(HALO, 8)
    ang = [angle_np(np.arange(64), r, 2048) for r in (main, halo)]
    return np.stack([np.cos(ang[0]), np.sin(ang[0]), np.cos(ang[1]), np.sin(ang[1])]).astype(np.float32)


def tile_table():
    t = np.arange(32)
    ang = angle_np(t, np.arange(64), 32)
    c, s = np.cos(ang), np.sin(ang)
    main = np.zeros((32, 2, 2, 2, 2, 64))
    for p in range(2):
        main[:, p, 0, 0, p] = c
        main[:, p, 1, 0, p] = -s
        main[:, p, 0, 1, p] = s
        main[:, p, 1, 1, p] = c
    ang = angle_np(t, HALO, 32)
    c, s = np.cos(ang), np.sin(ang)
    halo = np.zeros((32, 2, 2, 2, 2, 2, 2, 2, 16))
    for p in range(2):
        for x in range(2):
            halo[:, p, 0, x, 0, 0, x, p] = c
            halo[:, p, 1, x, 0, 0, x, p] = -s
            halo[:, p, 0, x, 1, 0, x, p] = s
            halo[:, p, 1, x, 1, 0, x, p] = c
            halo[:, p, 0, x, 0, 1, x, p] = s
            halo[:, p, 1, x, 0, 1, x, p] = c
            halo[:, p, 0, x, 1, 1, x, p] = -c
            halo[:, p, 1, x, 1, 1, x, p] = s
    table = np.concatenate([main.reshape(128, 256), halo.reshape(128, 512)], axis=1)
    return two_terms_np(table)


def fold_table():
    freq = np.arange(2)[:, None] + 2 * np.arange(4)[None]
    pos = np.arange(4 * COLS).reshape(4, COLS)
    ang = 2.0 * np.pi * ((freq[:, :, None, None] * pos) % PIXELS) / PIXELS
    return np.stack([np.cos(ang), np.sin(ang)], axis=1).astype(np.float32)


def forward_kernel(par_ref, x_ref, fold_ref, line_ref, o_ref):
    par = par_ref[1]
    sign = (1 - 2 * par).astype(F32)
    xe = [x_ref[f].astype(F32) + sign * x_ref[f + 4].astype(F32) for f in range(4)]
    parts = [[], []]
    for chi in range(2):
        rows_re, rows_im = [], []
        for clo in range(2):
            cos = fold_ref[par, 0, 2 * chi + clo]
            sin = fold_ref[par, 1, 2 * chi + clo]
            yr = xe[0] * cos[0:1]
            yi = xe[0] * sin[0:1]
            for f in range(1, 4):
                yr = yr + xe[f] * cos[f : f + 1]
                yi = yi + xe[f] * sin[f : f + 1]
            yi = -yi
            rows_re.append(jnp.concatenate([yr, yi], axis=1))
            rows_im.append(jnp.concatenate([yi, -yr], axis=1))
        for part, rows in enumerate((rows_re, rows_im)):
            r = jnp.concatenate(rows, axis=0).astype(BF)
            out = dot(line_ref[0, :, 256:768], r, LAST) + dot(line_ref[1, :, 256:768], r, LAST)
            parts[part].append(out.reshape(32, 8, 128))
    for part in range(2):
        both = jnp.concatenate(parts[part], axis=1)
        o_ref[:, part * 16 : (part + 1) * 16, :] = both.astype(BF)


def inverse_kernel(par_ref, t_ref, fold_ref, line_ref, o_ref):
    par = par_ref[1]
    sign = (1 - 2 * par).astype(F32)
    re = t_ref[:, 0:16, :].astype(F32)
    im = t_ref[:, 16:32, :].astype(F32)
    edge = t_ref[:, 32:40, :].astype(F32).reshape(256, 128).astype(BF)
    h = dot(edge, line_ref[0], FIRST) + dot(edge, line_ref[1], FIRST)
    h = h[0:64, 256:768] + h[64:128, 0:512]
    total = [None] * 4
    for chi in range(2):
        a = re[:, chi * 8 : chi * 8 + 8, :].reshape(256, 128).astype(BF)
        b = im[:, chi * 8 : chi * 8 + 8, :].reshape(256, 128).astype(BF)
        u = None
        for t in range(2):
            term = dot(a, line_ref[t, :, 256:768], FIRST) + dot(b, line_ref[t, :, 0:512], FIRST)
            u = term if u is None else u + term
        for clo in range(2):
            cls = 2 * chi + clo
            e = h[cls * 16 : cls * 16 + 16]
            whole = jnp.concatenate([e[0:8], u[clo * 64 : clo * 64 + 64], e[8:16]], axis=0)
            ur = whole[:, 0:256]
            ui = whole[:, 256:512]
            cos = fold_ref[par, 0, cls]
            sin = fold_ref[par, 1, cls]
            for f in range(4):
                g = ur * cos[f : f + 1] - ui * sin[f : f + 1]
                total[f] = g if total[f] is None else total[f] + g
    scale = 1.0 / (PIXELS * PIXELS)
    total = [g * scale for g in total]
    total = total + [sign * g for g in total]
    none = jnp.zeros((80, 128), F32)
    for f in range(8):
        before = total[f - 1][:, 128:256] if f > 0 else none
        after = total[f + 1][:, 0:128] if f < 7 else none
        line = jnp.concatenate([before, total[f], after], axis=1)
        o_ref[f] = pltpu.roll(line, 512 - 120, 1)[:, 0:384].astype(BF)


def tiles_kernel(where_ref, slots_ref, count_ref, tiles_ref, table_ref, o_ref, gram_ref):
    channel = where_ref[0]
    left = lax.broadcasted_iota(jnp.int32, (32, 128), 0)
    right = lax.broadcasted_iota(jnp.int32, (32, 128), 1)
    tile = jnp.full((32, 128), -1, jnp.int32)
    for k in range(SLOTS):
        slot = jnp.where(k < count_ref[channel, 0], slots_ref[channel, 0, k], -1)
        tile = jnp.where(left // 4 == k, slot, tile)
    pick = (tile == right // 4) & (left % 4 == right % 4)
    pick = jnp.where(pick, 1.0, 0.0).astype(BF)
    for k in range(SLOTS):
        gram_ref[k * 64 : k * 64 + 64, :] = tiles_ref[channel, 0, k].astype(F32).T.astype(BF)
    o_ref[...] = jnp.zeros_like(o_ref)
    for t in range(2):
        row = dot(pick, table_ref[t]).astype(BF)
        for j in range(2):
            for chi in range(2):
                p = 2 * j + chi
                rows = slice(p * 32, p * 32 + 32)
                o_ref[t, rows, p * 256 : p * 256 + 256] = row[:, 0:256]
                for comp in range(2):
                    at = 256 + chi * 256 + comp * 128
                    to = 1024 + comp * 256 + j * 128
                    o_ref[t, rows, to : to + 128] = row[:, at : at + 128]


def gram_kernel(d_ref, turn_ref, block_ref, e_ref, gram_ref, o_ref, rows, rhs, mid, edge):
    rows[0:1024, :] = d_ref[...].reshape(1024, 128).astype(F32)
    for p in range(16):
        lanes = slice(p * 128, p * 128 + 128)
        at = (p % 2) * 8 + p // 2
        rhs[0:32, lanes] = rows[pl.ds(at, 32, stride=32), :].astype(BF)
        rhs[32:64, lanes] = rows[pl.ds(16 + at, 32, stride=32), :].astype(BF)
    first = dot(block_ref[0], rhs[...]) + dot(block_ref[1], rhs[...])
    tc, ts, ec, es = turn_ref[0], turn_ref[1], turn_ref[2], turn_ref[3]
    for p in range(16):
        g = first[:, p * 128 : p * 128 + 128]
        gr = jnp.concatenate([g[0:32], g[0:32]], axis=0)
        gi = jnp.concatenate([g[32:64], g[32:64]], axis=0)
        mid[:, p * 256 : p * 256 + 128] = (gr * tc + gi * ts).astype(BF)
        mid[:, p * 256 + 128 : p * 256 + 256] = (gi * tc - gr * ts).astype(BF)
    pieces = []
    for g in range(4):
        m = mid[:, g * 1024 : (g + 1) * 1024]
        pieces.append((dot(m, e_ref[0, :, 0:1024], LAST) + dot(m, e_ref[1, :, 0:1024], LAST)).astype(BF))
    spec = jnp.concatenate(pieces, axis=1)
    mixed = dot(gram_ref[...], spec)
    lane_slot = (lax.broadcasted_iota(jnp.int32, (64, 512), 1) % 32) // 4
    weighted = jnp.where(lane_slot == 0, mixed[0:64], 0.0)
    for k in range(1, SLOTS):
        weighted = jnp.where(lane_slot == k, mixed[k * 64 : k * 64 + 64], weighted)
    weighted = weighted.astype(BF)
    for g in range(4):
        w = weighted[:, g * 128 : g * 128 + 128]
        z = dot(w, e_ref[0]) + dot(w, e_ref[1])
        for v in range(4):
            p = g * 4 + v
            zr = z[:, v * 256 : v * 256 + 128]
            zi = z[:, v * 256 + 128 : v * 256 + 256]
            hr = zr * tc - zi * ts
            hi = zi * tc + zr * ts
            rhs[0:32, p * 128 : p * 128 + 128] = (hr[0:32] + hr[32:64]).astype(BF)
            rhs[32:64, p * 128 : p * 128 + 128] = (hi[0:32] + hi[32:64]).astype(BF)
        for j in range(2):
            zr = z[:, 1024 + j * 128 : 1152 + j * 128]
            zi = z[:, 1280 + j * 128 : 1408 + j * 128]
            hr = zr * ec - zi * es
            hi = zi * ec + zr * es
            lanes = slice((2 * g + j) * 128, (2 * g + j) * 128 + 128)
            edge[0:32, lanes] = (hr[0:32] + hr[32:64]).astype(BF)
            edge[32:64, lanes] = (hi[0:32] + hi[32:64]).astype(BF)
    last = dot(block_ref[0], rhs[...], FIRST) + dot(block_ref[1], rhs[...], FIRST)
    outer = dot(block_ref[0, :, 0:32], edge[...], FIRST) + dot(block_ref[1, :, 0:32], edge[...], FIRST)
    for p in range(16):
        lanes = slice(p * 128, p * 128 + 128)
        at = (p % 2) * 8 + p // 2
        rows[pl.ds(at, 32, stride=40), :] = last[0:32, lanes]
        rows[pl.ds(16 + at, 32, stride=40), :] = last[32:64, lanes]
    for v in range(8):
        rows[pl.ds(32 + v, 32, stride=40), :] = outer[:, v * 128 : v * 128 + 128]
    o_ref[...] = rows[...].reshape(32, 40, 128).astype(BF)


def band_kernel(taps_ref, strip_ref, down_ref):
    lane = lax.broadcasted_iota(jnp.int32, (64, 256), 1)
    for k in range(FRAMES):
        wide = jnp.broadcast_to(taps_ref[k : k + 1, :], (128, 256))
        band = pltpu.roll(wide, 0, 1, stride=1, stride_axis=0)
        high = band.astype(BF)
        low = band - high.astype(F32)
        strip_ref[0, k] = high
        strip_ref[1, k] = low.astype(BF)
        high = jnp.where(lane < 80, high[0:64].astype(F32), 0.0)
        low = jnp.where(lane < 80, low[0:64], 0.0)
        row = high + pltpu.roll(high, 80, 1) + pltpu.roll(low, 160, 1)
        down_ref[k * 64 : k * 64 + 64, :] = row.astype(BF)


def synth_kernel(
    where_ref, live_ref, dual_ref, sky_ref, dirty_ref, strip_ref, o_ref, head_ref, tail_ref, across
):
    channels = sky_ref.shape[0]
    row = lax.broadcasted_iota(jnp.int32, (80, 272), 0) + where_ref[2] * ROWS - RADIUS
    col = lax.broadcasted_iota(jnp.int32, (80, 272), 1) + where_ref[3] * COLS - RADIUS
    inside = (row >= 0) & (row < PIXELS) & (col >= 0) & (col < PIXELS)
    for k in range(FRAMES):
        p = dual_ref[:, k + 1].reshape(channels * ROWS, COLS)
        both = jnp.concatenate([p[:, 0:128], p[:, 128:256]], axis=0)
        a = dot(both, strip_ref[0, k]) + dot(both, strip_ref[1, k])
        a0 = a[0 : channels * ROWS]
        a1 = a[channels * ROWS :]
        out = jnp.concatenate([a0[:, 0:128], a0[:, 128:256] + a1[:, 0:128], a1[:, 128:256]], axis=1)
        for c in range(channels):
            across[c, k * ROWS : (k + 1) * ROWS, :] = out[c * ROWS : (c + 1) * ROWS].astype(BF)
    live = lax.broadcasted_iota(jnp.int32, (ROWS, COLS), 0) < live_ref[0]
    none = jnp.zeros((ROWS, 128), F32)
    edge = jnp.zeros((8, 272), F32)
    for c in range(channels):
        total = None
        for t in range(2):
            for k in range(FRAMES):
                term = dot(
                    strip_ref[t, k][0:64, 0:128],
                    across[c, k * ROWS : (k + 1) * ROWS, :],
                    FIRST,
                )
                total = term if total is None else total + term
        sky = sky_ref[c]
        own = sky + STEP_PRIMAL * dirty_ref[c] - STEP_PRIMAL * dual_ref[c, 0].astype(F32)
        own = jnp.where(live, own, OUTSIDE)
        own = pltpu.roll(jnp.concatenate([own, none], axis=1), 8, 1)[:, 0:272]
        sky = pltpu.roll(jnp.concatenate([sky, none], axis=1), 8, 1)[:, 0:272]
        total = total[0:80, 0:272] * (-STEP_PRIMAL)
        total = total + jnp.concatenate([edge, own, edge], axis=0)
        total = jnp.where(inside, total, OUTSIDE)
        sky = jnp.concatenate([edge, sky, edge], axis=0)
        for at, cells in ((c, total), (channels + c, sky)):
            o_ref[at] = cells
            head_ref[at] = cells[0:16].astype(BF)
            tail_ref[at] = cells[64:80].astype(BF)


def frames_kernel(bound_ref, half_ref, base_ref, dual_ref, strip_ref, down_ref, image_ref, o_ref, probes, wide, down):
    step = pl.program_id(0)
    channels = image_ref.shape[0]
    bound = bound_ref[step]

    def finish(analysis):
        cand = [dual_ref[c, 0].astype(F32) + STEP_DUAL * analysis(c) for c in range(channels)]
        square = cand[0] * cand[0]
        for c in range(1, channels):
            square = square + cand[c] * cand[c]
        factor = bound * lax.rsqrt(jnp.maximum(square, bound * bound))
        for c in range(channels):
            o_ref[c, 0] = (cand[c] * factor).astype(BF)

    @pl.when(step == 0)
    def _():
        wide[...] = jnp.zeros_like(wide)
        for c in range(channels):
            gram = half_ref[2 * c, :, 0:272].astype(F32) + half_ref[2 * c + 1, :, 0:272].astype(F32)
            image = jnp.maximum(base_ref[c] - STEP_PRIMAL * gram, 0.0)
            probe = 2.0 * image - base_ref[channels + c]
            image_ref[c] = image[8:72, 8:264]
            probes[c] = probe[8:72, 8:264]
            high = probe.astype(BF)
            low = (probe - high.astype(F32)).astype(BF)
            wide[0:80, 0:272] = high
            wide[80:160, 0:272] = low
            wide[160:240, 0:272] = high
            d = dot(down_ref[...], wide[...])
            high = d.astype(BF)
            down[0, c] = high
            down[1, c] = (d - high.astype(F32)).astype(BF)
        finish(lambda c: probes[c])

    @pl.when(step > 0)
    def _():
        at = pl.multiple_of((step - 1) * ROWS, ROWS)
        a = None
        for t in range(2):
            d = jnp.concatenate([down[t, c, pl.ds(at, ROWS), :] for c in range(channels)], axis=0)
            both = jnp.concatenate([d[:, 0:256], d[:, 128:384]], axis=0)
            term = dot(both, strip_ref[0, 0], LAST)
            a = term if a is None else a + term
            if t == 0:
                a = a + dot(both, strip_ref[1, 0], LAST)
        rows = channels * ROWS
        finish(
            lambda c: jnp.concatenate(
                [a[c * ROWS : c * ROWS + ROWS], a[rows + c * ROWS : rows + c * ROWS + ROWS]], axis=1
            )
        )


VM = pl.BlockSpec(memory_space=pltpu.VMEM)
SM = pl.BlockSpec(memory_space=pltpu.SMEM)


def call(kernel, out_shape, scratch, flops, moved, *args, scalars=0):
    return pl.pallas_call(
        kernel,
        out_shape=out_shape,
        in_specs=[SM] * scalars + [VM] * (len(args) - scalars),
        out_specs=jax.tree.map(lambda _: VM, out_shape),
        scratch_shapes=scratch,
        compiler_params=pltpu.CompilerParams(vmem_limit_bytes=VMEM_LIMIT),
        cost_estimate=pl.CostEstimate(flops=flops, bytes_accessed=moved, transcendentals=0),
    )(*args)


def overlap_add(cells, head, tail, axis, dim):
    count = lax.axis_size(axis)
    room = cells.shape[dim] - 2 * RADIUS
    from_before = lax.ppermute(tail, axis, [(i, i + 1) for i in range(count - 1)])
    from_after = lax.ppermute(head, axis, [(i + 1, i) for i in range(count - 1)])
    width = [(0, 0)] * cells.ndim
    width[dim] = (0, room)
    cells = cells + jnp.pad(from_before, width).astype(F32)
    width[dim] = (room, 0)
    return cells + jnp.pad(from_after, width).astype(F32)


def after(values, event):
    return lax.optimization_barrier((*values, event))[:-1]


def body(
    sky_estimate,
    dual_coeffs,
    dirty_image,
    filters,
    thresholds,
    facet_rows,
    tile_slots,
    tile_count,
    gram_tiles,
):
    channels, tile_rows, tile_cols = sky_estimate.shape
    place = lax.axis_index("fou")
    where = jnp.stack([place >> 1, place & 1, lax.axis_index("img"), place]).astype(jnp.int32)

    sent = jnp.repeat(sky_estimate.astype(BF), 2, axis=0)
    lines = lax.all_to_all(sent, "fou", split_axis=0, concat_axis=0, tiled=True)

    line = np.stack(line_table())
    fold = fold_table()
    packed = call(
        forward_kernel,
        jax.ShapeDtypeStruct((PEERS_IMG, 32, 128), BF),
        [],
        1 << 29,
        1 << 20,
        where,
        lines,
        fold,
        line,
        scalars=1,
    )
    received = lax.all_to_all(packed, "img", split_axis=0, concat_axis=0, tiled=True)

    spread, gram = call(
        tiles_kernel,
        (jax.ShapeDtypeStruct((2, 128, 1536), BF), jax.ShapeDtypeStruct((SLOTS * 64, 64), BF)),
        [],
        1 << 23,
        1 << 20,
        where,
        tile_slots,
        tile_count,
        gram_tiles,
        np.stack(tile_table()),
        scalars=3,
    )

    scratch = [
        pltpu.VMEM((1280, 128), F32),
        pltpu.VMEM((64, 2048), BF),
        pltpu.VMEM((64, 4096), BF),
        pltpu.VMEM((64, 1024), BF),
    ]
    weighted = call(
        gram_kernel,
        jax.ShapeDtypeStruct((PEERS_IMG, 40, 128), BF),
        scratch,
        1 << 29,
        1 << 20,
        received,
        turn_table(),
        np.stack(block_table()),
        spread,
        gram,
    )
    returned = lax.all_to_all(weighted, "img", split_axis=0, concat_axis=0, tiled=True)
    blocks = call(
        inverse_kernel,
        jax.ShapeDtypeStruct((8, tile_rows + 16, 384), BF),
        [],
        1 << 29,
        1 << 20,
        where,
        returned,
        fold,
        line,
        scalars=1,
    )
    halves = lax.all_to_all(blocks, "fou", split_axis=0, concat_axis=0, tiled=True)

    strip, down = call(
        band_kernel,
        (
            jax.ShapeDtypeStruct((2, FRAMES, 128, 256), BF),
            jax.ShapeDtypeStruct((FRAMES * ROWS, 256), BF),
        ),
        [],
        1 << 20,
        1 << 20,
        jnp.pad(filters, ((0, 0), (0, 256 - filters.shape[1]))),
    )
    ends = jax.ShapeDtypeStruct((2 * channels, 16, tile_cols + 16), BF)
    base, head, tail = call(
        synth_kernel,
        (jax.ShapeDtypeStruct((2 * channels, tile_rows + 16, tile_cols + 16), F32), ends, ends),
        [pltpu.VMEM((channels, FRAMES * ROWS, 384), BF)],
        1 << 31,
        4 << 20,
        where,
        facet_rows,
        dual_coeffs,
        sky_estimate,
        dirty_image,
        strip,
        scalars=2,
    )
    head, tail = after((head, tail), packed)
    base = overlap_add(base, head, tail, "img", 1)
    head, tail = base[:, :, 0:16].astype(BF), base[:, :, tile_cols : tile_cols + 16].astype(BF)
    head, tail = after((head, tail), weighted)
    base = overlap_add(base, head, tail, "fou", 2)

    dual_spec = pl.BlockSpec((channels, 1, tile_rows, tile_cols), lambda f: (0, f, 0, 0))
    whole = lambda a: pl.BlockSpec(a.shape, lambda f: (0,) * a.ndim)
    return pl.pallas_call(
        frames_kernel,
        out_shape=(
            jax.ShapeDtypeStruct(sky_estimate.shape, F32),
            jax.ShapeDtypeStruct(dual_coeffs.shape, BF),
        ),
        grid=(FRAMES + 1,),
        in_specs=[
            SM,
            whole(halves),
            whole(base),
            dual_spec,
            pl.BlockSpec((2, 1, 128, 256), lambda f: (0, jnp.maximum(f - 1, 0), 0, 0)),
            whole(down),
        ],
        out_specs=(pl.BlockSpec(sky_estimate.shape, lambda f: (0, 0, 0)), dual_spec),
        scratch_shapes=[
            pltpu.VMEM(sky_estimate.shape, F32),
            pltpu.VMEM((256, 384), BF),
            pltpu.VMEM((2, channels, FRAMES * ROWS, 384), BF),
        ],
        compiler_params=pltpu.CompilerParams(vmem_limit_bytes=VMEM_LIMIT),
        cost_estimate=pl.CostEstimate(flops=1 << 31, bytes_accessed=3 << 20, transcendentals=0),
    )(thresholds, halves, base, dual_coeffs, strip, down)


def solution(mesh):
    in_specs = (
        P(None, "img", "fou"),
        P(None, None, "img", "fou"),
        P(None, "img", "fou"),
        P(),
        P(),
        P("img"),
        P(None, "img", None),
        P(None, "img"),
        P(None, "img", None, None, None),
    )
    out_specs = (P(None, "img", "fou"), P(None, None, "img", "fou"))
    return jax.shard_map(body, mesh=mesh, in_specs=in_specs, out_specs=out_specs, check_vma=False)
```

time: 127 us -> 96 us (0.76)
  the two profiles are of different devices: /device:TPU:160 before, /device:TPU:152 now
where the time goes in v1:
time: 96 us; the launch traced here: 95.2 us
  starting transfers between devices  45 us (47%)
  waiting for transfers between devices  19.7 us (21%)
  Pallas kernels  19.4 us (20%)
  local copies, waits for them, and re-layouts  7.37 us (8%)
  other arithmetic  2.24 us (2%)
  between operations  1.54 us (2%)
    pallas_call x6, Pallas kernels, call(): pl.pallas_call(kernel, out_shape=out_shape, in_specs=[SM] * scalars + [VM...  13 us
    ppermute x2, starting transfers between devices, overlap_add(): lax.ppermute(head, axis, [(i + 1, i) for i in range(count - 1)])  10.2 us
    all_to_all x1, starting transfers between devices, body(): lax.all_to_all(packed, 'img', split_axis=0, concat_axis=0, tiled=True)  9.83 us
    all_to_all x1, waiting for transfers between devices, body(): lax.all_to_all(packed, 'img', split_axis=0, concat_axis=0, tiled=True)  8.13 us
    all_to_all x1, starting transfers between devices, body(): lax.all_to_all(weighted, 'img', split_axis=0, concat_axis=0, tiled=True)  7.8 us
    unnamed x45, local copies, waits for them, and re-layouts  6.58 us
    all_to_all x1, starting transfers between devices, body(): lax.all_to_all(blocks, 'fou', split_axis=0, concat_axis=0, tiled=True)  6.44 us
    pallas_call x1, Pallas kernels, body(): pl.pallas_call(frames_kernel, out_shape=(jax.ShapeDtypeStruct(sky_estimat...  6.44 us
  transfers between devices with their start and end apart: 8, of which 4 were waited for; matrix products, arithmetic and copies ran while one was open for 1% of the time, Pallas kernels for 8%

profile of v1, /device:TPU:152, one launch (start us, length us, event | category | flops | bytes accessed | tf_op | source)
XLA Modules:
  0.0 95.2 jit_solution(14561413833974985893)
XLA Ops:
  0.6 0.0 copy-start.12
  0.6 0.0 copy-start.15
  0.7 1.0 %convert_element_type.27 = bf16[4,64,256]{2,1,0:T(8,128)(2,1)S(1)} convert(f32[4,64,256]{2,1,0:T(8,128)} %sky_ref.1) | non-fusion elementwise | flops 65536 | bytes 393216 | tf_op jit(solution)/shard_map/convert_element_type | solution.py:409
  1.7 0.7 broadcast_in_dim.3
  2.4 5.1 %all-to-all-start = ((bf16[8,64,256]{2,1,0:T(8,128)(2,1)}), bf16[8,64,256]{2,1,0:T(8,128)(2,1)S(1)}, u32[]{:S(2)}, u32[]{:S(2)}) async-start(bf16[8,64,256]{2,1,0:T(8,128)(2,1)} %bitcast.4), calls=%async_computation | async-start | bytes 524288 | tf_op jit(solution)/shard_map/all_to_all | solution.py:410
  7.6 0.1 pad_add_fusion.par_ref.where_ref
  7.7 0.0 copy-start.14
  7.7 4.7 %all-to-all-done.x_ref = bf16[8,64,256]{2,1,0:T(8,128)(2,1)S(1)} async-done(((bf16[8,64,256]{2,1,0:T(8,128)(2,1)}), bf16[8,64,256]{2,1,0:T(8,128)(2,1)S(1)}, u32[]{:S(2)}, u32[]{:S(2)}) %all-to-all-start) | async-done | bytes 262176 | tf_op jit(solution)/shard_map/all_to_all | solution.py:410
  12.4 0.0 copy-done.12
  12.4 0.0 copy-done.15
  12.4 2.0 %shard_map.149 = bf16[32,32,128]{2,1,0:T(8,128)(2,1)} custom-call(s32[4]{0:T(128)S(1)} %pad_add_fusion.par_ref.where_ref, bf16[8,64,256]{2,1,0:T(8,128)(2,1)S(1)} %all-to-all-done.x_ref, f32[2,2,4,4,256]{4,3,2,1,0:T(4,128)S(1)} %copy-done.15, bf16[2,256,768]{2,1,0:T(8,128)(2,1)S(1)} %copy-done.12), custom_call_target="tpu_custom_call" | custom-call | flops 536870912 | bytes 1048576 | tf_op jit(solution)/shard_map/pallas_call | solution.py:367
  14.4 9.8 %all-to-all-start.1 = ((bf16[32,32,128]{2,1,0:T(8,128)(2,1)}), bf16[32,32,128]{2,1,0:T(8,128)(2,1)S(1)}, u32[]{:S(2)}, u32[]{:S(2)}) async-start(bf16[32,32,128]{2,1,0:T(8,128)(2,1)} %shard_map.149), calls=%async_computation.1 | async-start | bytes 524288 | tf_op jit(solution)/shard_map/all_to_all | solution.py:426
  24.3 0.1 copy.16.count_ref
  24.4 0.8 shard_map.150
  25.2 8.1 %all-to-all-done.1.d_ref = bf16[32,32,128]{2,1,0:T(8,128)(2,1)S(1)} async-done(((bf16[32,32,128]{2,1,0:T(8,128)(2,1)}), bf16[32,32,128]{2,1,0:T(8,128)(2,1)S(1)}, u32[]{:S(2)}, u32[]{:S(2)}) %all-to-all-start.1) | async-done | bytes 262176 | tf_op jit(solution)/shard_map/all_to_all | solution.py:426
  33.3 0.8 copy-done.17
  34.1 3.1 %shard_map.151 = bf16[32,40,128]{2,1,0:T(8,128)(2,1)} custom-call(bf16[32,32,128]{2,1,0:T(8,128)(2,1)S(1)} %all-to-all-done.1.d_ref, f32[4,64,128]{2,1,0:T(8,128)S(1)} %copy-done.14, bf16[2,64,64]{2,1,0:T(8,128)(2,1)S(1)} %copy-done.17, bf16[2,128,1536]{2,1,0:T(8,128)(2,1)S(1)} %get-tuple-element.13.e_ref, bf16[384,64]{1,0:T(8,128)(2,1)S(1)} %get-tuple-element.14.gram_ref), custom_call_target="tpu_custom_call" | custom-call | flops 536870912 | bytes 1048576 | tf_op jit(solution)/shard_map/pallas_call | solution.py:367
  37.2 7.8 %all-to-all-start.2 = ((bf16[32,40,128]{2,1,0:T(8,128)(2,1)}), bf16[32,40,128]{2,1,0:T(8,128)(2,1)S(1)}, u32[]{:S(2)}, u32[]{:S(2)}) async-start(bf16[32,40,128]{2,1,0:T(8,128)(2,1)} %shard_map.151), calls=%async_computation.2 | async-start | bytes 655360 | tf_op jit(solution)/shard_map/all_to_all | solution.py:460
  45.6 0.8 shard_map.153
  46.5 0.0 copy-start.9
  46.5 0.7 copy-done.9
  47.2 0.0 copy-done.2
  47.2 1.1 %copy-done.8 = f32[4,64,256]{2,1,0:T(8,128)S(1)} copy-done((f32[4,64,256]{2,1,0:T(8,128)S(1)}, f32[4,64,256]{2,1,0:T(8,128)}, u32[]{:S(2)}) %copy-start.8) | copy-done | bytes 262168
  48.3 4.0 %shard_map.154 = (f32[8,80,272]{2,1,0:T(8,128)S(1)}, bf16[8,16,272]{2,1,0:T(8,128)(2,1)S(1)}, bf16[8,16,272]{2,1,0:T(8,128)(2,1)S(1)}) custom-call(s32[4]{0:T(128)S(1)} %pad_add_fusion.par_ref.where_ref, s32[1]{0:T(128)S(6)} %copy.17.live_ref, bf16[4,9,64,256]{3,2,1,0:T(8,128)(2,1)S(1)} %copy-done.4, f32[4,64,256]{2,1,0:T(8,128)S(1)} %copy-done.2, ...), custom_call_target="tpu_custom_call" | custom-call | flops 2147483648 | bytes 4194304 | tf_op jit(solution)/shard_map/pallas_call | solution.py:367
  52.4 2.1 %collective-permute-start = (bf16[8,16,272]{2,1,0:T(8,128)(2,1)S(1)}, bf16[8,16,272]{2,1,0:T(8,128)(2,1)S(1)}, u32[]{:S(2)}, u32[]{:S(2)}) collective-permute-start(bf16[8,16,272]{2,1,0:T(8,128)(2,1)S(1)} %get-tuple-element.19), channel_id=1, source_target_pairs={{0,8},{8,16},{16,24},{24,32},{32,40},{40,48},{48,56},{56,64},{64,7... | collective-permute-start | bytes 208904 | tf_op jit(solution)/shard_map/ppermute | solution.py:381
  54.4 7.7 %collective-permute-start.1 = (bf16[8,16,272]{2,1,0:T(8,128)(2,1)S(1)}, bf16[8,16,272]{2,1,0:T(8,128)(2,1)S(1)}, u32[]{:S(2)}, u32[]{:S(2)}) collective-permute-start(bf16[8,16,272]{2,1,0:T(8,128)(2,1)S(1)} %get-tuple-element.20), channel_id=1, source_target_pairs={{8,0},{16,8},{24,16},{32,24},{40,32},{48,40},{56,48},{64,56},{72,6... | collective-permute-start | bytes 208904 | tf_op jit(solution)/shard_map/ppermute | solution.py:382
  62.2 0.0 all-to-all-done.2.t_ref
  62.2 0.0 copy-done.16
  62.2 0.0 copy-start.13
  62.2 1.1 %copy-done.13 = bf16[2,256,768]{2,1,0:T(8,128)(2,1)S(1)} copy-done((bf16[2,256,768]{2,1,0:T(8,128)(2,1)S(1)}, bf16[2,256,768]{2,1,0:T(8,128)(2,1)}, u32[]{:S(2)}) %copy-start.13) | copy-done | bytes 786456
  63.3 2.2 %shard_map.152 = bf16[8,80,384]{2,1,0:T(8,128)(2,1)} custom-call(s32[4]{0:T(128)S(1)} %pad_add_fusion.par_ref.where_ref, bf16[32,40,128]{2,1,0:T(8,128)(2,1)S(1)} %all-to-all-done.2.t_ref, f32[2,2,4,4,256]{4,3,2,1,0:T(4,128)S(1)} %copy-done.16, bf16[2,256,768]{2,1,0:T(8,128)(2,1)S(1)} %copy-done.13), custom_call_target="tpu_custom_call" | custom-call | flops 536870912 | bytes 1048576 | tf_op jit(solution)/shard_map/pallas_call | solution.py:367
  65.5 6.4 %all-to-all-start.3 = ((bf16[8,80,384]{2,1,0:T(8,128)(2,1)}), bf16[8,80,384]{2,1,0:T(8,128)(2,1)S(1)}, u32[]{:S(2)}, u32[]{:S(2)}) async-start(bf16[8,80,384]{2,1,0:T(8,128)(2,1)} %shard_map.152), calls=%async_computation.3 | async-start | bytes 983040 | tf_op jit(solution)/shard_map/all_to_all | solution.py:473
  71.9 0.0 collective-permute-done
  71.9 0.0 collective-permute-done.1
  72.0 0.1 fusion
  72.0 0.1 fusion.1
  72.1 0.5 copy-done.19
  72.6 3.5 %collective-permute-start.2 = (bf16[8,80,16]{2,1,0:T(8,128)(2,1)S(1)}, bf16[8,80,16]{2,1,0:T(8,128)(2,1)S(1)}, u32[]{:S(2)}, u32[]{:S(2)}) collective-permute-start(bf16[8,80,16]{2,1,0:T(8,128)(2,1)S(1)} %get-tuple-element.21), channel_id=1, source_target_pairs={{0,1},{1,2},{2,3},{3,4},{4,5},{5,6},{6,7},{8,9},{9,10},{10,11},{11... | collective-permute-start | bytes 61448 | tf_op jit(solution)/shard_map/ppermute | solution.py:381
  76.1 2.5 %collective-permute-start.3 = (bf16[8,80,16]{2,1,0:T(8,128)(2,1)S(1)}, bf16[8,80,16]{2,1,0:T(8,128)(2,1)S(1)}, u32[]{:S(2)}, u32[]{:S(2)}) collective-permute-start(bf16[8,80,16]{2,1,0:T(8,128)(2,1)S(1)} %get-tuple-element.22), channel_id=1, source_target_pairs={{1,0},{2,1},{3,2},{4,3},{5,4},{6,5},{7,6},{9,8},{10,9},{11,10},{12... | collective-permute-start | bytes 61448 | tf_op jit(solution)/shard_map/ppermute | solution.py:382
  78.6 1.4 %collective-permute-done.2 = bf16[8,80,16]{2,1,0:T(8,128)(2,1)S(1)} collective-permute-done((bf16[8,80,16]{2,1,0:T(8,128)(2,1)S(1)}, bf16[8,80,16]{2,1,0:T(8,128)(2,1)S(1)}, u32[]{:S(2)}, u32[]{:S(2)}) %collective-permute-start.2) | collective-permute-done | bytes 20512 | tf_op jit(solution)/shard_map/ppermute | solution.py:381
  79.9 0.0 copy-done.18
  80.0 5.5 %collective-permute-done.3 = bf16[8,80,16]{2,1,0:T(8,128)(2,1)S(1)} collective-permute-done((bf16[8,80,16]{2,1,0:T(8,128)(2,1)S(1)}, bf16[8,80,16]{2,1,0:T(8,128)(2,1)S(1)}, u32[]{:S(2)}, u32[]{:S(2)}) %collective-permute-start.3) | collective-permute-done | bytes 20512 | tf_op jit(solution)/shard_map/ppermute | solution.py:382
  85.4 1.0 %convert_add_fusion.base_ref = f32[8,80,272]{2,1,0:T(8,128)S(1)} fusion(bf16[8,80,16]{2,1,0:T(8,128)(2,1)S(1)} %collective-permute-done.3, bf16[8,80,16]{2,1,0:T(8,128)(2,1)S(1)} %collective-permute-done.2, bf16[8,16,272]{2,1,0:T(8,128)(2,1)} %copy-done.19, f32[8,80,272]{2,1,0:T(8,128)S(1)} %get-tuple-element.16, bf16[8,16,272]{2,1,0:T(8,128)(2,1)} %copy-done.18), kind=kLoop, calls=%fused_computation | loop fusion | flops 1392640 | bytes 1572864 | tf_op jit(solution)/shard_map/add | solution.py:387
  86.5 0.0 all-to-all-done.3.half_ref
  86.5 0.0 copy-start.5
  86.5 1.3 %copy-done.5 = bf16[4,9,64,256]{3,2,1,0:T(8,128)(2,1)S(1)} copy-done((bf16[4,9,64,256]{3,2,1,0:T(8,128)(2,1)S(1)}, bf16[4,9,64,256]{3,2,1,0:T(8,128)(2,1)}, u32[]{:S(2)}) %copy-start.5) | copy-done | bytes 1179672
  87.8 0.9 copy-done.10
  88.7 6.4 %shard_map.155 = (f32[4,64,256]{2,1,0:T(8,128)}, bf16[4,9,64,256]{3,2,1,0:T(8,128)(2,1)}) custom-call(f32[9]{0:T(128)S(1)} %copy-done.11, bf16[8,80,384]{2,1,0:T(8,128)(2,1)S(1)} %all-to-all-done.3.half_ref, f32[8,80,272]{2,1,0:T(8,128)S(1)} %convert_add_fusion.base_ref, bf16[4,9,64,256]{3,2,1,0:T(8,128)(2,1)S(1)} %copy-done.5, ...), custom_call_target="tpu_custom_call" | custom-call | flops 2147483648 | bytes 3145728 | tf_op jit(solution)/shard_map/pallas_call | solution.py:509
  (27 shorter events, 0.1 us)
Async XLA Ops:
  0.6 11.7 %copy-start.12 = (bf16[2,256,768]{2,1,0:T(8,128)(2,1)S(1)}, bf16[2,256,768]{2,1,0:T(8,128)(2,1)}, u32[]{:S(2)}) copy-start(bf16[2,256,768]{2,1,0:T(8,128)(2,1)} %constant.27.clone.line_ref) | copy-start | bytes 2359300
  0.6 11.7 %copy-start.15 = (f32[2,2,4,4,256]{4,3,2,1,0:T(4,128)S(1)}, f32[2,2,4,4,256]{4,3,2,1,0:T(4,128)}, u32[]{:S(2)}) copy-start(f32[2,2,4,4,256]{4,3,2,1,0:T(4,128)} %constant.26.clone.fold_ref) | copy-start | bytes 196612
  2.4 10.0 %all-to-all-start = ((bf16[8,64,256]{2,1,0:T(8,128)(2,1)}), bf16[8,64,256]{2,1,0:T(8,128)(2,1)S(1)}, u32[]{:S(2)}, u32[]{:S(2)}) async-start(bf16[8,64,256]{2,1,0:T(8,128)(2,1)} %bitcast.4), calls=%async_computation | async-start | bytes 524288 | tf_op jit(solution)/shard_map/all_to_all | solution.py:410
  7.6 16.6 %copy-start.21 = (s32[4,1]{0,1:T(1,128)S(1)}, s32[4,1]{0,1:T(1,128)}, u32[]{:S(2)}) copy-start(s32[4,1]{0,1:T(1,128)} %param.21) | copy-start | bytes 52
  7.6 16.7 %copy-start = (bf16[4,1,6,64,64]{4,3,2,1,0:T(8,128)(2,1)S(1)}, bf16[4,1,6,64,64]{4,3,2,1,0:T(8,128)(2,1)}, u32[]{:S(2)}) copy-start(bf16[4,1,6,64,64]{4,3,2,1,0:T(8,128)(2,1)} %tiles_ref.1) | copy-start | bytes 589828
  7.6 16.7 %copy-start.1 = (bf16[2,128,768]{2,1,0:T(8,128)(2,1)S(1)}, bf16[2,128,768]{2,1,0:T(8,128)(2,1)}, u32[]{:S(2)}) copy-start(bf16[2,128,768]{2,1,0:T(8,128)(2,1)} %constant.28.clone.table_ref) | copy-start | bytes 1179652
  7.6 16.7 %copy-start.3 = (s32[4,1,6]{2,1,0:T(1,128)S(1)}, s32[4,1,6]{2,1,0:T(1,128)}, u32[]{:S(2)}) copy-start(s32[4,1,6]{2,1,0:T(1,128)} %slots_ref.1) | copy-start | bytes 292
  7.7 25.7 %copy-start.14 = (f32[4,64,128]{2,1,0:T(8,128)S(1)}, f32[4,64,128]{2,1,0:T(8,128)}, u32[]{:S(2)}) copy-start(f32[4,64,128]{2,1,0:T(8,128)} %constant.29.clone.turn_ref) | copy-start | bytes 393220
  14.4 18.9 %all-to-all-start.1 = ((bf16[32,32,128]{2,1,0:T(8,128)(2,1)}), bf16[32,32,128]{2,1,0:T(8,128)(2,1)S(1)}, u32[]{:S(2)}, u32[]{:S(2)}) async-start(bf16[32,32,128]{2,1,0:T(8,128)(2,1)} %shard_map.149), calls=%async_computation.1 | async-start | bytes 524288 | tf_op jit(solution)/shard_map/all_to_all | solution.py:426
  33.3 0.8 copy-start.17
  34.1 11.5 %copy-start.20 = (f32[8,17]{1,0:T(8,128)S(1)}, f32[8,17]{1,0:T(8,128)}, u32[]{:S(2)}) copy-start(f32[8,17]{1,0:T(8,128)} %param.17) | copy-start | bytes 1636
  34.1 13.1 %copy-start.2 = (f32[4,64,256]{2,1,0:T(8,128)S(1)}, f32[4,64,256]{2,1,0:T(8,128)}, u32[]{:S(2)}) copy-start(f32[4,64,256]{2,1,0:T(8,128)} %sky_ref.1) | copy-start | bytes 786436
  34.1 13.1 %copy-start.4 = (bf16[4,9,64,256]{3,2,1,0:T(8,128)(2,1)S(1)}, bf16[4,9,64,256]{3,2,1,0:T(8,128)(2,1)}, u32[]{:S(2)}) copy-start(bf16[4,9,64,256]{3,2,1,0:T(8,128)(2,1)} %dual_ref.3) | copy-start | bytes 3538948
  37.2 25.0 %all-to-all-start.2 = ((bf16[32,40,128]{2,1,0:T(8,128)(2,1)}), bf16[32,40,128]{2,1,0:T(8,128)(2,1)S(1)}, u32[]{:S(2)}, u32[]{:S(2)}) async-start(bf16[32,40,128]{2,1,0:T(8,128)(2,1)} %shard_map.151), calls=%async_computation.2 | async-start | bytes 655360 | tf_op jit(solution)/shard_map/all_to_all | solution.py:460
  46.5 0.7 copy-start.9
  47.2 5.2 %copy-start.6 = (bf16[2,8,128,256]{3,2,1,0:T(8,128)(2,1)}, bf16[2,8,128,256]{3,2,1,0:T(8,128)(2,1)S(1)}, u32[]{:S(2)}) copy-start(bf16[2,8,128,256]{3,2,1,0:T(8,128)(2,1)S(1)} %get-tuple-element.15.strip_ref) | copy-start | bytes 3145732
  47.2 1.1 %copy-start.8 = (f32[4,64,256]{2,1,0:T(8,128)S(1)}, f32[4,64,256]{2,1,0:T(8,128)}, u32[]{:S(2)}) copy-start(f32[4,64,256]{2,1,0:T(8,128)} %dirty_ref.1) | copy-start | bytes 786436
  48.3 13.8 %copy-start.16 = (f32[2,2,4,4,256]{4,3,2,1,0:T(4,128)S(1)}, f32[2,2,4,4,256]{4,3,2,1,0:T(4,128)}, u32[]{:S(2)}) copy-start(f32[2,2,4,4,256]{4,3,2,1,0:T(4,128)} %constant.26.clone.fold_ref) | copy-start | bytes 196612
  52.4 19.6 %collective-permute-start = (bf16[8,16,272]{2,1,0:T(8,128)(2,1)S(1)}, bf16[8,16,272]{2,1,0:T(8,128)(2,1)S(1)}, u32[]{:S(2)}, u32[]{:S(2)}) collective-permute-start(bf16[8,16,272]{2,1,0:T(8,128)(2,1)S(1)} %get-tuple-element.19), channel_id=1, source_target_pairs={{0,8},{8,16},{16,24},{24,32},{32,40},{40,48},{48,56},{56,64},{64,7... | collective-permute-start | bytes 208904 | tf_op jit(solution)/shard_map/ppermute | solution.py:381
  54.4 17.5 %collective-permute-start.1 = (bf16[8,16,272]{2,1,0:T(8,128)(2,1)S(1)}, bf16[8,16,272]{2,1,0:T(8,128)(2,1)S(1)}, u32[]{:S(2)}, u32[]{:S(2)}) collective-permute-start(bf16[8,16,272]{2,1,0:T(8,128)(2,1)S(1)} %get-tuple-element.20), channel_id=1, source_target_pairs={{8,0},{16,8},{24,16},{32,24},{40,32},{48,40},{56,48},{64,56},{72,6... | collective-permute-start | bytes 208904 | tf_op jit(solution)/shard_map/ppermute | solution.py:382
  62.2 1.1 %copy-start.13 = (bf16[2,256,768]{2,1,0:T(8,128)(2,1)S(1)}, bf16[2,256,768]{2,1,0:T(8,128)(2,1)}, u32[]{:S(2)}) copy-start(bf16[2,256,768]{2,1,0:T(8,128)(2,1)} %constant.27.clone.line_ref) | copy-start | bytes 2359300
  65.5 21.0 %all-to-all-start.3 = ((bf16[8,80,384]{2,1,0:T(8,128)(2,1)}), bf16[8,80,384]{2,1,0:T(8,128)(2,1)S(1)}, u32[]{:S(2)}, u32[]{:S(2)}) async-start(bf16[8,80,384]{2,1,0:T(8,128)(2,1)} %shard_map.152), calls=%async_computation.3 | async-start | bytes 983040 | tf_op jit(solution)/shard_map/all_to_all | solution.py:473
  71.9 8.0 %copy-start.18 = (bf16[8,16,272]{2,1,0:T(8,128)(2,1)}, bf16[8,16,272]{2,1,0:T(8,128)(2,1)S(1)}, u32[]{:S(2)}) copy-start(bf16[8,16,272]{2,1,0:T(8,128)(2,1)S(1)} %collective-permute-done) | copy-start | bytes 208900
  71.9 0.7 copy-start.19
  72.6 13.9 %copy-start.7 = (bf16[2,8,128,256]{3,2,1,0:T(8,128)(2,1)S(1)}, bf16[2,8,128,256]{3,2,1,0:T(8,128)(2,1)}, u32[]{:S(2)}) copy-start(bf16[2,8,128,256]{3,2,1,0:T(8,128)(2,1)} %copy-done.6) | copy-start | bytes 3145732
  72.6 13.9 %copy-start.11 = (f32[9]{0:T(128)S(1)}, f32[9]{0:T(128)}, u32[]{:S(2)}) copy-start(f32[9]{0:T(128)} %bound_ref.1) | copy-start | bytes 112
  72.6 7.3 %collective-permute-start.2 = (bf16[8,80,16]{2,1,0:T(8,128)(2,1)S(1)}, bf16[8,80,16]{2,1,0:T(8,128)(2,1)S(1)}, u32[]{:S(2)}, u32[]{:S(2)}) collective-permute-start(bf16[8,80,16]{2,1,0:T(8,128)(2,1)S(1)} %get-tuple-element.21), channel_id=1, source_target_pairs={{0,1},{1,2},{2,3},{3,4},{4,5},{5,6},{6,7},{8,9},{9,10},{10,11},{11... | collective-permute-start | bytes 61448 | tf_op jit(solution)/shard_map/ppermute | solution.py:381
  76.1 9.3 %collective-permute-start.3 = (bf16[8,80,16]{2,1,0:T(8,128)(2,1)S(1)}, bf16[8,80,16]{2,1,0:T(8,128)(2,1)S(1)}, u32[]{:S(2)}, u32[]{:S(2)}) collective-permute-start(bf16[8,80,16]{2,1,0:T(8,128)(2,1)S(1)} %get-tuple-element.22), channel_id=1, source_target_pairs={{1,0},{2,1},{3,2},{4,3},{5,4},{6,5},{7,6},{9,8},{10,9},{11,10},{12... | collective-permute-start | bytes 61448 | tf_op jit(solution)/shard_map/ppermute | solution.py:382
  86.5 1.3 %copy-start.5 = (bf16[4,9,64,256]{3,2,1,0:T(8,128)(2,1)S(1)}, bf16[4,9,64,256]{3,2,1,0:T(8,128)(2,1)}, u32[]{:S(2)}) copy-start(bf16[4,9,64,256]{3,2,1,0:T(8,128)(2,1)} %dual_ref.3) | copy-start | bytes 3538948
  87.8 0.9 copy-start.10

commit v2 on v1

--- a/solution.py
+++ b/solution.py
@@ -19,7 +19,8 @@
 STEP_DUAL = 0.5
 BF = jnp.bfloat16
 F32 = jnp.float32
-VMEM_LIMIT = 48 << 20
+VMEM_LIMIT = 20 << 20
+WIDE = 384
 OUTSIDE = -1.0e30
 LAST = ((1,), (1,))
 FIRST = ((0,), (0,))
@@ -46,7 +47,7 @@
 
 def line_table():
     ang = angle_np(np.arange(256), np.arange(256), 256)
-    return two_terms_np(np.concatenate([-np.sin(ang), np.cos(ang), np.sin(ang)], axis=1))
+    return two_terms_np(np.concatenate([np.cos(ang), np.sin(ang)], axis=1))
 
 
 def block_table():
@@ -62,7 +63,17 @@
     main = np.tile(np.arange(64), 2)
     halo = np.tile(HALO, 8)
     ang = [angle_np(np.arange(64), r, 2048) for r in (main, halo)]
-    return np.stack([np.cos(ang[0]), np.sin(ang[0]), np.cos(ang[1]), np.sin(ang[1])]).astype(np.float32)
+    return two_terms_np(
+        np.concatenate([np.cos(ang[0]), np.sin(ang[0]), np.cos(ang[1]), np.sin(ang[1])])
+    )
+
+
+def fixed_table():
+    table = np.zeros((256, 512), jnp.bfloat16)
+    for t in range(2):
+        table[:, t * 128 : t * 128 + 128] = turn_table()[t]
+        table[0:64, 256 + t * 128 : 320 + t * 128] = block_table()[t]
+    return table
 
 
 def tile_table():
@@ -119,29 +130,31 @@
             rows_im.append(jnp.concatenate([yi, -yr], axis=1))
         for part, rows in enumerate((rows_re, rows_im)):
             r = jnp.concatenate(rows, axis=0).astype(BF)
-            out = dot(line_ref[0, :, 256:768], r, LAST) + dot(line_ref[1, :, 256:768], r, LAST)
+            out = dot(line_ref[0], r, LAST) + dot(line_ref[1], r, LAST)
             parts[part].append(out.reshape(32, 8, 128))
     for part in range(2):
         both = jnp.concatenate(parts[part], axis=1)
         o_ref[:, part * 16 : (part + 1) * 16, :] = both.astype(BF)
 
 
-def inverse_kernel(par_ref, t_ref, fold_ref, line_ref, o_ref):
+def inverse_kernel(par_ref, t_ref, fold_ref, line_ref, base_ref, o_ref):
     par = par_ref[1]
+    me = par_ref[3]
     sign = (1 - 2 * par).astype(F32)
     re = t_ref[:, 0:16, :].astype(F32)
     im = t_ref[:, 16:32, :].astype(F32)
     edge = t_ref[:, 32:40, :].astype(F32).reshape(256, 128).astype(BF)
     h = dot(edge, line_ref[0], FIRST) + dot(edge, line_ref[1], FIRST)
-    h = h[0:64, 256:768] + h[64:128, 0:512]
+    h = jnp.concatenate(
+        [h[0:64, 0:256] - h[64:128, 256:512], h[0:64, 256:512] + h[64:128, 0:256]], axis=1
+    )
     total = [None] * 4
     for chi in range(2):
         a = re[:, chi * 8 : chi * 8 + 8, :].reshape(256, 128).astype(BF)
         b = im[:, chi * 8 : chi * 8 + 8, :].reshape(256, 128).astype(BF)
-        u = None
-        for t in range(2):
-            term = dot(a, line_ref[t, :, 256:768], FIRST) + dot(b, line_ref[t, :, 0:512], FIRST)
-            u = term if u is None else u + term
+        a = dot(a, line_ref[0], FIRST) + dot(a, line_ref[1], FIRST)
+        b = dot(b, line_ref[0], FIRST) + dot(b, line_ref[1], FIRST)
+        u = jnp.concatenate([a[:, 0:256] - b[:, 256:512], a[:, 256:512] + b[:, 0:256]], axis=1)
         for clo in range(2):
             cls = 2 * chi + clo
             e = h[cls * 16 : cls * 16 + 16]
@@ -157,14 +170,19 @@
     total = [g * scale for g in total]
     total = total + [sign * g for g in total]
     none = jnp.zeros((80, 128), F32)
+    lane = lax.broadcasted_iota(jnp.int32, (80, 128), 1)
     for f in range(8):
         before = total[f - 1][:, 128:256] if f > 0 else none
         after = total[f + 1][:, 0:128] if f < 7 else none
         line = jnp.concatenate([before, total[f], after], axis=1)
-        o_ref[f] = pltpu.roll(line, 512 - 120, 1)[:, 0:384].astype(BF)
-
-
-def tiles_kernel(where_ref, slots_ref, count_ref, tiles_ref, table_ref, o_ref, gram_ref):
+        line = pltpu.roll(line, 512 - 120, 1)
+        pack = jnp.where(f == me - 1, base_ref[0, :, WIDE:], 0.0)
+        pack = pack + jnp.where(f == me + 1, base_ref[1, :, WIDE:], 0.0)
+        o_ref[f, :, 0:256] = line[:, 0:256].astype(BF)
+        o_ref[f, :, 256:384] = (jnp.where(lane < 16, line[:, 256:384], 0.0) + pack).astype(BF)
+
+
+def tiles_kernel(where_ref, slots_ref, count_ref, tiles_ref, table_ref, fixed_ref, o_ref):
     channel = where_ref[0]
     left = lax.broadcasted_iota(jnp.int32, (32, 128), 0)
     right = lax.broadcasted_iota(jnp.int32, (32, 128), 1)
@@ -174,31 +192,34 @@
         tile = jnp.where(left // 4 == k, slot, tile)
     pick = (tile == right // 4) & (left % 4 == right % 4)
     pick = jnp.where(pick, 1.0, 0.0).astype(BF)
+    o_ref[...] = jnp.zeros_like(o_ref)
     for k in range(SLOTS):
-        gram_ref[k * 64 : k * 64 + 64, :] = tiles_ref[channel, 0, k].astype(F32).T.astype(BF)
-    o_ref[...] = jnp.zeros_like(o_ref)
+        o_ref[256 + k * 64 : 320 + k * 64, 0:64] = tiles_ref[channel, 0, k].astype(F32).T.astype(BF)
+    o_ref[256:512, 128:640] = fixed_ref[...]
     for t in range(2):
         row = dot(pick, table_ref[t]).astype(BF)
         for j in range(2):
             for chi in range(2):
                 p = 2 * j + chi
-                rows = slice(p * 32, p * 32 + 32)
-                o_ref[t, rows, p * 256 : p * 256 + 256] = row[:, 0:256]
+                rows = slice(t * 128 + p * 32, t * 128 + p * 32 + 32)
+                o_ref[rows, p * 256 : p * 256 + 256] = row[:, 0:256]
                 for comp in range(2):
                     at = 256 + chi * 256 + comp * 128
                     to = 1024 + comp * 256 + j * 128
-                    o_ref[t, rows, to : to + 128] = row[:, at : at + 128]
-
-
-def gram_kernel(d_ref, turn_ref, block_ref, e_ref, gram_ref, o_ref, rows, rhs, mid, edge):
+                    o_ref[rows, to : to + 128] = row[:, at : at + 128]
+
+
+def gram_kernel(d_ref, e_ref, o_ref, rows, rhs, mid, edge):
     rows[0:1024, :] = d_ref[...].reshape(1024, 128).astype(F32)
     for p in range(16):
         lanes = slice(p * 128, p * 128 + 128)
         at = (p % 2) * 8 + p // 2
         rhs[0:32, lanes] = rows[pl.ds(at, 32, stride=32), :].astype(BF)
         rhs[32:64, lanes] = rows[pl.ds(16 + at, 32, stride=32), :].astype(BF)
-    first = dot(block_ref[0], rhs[...]) + dot(block_ref[1], rhs[...])
-    tc, ts, ec, es = turn_ref[0], turn_ref[1], turn_ref[2], turn_ref[3]
+    block = [e_ref[256:320, 384 + t * 128 : 448 + t * 128] for t in range(2)]
+    turns = e_ref[256:512, 128:256].astype(F32) + e_ref[256:512, 256:384].astype(F32)
+    tc, ts, ec, es = (turns[n * 64 : n * 64 + 64] for n in range(4))
+    first = dot(block[0], rhs[...]) + dot(block[1], rhs[...])
     for p in range(16):
         g = first[:, p * 128 : p * 128 + 128]
         gr = jnp.concatenate([g[0:32], g[0:32]], axis=0)
@@ -208,9 +229,11 @@
     pieces = []
     for g in range(4):
         m = mid[:, g * 1024 : (g + 1) * 1024]
-        pieces.append((dot(m, e_ref[0, :, 0:1024], LAST) + dot(m, e_ref[1, :, 0:1024], LAST)).astype(BF))
+        pieces.append(
+            (dot(m, e_ref[0:128, 0:1024], LAST) + dot(m, e_ref[128:256, 0:1024], LAST)).astype(BF)
+        )
     spec = jnp.concatenate(pieces, axis=1)
-    mixed = dot(gram_ref[...], spec)
+    mixed = dot(e_ref[256:640, 0:64], spec)
     lane_slot = (lax.broadcasted_iota(jnp.int32, (64, 512), 1) % 32) // 4
     weighted = jnp.where(lane_slot == 0, mixed[0:64], 0.0)
     for k in range(1, SLOTS):
@@ -218,7 +241,7 @@
     weighted = weighted.astype(BF)
     for g in range(4):
         w = weighted[:, g * 128 : g * 128 + 128]
-        z = dot(w, e_ref[0]) + dot(w, e_ref[1])
+        z = dot(w, e_ref[0:128, :]) + dot(w, e_ref[128:256, :])
         for v in range(4):
             p = g * 4 + v
             zr = z[:, v * 256 : v * 256 + 128]
@@ -235,8 +258,8 @@
             lanes = slice((2 * g + j) * 128, (2 * g + j) * 128 + 128)
             edge[0:32, lanes] = (hr[0:32] + hr[32:64]).astype(BF)
             edge[32:64, lanes] = (hi[0:32] + hi[32:64]).astype(BF)
-    last = dot(block_ref[0], rhs[...], FIRST) + dot(block_ref[1], rhs[...], FIRST)
-    outer = dot(block_ref[0, :, 0:32], edge[...], FIRST) + dot(block_ref[1, :, 0:32], edge[...], FIRST)
+    last = dot(block[0], rhs[...], FIRST) + dot(block[1], rhs[...], FIRST)
+    outer = dot(block[0][:, 0:32], edge[...], FIRST) + dot(block[1][:, 0:32], edge[...], FIRST)
     for p in range(16):
         lanes = slice(p * 128, p * 128 + 128)
         at = (p % 2) * 8 + p // 2
@@ -266,8 +289,9 @@
     where_ref, live_ref, dual_ref, sky_ref, dirty_ref, strip_ref, o_ref, head_ref, tail_ref, across
 ):
     channels = sky_ref.shape[0]
-    row = lax.broadcasted_iota(jnp.int32, (80, 272), 0) + where_ref[2] * ROWS - RADIUS
-    col = lax.broadcasted_iota(jnp.int32, (80, 272), 1) + where_ref[3] * COLS - RADIUS
+    row = lax.broadcasted_iota(jnp.int32, (80, WIDE), 0) + where_ref[2] * ROWS - RADIUS
+    lane = lax.broadcasted_iota(jnp.int32, (80, WIDE), 1)
+    col = lane + where_ref[3] * COLS - RADIUS
     inside = (row >= 0) & (row < PIXELS) & (col >= 0) & (col < PIXELS)
     for k in range(FRAMES):
         p = dual_ref[:, k + 1].reshape(channels * ROWS, COLS)
@@ -280,7 +304,7 @@
             across[c, k * ROWS : (k + 1) * ROWS, :] = out[c * ROWS : (c + 1) * ROWS].astype(BF)
     live = lax.broadcasted_iota(jnp.int32, (ROWS, COLS), 0) < live_ref[0]
     none = jnp.zeros((ROWS, 128), F32)
-    edge = jnp.zeros((8, 272), F32)
+    edge = jnp.zeros((8, WIDE), F32)
     for c in range(channels):
         total = None
         for t in range(2):
@@ -294,11 +318,12 @@
         sky = sky_ref[c]
         own = sky + STEP_PRIMAL * dirty_ref[c] - STEP_PRIMAL * dual_ref[c, 0].astype(F32)
         own = jnp.where(live, own, OUTSIDE)
-        own = pltpu.roll(jnp.concatenate([own, none], axis=1), 8, 1)[:, 0:272]
-        sky = pltpu.roll(jnp.concatenate([sky, none], axis=1), 8, 1)[:, 0:272]
-        total = total[0:80, 0:272] * (-STEP_PRIMAL)
+        own = pltpu.roll(jnp.concatenate([own, none], axis=1), 8, 1)
+        sky = pltpu.roll(jnp.concatenate([sky, none], axis=1), 8, 1)
+        total = total[0:80] * (-STEP_PRIMAL)
         total = total + jnp.concatenate([edge, own, edge], axis=0)
         total = jnp.where(inside, total, OUTSIDE)
+        total = jnp.where(lane < COLS + 2 * RADIUS, total, 0.0)
         sky = jnp.concatenate([edge, sky, edge], axis=0)
         for at, cells in ((c, total), (channels + c, sky)):
             o_ref[at] = cells
@@ -306,7 +331,34 @@
             tail_ref[at] = cells[64:80].astype(BF)
 
 
-def frames_kernel(bound_ref, half_ref, base_ref, dual_ref, strip_ref, down_ref, image_ref, o_ref, probes, wide, down):
+def edge_kernel(base_ref, before_ref, after_ref, o_ref):
+    both = base_ref.shape[0]
+    lane = lax.broadcasted_iota(jnp.int32, (80, 128), 1)
+    head = jnp.zeros((80, 128), F32)
+    tail = jnp.zeros((80, 128), F32)
+    for c in range(both):
+        o_ref[c, 0:16, 0:WIDE] = base_ref[c, 0:16] + before_ref[c].astype(F32)
+        o_ref[c, 16:64, 0:WIDE] = base_ref[c, 16:64]
+        o_ref[c, 64:80, 0:WIDE] = base_ref[c, 64:80] + after_ref[c].astype(F32)
+        first = o_ref[c, :, 0:128]
+        final = o_ref[c, :, 256:384]
+        if c < both // 2:
+            at = 16 + 16 * c
+            head = head + pltpu.roll(jnp.where(lane < 16, first, 0.0), at, 1)
+            tail = tail + pltpu.roll(jnp.where(lane < 16, final, 0.0), at, 1)
+        else:
+            at = 80 + 8 * (c - both // 2)
+            head = head + pltpu.roll(jnp.where((lane >= 8) & (lane < 16), first, 0.0), at - 8, 1)
+            tail = tail + pltpu.roll(jnp.where(lane < 8, final, 0.0), at, 1)
+    o_ref[0, :, WIDE:] = head
+    o_ref[1, :, WIDE:] = tail
+    for c in range(2, both):
+        o_ref[c, :, WIDE:] = jnp.zeros((80, 128), F32)
+
+
+def frames_kernel(
+    bound_ref, where_ref, half_ref, base_ref, dual_ref, strip_ref, down_ref, image_ref, o_ref, probes, wide, down
+):
     step = pl.program_id(0)
     channels = image_ref.shape[0]
     bound = bound_ref[step]
@@ -323,17 +375,35 @@
     @pl.when(step == 0)
     def _():
         wide[...] = jnp.zeros_like(wide)
+        me = where_ref[3]
+        last = half_ref.shape[0] - 1
+        lane = lax.broadcasted_iota(jnp.int32, (80, 128), 1)
+        left = half_ref[jnp.maximum(me - 1, 0), :, 256:384].astype(F32)
+        left = jnp.where(me > 0, left, 0.0)
+        right = half_ref[jnp.minimum(me + 1, last), :, 256:384].astype(F32)
+        right = jnp.where(me < last, right, 0.0)
         for c in range(channels):
-            gram = half_ref[2 * c, :, 0:272].astype(F32) + half_ref[2 * c + 1, :, 0:272].astype(F32)
-            image = jnp.maximum(base_ref[c] - STEP_PRIMAL * gram, 0.0)
-            probe = 2.0 * image - base_ref[channels + c]
-            image_ref[c] = image[8:72, 8:264]
-            probes[c] = probe[8:72, 8:264]
+            gram = half_ref[2 * c].astype(F32) + half_ref[2 * c + 1].astype(F32)
+            gram = [gram[:, 0:128], gram[:, 128:256], jnp.where(lane < 16, gram[:, 256:384], 0.0)]
+            base = [base_ref[c, :, b * 128 : b * 128 + 128] for b in range(3)]
+            sky = [base_ref[channels + c, :, b * 128 : b * 128 + 128] for b in range(3)]
+            at = 16 + 16 * c
+            base[0] = base[0] + jnp.where(lane < 16, pltpu.roll(left, 128 - at, 1), 0.0)
+            base[2] = base[2] + jnp.where(lane < 16, pltpu.roll(right, 128 - at, 1), 0.0)
+            at = 80 + 8 * c
+            sky[0] = sky[0] + jnp.where(lane < 8, pltpu.roll(left, 128 - at, 1), 0.0)
+            shown = (lane >= 8) & (lane < 16)
+            sky[2] = sky[2] + jnp.where(shown, pltpu.roll(right, 136 - at, 1), 0.0)
+            image = [jnp.maximum(base[b] - STEP_PRIMAL * gram[b], 0.0) for b in range(3)]
+            probe = jnp.concatenate([2.0 * image[b] - sky[b] for b in range(3)], axis=1)
+            image = pltpu.roll(jnp.concatenate(image, axis=1), WIDE - 8, 1)
+            image_ref[c] = image[8:72, 0:256]
+            probes[c] = pltpu.roll(probe, WIDE - 8, 1)[8:72, 0:256]
             high = probe.astype(BF)
             low = (probe - high.astype(F32)).astype(BF)
-            wide[0:80, 0:272] = high
-            wide[80:160, 0:272] = low
-            wide[160:240, 0:272] = high
+            wide[0:80, :] = high
+            wide[80:160, :] = low
+            wide[160:240, :] = high
             d = dot(down_ref[...], wide[...])
             high = d.astype(BF)
             down[0, c] = high
@@ -347,10 +417,12 @@
         for t in range(2):
             d = jnp.concatenate([down[t, c, pl.ds(at, ROWS), :] for c in range(channels)], axis=0)
             both = jnp.concatenate([d[:, 0:256], d[:, 128:384]], axis=0)
-            term = dot(both, strip_ref[0, 0], LAST)
-            a = term if a is None else a + term
             if t == 0:
-                a = a + dot(both, strip_ref[1, 0], LAST)
+                band = jnp.concatenate([strip_ref[0, 0], strip_ref[1, 0]], axis=0)
+                term = dot(both, band, LAST)
+                a = term[:, 0:128] + term[:, 128:256]
+            else:
+                a = a + dot(both, strip_ref[0, 0], LAST)
         rows = channels * ROWS
         finish(
             lambda c: jnp.concatenate(
@@ -373,18 +445,6 @@
         compiler_params=pltpu.CompilerParams(vmem_limit_bytes=VMEM_LIMIT),
         cost_estimate=pl.CostEstimate(flops=flops, bytes_accessed=moved, transcendentals=0),
     )(*args)
-
-
-def overlap_add(cells, head, tail, axis, dim):
-    count = lax.axis_size(axis)
-    room = cells.shape[dim] - 2 * RADIUS
-    from_before = lax.ppermute(tail, axis, [(i, i + 1) for i in range(count - 1)])
-    from_after = lax.ppermute(head, axis, [(i + 1, i) for i in range(count - 1)])
-    width = [(0, 0)] * cells.ndim
-    width[dim] = (0, room)
-    cells = cells + jnp.pad(from_before, width).astype(F32)
-    width[dim] = (room, 0)
-    return cells + jnp.pad(from_after, width).astype(F32)
 
 
 def after(values, event):
@@ -425,9 +485,9 @@
     )
     received = lax.all_to_all(packed, "img", split_axis=0, concat_axis=0, tiled=True)
 
-    spread, gram = call(
+    spread = call(
         tiles_kernel,
-        (jax.ShapeDtypeStruct((2, 128, 1536), BF), jax.ShapeDtypeStruct((SLOTS * 64, 64), BF)),
+        jax.ShapeDtypeStruct((640, 1536), BF),
         [],
         1 << 23,
         1 << 20,
@@ -436,8 +496,39 @@
         tile_count,
         gram_tiles,
         np.stack(tile_table()),
+        fixed_table(),
         scalars=3,
     )
+
+    strip, down = call(
+        band_kernel,
+        (
+            jax.ShapeDtypeStruct((2, FRAMES, 128, 256), BF),
+            jax.ShapeDtypeStruct((FRAMES * ROWS, 256), BF),
+        ),
+        [],
+        1 << 20,
+        1 << 20,
+        jnp.pad(filters, ((0, 0), (0, 256 - filters.shape[1]))),
+    )
+    ends = jax.ShapeDtypeStruct((2 * channels, 16, WIDE), BF)
+    extended = jax.ShapeDtypeStruct((2 * channels, tile_rows + 16, WIDE), F32)
+    (late_where,) = after((where,), packed)
+    base, head, tail = call(
+        synth_kernel,
+        (extended, ends, ends),
+        [pltpu.VMEM((channels, FRAMES * ROWS, WIDE), BF)],
+        1 << 31,
+        4 << 20,
+        late_where,
+        facet_rows,
+        dual_coeffs,
+        sky_estimate,
+        dirty_image,
+        strip,
+        scalars=2,
+    )
+    (received,) = after((received,), head)
 
     scratch = [
         pltpu.VMEM((1280, 128), F32),
@@ -452,15 +543,27 @@
         1 << 29,
         1 << 20,
         received,
-        turn_table(),
-        np.stack(block_table()),
         spread,
-        gram,
     )
     returned = lax.all_to_all(weighted, "img", split_axis=0, concat_axis=0, tiled=True)
+
+    head, tail = after((head, tail), weighted)
+    steps = [(i, i + 1) for i in range(PEERS_IMG - 1)]
+    from_before = lax.ppermute(tail, "img", steps)
+    from_after = lax.ppermute(head, "img", [(j, i) for i, j in steps])
+    base = call(
+        edge_kernel,
+        jax.ShapeDtypeStruct((2 * channels, tile_rows + 16, WIDE + 128), F32),
+        [],
+        1 << 20,
+        4 << 20,
+        base,
+        from_before,
+        from_after,
+    )
     blocks = call(
         inverse_kernel,
-        jax.ShapeDtypeStruct((8, tile_rows + 16, 384), BF),
+        jax.ShapeDtypeStruct((8, tile_rows + 16, WIDE), BF),
         [],
         1 << 29,
         1 << 20,
@@ -468,41 +571,10 @@
         returned,
         fold,
         line,
+        base,
         scalars=1,
     )
     halves = lax.all_to_all(blocks, "fou", split_axis=0, concat_axis=0, tiled=True)
-
-    strip, down = call(
-        band_kernel,
-        (
-            jax.ShapeDtypeStruct((2, FRAMES, 128, 256), BF),
-            jax.ShapeDtypeStruct((FRAMES * ROWS, 256), BF),
-        ),
-        [],
-        1 << 20,
-        1 << 20,
-        jnp.pad(filters, ((0, 0), (0, 256 - filters.shape[1]))),
-    )
-    ends = jax.ShapeDtypeStruct((2 * channels, 16, tile_cols + 16), BF)
-    base, head, tail = call(
-        synth_kernel,
-        (jax.ShapeDtypeStruct((2 * channels, tile_rows + 16, tile_cols + 16), F32), ends, ends),
-        [pltpu.VMEM((channels, FRAMES * ROWS, 384), BF)],
-        1 << 31,
-        4 << 20,
-        where,
-        facet_rows,
-        dual_coeffs,
-        sky_estimate,
-        dirty_image,
-        strip,
-        scalars=2,
-    )
-    head, tail = after((head, tail), packed)
-    base = overlap_add(base, head, tail, "img", 1)
-    head, tail = base[:, :, 0:16].astype(BF), base[:, :, tile_cols : tile_cols + 16].astype(BF)
-    head, tail = after((head, tail), weighted)
-    base = overlap_add(base, head, tail, "fou", 2)
 
     dual_spec = pl.BlockSpec((channels, 1, tile_rows, tile_cols), lambda f: (0, f, 0, 0))
     whole = lambda a: pl.BlockSpec(a.shape, lambda f: (0,) * a.ndim)
@@ -514,6 +586,7 @@
         ),
         grid=(FRAMES + 1,),
         in_specs=[
+            SM,
             SM,
             whole(halves),
             whole(base),
@@ -529,7 +602,7 @@
         ],
         compiler_params=pltpu.CompilerParams(vmem_limit_bytes=VMEM_LIMIT),
         cost_estimate=pl.CostEstimate(flops=1 << 31, bytes_accessed=3 << 20, transcendentals=0),
-    )(thresholds, halves, base, dual_coeffs, strip, down)
+    )(thresholds, where, halves, base, dual_coeffs, strip, down)
 
 
 def solution(mesh):

time: 96 us -> 84.9 us (0.88)
  the two profiles are of different devices: /device:TPU:152 before, /device:TPU:1 now
where the time goes in v2:
time: 84.9 us; the launch traced here: 84.4 us
  starting transfers between devices  29.1 us (34%)
  waiting for transfers between devices  19.6 us (23%)
  Pallas kernels  18.8 us (22%)
  blocking collectives  11.8 us (14%)
  local copies, waits for them, and re-layouts  2.44 us (3%)
  between operations  1.52 us (2%)
  other arithmetic  1.1 us (1%)
    pallas_call x7, Pallas kernels, call(): pl.pallas_call(kernel, out_shape=out_shape, in_specs=[SM] * scalars + [VM...  12.4 us
    all_to_all x1, starting transfers between devices, body(): lax.all_to_all(packed, 'img', split_axis=0, concat_axis=0, tiled=True)  12.3 us
    all_to_all x1, blocking collectives, body(): lax.all_to_all(blocks, 'fou', split_axis=0, concat_axis=0, tiled=True)  11.8 us
    pallas_call x1, Pallas kernels, body(): pl.pallas_call(frames_kernel, out_shape=(jax.ShapeDtypeStruct(sky_estimat...  6.42 us
    all_to_all x1, starting transfers between devices, body(): lines = lax.all_to_all(sent, 'fou', split_axis=0, concat_axis=0, tiled=True)  6.37 us
    all_to_all x1, waiting for transfers between devices, body(): lines = lax.all_to_all(sent, 'fou', split_axis=0, concat_axis=0, tiled=True)  5.96 us
    ppermute x1, waiting for transfers between devices, body(): from_after = lax.ppermute(head, 'img', [(j, i) for i, j in steps])  5.39 us
    all_to_all x1, starting transfers between devices, body(): lax.all_to_all(weighted, 'img', split_axis=0, concat_axis=0, tiled=True)  4.91 us
  transfers between devices with their start and end apart: 5, of which 4 were waited for; matrix products, arithmetic and copies ran while one was open for 0% of the time, Pallas kernels for 7%

profile of v2, /device:TPU:1, one launch (start us, length us, event | category | flops | bytes accessed | tf_op | source)
XLA Modules:
  0.0 84.4 jit_solution(1515728578845946127)
XLA Ops:
  0.6 0.0 copy-start
  0.6 0.0 copy-start.6
  0.7 1.0 %convert_element_type.5 = bf16[4,64,256]{2,1,0:T(8,128)(2,1)S(1)} convert(f32[4,64,256]{2,1,0:T(8,128)} %sky_ref.1) | non-fusion elementwise | flops 65536 | bytes 393216 | tf_op jit(solution)/shard_map/convert_element_type | solution.py:469
  1.7 0.7 broadcast_in_dim.3
  2.4 6.4 %all-to-all-start = ((bf16[8,64,256]{2,1,0:T(8,128)(2,1)}), bf16[8,64,256]{2,1,0:T(8,128)(2,1)S(1)}, u32[]{:S(2)}, u32[]{:S(2)}) async-start(bf16[8,64,256]{2,1,0:T(8,128)(2,1)} %bitcast.4), calls=%async_computation | async-start | bytes 524288 | tf_op jit(solution)/shard_map/all_to_all | solution.py:470
  8.8 0.0 copy-start.16
  8.8 0.0 copy-start.2
  8.8 0.0 copy-start.3
  8.8 0.0 copy-start.4
  8.8 0.0 copy-start.7
  8.8 0.1 pad_add_fusion.par_ref.where_ref
  8.9 6.0 %all-to-all-done.x_ref = bf16[8,64,256]{2,1,0:T(8,128)(2,1)S(1)} async-done(((bf16[8,64,256]{2,1,0:T(8,128)(2,1)}), bf16[8,64,256]{2,1,0:T(8,128)(2,1)S(1)}, u32[]{:S(2)}, u32[]{:S(2)}) %all-to-all-start) | async-done | bytes 262176 | tf_op jit(solution)/shard_map/all_to_all | solution.py:470
  14.9 0.0 copy-done
  14.9 0.0 copy-done.6
  14.9 2.0 %shard_map.140 = bf16[32,32,128]{2,1,0:T(8,128)(2,1)} custom-call(s32[4]{0:T(128)S(1)} %pad_add_fusion.par_ref.where_ref, bf16[8,64,256]{2,1,0:T(8,128)(2,1)S(1)} %all-to-all-done.x_ref, f32[2,2,4,4,256]{4,3,2,1,0:T(4,128)S(1)} %copy-done.6, bf16[2,256,512]{2,1,0:T(8,128)(2,1)S(1)} %copy-done), custom_call_target="tpu_custom_call" | custom-call | flops 536870912 | bytes 1048576 | tf_op jit(solution)/shard_map/pallas_call | solution.py:439
  16.9 12.3 %all-to-all-start.1 = ((bf16[32,32,128]{2,1,0:T(8,128)(2,1)}), bf16[32,32,128]{2,1,0:T(8,128)(2,1)S(1)}, u32[]{:S(2)}, u32[]{:S(2)}) async-start(bf16[32,32,128]{2,1,0:T(8,128)(2,1)} %shard_map.140), calls=%async_computation.1 | async-start | bytes 524288 | tf_op jit(solution)/shard_map/all_to_all | solution.py:486
  29.8 0.0 copy-done.17
  29.8 0.1 copy.15.count_ref
  29.9 0.0 copy-done.16
  29.9 0.8 %shard_map.141 = (bf16[2,8,128,256]{3,2,1,0:T(8,128)(2,1)S(1)}, bf16[512,256]{1,0:T(8,128)(2,1)S(1)}) custom-call(f32[8,256]{1,0:T(8,128)S(1)} %pad.4.taps_ref), custom_call_target="tpu_custom_call" | custom-call | flops 1048576 | bytes 1048576 | tf_op jit(solution)/shard_map/pallas_call | solution.py:439
  30.8 0.0 copy-start.13
  30.8 0.7 copy-done.13
  31.5 0.0 copy-start.10
  31.5 0.0 copy-start.5
  31.5 0.0 copy-start.8
  31.6 0.0 copy-start.12
  31.6 0.9 %shard_map.143.e_ref = bf16[640,1536]{1,0:T(8,128)(2,1)S(1)} custom-call(s32[4]{0:T(128)S(1)} %pad_add_fusion.par_ref.where_ref, s32[4,1,6]{2,1,0:T(1,128)S(1)} %copy-done.7, s32[4,1]{1,0:T(4,128)S(1)} %copy.15.count_ref, bf16[4,1,6,64,64]{4,3,2,1,0:T(8,128)(2,1)S(1)} %copy-done.2, bf16[2,128,768]{2,1,0:T(8,128)(2,1)S(1)} %copy-done.3, ...), custom_call_target="tpu_custom_call" | custom-call | flops 8388608 | bytes 1048576 | tf_op jit(solution)/shard_map/pallas_call | solution.py:439
  32.5 0.0 copy-done.10
  32.5 0.2 copy-done.5
  32.7 0.6 copy-done.8
  33.3 0.0 copy-done.12
  33.3 4.0 %shard_map.142 = (f32[8,80,384]{2,1,0:T(8,128)S(1)}, bf16[8,16,384]{2,1,0:T(8,128)(2,1)S(1)}, bf16[8,16,384]{2,1,0:T(8,128)(2,1)S(1)}) custom-call(s32[4]{0:T(128)S(1)} %pad_add_fusion.par_ref.where_ref, s32[1]{0:T(128)S(6)} %copy.16.live_ref, bf16[4,9,64,256]{3,2,1,0:T(8,128)(2,1)S(1)} %copy-done.8, f32[4,64,256]{2,1,0:T(8,128)S(1)} %copy-done.5, ...), custom_call_target="tpu_custom_call" | custom-call | flops 2147483648 | bytes 4194304 | tf_op jit(solution)/shard_map/pallas_call | solution.py:439
  37.3 4.9 %all-to-all-done.1.d_ref = bf16[32,32,128]{2,1,0:T(8,128)(2,1)S(1)} async-done(((bf16[32,32,128]{2,1,0:T(8,128)(2,1)}), bf16[32,32,128]{2,1,0:T(8,128)(2,1)S(1)}, u32[]{:S(2)}, u32[]{:S(2)}) %all-to-all-start.1) | async-done | bytes 262176 | tf_op jit(solution)/shard_map/all_to_all | solution.py:486
  42.2 3.0 %shard_map.144 = bf16[32,40,128]{2,1,0:T(8,128)(2,1)} custom-call(bf16[32,32,128]{2,1,0:T(8,128)(2,1)S(1)} %all-to-all-done.1.d_ref, bf16[640,1536]{1,0:T(8,128)(2,1)S(1)} %shard_map.143.e_ref), custom_call_target="tpu_custom_call" | custom-call | flops 536870912 | bytes 1048576 | tf_op jit(solution)/shard_map/pallas_call | solution.py:439
  45.2 4.9 %all-to-all-start.2 = ((bf16[32,40,128]{2,1,0:T(8,128)(2,1)}), bf16[32,40,128]{2,1,0:T(8,128)(2,1)S(1)}, u32[]{:S(2)}, u32[]{:S(2)}) async-start(bf16[32,40,128]{2,1,0:T(8,128)(2,1)} %shard_map.144), calls=%async_computation.2 | async-start | bytes 655360 | tf_op jit(solution)/shard_map/all_to_all | solution.py:548
  50.2 0.0 copy-start.1
  50.2 3.7 %collective-permute-start = (bf16[8,16,384]{2,1,0:T(8,128)(2,1)S(1)}, bf16[8,16,384]{2,1,0:T(8,128)(2,1)S(1)}, u32[]{:S(2)}, u32[]{:S(2)}) collective-permute-start(bf16[8,16,384]{2,1,0:T(8,128)(2,1)S(1)} %get-tuple-element.17), channel_id=1, source_target_pairs={{0,8},{8,16},{16,24},{24,32},{32,40},{40,48},{48,56},{56,64},{64,7... | collective-permute-start | bytes 294920 | tf_op jit(solution)/shard_map/ppermute | solution.py:552
  53.8 1.9 %collective-permute-start.1 = (bf16[8,16,384]{2,1,0:T(8,128)(2,1)S(1)}, bf16[8,16,384]{2,1,0:T(8,128)(2,1)S(1)}, u32[]{:S(2)}, u32[]{:S(2)}) collective-permute-start(bf16[8,16,384]{2,1,0:T(8,128)(2,1)S(1)} %get-tuple-element.18), channel_id=1, source_target_pairs={{8,0},{16,8},{24,16},{32,24},{40,32},{48,40},{56,48},{64,56},{72,6... | collective-permute-start | bytes 294920 | tf_op jit(solution)/shard_map/ppermute | solution.py:553
  55.8 0.0 collective-permute-done.before_ref
  55.8 5.4 %collective-permute-done.1.after_ref = bf16[8,16,384]{2,1,0:T(8,128)(2,1)S(1)} collective-permute-done((bf16[8,16,384]{2,1,0:T(8,128)(2,1)S(1)}, bf16[8,16,384]{2,1,0:T(8,128)(2,1)S(1)}, u32[]{:S(2)}, u32[]{:S(2)}) %collective-permute-start.1) | collective-permute-done | bytes 98336 | tf_op jit(solution)/shard_map/ppermute | solution.py:553
  61.2 0.3 shard_map.145.base_ref
  61.5 0.0 copy-start.11
  61.5 0.0 copy-start.15
  61.5 3.3 %all-to-all-done.2.t_ref = bf16[32,40,128]{2,1,0:T(8,128)(2,1)S(1)} async-done(((bf16[32,40,128]{2,1,0:T(8,128)(2,1)}), bf16[32,40,128]{2,1,0:T(8,128)(2,1)S(1)}, u32[]{:S(2)}, u32[]{:S(2)}) %all-to-all-start.2) | async-done | bytes 327712 | tf_op jit(solution)/shard_map/all_to_all | solution.py:548
  64.8 1.3 %shard_map.146 = bf16[8,80,384]{2,1,0:T(8,128)(2,1)S(1)} custom-call(s32[4]{0:T(128)S(1)} %pad_add_fusion.par_ref.where_ref, bf16[32,40,128]{2,1,0:T(8,128)(2,1)S(1)} %all-to-all-done.2.t_ref, f32[2,2,4,4,256]{4,3,2,1,0:T(4,128)S(1)} %copy-done.6, bf16[2,256,512]{2,1,0:T(8,128)(2,1)S(1)} %copy-done.1, f32[8,80,512]{2,1,0:T(8,128)S(1)} %shard_map.145.base_ref), custom_call_target="tpu_custom_call" | custom-call | flops 536870912 | bytes 1048576 | tf_op jit(solution)/shard_map/pallas_call | solution.py:439
  66.1 11.8 %all_to_all.20.half_ref = bf16[8,80,384]{2,1,0:T(8,128)(2,1)S(1)} all-to-all(bf16[8,80,384]{2,1,0:T(8,128)(2,1)S(1)} %shard_map.146), channel_id=1, replica_groups=mesh['img'=32,'fou'=8] {'fou'}, dimensions={0} | all-to-all | bytes 983040 | tf_op jit(solution)/shard_map/all_to_all | solution.py:577
  78.0 0.0 copy-done.14
  78.0 6.4 %shard_map.147 = (f32[4,64,256]{2,1,0:T(8,128)}, bf16[4,9,64,256]{3,2,1,0:T(8,128)(2,1)}) custom-call(f32[9]{0:T(128)S(1)} %copy-done.15, s32[4]{0:T(128)S(1)} %pad_add_fusion.par_ref.where_ref, bf16[8,80,384]{2,1,0:T(8,128)(2,1)S(1)} %all_to_all.20.half_ref, f32[8,80,512]{2,1,0:T(8,128)S(1)} %shard_map.145.base_ref, bf16[4,9,64,256]{3,2,1,0:T(8,128)(2,1)S(1)} %copy-done.9, ...), custom_call_target="tpu_custom_call" | custom-call | flops 2147483648 | bytes 3145728 | tf_op jit(solution)/shard_map/pallas_call | solution.py:581
  (12 shorter events, 0.0 us)
Async XLA Ops:
  0.6 14.3 %copy-start = (bf16[2,256,512]{2,1,0:T(8,128)(2,1)S(1)}, bf16[2,256,512]{2,1,0:T(8,128)(2,1)}, u32[]{:S(2)}) copy-start(bf16[2,256,512]{2,1,0:T(8,128)(2,1)} %constant.23.clone.line_ref) | copy-start | bytes 1572868
  0.6 14.2 %copy-start.6 = (f32[2,2,4,4,256]{4,3,2,1,0:T(4,128)S(1)}, f32[2,2,4,4,256]{4,3,2,1,0:T(4,128)}, u32[]{:S(2)}) copy-start(f32[2,2,4,4,256]{4,3,2,1,0:T(4,128)} %constant.22.clone.fold_ref) | copy-start | bytes 196612
  2.4 12.5 %all-to-all-start = ((bf16[8,64,256]{2,1,0:T(8,128)(2,1)}), bf16[8,64,256]{2,1,0:T(8,128)(2,1)S(1)}, u32[]{:S(2)}, u32[]{:S(2)}) async-start(bf16[8,64,256]{2,1,0:T(8,128)(2,1)} %bitcast.4), calls=%async_computation | async-start | bytes 524288 | tf_op jit(solution)/shard_map/all_to_all | solution.py:470
  8.8 21.1 %copy-start.17 = (s32[4,1]{0,1:T(1,128)S(1)}, s32[4,1]{0,1:T(1,128)}, u32[]{:S(2)}) copy-start(s32[4,1]{0,1:T(1,128)} %param.20) | copy-start | bytes 52
  8.8 21.2 %copy-start.16 = (f32[8,17]{1,0:T(8,128)S(1)}, f32[8,17]{1,0:T(8,128)}, u32[]{:S(2)}) copy-start(f32[8,17]{1,0:T(8,128)} %param.16) | copy-start | bytes 1636
  8.8 22.7 %copy-start.2 = (bf16[4,1,6,64,64]{4,3,2,1,0:T(8,128)(2,1)S(1)}, bf16[4,1,6,64,64]{4,3,2,1,0:T(8,128)(2,1)}, u32[]{:S(2)}) copy-start(bf16[4,1,6,64,64]{4,3,2,1,0:T(8,128)(2,1)} %tiles_ref.1) | copy-start | bytes 589828
  8.8 22.7 %copy-start.3 = (bf16[2,128,768]{2,1,0:T(8,128)(2,1)S(1)}, bf16[2,128,768]{2,1,0:T(8,128)(2,1)}, u32[]{:S(2)}) copy-start(bf16[2,128,768]{2,1,0:T(8,128)(2,1)} %constant.24.clone.table_ref) | copy-start | bytes 1179652
  8.8 22.7 %copy-start.4 = (bf16[256,512]{1,0:T(8,128)(2,1)S(1)}, bf16[256,512]{1,0:T(8,128)(2,1)}, u32[]{:S(2)}) copy-start(bf16[256,512]{1,0:T(8,128)(2,1)} %constant.25.clone.fixed_ref) | copy-start | bytes 786436
  8.8 22.7 %copy-start.7 = (s32[4,1,6]{2,1,0:T(1,128)S(1)}, s32[4,1,6]{2,1,0:T(1,128)}, u32[]{:S(2)}) copy-start(s32[4,1,6]{2,1,0:T(1,128)} %slots_ref.1) | copy-start | bytes 292
  16.9 25.3 %all-to-all-start.1 = ((bf16[32,32,128]{2,1,0:T(8,128)(2,1)}), bf16[32,32,128]{2,1,0:T(8,128)(2,1)S(1)}, u32[]{:S(2)}, u32[]{:S(2)}) async-start(bf16[32,32,128]{2,1,0:T(8,128)(2,1)} %shard_map.140), calls=%async_computation.1 | async-start | bytes 524288 | tf_op jit(solution)/shard_map/all_to_all | solution.py:486
  30.8 0.7 copy-start.13
  31.5 1.0 %copy-start.10 = (bf16[2,8,128,256]{3,2,1,0:T(8,128)(2,1)}, bf16[2,8,128,256]{3,2,1,0:T(8,128)(2,1)S(1)}, u32[]{:S(2)}) copy-start(bf16[2,8,128,256]{3,2,1,0:T(8,128)(2,1)S(1)} %get-tuple-element.12.strip_ref) | copy-start | bytes 3145732
  31.5 1.1 %copy-start.5 = (f32[4,64,256]{2,1,0:T(8,128)S(1)}, f32[4,64,256]{2,1,0:T(8,128)}, u32[]{:S(2)}) copy-start(f32[4,64,256]{2,1,0:T(8,128)} %sky_ref.1) | copy-start | bytes 786436
  31.5 1.7 %copy-start.8 = (bf16[4,9,64,256]{3,2,1,0:T(8,128)(2,1)S(1)}, bf16[4,9,64,256]{3,2,1,0:T(8,128)(2,1)}, u32[]{:S(2)}) copy-start(bf16[4,9,64,256]{3,2,1,0:T(8,128)(2,1)} %dual_ref.3) | copy-start | bytes 3538948
  31.6 1.7 %copy-start.12 = (f32[4,64,256]{2,1,0:T(8,128)S(1)}, f32[4,64,256]{2,1,0:T(8,128)}, u32[]{:S(2)}) copy-start(f32[4,64,256]{2,1,0:T(8,128)} %dirty_ref.1) | copy-start | bytes 786436
  45.2 19.6 %all-to-all-start.2 = ((bf16[32,40,128]{2,1,0:T(8,128)(2,1)}), bf16[32,40,128]{2,1,0:T(8,128)(2,1)S(1)}, u32[]{:S(2)}, u32[]{:S(2)}) async-start(bf16[32,40,128]{2,1,0:T(8,128)(2,1)} %shard_map.144), calls=%async_computation.2 | async-start | bytes 655360 | tf_op jit(solution)/shard_map/all_to_all | solution.py:548
  50.2 14.6 %copy-start.1 = (bf16[2,256,512]{2,1,0:T(8,128)(2,1)S(1)}, bf16[2,256,512]{2,1,0:T(8,128)(2,1)}, u32[]{:S(2)}) copy-start(bf16[2,256,512]{2,1,0:T(8,128)(2,1)} %constant.23.clone.line_ref) | copy-start | bytes 1572868
  50.2 5.6 %collective-permute-start = (bf16[8,16,384]{2,1,0:T(8,128)(2,1)S(1)}, bf16[8,16,384]{2,1,0:T(8,128)(2,1)S(1)}, u32[]{:S(2)}, u32[]{:S(2)}) collective-permute-start(bf16[8,16,384]{2,1,0:T(8,128)(2,1)S(1)} %get-tuple-element.17), channel_id=1, source_target_pairs={{0,8},{8,16},{16,24},{24,32},{32,40},{40,48},{48,56},{56,64},{64,7... | collective-permute-start | bytes 294920 | tf_op jit(solution)/shard_map/ppermute | solution.py:552
  53.8 7.3 %collective-permute-start.1 = (bf16[8,16,384]{2,1,0:T(8,128)(2,1)S(1)}, bf16[8,16,384]{2,1,0:T(8,128)(2,1)S(1)}, u32[]{:S(2)}, u32[]{:S(2)}) collective-permute-start(bf16[8,16,384]{2,1,0:T(8,128)(2,1)S(1)} %get-tuple-element.18), channel_id=1, source_target_pairs={{8,0},{16,8},{24,16},{32,24},{40,32},{48,40},{56,48},{64,56},{72,6... | collective-permute-start | bytes 294920 | tf_op jit(solution)/shard_map/ppermute | solution.py:553
  61.5 16.5 %copy-start.11 = (bf16[2,8,128,256]{3,2,1,0:T(8,128)(2,1)S(1)}, bf16[2,8,128,256]{3,2,1,0:T(8,128)(2,1)}, u32[]{:S(2)}) copy-start(bf16[2,8,128,256]{3,2,1,0:T(8,128)(2,1)} %copy-done.10) | copy-start | bytes 3145732
  61.5 16.5 %copy-start.15 = (f32[9]{0:T(128)S(1)}, f32[9]{0:T(128)}, u32[]{:S(2)}) copy-start(f32[9]{0:T(128)} %bound_ref.1) | copy-start | bytes 112
  64.8 13.2 %copy-start.9 = (bf16[4,9,64,256]{3,2,1,0:T(8,128)(2,1)S(1)}, bf16[4,9,64,256]{3,2,1,0:T(8,128)(2,1)}, u32[]{:S(2)}) copy-start(bf16[4,9,64,256]{3,2,1,0:T(8,128)(2,1)} %dual_ref.3) | copy-start | bytes 3538948
  64.8 13.2 %copy-start.14 = (bf16[512,256]{1,0:T(8,128)(2,1)S(1)}, bf16[512,256]{1,0:T(8,128)(2,1)}, u32[]{:S(2)}) copy-start(bf16[512,256]{1,0:T(8,128)(2,1)} %copy-done.13) | copy-start | bytes 786436

commit v3 on v2

--- a/solution.py
+++ b/solution.py
@@ -110,30 +110,47 @@
     return np.stack([np.cos(ang), np.sin(ang)], axis=1).astype(np.float32)
 
 
+def send_kernel(sky_ref, o_ref, taken, rounded, in_sem, out_sem):
+    channels = taken.shape[0]
+
+    def fetch(c):
+        return pltpu.make_async_copy(sky_ref.at[c], taken.at[c], in_sem.at[c])
+
+    def place(c, h):
+        return pltpu.make_async_copy(rounded.at[c], o_ref.at[2 * c + h], out_sem.at[c, h])
+
+    for c in range(channels):
+        fetch(c).start()
+    for c in range(channels):
+        fetch(c).wait()
+        rounded[c] = taken[c].astype(BF)
+        for h in range(2):
+            place(c, h).start()
+    for c in range(channels):
+        for h in range(2):
+            place(c, h).wait()
+
+
 def forward_kernel(par_ref, x_ref, fold_ref, line_ref, o_ref):
     par = par_ref[1]
     sign = (1 - 2 * par).astype(F32)
     xe = [x_ref[f].astype(F32) + sign * x_ref[f + 4].astype(F32) for f in range(4)]
-    parts = [[], []]
-    for chi in range(2):
-        rows_re, rows_im = [], []
-        for clo in range(2):
-            cos = fold_ref[par, 0, 2 * chi + clo]
-            sin = fold_ref[par, 1, 2 * chi + clo]
-            yr = xe[0] * cos[0:1]
-            yi = xe[0] * sin[0:1]
-            for f in range(1, 4):
-                yr = yr + xe[f] * cos[f : f + 1]
-                yi = yi + xe[f] * sin[f : f + 1]
-            yi = -yi
-            rows_re.append(jnp.concatenate([yr, yi], axis=1))
-            rows_im.append(jnp.concatenate([yi, -yr], axis=1))
-        for part, rows in enumerate((rows_re, rows_im)):
-            r = jnp.concatenate(rows, axis=0).astype(BF)
-            out = dot(line_ref[0], r, LAST) + dot(line_ref[1], r, LAST)
-            parts[part].append(out.reshape(32, 8, 128))
+    rows = [[], []]
+    for cls in range(4):
+        cos = fold_ref[par, 0, cls]
+        sin = fold_ref[par, 1, cls]
+        yr = xe[0] * cos[0:1]
+        yi = xe[0] * sin[0:1]
+        for f in range(1, 4):
+            yr = yr + xe[f] * cos[f : f + 1]
+            yi = yi + xe[f] * sin[f : f + 1]
+        rows[0].append(jnp.concatenate([yr, -yi], axis=1).astype(BF))
+        rows[1].append(jnp.concatenate([-yi, -yr], axis=1).astype(BF))
     for part in range(2):
-        both = jnp.concatenate(parts[part], axis=1)
+        r = jnp.concatenate(rows[part], axis=0)
+        out = dot(line_ref[0], r, LAST) + dot(line_ref[1], r, LAST)
+        both = [out[:, chi * 128 : chi * 128 + 128].reshape(32, 8, 128) for chi in range(2)]
+        both = jnp.concatenate(both, axis=1)
         o_ref[:, part * 16 : (part + 1) * 16, :] = both.astype(BF)
 
 
@@ -143,18 +160,18 @@
     sign = (1 - 2 * par).astype(F32)
     re = t_ref[:, 0:16, :].astype(F32)
     im = t_ref[:, 16:32, :].astype(F32)
-    edge = t_ref[:, 32:40, :].astype(F32).reshape(256, 128).astype(BF)
-    h = dot(edge, line_ref[0], FIRST) + dot(edge, line_ref[1], FIRST)
-    h = jnp.concatenate(
-        [h[0:64, 0:256] - h[64:128, 256:512], h[0:64, 256:512] + h[64:128, 0:256]], axis=1
-    )
+    edge = t_ref[:, 32:40, :].astype(F32)
+    data = [re[:, 0:8], im[:, 0:8], re[:, 8:16], im[:, 8:16], edge]
+    data = jnp.concatenate([d.reshape(256, 128).astype(BF) for d in data], axis=1)
+    wave = dot(data, line_ref[0], FIRST) + dot(data, line_ref[1], FIRST)
+
+    def joined(a, b):
+        return jnp.concatenate([a[:, 0:256] - b[:, 256:512], a[:, 256:512] + b[:, 0:256]], axis=1)
+
+    h = joined(wave[512:576], wave[576:640])
     total = [None] * 4
     for chi in range(2):
-        a = re[:, chi * 8 : chi * 8 + 8, :].reshape(256, 128).astype(BF)
-        b = im[:, chi * 8 : chi * 8 + 8, :].reshape(256, 128).astype(BF)
-        a = dot(a, line_ref[0], FIRST) + dot(a, line_ref[1], FIRST)
-        b = dot(b, line_ref[0], FIRST) + dot(b, line_ref[1], FIRST)
-        u = jnp.concatenate([a[:, 0:256] - b[:, 256:512], a[:, 256:512] + b[:, 0:256]], axis=1)
+        u = joined(wave[chi * 256 : chi * 256 + 128], wave[chi * 256 + 128 : chi * 256 + 256])
         for clo in range(2):
             cls = 2 * chi + clo
             e = h[cls * 16 : cls * 16 + 16]
@@ -176,10 +193,10 @@
         after = total[f + 1][:, 0:128] if f < 7 else none
         line = jnp.concatenate([before, total[f], after], axis=1)
         line = pltpu.roll(line, 512 - 120, 1)
-        pack = jnp.where(f == me - 1, base_ref[0, :, WIDE:], 0.0)
-        pack = pack + jnp.where(f == me + 1, base_ref[1, :, WIDE:], 0.0)
+        pack = jnp.where(f == me - 1, base_ref[0, :, 256:384], 0.0)
+        pack = pack + jnp.where(f == me + 1, base_ref[1, :, 256:384], 0.0)
         o_ref[f, :, 0:256] = line[:, 0:256].astype(BF)
-        o_ref[f, :, 256:384] = (jnp.where(lane < 16, line[:, 256:384], 0.0) + pack).astype(BF)
+        o_ref[f, :, 256:384] = jnp.where(lane < 16, line[:, 256:384], pack).astype(BF)
 
 
 def tiles_kernel(where_ref, slots_ref, count_ref, tiles_ref, table_ref, fixed_ref, o_ref):
@@ -219,29 +236,29 @@
     block = [e_ref[256:320, 384 + t * 128 : 448 + t * 128] for t in range(2)]
     turns = e_ref[256:512, 128:256].astype(F32) + e_ref[256:512, 256:384].astype(F32)
     tc, ts, ec, es = (turns[n * 64 : n * 64 + 64] for n in range(4))
-    first = dot(block[0], rhs[...]) + dot(block[1], rhs[...])
+    first = dot(jnp.concatenate(block, axis=0), rhs[...])
+    first = first[0:64] + first[64:128]
     for p in range(16):
         g = first[:, p * 128 : p * 128 + 128]
         gr = jnp.concatenate([g[0:32], g[0:32]], axis=0)
         gi = jnp.concatenate([g[32:64], g[32:64]], axis=0)
-        mid[:, p * 256 : p * 256 + 128] = (gr * tc + gi * ts).astype(BF)
-        mid[:, p * 256 + 128 : p * 256 + 256] = (gi * tc - gr * ts).astype(BF)
-    pieces = []
-    for g in range(4):
-        m = mid[:, g * 1024 : (g + 1) * 1024]
-        pieces.append(
-            (dot(m, e_ref[0:128, 0:1024], LAST) + dot(m, e_ref[128:256, 0:1024], LAST)).astype(BF)
-        )
-    spec = jnp.concatenate(pieces, axis=1)
+        down = slice(p // 4 * 64, p // 4 * 64 + 64)
+        at = p % 4 * 256
+        mid[down, at : at + 128] = (gr * tc + gi * ts).astype(BF)
+        mid[down, at + 128 : at + 256] = (gi * tc - gr * ts).astype(BF)
+    spec = dot(mid[...], e_ref[0:256, 0:1024], LAST)
+    spec = (spec[:, 0:128] + spec[:, 128:256]).astype(BF)
+    spec = jnp.concatenate([spec[g * 64 : g * 64 + 64] for g in range(4)], axis=1)
     mixed = dot(e_ref[256:640, 0:64], spec)
     lane_slot = (lax.broadcasted_iota(jnp.int32, (64, 512), 1) % 32) // 4
     weighted = jnp.where(lane_slot == 0, mixed[0:64], 0.0)
     for k in range(1, SLOTS):
         weighted = jnp.where(lane_slot == k, mixed[k * 64 : k * 64 + 64], weighted)
     weighted = weighted.astype(BF)
+    w = jnp.concatenate([weighted[:, g * 128 : g * 128 + 128] for g in range(4)], axis=0)
+    spreads = dot(jnp.concatenate([w, w], axis=1), e_ref[0:256, :])
     for g in range(4):
-        w = weighted[:, g * 128 : g * 128 + 128]
-        z = dot(w, e_ref[0:128, :]) + dot(w, e_ref[128:256, :])
+        z = spreads[g * 64 : g * 64 + 64]
         for v in range(4):
             p = g * 4 + v
             zr = z[:, v * 256 : v * 256 + 128]
@@ -258,8 +275,11 @@
             lanes = slice((2 * g + j) * 128, (2 * g + j) * 128 + 128)
             edge[0:32, lanes] = (hr[0:32] + hr[32:64]).astype(BF)
             edge[32:64, lanes] = (hi[0:32] + hi[32:64]).astype(BF)
-    last = dot(block[0], rhs[...], FIRST) + dot(block[1], rhs[...], FIRST)
-    outer = dot(block[0][:, 0:32], edge[...], FIRST) + dot(block[1][:, 0:32], edge[...], FIRST)
+    block = jnp.concatenate(block, axis=1)
+    last = dot(block, rhs[...], FIRST)
+    last = last[0:64] + last[64:128]
+    outer = dot(block, edge[...], FIRST)
+    outer = outer[0:32] + outer[64:96]
     for p in range(16):
         lanes = slice(p * 128, p * 128 + 128)
         at = (p % 2) * 8 + p // 2
@@ -270,23 +290,32 @@
     o_ref[...] = rows[...].reshape(32, 40, 128).astype(BF)
 
 
-def band_kernel(taps_ref, strip_ref, down_ref):
+def band_kernel(taps_ref, strip_ref):
+    for k in range(FRAMES):
+        wide = jnp.broadcast_to(taps_ref[k : k + 1, :], (128, 256))
+        band = pltpu.roll(wide, 0, 1, stride=1, stride_axis=0)
+        high = band.astype(BF)
+        strip_ref[0, k] = high
+        strip_ref[1, k] = (band - high.astype(F32)).astype(BF)
+
+
+def bands_kernel(taps_ref, o_ref):
     lane = lax.broadcasted_iota(jnp.int32, (64, 256), 1)
     for k in range(FRAMES):
         wide = jnp.broadcast_to(taps_ref[k : k + 1, :], (128, 256))
         band = pltpu.roll(wide, 0, 1, stride=1, stride_axis=0)
         high = band.astype(BF)
         low = band - high.astype(F32)
-        strip_ref[0, k] = high
-        strip_ref[1, k] = low.astype(BF)
+        o_ref[k * 128 : k * 128 + 128, :] = high
+        o_ref[1024 + k * 128 : 1152 + k * 128, :] = low.astype(BF)
+        low = jnp.where(lane < 80, low[0:64], 0.0)
         high = jnp.where(lane < 80, high[0:64].astype(F32), 0.0)
-        low = jnp.where(lane < 80, low[0:64], 0.0)
         row = high + pltpu.roll(high, 80, 1) + pltpu.roll(low, 160, 1)
-        down_ref[k * 64 : k * 64 + 64, :] = row.astype(BF)
+        o_ref[2048 + k * 64 : 2112 + k * 64, :] = row.astype(BF)
 
 
 def synth_kernel(
-    where_ref, live_ref, dual_ref, sky_ref, dirty_ref, strip_ref, o_ref, head_ref, tail_ref, across
+    where_ref, live_ref, dual_ref, sky_ref, dirty_ref, strip_ref, o_ref, across
 ):
     channels = sky_ref.shape[0]
     row = lax.broadcasted_iota(jnp.int32, (80, WIDE), 0) + where_ref[2] * ROWS - RADIUS
@@ -325,10 +354,20 @@
         total = jnp.where(inside, total, OUTSIDE)
         total = jnp.where(lane < COLS + 2 * RADIUS, total, 0.0)
         sky = jnp.concatenate([edge, sky, edge], axis=0)
-        for at, cells in ((c, total), (channels + c, sky)):
-            o_ref[at] = cells
-            head_ref[at] = cells[0:16].astype(BF)
-            tail_ref[at] = cells[64:80].astype(BF)
+        o_ref[c] = total
+        o_ref[channels + c] = sky
+
+
+def head_kernel(base_ref, o_ref):
+    o_ref[...] = base_ref[:, 0:16].astype(BF)
+
+
+def tail_kernel(base_ref, o_ref):
+    o_ref[...] = base_ref[:, 64:80].astype(BF)
+
+
+def take_kernel(where_ref, dual_ref, o_ref):
+    o_ref[...] = dual_ref[...]
 
 
 def edge_kernel(base_ref, before_ref, after_ref, o_ref):
@@ -337,9 +376,9 @@
     head = jnp.zeros((80, 128), F32)
     tail = jnp.zeros((80, 128), F32)
     for c in range(both):
-        o_ref[c, 0:16, 0:WIDE] = base_ref[c, 0:16] + before_ref[c].astype(F32)
-        o_ref[c, 16:64, 0:WIDE] = base_ref[c, 16:64]
-        o_ref[c, 64:80, 0:WIDE] = base_ref[c, 64:80] + after_ref[c].astype(F32)
+        o_ref[c, 0:16] = base_ref[c, 0:16] + before_ref[c].astype(F32)
+        o_ref[c, 16:64] = base_ref[c, 16:64]
+        o_ref[c, 64:80] = base_ref[c, 64:80] + after_ref[c].astype(F32)
         first = o_ref[c, :, 0:128]
         final = o_ref[c, :, 256:384]
         if c < both // 2:
@@ -350,85 +389,113 @@
             at = 80 + 8 * (c - both // 2)
             head = head + pltpu.roll(jnp.where((lane >= 8) & (lane < 16), first, 0.0), at - 8, 1)
             tail = tail + pltpu.roll(jnp.where(lane < 8, final, 0.0), at, 1)
-    o_ref[0, :, WIDE:] = head
-    o_ref[1, :, WIDE:] = tail
-    for c in range(2, both):
-        o_ref[c, :, WIDE:] = jnp.zeros((80, 128), F32)
+    o_ref[0, :, 256:384] = o_ref[0, :, 256:384] + head
+    o_ref[1, :, 256:384] = o_ref[1, :, 256:384] + tail
 
 
 def frames_kernel(
-    bound_ref, where_ref, half_ref, base_ref, dual_ref, strip_ref, down_ref, image_ref, o_ref, probes, wide, down
+    bound_ref,
+    where_ref,
+    half_ref,
+    base_ref,
+    dual_ref,
+    bands_ref,
+    image_ref,
+    o_ref,
+    given,
+    image_buf,
+    dual_buf,
+    probes,
+    wide,
+    down,
+    given_sem,
+    image_sem,
+    dual_sem,
 ):
-    step = pl.program_id(0)
-    channels = image_ref.shape[0]
-    bound = bound_ref[step]
-
-    def finish(analysis):
-        cand = [dual_ref[c, 0].astype(F32) + STEP_DUAL * analysis(c) for c in range(channels)]
+    channels = image_buf.shape[0]
+    rows = channels * ROWS
+
+    def given_copy(k):
+        return pltpu.make_async_copy(dual_ref.at[:, k], given.at[k], given_sem.at[k])
+
+    for k in range(FRAMES + 1):
+        given_copy(k).start()
+
+    def dual_copy(k):
+        return pltpu.make_async_copy(dual_buf.at[k], o_ref.at[:, k], dual_sem.at[k])
+
+    def finish(k, analysis):
+        bound = bound_ref[k]
+        given_copy(k).wait()
+        cand = [given[k, c].astype(F32) + STEP_DUAL * analysis(c) for c in range(channels)]
         square = cand[0] * cand[0]
         for c in range(1, channels):
             square = square + cand[c] * cand[c]
         factor = bound * lax.rsqrt(jnp.maximum(square, bound * bound))
         for c in range(channels):
-            o_ref[c, 0] = (cand[c] * factor).astype(BF)
-
-    @pl.when(step == 0)
-    def _():
-        wide[...] = jnp.zeros_like(wide)
-        me = where_ref[3]
-        last = half_ref.shape[0] - 1
-        lane = lax.broadcasted_iota(jnp.int32, (80, 128), 1)
-        left = half_ref[jnp.maximum(me - 1, 0), :, 256:384].astype(F32)
-        left = jnp.where(me > 0, left, 0.0)
-        right = half_ref[jnp.minimum(me + 1, last), :, 256:384].astype(F32)
-        right = jnp.where(me < last, right, 0.0)
-        for c in range(channels):
-            gram = half_ref[2 * c].astype(F32) + half_ref[2 * c + 1].astype(F32)
-            gram = [gram[:, 0:128], gram[:, 128:256], jnp.where(lane < 16, gram[:, 256:384], 0.0)]
-            base = [base_ref[c, :, b * 128 : b * 128 + 128] for b in range(3)]
-            sky = [base_ref[channels + c, :, b * 128 : b * 128 + 128] for b in range(3)]
-            at = 16 + 16 * c
-            base[0] = base[0] + jnp.where(lane < 16, pltpu.roll(left, 128 - at, 1), 0.0)
-            base[2] = base[2] + jnp.where(lane < 16, pltpu.roll(right, 128 - at, 1), 0.0)
-            at = 80 + 8 * c
-            sky[0] = sky[0] + jnp.where(lane < 8, pltpu.roll(left, 128 - at, 1), 0.0)
-            shown = (lane >= 8) & (lane < 16)
-            sky[2] = sky[2] + jnp.where(shown, pltpu.roll(right, 136 - at, 1), 0.0)
-            image = [jnp.maximum(base[b] - STEP_PRIMAL * gram[b], 0.0) for b in range(3)]
-            probe = jnp.concatenate([2.0 * image[b] - sky[b] for b in range(3)], axis=1)
-            image = pltpu.roll(jnp.concatenate(image, axis=1), WIDE - 8, 1)
-            image_ref[c] = image[8:72, 0:256]
-            probes[c] = pltpu.roll(probe, WIDE - 8, 1)[8:72, 0:256]
-            high = probe.astype(BF)
-            low = (probe - high.astype(F32)).astype(BF)
-            wide[0:80, :] = high
-            wide[80:160, :] = low
-            wide[160:240, :] = high
-            d = dot(down_ref[...], wide[...])
-            high = d.astype(BF)
-            down[0, c] = high
-            down[1, c] = (d - high.astype(F32)).astype(BF)
-        finish(lambda c: probes[c])
-
-    @pl.when(step > 0)
-    def _():
-        at = pl.multiple_of((step - 1) * ROWS, ROWS)
+            dual_buf[k, c] = (cand[c] * factor).astype(BF)
+        dual_copy(k).start()
+
+    wide[...] = jnp.zeros_like(wide)
+    me = where_ref[3]
+    last = half_ref.shape[0] - 1
+    lane = lax.broadcasted_iota(jnp.int32, (80, 128), 1)
+    left = half_ref[jnp.maximum(me - 1, 0), :, 256:384].astype(F32)
+    left = jnp.where(me > 0, left, 0.0)
+    right = half_ref[jnp.minimum(me + 1, last), :, 256:384].astype(F32)
+    right = jnp.where(me < last, right, 0.0)
+    for c in range(channels):
+        gram = half_ref[2 * c].astype(F32) + half_ref[2 * c + 1].astype(F32)
+        gram = [gram[:, 0:128], gram[:, 128:256], jnp.where(lane < 16, gram[:, 256:384], 0.0)]
+        base = [base_ref[c, :, b * 128 : b * 128 + 128] for b in range(3)]
+        sky = [base_ref[channels + c, :, b * 128 : b * 128 + 128] for b in range(3)]
+        base[2] = jnp.where(lane < 16, base[2], 0.0)
+        at = 16 + 16 * c
+        base[0] = base[0] + jnp.where(lane < 16, pltpu.roll(left, 128 - at, 1), 0.0)
+        base[2] = base[2] + jnp.where(lane < 16, pltpu.roll(right, 128 - at, 1), 0.0)
+        at = 80 + 8 * c
+        sky[0] = sky[0] + jnp.where(lane < 8, pltpu.roll(left, 128 - at, 1), 0.0)
+        shown = (lane >= 8) & (lane < 16)
+        sky[2] = sky[2] + jnp.where(shown, pltpu.roll(right, 136 - at, 1), 0.0)
+        image = [jnp.maximum(base[b] - STEP_PRIMAL * gram[b], 0.0) for b in range(3)]
+        probe = jnp.concatenate([2.0 * image[b] - sky[b] for b in range(3)], axis=1)
+        image = pltpu.roll(jnp.concatenate(image, axis=1), WIDE - 8, 1)
+        image_buf[c] = image[8:72, 0:256]
+        probes[c] = pltpu.roll(probe, WIDE - 8, 1)[8:72, 0:256]
+        high = probe.astype(BF)
+        low = (probe - high.astype(F32)).astype(BF)
+        wide[0:80, :] = high
+        wide[80:160, :] = low
+        wide[160:240, :] = high
+        d = dot(bands_ref[2048:2560, :], wide[...])
+        high = d.astype(BF)
+        down[0, c] = high
+        down[1, c] = (d - high.astype(F32)).astype(BF)
+    image_copy = pltpu.make_async_copy(image_buf, image_ref, image_sem)
+    image_copy.start()
+    finish(0, lambda c: probes[c])
+    for k in range(1, FRAMES + 1):
+        at = (k - 1) * ROWS
         a = None
         for t in range(2):
-            d = jnp.concatenate([down[t, c, pl.ds(at, ROWS), :] for c in range(channels)], axis=0)
+            d = jnp.concatenate([down[t, c, at : at + ROWS, :] for c in range(channels)], axis=0)
             both = jnp.concatenate([d[:, 0:256], d[:, 128:384]], axis=0)
+            high = bands_ref[(k - 1) * 128 : k * 128, :]
             if t == 0:
-                band = jnp.concatenate([strip_ref[0, 0], strip_ref[1, 0]], axis=0)
+                band = jnp.concatenate([high, bands_ref[896 + k * 128 : 1024 + k * 128, :]], axis=0)
                 term = dot(both, band, LAST)
                 a = term[:, 0:128] + term[:, 128:256]
             else:
-                a = a + dot(both, strip_ref[0, 0], LAST)
-        rows = channels * ROWS
+                a = a + dot(both, high, LAST)
         finish(
+            k,
             lambda c: jnp.concatenate(
                 [a[c * ROWS : c * ROWS + ROWS], a[rows + c * ROWS : rows + c * ROWS + ROWS]], axis=1
-            )
+            ),
         )
+    image_copy.wait()
+    for k in range(FRAMES + 1):
+        dual_copy(k).wait()
 
 
 VM = pl.BlockSpec(memory_space=pltpu.VMEM)
@@ -447,8 +514,32 @@
     )(*args)
 
 
-def after(values, event):
-    return lax.optimization_barrier((*values, event))[:-1]
+def frames_call(thresholds, where, halves, base, dual, bands):
+    channels = dual.shape[0]
+    block = (channels, ROWS, COLS)
+    return pl.pallas_call(
+        frames_kernel,
+        out_shape=(jax.ShapeDtypeStruct(block, F32), jax.ShapeDtypeStruct(dual.shape, BF)),
+        in_specs=[SM, SM, VM, VM, pl.BlockSpec(memory_space=pltpu.HBM), VM],
+        out_specs=(pl.BlockSpec(memory_space=pl.ANY), pl.BlockSpec(memory_space=pl.ANY)),
+        scratch_shapes=[
+            pltpu.VMEM((FRAMES + 1, *block), BF),
+            pltpu.VMEM(block, F32),
+            pltpu.VMEM((FRAMES + 1, *block), BF),
+            pltpu.VMEM(block, F32),
+            pltpu.VMEM((256, WIDE), BF),
+            pltpu.VMEM((2, channels, FRAMES * ROWS, WIDE), BF),
+            pltpu.SemaphoreType.DMA((FRAMES + 1,)),
+            pltpu.SemaphoreType.DMA(()),
+            pltpu.SemaphoreType.DMA((FRAMES + 1,)),
+        ],
+        compiler_params=pltpu.CompilerParams(vmem_limit_bytes=VMEM_LIMIT),
+        cost_estimate=pl.CostEstimate(flops=1 << 31, bytes_accessed=3 << 20, transcendentals=0),
+    )(thresholds, where, halves, base, dual, bands)
+
+
+def after(values, *events):
+    return lax.optimization_barrier((*values, *events))[: len(values)]
 
 
 def body(
@@ -466,24 +557,20 @@
     place = lax.axis_index("fou")
     where = jnp.stack([place >> 1, place & 1, lax.axis_index("img"), place]).astype(jnp.int32)
 
-    sent = jnp.repeat(sky_estimate.astype(BF), 2, axis=0)
+    sent = pl.pallas_call(
+        send_kernel,
+        out_shape=jax.ShapeDtypeStruct((2 * channels, tile_rows, tile_cols), BF),
+        in_specs=[pl.BlockSpec(memory_space=pltpu.HBM)],
+        out_specs=pl.BlockSpec(memory_space=pltpu.HBM),
+        scratch_shapes=[
+            pltpu.VMEM(sky_estimate.shape, F32),
+            pltpu.VMEM(sky_estimate.shape, BF),
+            pltpu.SemaphoreType.DMA((channels,)),
+            pltpu.SemaphoreType.DMA((channels, 2)),
+        ],
+        compiler_params=pltpu.CompilerParams(vmem_limit_bytes=62 << 20),
+    )(sky_estimate)
     lines = lax.all_to_all(sent, "fou", split_axis=0, concat_axis=0, tiled=True)
-
-    line = np.stack(line_table())
-    fold = fold_table()
-    packed = call(
-        forward_kernel,
-        jax.ShapeDtypeStruct((PEERS_IMG, 32, 128), BF),
-        [],
-        1 << 29,
-        1 << 20,
-        where,
-        lines,
-        fold,
-        line,
-        scalars=1,
-    )
-    received = lax.all_to_all(packed, "img", split_axis=0, concat_axis=0, tiled=True)
 
     spread = call(
         tiles_kernel,
@@ -500,23 +587,34 @@
         scalars=3,
     )
 
-    strip, down = call(
-        band_kernel,
-        (
-            jax.ShapeDtypeStruct((2, FRAMES, 128, 256), BF),
-            jax.ShapeDtypeStruct((FRAMES * ROWS, 256), BF),
-        ),
+    taps = jnp.pad(filters, ((0, 0), (0, 256 - filters.shape[1])))
+    strip = call(
+        band_kernel, jax.ShapeDtypeStruct((2, FRAMES, 128, 256), BF), [], 1 << 20, 1 << 20, taps
+    )
+
+    (ready_where,) = after((where,), strip)
+
+    line = np.stack(line_table())
+    fold = fold_table()
+    packed = call(
+        forward_kernel,
+        jax.ShapeDtypeStruct((PEERS_IMG, 32, 128), BF),
         [],
+        1 << 29,
         1 << 20,
-        1 << 20,
-        jnp.pad(filters, ((0, 0), (0, 256 - filters.shape[1]))),
-    )
-    ends = jax.ShapeDtypeStruct((2 * channels, 16, WIDE), BF)
+        ready_where,
+        lines,
+        fold,
+        line,
+        scalars=1,
+    )
+    received = lax.all_to_all(packed, "img", split_axis=0, concat_axis=0, tiled=True)
+
     extended = jax.ShapeDtypeStruct((2 * channels, tile_rows + 16, WIDE), F32)
     (late_where,) = after((where,), packed)
-    base, head, tail = call(
+    base = call(
         synth_kernel,
-        (extended, ends, ends),
+        extended,
         [pltpu.VMEM((channels, FRAMES * ROWS, WIDE), BF)],
         1 << 31,
         4 << 20,
@@ -528,12 +626,15 @@
         strip,
         scalars=2,
     )
-    (received,) = after((received,), head)
+    ends = jax.ShapeDtypeStruct((2 * channels, 16, WIDE), BF)
+    head = call(head_kernel, ends, [], 1 << 16, 1 << 18, base)
+    tail = call(tail_kernel, ends, [], 1 << 16, 1 << 18, base)
+    (received,) = after((received,), head, tail)
 
     scratch = [
         pltpu.VMEM((1280, 128), F32),
         pltpu.VMEM((64, 2048), BF),
-        pltpu.VMEM((64, 4096), BF),
+        pltpu.VMEM((256, 1024), BF),
         pltpu.VMEM((64, 1024), BF),
     ]
     weighted = call(
@@ -553,7 +654,7 @@
     from_after = lax.ppermute(head, "img", [(j, i) for i, j in steps])
     base = call(
         edge_kernel,
-        jax.ShapeDtypeStruct((2 * channels, tile_rows + 16, WIDE + 128), F32),
+        extended,
         [],
         1 << 20,
         4 << 20,
@@ -576,33 +677,11 @@
     )
     halves = lax.all_to_all(blocks, "fou", split_axis=0, concat_axis=0, tiled=True)
 
-    dual_spec = pl.BlockSpec((channels, 1, tile_rows, tile_cols), lambda f: (0, f, 0, 0))
-    whole = lambda a: pl.BlockSpec(a.shape, lambda f: (0,) * a.ndim)
-    return pl.pallas_call(
-        frames_kernel,
-        out_shape=(
-            jax.ShapeDtypeStruct(sky_estimate.shape, F32),
-            jax.ShapeDtypeStruct(dual_coeffs.shape, BF),
-        ),
-        grid=(FRAMES + 1,),
-        in_specs=[
-            SM,
-            SM,
-            whole(halves),
-            whole(base),
-            dual_spec,
-            pl.BlockSpec((2, 1, 128, 256), lambda f: (0, jnp.maximum(f - 1, 0), 0, 0)),
-            whole(down),
-        ],
-        out_specs=(pl.BlockSpec(sky_estimate.shape, lambda f: (0, 0, 0)), dual_spec),
-        scratch_shapes=[
-            pltpu.VMEM(sky_estimate.shape, F32),
-            pltpu.VMEM((256, 384), BF),
-            pltpu.VMEM((2, channels, FRAMES * ROWS, 384), BF),
-        ],
-        compiler_params=pltpu.CompilerParams(vmem_limit_bytes=VMEM_LIMIT),
-        cost_estimate=pl.CostEstimate(flops=1 << 31, bytes_accessed=3 << 20, transcendentals=0),
-    )(thresholds, where, halves, base, dual_coeffs, strip, down)
+    (late_taps,) = after((taps,), blocks)
+    bands = call(
+        bands_kernel, jax.ShapeDtypeStruct((2560, 256), BF), [], 1 << 20, 1 << 20, late_taps
+    )
+    return frames_call(thresholds, where, halves, base, pltpu.with_memory_space_constraint(dual_coeffs, pltpu.HBM), bands)
 
 
 def solution(mesh):

time: 84.9 us -> 84.6 us (level)
  blocking collectives: 11.8 us -> 0 us
  waiting for transfers between devices: 19.6 us -> 26.8 us
  starting transfers between devices: 29.1 us -> 32.6 us
  Pallas kernels: 18.8 us -> 20 us
  other arithmetic: 1.1 us -> 0.08 us
    all_to_all x1 -> x0, blocking collectives: 11.8 us -> none  [body(): lax.all_to_all(blocks, 'fou', split_axis=0, concat_axis=0, tiled=True)]
    all_to_all x0 -> x1, waiting for transfers between devices: none -> 7.92 us  [body(): lax.all_to_all(blocks, 'fou', split_axis=0, concat_axis=0, tiled=True)]
    all_to_all x0 -> x1, starting transfers between devices: none -> 3.62 us  [body(): lax.all_to_all(blocks, 'fou', split_axis=0, concat_axis=0, tiled=True)]
    convert_element_type x1 -> x0, other arithmetic: 1.02 us -> none  [body(): sent = jnp.repeat(sky_estimate.astype(BF), 2, axis=0)]
    all_to_all x1, waiting for transfers between devices: 5.96 us -> 4.96 us  [body(): lines = lax.all_to_all(sent, 'fou', split_axis=0, concat_axis=0, tiled=True)]
    pallas_call x1 -> x2, Pallas kernels: 6.42 us -> 7.19 us  [the longest x1 5.46 us: frames_call(): pl.pallas_call(frames_kernel, out_shape=(jax.ShapeDtypeStruct(block, F32)...]
    unnamed x37 -> x25, local copies, waits for them, and re-layouts: 1.72 us -> 2.36 us
    pallas_call x7 -> x10, Pallas kernels: 12.4 us -> 12.8 us  [call(): pl.pallas_call(kernel, out_shape=out_shape, in_specs=[SM] * scalars + [VM...]
  transfers between devices with their start and end apart: 5 -> 6, of which waited for: 4 -> 5; matrix products, arithmetic and copies ran while one was open for 0% -> 1% of each run, Pallas kernels for 7% -> 8%
where the time goes in v3:
time: 84.6 us; the launch traced here: 84 us
  starting transfers between devices  32.6 us (39%)
  waiting for transfers between devices  26.8 us (32%)
  Pallas kernels  20 us (24%)
  local copies, waits for them, and re-layouts  3.05 us (4%)
  between operations  1.47 us (2%)
    pallas_call x10, Pallas kernels, call(): pl.pallas_call(kernel, out_shape=out_shape, in_specs=[SM] * scalars + [VM...  12.8 us
    all_to_all x1, starting transfers between devices, body(): lax.all_to_all(packed, 'img', split_axis=0, concat_axis=0, tiled=True)  12.3 us
    all_to_all x1, waiting for transfers between devices, body(): lax.all_to_all(blocks, 'fou', split_axis=0, concat_axis=0, tiled=True)  7.92 us
    all_to_all x1, starting transfers between devices, body(): lines = lax.all_to_all(sent, 'fou', split_axis=0, concat_axis=0, tiled=True)  6.39 us
    pallas_call x1, Pallas kernels, frames_call(): pl.pallas_call(frames_kernel, out_shape=(jax.ShapeDtypeStruct(block, F32)...  5.46 us
    ppermute x1, waiting for transfers between devices, body(): from_after = lax.ppermute(head, 'img', [(j, i) for i, j in steps])  5.41 us
    all_to_all x1, waiting for transfers between devices, body(): lax.all_to_all(packed, 'img', split_axis=0, concat_axis=0, tiled=True)  5.04 us
    all_to_all x1, waiting for transfers between devices, body(): lines = lax.all_to_all(sent, 'fou', split_axis=0, concat_axis=0, tiled=True)  4.96 us
  transfers between devices with their start and end apart: 6, of which 5 were waited for; matrix products, arithmetic and copies ran while one was open for 1% of the time, Pallas kernels for 8%

profile of v3, /device:TPU:1, one launch (start us, length us, event | category | flops | bytes accessed | tf_op | source)
XLA Modules:
  0.0 84.0 jit_solution(10814198792036494746)
XLA Ops:
  0.6 0.0 copy-start
  0.6 0.0 copy-start.6
  0.7 1.7 %shard_map.141 = bf16[8,64,256]{2,1,0:T(8,128)(2,1)} custom-call(f32[4,64,256]{2,1,0:T(8,128)} %sky_ref.3), custom_call_target="tpu_custom_call" | custom-call | tf_op jit(solution)/shard_map/pallas_call | solution.py:560
  2.4 6.4 %all-to-all-start = ((bf16[8,64,256]{2,1,0:T(8,128)(2,1)}), bf16[8,64,256]{2,1,0:T(8,128)(2,1)S(1)}, u32[]{:S(2)}, u32[]{:S(2)}) async-start(bf16[8,64,256]{2,1,0:T(8,128)(2,1)} %shard_map.141), calls=%async_computation | async-start | bytes 524288 | tf_op jit(solution)/shard_map/all_to_all | solution.py:573
  8.8 0.7 pad.4.taps_ref
  9.5 0.3 shard_map.140.strip_ref
  9.8 0.0 copy-start.11
  9.8 0.0 copy-start.5
  9.8 0.1 pad_add_fusion.par_ref.where_ref
  9.9 5.0 %all-to-all-done.x_ref = bf16[8,64,256]{2,1,0:T(8,128)(2,1)S(1)} async-done(((bf16[8,64,256]{2,1,0:T(8,128)(2,1)}), bf16[8,64,256]{2,1,0:T(8,128)(2,1)S(1)}, u32[]{:S(2)}, u32[]{:S(2)}) %all-to-all-start) | async-done | bytes 262176 | tf_op jit(solution)/shard_map/all_to_all | solution.py:573
  14.9 0.0 copy-done
  14.9 0.0 copy-done.6
  14.9 1.8 %shard_map.142 = bf16[32,32,128]{2,1,0:T(8,128)(2,1)} custom-call(s32[4]{0:T(128)S(1)} %pad_add_fusion.par_ref.where_ref, bf16[8,64,256]{2,1,0:T(8,128)(2,1)S(1)} %all-to-all-done.x_ref, f32[2,2,4,4,256]{4,3,2,1,0:T(4,128)S(1)} %copy-done.6, bf16[2,256,512]{2,1,0:T(8,128)(2,1)S(1)} %copy-done), custom_call_target="tpu_custom_call" | custom-call | flops 536870912 | bytes 1048576 | tf_op jit(solution)/shard_map/pallas_call | solution.py:506
  16.7 12.3 %all-to-all-start.1 = ((bf16[32,32,128]{2,1,0:T(8,128)(2,1)}), bf16[32,32,128]{2,1,0:T(8,128)(2,1)S(1)}, u32[]{:S(2)}, u32[]{:S(2)}) async-start(bf16[32,32,128]{2,1,0:T(8,128)(2,1)} %shard_map.142), calls=%async_computation.1 | async-start | bytes 524288 | tf_op jit(solution)/shard_map/all_to_all | solution.py:611
  29.6 0.0 copy-done.11
  29.6 0.1 copy.15.count_ref
  29.7 0.0 copy-done.5
  29.7 0.0 copy-start.8
  29.7 1.3 %copy-done.8 = bf16[4,9,64,256]{3,2,1,0:T(8,128)(2,1)S(1)} copy-done((bf16[4,9,64,256]{3,2,1,0:T(8,128)(2,1)S(1)}, bf16[4,9,64,256]{3,2,1,0:T(8,128)(2,1)}, u32[]{:S(2)}) %copy-start.8) | copy-done | bytes 1179672
  31.0 0.0 copy-start.9
  31.0 0.9 %copy-done.9 = f32[4,64,256]{2,1,0:T(8,128)S(1)} copy-done((f32[4,64,256]{2,1,0:T(8,128)S(1)}, f32[4,64,256]{2,1,0:T(8,128)}, u32[]{:S(2)}) %copy-start.9) | copy-done | bytes 262168
  32.0 0.0 copy-start.2
  32.0 0.0 copy-start.3
  32.0 0.0 copy-start.4
  32.0 0.0 copy-start.7
  32.0 4.0 %shard_map.143.base_ref = f32[8,80,384]{2,1,0:T(8,128)S(1)} custom-call(s32[4]{0:T(128)S(1)} %pad_add_fusion.par_ref.where_ref, s32[1]{0:T(128)S(6)} %copy.16.live_ref, bf16[4,9,64,256]{3,2,1,0:T(8,128)(2,1)S(1)} %copy-done.8, f32[4,64,256]{2,1,0:T(8,128)S(1)} %copy-done.5, f32[4,64,256]{2,1,0:T(8,128)S(1)} %copy-done.9, ...), custom_call_target="tpu_custom_call" | custom-call | flops 2147483648 | bytes 4194304 | tf_op jit(solution)/shard_map/pallas_call | solution.py:506
  36.0 0.0 copy-done.2
  36.0 0.0 copy-done.3
  36.0 0.0 copy-done.4
  36.0 0.0 copy-done.7
  36.0 0.9 %shard_map.146.e_ref = bf16[640,1536]{1,0:T(8,128)(2,1)S(1)} custom-call(s32[4]{0:T(128)S(1)} %pad_add_fusion.par_ref.where_ref, s32[4,1,6]{2,1,0:T(1,128)S(1)} %copy-done.7, s32[4,1]{1,0:T(4,128)S(1)} %copy.15.count_ref, bf16[4,1,6,64,64]{4,3,2,1,0:T(8,128)(2,1)S(1)} %copy-done.2, bf16[2,128,768]{2,1,0:T(8,128)(2,1)S(1)} %copy-done.3, ...), custom_call_target="tpu_custom_call" | custom-call | flops 8388608 | bytes 1048576 | tf_op jit(solution)/shard_map/pallas_call | solution.py:506
  37.0 5.0 %all-to-all-done.1.d_ref = bf16[32,32,128]{2,1,0:T(8,128)(2,1)S(1)} async-done(((bf16[32,32,128]{2,1,0:T(8,128)(2,1)}), bf16[32,32,128]{2,1,0:T(8,128)(2,1)S(1)}, u32[]{:S(2)}, u32[]{:S(2)}) %all-to-all-start.1) | async-done | bytes 262176 | tf_op jit(solution)/shard_map/all_to_all | solution.py:611
  42.0 2.5 %shard_map.147 = bf16[32,40,128]{2,1,0:T(8,128)(2,1)} custom-call(bf16[32,32,128]{2,1,0:T(8,128)(2,1)S(1)} %all-to-all-done.1.d_ref, bf16[640,1536]{1,0:T(8,128)(2,1)S(1)} %shard_map.146.e_ref), custom_call_target="tpu_custom_call" | custom-call | flops 536870912 | bytes 1048576 | tf_op jit(solution)/shard_map/pallas_call | solution.py:506
  44.5 0.0 copy-start.1
  44.5 4.9 %all-to-all-start.2 = ((bf16[32,40,128]{2,1,0:T(8,128)(2,1)}), bf16[32,40,128]{2,1,0:T(8,128)(2,1)S(1)}, u32[]{:S(2)}, u32[]{:S(2)}) async-start(bf16[32,40,128]{2,1,0:T(8,128)(2,1)} %shard_map.147), calls=%async_computation.2 | async-start | bytes 655360 | tf_op jit(solution)/shard_map/all_to_all | solution.py:649
  49.4 3.5 %collective-permute-start = (bf16[8,16,384]{2,1,0:T(8,128)(2,1)S(1)}, bf16[8,16,384]{2,1,0:T(8,128)(2,1)S(1)}, u32[]{:S(2)}, u32[]{:S(2)}) collective-permute-start(bf16[8,16,384]{2,1,0:T(8,128)(2,1)S(1)} %shard_map.145), channel_id=1, source_target_pairs={{0,8},{8,16},{16,24},{24,32},{32,40},{40,48},{48,56},{56,64},{64,7... | collective-permute-start | bytes 294920 | tf_op jit(solution)/shard_map/ppermute | solution.py:653
  52.9 1.9 %collective-permute-start.1 = (bf16[8,16,384]{2,1,0:T(8,128)(2,1)S(1)}, bf16[8,16,384]{2,1,0:T(8,128)(2,1)S(1)}, u32[]{:S(2)}, u32[]{:S(2)}) collective-permute-start(bf16[8,16,384]{2,1,0:T(8,128)(2,1)S(1)} %shard_map.144), channel_id=1, source_target_pairs={{8,0},{16,8},{24,16},{32,24},{40,32},{48,40},{56,48},{64,56},{72,6... | collective-permute-start | bytes 294920 | tf_op jit(solution)/shard_map/ppermute | solution.py:654
  54.9 0.0 collective-permute-done.before_ref
  54.9 5.4 %collective-permute-done.1.after_ref = bf16[8,16,384]{2,1,0:T(8,128)(2,1)S(1)} collective-permute-done((bf16[8,16,384]{2,1,0:T(8,128)(2,1)S(1)}, bf16[8,16,384]{2,1,0:T(8,128)(2,1)S(1)}, u32[]{:S(2)}, u32[]{:S(2)}) %collective-permute-start.1) | collective-permute-done | bytes 98336 | tf_op jit(solution)/shard_map/ppermute | solution.py:654
  60.3 0.2 shard_map.148.base_ref
  60.5 3.5 %all-to-all-done.2.t_ref = bf16[32,40,128]{2,1,0:T(8,128)(2,1)S(1)} async-done(((bf16[32,40,128]{2,1,0:T(8,128)(2,1)}), bf16[32,40,128]{2,1,0:T(8,128)(2,1)S(1)}, u32[]{:S(2)}, u32[]{:S(2)}) %all-to-all-start.2) | async-done | bytes 327712 | tf_op jit(solution)/shard_map/all_to_all | solution.py:649
  64.0 0.0 copy-done.1
  64.0 2.1 %shard_map.149 = bf16[8,80,384]{2,1,0:T(8,128)(2,1)} custom-call(s32[4]{0:T(128)S(1)} %pad_add_fusion.par_ref.where_ref, bf16[32,40,128]{2,1,0:T(8,128)(2,1)S(1)} %all-to-all-done.2.t_ref, f32[2,2,4,4,256]{4,3,2,1,0:T(4,128)S(1)} %copy-done.6, bf16[2,256,512]{2,1,0:T(8,128)(2,1)S(1)} %copy-done.1, f32[8,80,384]{2,1,0:T(8,128)S(1)} %shard_map.148.base_ref), custom_call_target="tpu_custom_call" | custom-call | flops 536870912 | bytes 1048576 | tf_op jit(solution)/shard_map/pallas_call | solution.py:506
  66.1 3.6 %all-to-all-start.3 = ((bf16[8,80,384]{2,1,0:T(8,128)(2,1)}), bf16[8,80,384]{2,1,0:T(8,128)(2,1)S(1)}, u32[]{:S(2)}, u32[]{:S(2)}) async-start(bf16[8,80,384]{2,1,0:T(8,128)(2,1)} %shard_map.149), calls=%async_computation.3 | async-start | bytes 983040 | tf_op jit(solution)/shard_map/all_to_all | solution.py:678
  69.8 0.8 %shard_map.150.bands_ref = bf16[2560,256]{1,0:T(8,128)(2,1)S(1)} custom-call(f32[8,256]{1,0:T(8,128)S(1)} %pad.4.taps_ref), custom_call_target="tpu_custom_call" | custom-call | flops 1048576 | bytes 1048576 | tf_op jit(solution)/shard_map/pallas_call | solution.py:506
  70.6 7.9 %all-to-all-done.3.half_ref = bf16[8,80,384]{2,1,0:T(8,128)(2,1)S(1)} async-done(((bf16[8,80,384]{2,1,0:T(8,128)(2,1)}), bf16[8,80,384]{2,1,0:T(8,128)(2,1)S(1)}, u32[]{:S(2)}, u32[]{:S(2)}) %all-to-all-start.3) | async-done | bytes 491552 | tf_op jit(solution)/shard_map/all_to_all | solution.py:678
  78.5 0.0 copy-done.10
  78.5 5.5 %shard_map.151 = (f32[4,64,256]{2,1,0:T(8,128)}, bf16[4,9,64,256]{3,2,1,0:T(8,128)(2,1)}) custom-call(f32[9]{0:T(128)S(1)} %copy-done.10, s32[4]{0:T(128)S(1)} %pad_add_fusion.par_ref.where_ref, bf16[8,80,384]{2,1,0:T(8,128)(2,1)S(1)} %all-to-all-done.3.half_ref, f32[8,80,384]{2,1,0:T(8,128)S(1)} %shard_map.148.base_ref, bf16[4,9,64,256]{3,2,1,0:T(8,128)(2,1)} %dual_ref.3, ...), custom_call_target="tpu_custom_call" | custom-call | flops 2147483648 | bytes 3145728 | tf_op jit(solution)/shard_map/pallas_call | solution.py:520
  (3 shorter events, 0.0 us)
Async XLA Ops:
  0.6 14.3 %copy-start = (bf16[2,256,512]{2,1,0:T(8,128)(2,1)S(1)}, bf16[2,256,512]{2,1,0:T(8,128)(2,1)}, u32[]{:S(2)}) copy-start(bf16[2,256,512]{2,1,0:T(8,128)(2,1)} %constant.25.clone.line_ref) | copy-start | bytes 1572868
  0.6 14.2 %copy-start.6 = (f32[2,2,4,4,256]{4,3,2,1,0:T(4,128)S(1)}, f32[2,2,4,4,256]{4,3,2,1,0:T(4,128)}, u32[]{:S(2)}) copy-start(f32[2,2,4,4,256]{4,3,2,1,0:T(4,128)} %constant.24.clone.fold_ref) | copy-start | bytes 196612
  2.4 12.5 %all-to-all-start = ((bf16[8,64,256]{2,1,0:T(8,128)(2,1)}), bf16[8,64,256]{2,1,0:T(8,128)(2,1)S(1)}, u32[]{:S(2)}, u32[]{:S(2)}) async-start(bf16[8,64,256]{2,1,0:T(8,128)(2,1)} %shard_map.141), calls=%async_computation | async-start | bytes 524288 | tf_op jit(solution)/shard_map/all_to_all | solution.py:573
  9.8 19.8 %copy-start.11 = (s32[4,1]{0,1:T(1,128)S(1)}, s32[4,1]{0,1:T(1,128)}, u32[]{:S(2)}) copy-start(s32[4,1]{0,1:T(1,128)} %param.20) | copy-start | bytes 52
  9.8 19.9 %copy-start.5 = (f32[4,64,256]{2,1,0:T(8,128)S(1)}, f32[4,64,256]{2,1,0:T(8,128)}, u32[]{:S(2)}) copy-start(f32[4,64,256]{2,1,0:T(8,128)} %sky_ref.3) | copy-start | bytes 786436
  16.7 25.3 %all-to-all-start.1 = ((bf16[32,32,128]{2,1,0:T(8,128)(2,1)}), bf16[32,32,128]{2,1,0:T(8,128)(2,1)S(1)}, u32[]{:S(2)}, u32[]{:S(2)}) async-start(bf16[32,32,128]{2,1,0:T(8,128)(2,1)} %shard_map.142), calls=%async_computation.1 | async-start | bytes 524288 | tf_op jit(solution)/shard_map/all_to_all | solution.py:611
  29.7 1.3 %copy-start.8 = (bf16[4,9,64,256]{3,2,1,0:T(8,128)(2,1)S(1)}, bf16[4,9,64,256]{3,2,1,0:T(8,128)(2,1)}, u32[]{:S(2)}) copy-start(bf16[4,9,64,256]{3,2,1,0:T(8,128)(2,1)} %dual_ref.3) | copy-start | bytes 3538948
  31.0 0.9 %copy-start.9 = (f32[4,64,256]{2,1,0:T(8,128)S(1)}, f32[4,64,256]{2,1,0:T(8,128)}, u32[]{:S(2)}) copy-start(f32[4,64,256]{2,1,0:T(8,128)} %dirty_ref.1) | copy-start | bytes 786436
  32.0 4.0 %copy-start.2 = (bf16[4,1,6,64,64]{4,3,2,1,0:T(8,128)(2,1)S(1)}, bf16[4,1,6,64,64]{4,3,2,1,0:T(8,128)(2,1)}, u32[]{:S(2)}) copy-start(bf16[4,1,6,64,64]{4,3,2,1,0:T(8,128)(2,1)} %tiles_ref.1) | copy-start | bytes 589828
  32.0 4.0 %copy-start.3 = (bf16[2,128,768]{2,1,0:T(8,128)(2,1)S(1)}, bf16[2,128,768]{2,1,0:T(8,128)(2,1)}, u32[]{:S(2)}) copy-start(bf16[2,128,768]{2,1,0:T(8,128)(2,1)} %constant.22.clone.table_ref) | copy-start | bytes 1179652
  32.0 4.0 %copy-start.4 = (bf16[256,512]{1,0:T(8,128)(2,1)S(1)}, bf16[256,512]{1,0:T(8,128)(2,1)}, u32[]{:S(2)}) copy-start(bf16[256,512]{1,0:T(8,128)(2,1)} %constant.23.clone.fixed_ref) | copy-start | bytes 786436
  32.0 4.1 %copy-start.7 = (s32[4,1,6]{2,1,0:T(1,128)S(1)}, s32[4,1,6]{2,1,0:T(1,128)}, u32[]{:S(2)}) copy-start(s32[4,1,6]{2,1,0:T(1,128)} %slots_ref.1) | copy-start | bytes 292
  44.5 19.6 %copy-start.1 = (bf16[2,256,512]{2,1,0:T(8,128)(2,1)S(1)}, bf16[2,256,512]{2,1,0:T(8,128)(2,1)}, u32[]{:S(2)}) copy-start(bf16[2,256,512]{2,1,0:T(8,128)(2,1)} %constant.25.clone.line_ref) | copy-start | bytes 1572868
  44.5 19.6 %all-to-all-start.2 = ((bf16[32,40,128]{2,1,0:T(8,128)(2,1)}), bf16[32,40,128]{2,1,0:T(8,128)(2,1)S(1)}, u32[]{:S(2)}, u32[]{:S(2)}) async-start(bf16[32,40,128]{2,1,0:T(8,128)(2,1)} %shard_map.147), calls=%async_computation.2 | async-start | bytes 655360 | tf_op jit(solution)/shard_map/all_to_all | solution.py:649
  49.4 5.5 %collective-permute-start = (bf16[8,16,384]{2,1,0:T(8,128)(2,1)S(1)}, bf16[8,16,384]{2,1,0:T(8,128)(2,1)S(1)}, u32[]{:S(2)}, u32[]{:S(2)}) collective-permute-start(bf16[8,16,384]{2,1,0:T(8,128)(2,1)S(1)} %shard_map.145), channel_id=1, source_target_pairs={{0,8},{8,16},{16,24},{24,32},{32,40},{40,48},{48,56},{56,64},{64,7... | collective-permute-start | bytes 294920 | tf_op jit(solution)/shard_map/ppermute | solution.py:653
  52.9 7.3 %collective-permute-start.1 = (bf16[8,16,384]{2,1,0:T(8,128)(2,1)S(1)}, bf16[8,16,384]{2,1,0:T(8,128)(2,1)S(1)}, u32[]{:S(2)}, u32[]{:S(2)}) collective-permute-start(bf16[8,16,384]{2,1,0:T(8,128)(2,1)S(1)} %shard_map.144), channel_id=1, source_target_pairs={{8,0},{16,8},{24,16},{32,24},{40,32},{48,40},{56,48},{64,56},{72,6... | collective-permute-start | bytes 294920 | tf_op jit(solution)/shard_map/ppermute | solution.py:654
  66.1 12.4 %copy-start.10 = (f32[9]{0:T(128)S(1)}, f32[9]{0:T(128)}, u32[]{:S(2)}) copy-start(f32[9]{0:T(128)} %bound_ref.1) | copy-start | bytes 112
  66.1 12.4 %all-to-all-start.3 = ((bf16[8,80,384]{2,1,0:T(8,128)(2,1)}), bf16[8,80,384]{2,1,0:T(8,128)(2,1)S(1)}, u32[]{:S(2)}, u32[]{:S(2)}) async-start(bf16[8,80,384]{2,1,0:T(8,128)(2,1)} %shard_map.149), calls=%async_computation.3 | async-start | bytes 983040 | tf_op jit(solution)/shard_map/all_to_all | solution.py:678

commit v4 on v3

--- a/solution.py
+++ b/solution.py
@@ -103,11 +103,22 @@
     return two_terms_np(table)
 
 
-def fold_table():
+def wave_table():
     freq = np.arange(2)[:, None] + 2 * np.arange(4)[None]
     pos = np.arange(4 * COLS).reshape(4, COLS)
     ang = 2.0 * np.pi * ((freq[:, :, None, None] * pos) % PIXELS) / PIXELS
-    return np.stack([np.cos(ang), np.sin(ang)], axis=1).astype(np.float32)
+    fold = np.concatenate([np.cos(ang), np.sin(ang)], axis=3).reshape(32, 2 * COLS)
+    return np.concatenate([np.stack(line_table()), np.stack(two_terms_np(fold))], axis=1)
+
+
+def fold_rows(line_ref, par):
+    at = pl.multiple_of(256 + 16 * par, 16)
+    fold = line_ref[0, pl.ds(at, 16), :].astype(F32) + line_ref[1, pl.ds(at, 16), :].astype(F32)
+    return fold[:, 0:256], fold[:, 256:512]
+
+
+def hold_kernel(table_ref, o_ref):
+    o_ref[...] = table_ref[...]
 
 
 def send_kernel(sky_ref, o_ref, taken, rounded, in_sem, out_sem):
@@ -131,14 +142,15 @@
             place(c, h).wait()
 
 
-def forward_kernel(par_ref, x_ref, fold_ref, line_ref, o_ref):
+def forward_kernel(par_ref, x_ref, line_ref, o_ref):
     par = par_ref[1]
+    folds = fold_rows(line_ref, par)
     sign = (1 - 2 * par).astype(F32)
     xe = [x_ref[f].astype(F32) + sign * x_ref[f + 4].astype(F32) for f in range(4)]
     rows = [[], []]
     for cls in range(4):
-        cos = fold_ref[par, 0, cls]
-        sin = fold_ref[par, 1, cls]
+        cos = folds[0][cls * 4 : cls * 4 + 4]
+        sin = folds[1][cls * 4 : cls * 4 + 4]
         yr = xe[0] * cos[0:1]
         yi = xe[0] * sin[0:1]
         for f in range(1, 4):
@@ -148,14 +160,15 @@
         rows[1].append(jnp.concatenate([-yi, -yr], axis=1).astype(BF))
     for part in range(2):
         r = jnp.concatenate(rows[part], axis=0)
-        out = dot(line_ref[0], r, LAST) + dot(line_ref[1], r, LAST)
+        out = dot(line_ref[0, 0:256], r, LAST) + dot(line_ref[1, 0:256], r, LAST)
         both = [out[:, chi * 128 : chi * 128 + 128].reshape(32, 8, 128) for chi in range(2)]
         both = jnp.concatenate(both, axis=1)
         o_ref[:, part * 16 : (part + 1) * 16, :] = both.astype(BF)
 
 
-def inverse_kernel(par_ref, t_ref, fold_ref, line_ref, base_ref, o_ref):
+def inverse_kernel(par_ref, t_ref, line_ref, base_ref, o_ref):
     par = par_ref[1]
+    folds = fold_rows(line_ref, par)
     me = par_ref[3]
     sign = (1 - 2 * par).astype(F32)
     re = t_ref[:, 0:16, :].astype(F32)
@@ -163,7 +176,7 @@
     edge = t_ref[:, 32:40, :].astype(F32)
     data = [re[:, 0:8], im[:, 0:8], re[:, 8:16], im[:, 8:16], edge]
     data = jnp.concatenate([d.reshape(256, 128).astype(BF) for d in data], axis=1)
-    wave = dot(data, line_ref[0], FIRST) + dot(data, line_ref[1], FIRST)
+    wave = dot(data, line_ref[0, 0:256], FIRST) + dot(data, line_ref[1, 0:256], FIRST)
 
     def joined(a, b):
         return jnp.concatenate([a[:, 0:256] - b[:, 256:512], a[:, 256:512] + b[:, 0:256]], axis=1)
@@ -178,8 +191,8 @@
             whole = jnp.concatenate([e[0:8], u[clo * 64 : clo * 64 + 64], e[8:16]], axis=0)
             ur = whole[:, 0:256]
             ui = whole[:, 256:512]
-            cos = fold_ref[par, 0, cls]
-            sin = fold_ref[par, 1, cls]
+            cos = folds[0][cls * 4 : cls * 4 + 4]
+            sin = folds[1][cls * 4 : cls * 4 + 4]
             for f in range(4):
                 g = ur * cos[f : f + 1] - ui * sin[f : f + 1]
                 total[f] = g if total[f] is None else total[f] + g
@@ -290,32 +303,23 @@
     o_ref[...] = rows[...].reshape(32, 40, 128).astype(BF)
 
 
-def band_kernel(taps_ref, strip_ref):
-    for k in range(FRAMES):
-        wide = jnp.broadcast_to(taps_ref[k : k + 1, :], (128, 256))
-        band = pltpu.roll(wide, 0, 1, stride=1, stride_axis=0)
-        high = band.astype(BF)
-        strip_ref[0, k] = high
-        strip_ref[1, k] = (band - high.astype(F32)).astype(BF)
-
-
-def bands_kernel(taps_ref, o_ref):
+def band_kernel(taps_ref, strip_ref, down_ref):
     lane = lax.broadcasted_iota(jnp.int32, (64, 256), 1)
     for k in range(FRAMES):
         wide = jnp.broadcast_to(taps_ref[k : k + 1, :], (128, 256))
         band = pltpu.roll(wide, 0, 1, stride=1, stride_axis=0)
         high = band.astype(BF)
         low = band - high.astype(F32)
-        o_ref[k * 128 : k * 128 + 128, :] = high
-        o_ref[1024 + k * 128 : 1152 + k * 128, :] = low.astype(BF)
+        strip_ref[0, k] = high
+        strip_ref[1, k] = low.astype(BF)
+        high = jnp.where(lane < 80, high[0:64].astype(F32), 0.0)
         low = jnp.where(lane < 80, low[0:64], 0.0)
-        high = jnp.where(lane < 80, high[0:64].astype(F32), 0.0)
         row = high + pltpu.roll(high, 80, 1) + pltpu.roll(low, 160, 1)
-        o_ref[2048 + k * 64 : 2112 + k * 64, :] = row.astype(BF)
+        down_ref[k * 64 : k * 64 + 64, :] = row.astype(BF)
 
 
 def synth_kernel(
-    where_ref, live_ref, dual_ref, sky_ref, dirty_ref, strip_ref, o_ref, across
+    where_ref, live_ref, dual_ref, sky_ref, dirty_ref, strip_ref, o_ref, head_ref, tail_ref, across
 ):
     channels = sky_ref.shape[0]
     row = lax.broadcasted_iota(jnp.int32, (80, WIDE), 0) + where_ref[2] * ROWS - RADIUS
@@ -354,20 +358,10 @@
         total = jnp.where(inside, total, OUTSIDE)
         total = jnp.where(lane < COLS + 2 * RADIUS, total, 0.0)
         sky = jnp.concatenate([edge, sky, edge], axis=0)
-        o_ref[c] = total
-        o_ref[channels + c] = sky
-
-
-def head_kernel(base_ref, o_ref):
-    o_ref[...] = base_ref[:, 0:16].astype(BF)
-
-
-def tail_kernel(base_ref, o_ref):
-    o_ref[...] = base_ref[:, 64:80].astype(BF)
-
-
-def take_kernel(where_ref, dual_ref, o_ref):
-    o_ref[...] = dual_ref[...]
+        for at, cells in ((c, total), (channels + c, sky)):
+            o_ref[at] = cells
+            head_ref[at] = cells[0:16].astype(BF)
+            tail_ref[at] = cells[64:80].astype(BF)
 
 
 def edge_kernel(base_ref, before_ref, after_ref, o_ref):
@@ -399,35 +393,27 @@
     half_ref,
     base_ref,
     dual_ref,
-    bands_ref,
+    strip_ref,
+    down_ref,
     image_ref,
     o_ref,
-    given,
     image_buf,
     dual_buf,
     probes,
     wide,
     down,
-    given_sem,
     image_sem,
     dual_sem,
 ):
     channels = image_buf.shape[0]
     rows = channels * ROWS
 
-    def given_copy(k):
-        return pltpu.make_async_copy(dual_ref.at[:, k], given.at[k], given_sem.at[k])
-
-    for k in range(FRAMES + 1):
-        given_copy(k).start()
-
     def dual_copy(k):
         return pltpu.make_async_copy(dual_buf.at[k], o_ref.at[:, k], dual_sem.at[k])
 
     def finish(k, analysis):
         bound = bound_ref[k]
-        given_copy(k).wait()
-        cand = [given[k, c].astype(F32) + STEP_DUAL * analysis(c) for c in range(channels)]
+        cand = [dual_ref[c, k].astype(F32) + STEP_DUAL * analysis(c) for c in range(channels)]
         square = cand[0] * cand[0]
         for c in range(1, channels):
             square = square + cand[c] * cand[c]
@@ -467,7 +453,7 @@
         wide[0:80, :] = high
         wide[80:160, :] = low
         wide[160:240, :] = high
-        d = dot(bands_ref[2048:2560, :], wide[...])
+        d = dot(down_ref[...], wide[...])
         high = d.astype(BF)
         down[0, c] = high
         down[1, c] = (d - high.astype(F32)).astype(BF)
@@ -480,13 +466,12 @@
         for t in range(2):
             d = jnp.concatenate([down[t, c, at : at + ROWS, :] for c in range(channels)], axis=0)
             both = jnp.concatenate([d[:, 0:256], d[:, 128:384]], axis=0)
-            high = bands_ref[(k - 1) * 128 : k * 128, :]
             if t == 0:
-                band = jnp.concatenate([high, bands_ref[896 + k * 128 : 1024 + k * 128, :]], axis=0)
+                band = jnp.concatenate([strip_ref[0, k - 1], strip_ref[1, k - 1]], axis=0)
                 term = dot(both, band, LAST)
                 a = term[:, 0:128] + term[:, 128:256]
             else:
-                a = a + dot(both, high, LAST)
+                a = a + dot(both, strip_ref[0, k - 1], LAST)
         finish(
             k,
             lambda c: jnp.concatenate(
@@ -514,28 +499,26 @@
     )(*args)
 
 
-def frames_call(thresholds, where, halves, base, dual, bands):
+def frames_call(thresholds, where, halves, base, dual, strip, down):
     channels = dual.shape[0]
     block = (channels, ROWS, COLS)
     return pl.pallas_call(
         frames_kernel,
         out_shape=(jax.ShapeDtypeStruct(block, F32), jax.ShapeDtypeStruct(dual.shape, BF)),
-        in_specs=[SM, SM, VM, VM, pl.BlockSpec(memory_space=pltpu.HBM), VM],
+        in_specs=[SM, SM, VM, VM, VM, VM, VM],
         out_specs=(pl.BlockSpec(memory_space=pl.ANY), pl.BlockSpec(memory_space=pl.ANY)),
         scratch_shapes=[
-            pltpu.VMEM((FRAMES + 1, *block), BF),
             pltpu.VMEM(block, F32),
             pltpu.VMEM((FRAMES + 1, *block), BF),
             pltpu.VMEM(block, F32),
             pltpu.VMEM((256, WIDE), BF),
             pltpu.VMEM((2, channels, FRAMES * ROWS, WIDE), BF),
-            pltpu.SemaphoreType.DMA((FRAMES + 1,)),
             pltpu.SemaphoreType.DMA(()),
             pltpu.SemaphoreType.DMA((FRAMES + 1,)),
         ],
         compiler_params=pltpu.CompilerParams(vmem_limit_bytes=VMEM_LIMIT),
         cost_estimate=pl.CostEstimate(flops=1 << 31, bytes_accessed=3 << 20, transcendentals=0),
-    )(thresholds, where, halves, base, dual, bands)
+    )(thresholds, where, halves, base, dual, strip, down)
 
 
 def after(values, *events):
@@ -568,9 +551,36 @@
             pltpu.SemaphoreType.DMA((channels,)),
             pltpu.SemaphoreType.DMA((channels, 2)),
         ],
-        compiler_params=pltpu.CompilerParams(vmem_limit_bytes=62 << 20),
-    )(sky_estimate)
+        compiler_params=pltpu.CompilerParams(vmem_limit_bytes=VMEM_LIMIT),
+    )(pltpu.with_memory_space_constraint(sky_estimate, pltpu.HBM))
     lines = lax.all_to_all(sent, "fou", split_axis=0, concat_axis=0, tiled=True)
+
+    strip, down = call(
+        band_kernel,
+        (
+            jax.ShapeDtypeStruct((2, FRAMES, 128, 256), BF),
+            jax.ShapeDtypeStruct((FRAMES * ROWS, 256), BF),
+        ),
+        [],
+        1 << 20,
+        1 << 20,
+        jnp.pad(filters, ((0, 0), (0, 256 - filters.shape[1]))),
+    )
+    (ready_where,) = after((where,), strip)
+    line = wave_table()
+    held = call(hold_kernel, jax.ShapeDtypeStruct(line.shape, BF), [], 1 << 10, 1 << 20, line)
+    packed = call(
+        forward_kernel,
+        jax.ShapeDtypeStruct((PEERS_IMG, 32, 128), BF),
+        [],
+        1 << 29,
+        1 << 20,
+        ready_where,
+        lines,
+        held,
+        scalars=1,
+    )
+    received = lax.all_to_all(packed, "img", split_axis=0, concat_axis=0, tiled=True)
 
     spread = call(
         tiles_kernel,
@@ -587,34 +597,12 @@
         scalars=3,
     )
 
-    taps = jnp.pad(filters, ((0, 0), (0, 256 - filters.shape[1])))
-    strip = call(
-        band_kernel, jax.ShapeDtypeStruct((2, FRAMES, 128, 256), BF), [], 1 << 20, 1 << 20, taps
-    )
-
-    (ready_where,) = after((where,), strip)
-
-    line = np.stack(line_table())
-    fold = fold_table()
-    packed = call(
-        forward_kernel,
-        jax.ShapeDtypeStruct((PEERS_IMG, 32, 128), BF),
-        [],
-        1 << 29,
-        1 << 20,
-        ready_where,
-        lines,
-        fold,
-        line,
-        scalars=1,
-    )
-    received = lax.all_to_all(packed, "img", split_axis=0, concat_axis=0, tiled=True)
-
+    ends = jax.ShapeDtypeStruct((2 * channels, 16, WIDE), BF)
     extended = jax.ShapeDtypeStruct((2 * channels, tile_rows + 16, WIDE), F32)
     (late_where,) = after((where,), packed)
-    base = call(
+    base, head, tail = call(
         synth_kernel,
-        extended,
+        (extended, ends, ends),
         [pltpu.VMEM((channels, FRAMES * ROWS, WIDE), BF)],
         1 << 31,
         4 << 20,
@@ -626,10 +614,7 @@
         strip,
         scalars=2,
     )
-    ends = jax.ShapeDtypeStruct((2 * channels, 16, WIDE), BF)
-    head = call(head_kernel, ends, [], 1 << 16, 1 << 18, base)
-    tail = call(tail_kernel, ends, [], 1 << 16, 1 << 18, base)
-    (received,) = after((received,), head, tail)
+    (received,) = after((received,), head)
 
     scratch = [
         pltpu.VMEM((1280, 128), F32),
@@ -670,18 +655,13 @@
         1 << 20,
         where,
         returned,
-        fold,
         line,
         base,
         scalars=1,
     )
     halves = lax.all_to_all(blocks, "fou", split_axis=0, concat_axis=0, tiled=True)
 
-    (late_taps,) = after((taps,), blocks)
-    bands = call(
-        bands_kernel, jax.ShapeDtypeStruct((2560, 256), BF), [], 1 << 20, 1 << 20, late_taps
-    )
-    return frames_call(thresholds, where, halves, base, pltpu.with_memory_space_constraint(dual_coeffs, pltpu.HBM), bands)
+    return frames_call(thresholds, where, halves, base, dual_coeffs, strip, down)
 
 
 def solution(mesh):

time: 84.6 us -> 81.5 us (0.963)
  blocking collectives: 0 us -> 11.8 us
  waiting for transfers between devices: 26.8 us -> 16.4 us
  starting transfers between devices: 32.6 us -> 29.3 us
  Pallas kernels: 20 us -> 16.9 us
  local copies, waits for them, and re-layouts: 3.05 us -> 5.06 us
    all_to_all x0 -> x1, blocking collectives: none -> 11.8 us  [body(): lax.all_to_all(blocks, 'fou', split_axis=0, concat_axis=0, tiled=True)]
    all_to_all x1 -> x0, waiting for transfers between devices: 7.92 us -> none  [body(): lax.all_to_all(blocks, 'fou', split_axis=0, concat_axis=0, tiled=True)]
    all_to_all x1 -> x0, starting transfers between devices: 3.62 us -> none  [body(): lax.all_to_all(blocks, 'fou', split_axis=0, concat_axis=0, tiled=True)]
    unnamed x25 -> x39, local copies, waits for them, and re-layouts: 2.36 us -> 5.05 us
    pallas_call x1, Pallas kernels: 5.46 us -> 3.47 us  [frames_call(): pl.pallas_call(frames_kernel, out_shape=(jax.ShapeDtypeStruct(block, F32)...]
    all_to_all x1, waiting for transfers between devices: 3.49 us -> 2.27 us  [body(): lax.all_to_all(weighted, 'img', split_axis=0, concat_axis=0, tiled=True)]
    pallas_call x10 -> x8, Pallas kernels: 12.8 us -> 11.7 us  [call(): pl.pallas_call(kernel, out_shape=out_shape, in_specs=[SM] * scalars + [VM...]
    all_to_all x1, waiting for transfers between devices: 4.96 us -> 4.11 us  [body(): lines = lax.all_to_all(sent, 'fou', split_axis=0, concat_axis=0, tiled=True)]
  transfers between devices with their start and end apart: 6 -> 5, of which waited for: 5 -> 4; matrix products, arithmetic and copies ran while one was open for 1% -> 0% of each run, Pallas kernels for 8% -> 7%
where the time goes in v4:
time: 81.5 us; the launch traced here: 81 us
  starting transfers between devices  29.3 us (36%)
  Pallas kernels  16.9 us (21%)
  waiting for transfers between devices  16.4 us (20%)
  blocking collectives  11.8 us (14%)
  local copies, waits for them, and re-layouts  5.06 us (6%)
  between operations  1.49 us (2%)
    all_to_all x1, starting transfers between devices, body(): lax.all_to_all(packed, 'img', split_axis=0, concat_axis=0, tiled=True)  12.3 us
    all_to_all x1, blocking collectives, body(): lax.all_to_all(blocks, 'fou', split_axis=0, concat_axis=0, tiled=True)  11.8 us
    pallas_call x8, Pallas kernels, call(): pl.pallas_call(kernel, out_shape=out_shape, in_specs=[SM] * scalars + [VM...  11.7 us
    all_to_all x1, starting transfers between devices, body(): lines = lax.all_to_all(sent, 'fou', split_axis=0, concat_axis=0, tiled=True)  6.39 us
    ppermute x1, waiting for transfers between devices, body(): from_after = lax.ppermute(head, 'img', [(j, i) for i, j in steps])  5.41 us
    all_to_all x1, starting transfers between devices, body(): lax.all_to_all(weighted, 'img', split_axis=0, concat_axis=0, tiled=True)  5.22 us
    unnamed x39, local copies, waits for them, and re-layouts  5.05 us
    all_to_all x1, waiting for transfers between devices, body(): lax.all_to_all(packed, 'img', split_axis=0, concat_axis=0, tiled=True)  4.57 us
  transfers between devices with their start and end apart: 5, of which 4 were waited for; matrix products, arithmetic and copies ran while one was open for 0% of the time, Pallas kernels for 7%

profile of v4, /device:TPU:1, one launch (start us, length us, event | category | flops | bytes accessed | tf_op | source)
XLA Modules:
  0.0 81.0 jit_solution(8598508733253720608)
XLA Ops:
  0.6 0.0 copy-start
  0.6 0.0 copy-start.17
  0.7 1.7 %shard_map.132 = bf16[8,64,256]{2,1,0:T(8,128)(2,1)} custom-call(f32[4,64,256]{2,1,0:T(8,128)} %sky_ref.3), custom_call_target="tpu_custom_call" | custom-call | tf_op jit(solution)/shard_map/pallas_call | solution.py:543
  2.4 6.4 %all-to-all-start = ((bf16[8,64,256]{2,1,0:T(8,128)(2,1)}), bf16[8,64,256]{2,1,0:T(8,128)(2,1)S(1)}, u32[]{:S(2)}, u32[]{:S(2)}) async-start(bf16[8,64,256]{2,1,0:T(8,128)(2,1)} %shard_map.132), calls=%async_computation | async-start | bytes 524288 | tf_op jit(solution)/shard_map/all_to_all | solution.py:556
  8.8 0.0 copy-done
  8.8 0.0 copy-done.17
  8.9 0.8 %shard_map.131 = (bf16[2,8,128,256]{3,2,1,0:T(8,128)(2,1)S(1)}, bf16[512,256]{1,0:T(8,128)(2,1)S(1)}) custom-call(f32[8,256]{1,0:T(8,128)S(1)} %pad.4.taps_ref), custom_call_target="tpu_custom_call" | custom-call | flops 1048576 | bytes 1048576 | tf_op jit(solution)/shard_map/pallas_call | solution.py:491
  9.7 0.0 copy-start.10
  9.7 1.0 %copy-done.10 = bf16[2,8,128,256]{3,2,1,0:T(8,128)(2,1)} copy-done((bf16[2,8,128,256]{3,2,1,0:T(8,128)(2,1)}, bf16[2,8,128,256]{3,2,1,0:T(8,128)(2,1)S(1)}, u32[]{:S(2)}) %copy-start.10) | copy-done | bytes 1048600
  10.7 0.1 pad_add_fusion.par_ref.where_ref
  10.8 4.1 %all-to-all-done.x_ref = bf16[8,64,256]{2,1,0:T(8,128)(2,1)S(1)} async-done(((bf16[8,64,256]{2,1,0:T(8,128)(2,1)}), bf16[8,64,256]{2,1,0:T(8,128)(2,1)S(1)}, u32[]{:S(2)}, u32[]{:S(2)}) %all-to-all-start) | async-done | bytes 262176 | tf_op jit(solution)/shard_map/all_to_all | solution.py:556
  14.9 1.8 %shard_map.134 = bf16[32,32,128]{2,1,0:T(8,128)(2,1)} custom-call(s32[4]{0:T(128)S(1)} %pad_add_fusion.par_ref.where_ref, bf16[8,64,256]{2,1,0:T(8,128)(2,1)S(1)} %all-to-all-done.x_ref, bf16[2,288,512]{2,1,0:T(8,128)(2,1)S(1)} %shard_map.133.line_ref), custom_call_target="tpu_custom_call" | custom-call | flops 536870912 | bytes 1048576 | tf_op jit(solution)/shard_map/pallas_call | solution.py:491
  16.7 0.0 copy-done.14
  16.7 12.3 %all-to-all-start.1 = ((bf16[32,32,128]{2,1,0:T(8,128)(2,1)}), bf16[32,32,128]{2,1,0:T(8,128)(2,1)S(1)}, u32[]{:S(2)}, u32[]{:S(2)}) async-start(bf16[32,32,128]{2,1,0:T(8,128)(2,1)} %shard_map.134), calls=%async_computation.1 | async-start | bytes 524288 | tf_op jit(solution)/shard_map/all_to_all | solution.py:583
  29.6 0.0 copy-done.18
  29.6 0.1 copy.14.count_ref
  29.7 0.0 copy-done.3
  29.7 0.0 copy-done.5
  29.7 0.0 copy-done.7
  29.8 0.0 copy-start.4
  29.8 1.0 %copy-done.4 = bf16[2,128,768]{2,1,0:T(8,128)(2,1)S(1)} copy-done((bf16[2,128,768]{2,1,0:T(8,128)(2,1)S(1)}, bf16[2,128,768]{2,1,0:T(8,128)(2,1)}, u32[]{:S(2)}) %copy-start.4) | copy-done | bytes 393240
  30.8 0.9 %shard_map.136.e_ref = bf16[640,1536]{1,0:T(8,128)(2,1)S(1)} custom-call(s32[4]{0:T(128)S(1)} %pad_add_fusion.par_ref.where_ref, s32[4,1,6]{2,1,0:T(1,128)S(1)} %copy-done.7, s32[4,1]{1,0:T(4,128)S(1)} %copy.14.count_ref, bf16[4,1,6,64,64]{4,3,2,1,0:T(8,128)(2,1)S(1)} %copy-done.3, bf16[2,128,768]{2,1,0:T(8,128)(2,1)S(1)} %copy-done.4, ...), custom_call_target="tpu_custom_call" | custom-call | flops 8388608 | bytes 1048576 | tf_op jit(solution)/shard_map/pallas_call | solution.py:491
  31.7 0.0 copy-done.6
  31.7 0.4 copy-done.8
  32.1 0.3 copy-done.11
  32.4 0.0 copy-done.13
  32.4 4.0 %shard_map.135 = (f32[8,80,384]{2,1,0:T(8,128)S(1)}, bf16[8,16,384]{2,1,0:T(8,128)(2,1)S(1)}, bf16[8,16,384]{2,1,0:T(8,128)(2,1)S(1)}) custom-call(s32[4]{0:T(128)S(1)} %pad_add_fusion.par_ref.where_ref, s32[1]{0:T(128)S(6)} %copy.15.live_ref, bf16[4,9,64,256]{3,2,1,0:T(8,128)(2,1)S(1)} %copy-done.8, f32[4,64,256]{2,1,0:T(8,128)S(1)} %copy-done.6, ...), custom_call_target="tpu_custom_call" | custom-call | flops 2147483648 | bytes 4194304 | tf_op jit(solution)/shard_map/pallas_call | solution.py:491
  36.5 0.0 copy-start.1
  36.5 1.0 %copy-done.1 = f32[8,80,384]{2,1,0:T(8,128)} copy-done((f32[8,80,384]{2,1,0:T(8,128)}, f32[8,80,384]{2,1,0:T(8,128)S(1)}, u32[]{:S(2)}) %copy-start.1) | copy-done | bytes 983064
  37.4 4.6 %all-to-all-done.1.d_ref = bf16[32,32,128]{2,1,0:T(8,128)(2,1)S(1)} async-done(((bf16[32,32,128]{2,1,0:T(8,128)(2,1)}), bf16[32,32,128]{2,1,0:T(8,128)(2,1)S(1)}, u32[]{:S(2)}, u32[]{:S(2)}) %all-to-all-start.1) | async-done | bytes 262176 | tf_op jit(solution)/shard_map/all_to_all | solution.py:583
  42.0 2.5 %shard_map.137 = bf16[32,40,128]{2,1,0:T(8,128)(2,1)} custom-call(bf16[32,32,128]{2,1,0:T(8,128)(2,1)S(1)} %all-to-all-done.1.d_ref, bf16[640,1536]{1,0:T(8,128)(2,1)S(1)} %shard_map.136.e_ref), custom_call_target="tpu_custom_call" | custom-call | flops 536870912 | bytes 1048576 | tf_op jit(solution)/shard_map/pallas_call | solution.py:491
  44.5 5.2 %all-to-all-start.2 = ((bf16[32,40,128]{2,1,0:T(8,128)(2,1)}), bf16[32,40,128]{2,1,0:T(8,128)(2,1)S(1)}, u32[]{:S(2)}, u32[]{:S(2)}) async-start(bf16[32,40,128]{2,1,0:T(8,128)(2,1)} %shard_map.137), calls=%async_computation.2 | async-start | bytes 655360 | tf_op jit(solution)/shard_map/all_to_all | solution.py:634
  49.7 3.5 %collective-permute-start = (bf16[8,16,384]{2,1,0:T(8,128)(2,1)S(1)}, bf16[8,16,384]{2,1,0:T(8,128)(2,1)S(1)}, u32[]{:S(2)}, u32[]{:S(2)}) collective-permute-start(bf16[8,16,384]{2,1,0:T(8,128)(2,1)S(1)} %get-tuple-element.19), channel_id=1, source_target_pairs={{0,8},{8,16},{16,24},{24,32},{32,40},{40,48},{48,56},{56,64},{64,7... | collective-permute-start | bytes 294920 | tf_op jit(solution)/shard_map/ppermute | solution.py:638
  53.3 1.9 %collective-permute-start.1 = (bf16[8,16,384]{2,1,0:T(8,128)(2,1)S(1)}, bf16[8,16,384]{2,1,0:T(8,128)(2,1)S(1)}, u32[]{:S(2)}, u32[]{:S(2)}) collective-permute-start(bf16[8,16,384]{2,1,0:T(8,128)(2,1)S(1)} %get-tuple-element.20), channel_id=1, source_target_pairs={{8,0},{16,8},{24,16},{32,24},{40,32},{48,40},{56,48},{64,56},{72,6... | collective-permute-start | bytes 294920 | tf_op jit(solution)/shard_map/ppermute | solution.py:639
  55.2 0.0 collective-permute-done.before_ref
  55.2 5.4 %collective-permute-done.1.after_ref = bf16[8,16,384]{2,1,0:T(8,128)(2,1)S(1)} collective-permute-done((bf16[8,16,384]{2,1,0:T(8,128)(2,1)S(1)}, bf16[8,16,384]{2,1,0:T(8,128)(2,1)S(1)}, u32[]{:S(2)}, u32[]{:S(2)}) %collective-permute-start.1) | collective-permute-done | bytes 98336 | tf_op jit(solution)/shard_map/ppermute | solution.py:639
  60.6 1.2 %copy-done.2 = f32[8,80,384]{2,1,0:T(8,128)S(1)} copy-done((f32[8,80,384]{2,1,0:T(8,128)S(1)}, f32[8,80,384]{2,1,0:T(8,128)}, u32[]{:S(2)}) %copy-start.2) | copy-done | bytes 983064
  61.8 0.2 shard_map.138.base_ref
  62.1 0.0 copy-start.15
  62.1 0.0 copy-start.16
  62.1 2.3 %all-to-all-done.2.t_ref = bf16[32,40,128]{2,1,0:T(8,128)(2,1)S(1)} async-done(((bf16[32,40,128]{2,1,0:T(8,128)(2,1)}), bf16[32,40,128]{2,1,0:T(8,128)(2,1)S(1)}, u32[]{:S(2)}, u32[]{:S(2)}) %all-to-all-start.2) | async-done | bytes 327712 | tf_op jit(solution)/shard_map/all_to_all | solution.py:634
  64.4 1.3 %shard_map.139 = bf16[8,80,384]{2,1,0:T(8,128)(2,1)S(1)} custom-call(s32[4]{0:T(128)S(1)} %pad_add_fusion.par_ref.where_ref, bf16[32,40,128]{2,1,0:T(8,128)(2,1)S(1)} %all-to-all-done.2.t_ref, bf16[2,288,512]{2,1,0:T(8,128)(2,1)S(1)} %copy-done, f32[8,80,384]{2,1,0:T(8,128)S(1)} %shard_map.138.base_ref), custom_call_target="tpu_custom_call" | custom-call | flops 536870912 | bytes 1048576 | tf_op jit(solution)/shard_map/pallas_call | solution.py:491
  65.7 11.8 %all_to_all.20.half_ref = bf16[8,80,384]{2,1,0:T(8,128)(2,1)S(1)} all-to-all(bf16[8,80,384]{2,1,0:T(8,128)(2,1)S(1)} %shard_map.139), channel_id=1, replica_groups=mesh['img'=32,'fou'=8] {'fou'}, dimensions={0} | all-to-all | bytes 983040 | tf_op jit(solution)/shard_map/all_to_all | solution.py:662
  77.5 0.0 copy-done.15
  77.5 0.0 copy-done.16
  77.5 0.0 copy-done.9
  77.5 0.0 copy-done.12
  77.5 3.5 %shard_map.140 = (f32[4,64,256]{2,1,0:T(8,128)}, bf16[4,9,64,256]{3,2,1,0:T(8,128)(2,1)}) custom-call(f32[9]{0:T(128)S(1)} %copy-done.16, s32[4]{0:T(128)S(1)} %pad_add_fusion.par_ref.where_ref, bf16[8,80,384]{2,1,0:T(8,128)(2,1)S(1)} %all_to_all.20.half_ref, f32[8,80,384]{2,1,0:T(8,128)S(1)} %shard_map.138.base_ref, bf16[4,9,64,256]{3,2,1,0:T(8,128)(2,1)S(1)} %copy-done.9, ...), custom_call_target="tpu_custom_call" | custom-call | flops 2147483648 | bytes 3145728 | tf_op jit(solution)/shard_map/pallas_call | solution.py:505
  (14 shorter events, 0.1 us)
Async XLA Ops:
  0.6 8.1 %copy-start = (bf16[2,288,512]{2,1,0:T(8,128)(2,1)S(1)}, bf16[2,288,512]{2,1,0:T(8,128)(2,1)}, u32[]{:S(2)}) copy-start(bf16[2,288,512]{2,1,0:T(8,128)(2,1)} %constant.20.clone.table_ref.line_ref) | copy-start | bytes 1769476
  0.6 8.2 %copy-start.17 = (f32[8,17]{1,0:T(8,128)S(1)}, f32[8,17]{1,0:T(8,128)}, u32[]{:S(2)}) copy-start(f32[8,17]{1,0:T(8,128)} %param.15) | copy-start | bytes 1636
  2.4 12.5 %all-to-all-start = ((bf16[8,64,256]{2,1,0:T(8,128)(2,1)}), bf16[8,64,256]{2,1,0:T(8,128)(2,1)S(1)}, u32[]{:S(2)}, u32[]{:S(2)}) async-start(bf16[8,64,256]{2,1,0:T(8,128)(2,1)} %shard_map.132), calls=%async_computation | async-start | bytes 524288 | tf_op jit(solution)/shard_map/all_to_all | solution.py:556
  9.7 1.0 %copy-start.10 = (bf16[2,8,128,256]{3,2,1,0:T(8,128)(2,1)}, bf16[2,8,128,256]{3,2,1,0:T(8,128)(2,1)S(1)}, u32[]{:S(2)}) copy-start(bf16[2,8,128,256]{3,2,1,0:T(8,128)(2,1)S(1)} %get-tuple-element.12.strip_ref) | copy-start | bytes 3145732
  10.7 6.0 %copy-start.14 = (bf16[512,256]{1,0:T(8,128)(2,1)}, bf16[512,256]{1,0:T(8,128)(2,1)S(1)}, u32[]{:S(2)}) copy-start(bf16[512,256]{1,0:T(8,128)(2,1)S(1)} %get-tuple-element.21.down_ref) | copy-start | bytes 786436
  10.8 18.9 %copy-start.18 = (s32[4,1]{0,1:T(1,128)S(1)}, s32[4,1]{0,1:T(1,128)}, u32[]{:S(2)}) copy-start(s32[4,1]{0,1:T(1,128)} %param.19) | copy-start | bytes 52
  10.8 19.0 %copy-start.3 = (bf16[4,1,6,64,64]{4,3,2,1,0:T(8,128)(2,1)S(1)}, bf16[4,1,6,64,64]{4,3,2,1,0:T(8,128)(2,1)}, u32[]{:S(2)}) copy-start(bf16[4,1,6,64,64]{4,3,2,1,0:T(8,128)(2,1)} %tiles_ref.1) | copy-start | bytes 589828
  10.8 19.0 %copy-start.5 = (bf16[256,512]{1,0:T(8,128)(2,1)S(1)}, bf16[256,512]{1,0:T(8,128)(2,1)}, u32[]{:S(2)}) copy-start(bf16[256,512]{1,0:T(8,128)(2,1)} %constant.22.clone.fixed_ref) | copy-start | bytes 786436
  10.8 19.0 %copy-start.7 = (s32[4,1,6]{2,1,0:T(1,128)S(1)}, s32[4,1,6]{2,1,0:T(1,128)}, u32[]{:S(2)}) copy-start(s32[4,1,6]{2,1,0:T(1,128)} %slots_ref.1) | copy-start | bytes 292
  16.7 25.3 %all-to-all-start.1 = ((bf16[32,32,128]{2,1,0:T(8,128)(2,1)}), bf16[32,32,128]{2,1,0:T(8,128)(2,1)S(1)}, u32[]{:S(2)}, u32[]{:S(2)}) async-start(bf16[32,32,128]{2,1,0:T(8,128)(2,1)} %shard_map.134), calls=%async_computation.1 | async-start | bytes 524288 | tf_op jit(solution)/shard_map/all_to_all | solution.py:583
  29.8 1.0 %copy-start.4 = (bf16[2,128,768]{2,1,0:T(8,128)(2,1)S(1)}, bf16[2,128,768]{2,1,0:T(8,128)(2,1)}, u32[]{:S(2)}) copy-start(bf16[2,128,768]{2,1,0:T(8,128)(2,1)} %constant.21.clone.table_ref) | copy-start | bytes 1179652
  30.7 0.9 %copy-start.6 = (f32[4,64,256]{2,1,0:T(8,128)S(1)}, f32[4,64,256]{2,1,0:T(8,128)}, u32[]{:S(2)}) copy-start(f32[4,64,256]{2,1,0:T(8,128)} %sky_ref.3) | copy-start | bytes 786436
  30.8 1.4 %copy-start.8 = (bf16[4,9,64,256]{3,2,1,0:T(8,128)(2,1)S(1)}, bf16[4,9,64,256]{3,2,1,0:T(8,128)(2,1)}, u32[]{:S(2)}) copy-start(bf16[4,9,64,256]{3,2,1,0:T(8,128)(2,1)} %dual_ref.3) | copy-start | bytes 3538948
  30.8 1.7 %copy-start.11 = (bf16[2,8,128,256]{3,2,1,0:T(8,128)(2,1)S(1)}, bf16[2,8,128,256]{3,2,1,0:T(8,128)(2,1)}, u32[]{:S(2)}) copy-start(bf16[2,8,128,256]{3,2,1,0:T(8,128)(2,1)} %copy-done.10) | copy-start | bytes 3145732
  30.8 1.7 %copy-start.13 = (f32[4,64,256]{2,1,0:T(8,128)S(1)}, f32[4,64,256]{2,1,0:T(8,128)}, u32[]{:S(2)}) copy-start(f32[4,64,256]{2,1,0:T(8,128)} %dirty_ref.1) | copy-start | bytes 786436
  36.5 1.0 %copy-start.1 = (f32[8,80,384]{2,1,0:T(8,128)}, f32[8,80,384]{2,1,0:T(8,128)S(1)}, u32[]{:S(2)}) copy-start(f32[8,80,384]{2,1,0:T(8,128)S(1)} %get-tuple-element.17.base_ref) | copy-start | bytes 2949124
  44.5 19.9 %all-to-all-start.2 = ((bf16[32,40,128]{2,1,0:T(8,128)(2,1)}), bf16[32,40,128]{2,1,0:T(8,128)(2,1)S(1)}, u32[]{:S(2)}, u32[]{:S(2)}) async-start(bf16[32,40,128]{2,1,0:T(8,128)(2,1)} %shard_map.137), calls=%async_computation.2 | async-start | bytes 655360 | tf_op jit(solution)/shard_map/all_to_all | solution.py:634
  49.7 5.5 %collective-permute-start = (bf16[8,16,384]{2,1,0:T(8,128)(2,1)S(1)}, bf16[8,16,384]{2,1,0:T(8,128)(2,1)S(1)}, u32[]{:S(2)}, u32[]{:S(2)}) collective-permute-start(bf16[8,16,384]{2,1,0:T(8,128)(2,1)S(1)} %get-tuple-element.19), channel_id=1, source_target_pairs={{0,8},{8,16},{16,24},{24,32},{32,40},{40,48},{48,56},{56,64},{64,7... | collective-permute-start | bytes 294920 | tf_op jit(solution)/shard_map/ppermute | solution.py:638
  53.3 7.3 %collective-permute-start.1 = (bf16[8,16,384]{2,1,0:T(8,128)(2,1)S(1)}, bf16[8,16,384]{2,1,0:T(8,128)(2,1)S(1)}, u32[]{:S(2)}, u32[]{:S(2)}) collective-permute-start(bf16[8,16,384]{2,1,0:T(8,128)(2,1)S(1)} %get-tuple-element.20), channel_id=1, source_target_pairs={{8,0},{16,8},{24,16},{32,24},{40,32},{48,40},{56,48},{64,56},{72,6... | collective-permute-start | bytes 294920 | tf_op jit(solution)/shard_map/ppermute | solution.py:639
  60.6 1.2 %copy-start.2 = (f32[8,80,384]{2,1,0:T(8,128)S(1)}, f32[8,80,384]{2,1,0:T(8,128)}, u32[]{:S(2)}) copy-start(f32[8,80,384]{2,1,0:T(8,128)} %copy-done.1) | copy-start | bytes 2949124
  62.1 15.4 %copy-start.15 = (bf16[512,256]{1,0:T(8,128)(2,1)S(1)}, bf16[512,256]{1,0:T(8,128)(2,1)}, u32[]{:S(2)}) copy-start(bf16[512,256]{1,0:T(8,128)(2,1)} %copy-done.14) | copy-start | bytes 786436
  62.1 15.4 %copy-start.16 = (f32[9]{0:T(128)S(1)}, f32[9]{0:T(128)}, u32[]{:S(2)}) copy-start(f32[9]{0:T(128)} %bound_ref.1) | copy-start | bytes 112
  64.4 13.1 %copy-start.9 = (bf16[4,9,64,256]{3,2,1,0:T(8,128)(2,1)S(1)}, bf16[4,9,64,256]{3,2,1,0:T(8,128)(2,1)}, u32[]{:S(2)}) copy-start(bf16[4,9,64,256]{3,2,1,0:T(8,128)(2,1)} %dual_ref.3) | copy-start | bytes 3538948
  64.4 13.1 %copy-start.12 = (bf16[2,8,128,256]{3,2,1,0:T(8,128)(2,1)S(1)}, bf16[2,8,128,256]{3,2,1,0:T(8,128)(2,1)}, u32[]{:S(2)}) copy-start(bf16[2,8,128,256]{3,2,1,0:T(8,128)(2,1)} %copy-done.10) | copy-start | bytes 3145732

commit v5 on v4

--- a/solution.py
+++ b/solution.py
@@ -69,11 +69,8 @@
 
 
 def fixed_table():
-    table = np.zeros((256, 512), jnp.bfloat16)
-    for t in range(2):
-        table[:, t * 128 : t * 128 + 128] = turn_table()[t]
-        table[0:64, 256 + t * 128 : 320 + t * 128] = block_table()[t]
-    return table
+    turns = [np.concatenate(np.split(t, 4), axis=1) for t in turn_table()]
+    return np.concatenate([*block_table(), *turns], axis=1)
 
 
 def tile_table():
@@ -223,9 +220,10 @@
     pick = (tile == right // 4) & (left % 4 == right % 4)
     pick = jnp.where(pick, 1.0, 0.0).astype(BF)
     o_ref[...] = jnp.zeros_like(o_ref)
-    for k in range(SLOTS):
-        o_ref[256 + k * 64 : 320 + k * 64, 0:64] = tiles_ref[channel, 0, k].astype(F32).T.astype(BF)
-    o_ref[256:512, 128:640] = fixed_ref[...]
+    for k in range(0, SLOTS, 2):
+        pair = [tiles_ref[channel, 0, k + n].astype(F32).T for n in range(2)]
+        o_ref[256:320, k * 64 : k * 64 + 128] = jnp.concatenate(pair, axis=1).astype(BF)
+    o_ref[256:320, 384:1536] = fixed_ref[...]
     for t in range(2):
         row = dot(pick, table_ref[t]).astype(BF)
         for j in range(2):
@@ -239,16 +237,17 @@
                     o_ref[rows, to : to + 128] = row[:, at : at + 128]
 
 
-def gram_kernel(d_ref, e_ref, o_ref, rows, rhs, mid, edge):
+def gram_kernel(d_ref, e_ref, o_ref, rows, rhs, mid, edge, out, sem):
     rows[0:1024, :] = d_ref[...].reshape(1024, 128).astype(F32)
     for p in range(16):
         lanes = slice(p * 128, p * 128 + 128)
         at = (p % 2) * 8 + p // 2
         rhs[0:32, lanes] = rows[pl.ds(at, 32, stride=32), :].astype(BF)
         rhs[32:64, lanes] = rows[pl.ds(16 + at, 32, stride=32), :].astype(BF)
-    block = [e_ref[256:320, 384 + t * 128 : 448 + t * 128] for t in range(2)]
-    turns = e_ref[256:512, 128:256].astype(F32) + e_ref[256:512, 256:384].astype(F32)
-    tc, ts, ec, es = (turns[n * 64 : n * 64 + 64] for n in range(4))
+    fixed = e_ref[256:320, :]
+    block = [fixed[:, 384:448], fixed[:, 448:512]]
+    turns = fixed[:, 512:1024].astype(F32) + fixed[:, 1024:1536].astype(F32)
+    tc, ts, ec, es = (turns[:, n * 128 : n * 128 + 128] for n in range(4))
     first = dot(jnp.concatenate(block, axis=0), rhs[...])
     first = first[0:64] + first[64:128]
     for p in range(16):
@@ -262,7 +261,8 @@
     spec = dot(mid[...], e_ref[0:256, 0:1024], LAST)
     spec = (spec[:, 0:128] + spec[:, 128:256]).astype(BF)
     spec = jnp.concatenate([spec[g * 64 : g * 64 + 64] for g in range(4)], axis=1)
-    mixed = dot(e_ref[256:640, 0:64], spec)
+    tiles = [fixed[:, k * 64 : k * 64 + 64] for k in range(SLOTS)]
+    mixed = dot(jnp.concatenate(tiles, axis=0), spec)
     lane_slot = (lax.broadcasted_iota(jnp.int32, (64, 512), 1) % 32) // 4
     weighted = jnp.where(lane_slot == 0, mixed[0:64], 0.0)
     for k in range(1, SLOTS):
@@ -300,60 +300,96 @@
         rows[pl.ds(16 + at, 32, stride=40), :] = last[32:64, lanes]
     for v in range(8):
         rows[pl.ds(32 + v, 32, stride=40), :] = outer[:, v * 128 : v * 128 + 128]
-    o_ref[...] = rows[...].reshape(32, 40, 128).astype(BF)
-
-
-def band_kernel(taps_ref, strip_ref, down_ref):
+    leave = []
+    for n in range(2):
+        half = rows[n * 640 : n * 640 + 640, :]
+        out[n] = half.reshape(16, 40, 128).astype(BF)
+        to = o_ref.at[pl.ds(n * 16, 16)]
+        leave.append(pltpu.make_async_copy(out.at[n], to, sem.at[n]))
+        leave[n].start()
+    for n in range(2):
+        leave[n].wait()
+
+
+def bands_kernel(taps_ref, o_ref):
     lane = lax.broadcasted_iota(jnp.int32, (64, 256), 1)
     for k in range(FRAMES):
         wide = jnp.broadcast_to(taps_ref[k : k + 1, :], (128, 256))
         band = pltpu.roll(wide, 0, 1, stride=1, stride_axis=0)
         high = band.astype(BF)
         low = band - high.astype(F32)
-        strip_ref[0, k] = high
-        strip_ref[1, k] = low.astype(BF)
+        o_ref[k * 128 : k * 128 + 128, :] = high
+        o_ref[1024 + k * 128 : 1152 + k * 128, :] = low.astype(BF)
+        low = jnp.where(lane < 80, low[0:64], 0.0)
         high = jnp.where(lane < 80, high[0:64].astype(F32), 0.0)
-        low = jnp.where(lane < 80, low[0:64], 0.0)
         row = high + pltpu.roll(high, 80, 1) + pltpu.roll(low, 160, 1)
-        down_ref[k * 64 : k * 64 + 64, :] = row.astype(BF)
+        o_ref[2048 + k * 64 : 2112 + k * 64, :] = row.astype(BF)
 
 
 def synth_kernel(
-    where_ref, live_ref, dual_ref, sky_ref, dirty_ref, strip_ref, o_ref, head_ref, tail_ref, across
+    where_ref,
+    live_ref,
+    dual_hbm,
+    sky_hbm,
+    dirty_hbm,
+    bands_ref,
+    o_ref,
+    head_ref,
+    tail_ref,
+    dual_ref,
+    sky_ref,
+    dirty_ref,
+    across,
+    dual_sem,
+    sky_sem,
+    dirty_sem,
 ):
     channels = sky_ref.shape[0]
+    copies = [
+        pltpu.make_async_copy(dual_hbm.at[:, k], dual_ref.at[k], dual_sem.at[k])
+        for k in range(FRAMES + 1)
+    ]
+    for k in range(1, FRAMES + 1):
+        copies[k].start()
+    copies[0].start()
+    sky_copy = pltpu.make_async_copy(sky_hbm, sky_ref, sky_sem)
+    sky_copy.start()
+    dirty_copy = pltpu.make_async_copy(dirty_hbm, dirty_ref, dirty_sem)
+    dirty_copy.start()
     row = lax.broadcasted_iota(jnp.int32, (80, WIDE), 0) + where_ref[2] * ROWS - RADIUS
     lane = lax.broadcasted_iota(jnp.int32, (80, WIDE), 1)
     col = lane + where_ref[3] * COLS - RADIUS
     inside = (row >= 0) & (row < PIXELS) & (col >= 0) & (col < PIXELS)
     for k in range(FRAMES):
-        p = dual_ref[:, k + 1].reshape(channels * ROWS, COLS)
+        copies[k + 1].wait()
+        p = dual_ref[k + 1].reshape(channels * ROWS, COLS)
         both = jnp.concatenate([p[:, 0:128], p[:, 128:256]], axis=0)
-        a = dot(both, strip_ref[0, k]) + dot(both, strip_ref[1, k])
+        both = jnp.concatenate([both, both], axis=1)
+        at = k * 128
+        band = jnp.concatenate(
+            [bands_ref[at : at + 128, :], bands_ref[1024 + at : 1152 + at, :]], axis=0
+        )
+        a = dot(both, band)
         a0 = a[0 : channels * ROWS]
         a1 = a[channels * ROWS :]
         out = jnp.concatenate([a0[:, 0:128], a0[:, 128:256] + a1[:, 0:128], a1[:, 128:256]], axis=1)
         for c in range(channels):
             across[c, k * ROWS : (k + 1) * ROWS, :] = out[c * ROWS : (c + 1) * ROWS].astype(BF)
+    copies[0].wait()
+    sky_copy.wait()
+    dirty_copy.wait()
     live = lax.broadcasted_iota(jnp.int32, (ROWS, COLS), 0) < live_ref[0]
     none = jnp.zeros((ROWS, 128), F32)
     edge = jnp.zeros((8, WIDE), F32)
     for c in range(channels):
-        total = None
-        for t in range(2):
-            for k in range(FRAMES):
-                term = dot(
-                    strip_ref[t, k][0:64, 0:128],
-                    across[c, k * ROWS : (k + 1) * ROWS, :],
-                    FIRST,
-                )
-                total = term if total is None else total + term
+        total = dot(bands_ref[2048:2560, :], across[c], FIRST)
+        total = total[0:80] + total[160:240]
         sky = sky_ref[c]
-        own = sky + STEP_PRIMAL * dirty_ref[c] - STEP_PRIMAL * dual_ref[c, 0].astype(F32)
+        own = sky + STEP_PRIMAL * dirty_ref[c] - STEP_PRIMAL * dual_ref[0, c].astype(F32)
         own = jnp.where(live, own, OUTSIDE)
         own = pltpu.roll(jnp.concatenate([own, none], axis=1), 8, 1)
         sky = pltpu.roll(jnp.concatenate([sky, none], axis=1), 8, 1)
-        total = total[0:80] * (-STEP_PRIMAL)
+        total = total * (-STEP_PRIMAL)
         total = total + jnp.concatenate([edge, own, edge], axis=0)
         total = jnp.where(inside, total, OUTSIDE)
         total = jnp.where(lane < COLS + 2 * RADIUS, total, 0.0)
@@ -393,8 +429,7 @@
     half_ref,
     base_ref,
     dual_ref,
-    strip_ref,
-    down_ref,
+    bands_ref,
     image_ref,
     o_ref,
     image_buf,
@@ -453,7 +488,7 @@
         wide[0:80, :] = high
         wide[80:160, :] = low
         wide[160:240, :] = high
-        d = dot(down_ref[...], wide[...])
+        d = dot(bands_ref[2048:2560, :], wide[...])
         high = d.astype(BF)
         down[0, c] = high
         down[1, c] = (d - high.astype(F32)).astype(BF)
@@ -466,12 +501,13 @@
         for t in range(2):
             d = jnp.concatenate([down[t, c, at : at + ROWS, :] for c in range(channels)], axis=0)
             both = jnp.concatenate([d[:, 0:256], d[:, 128:384]], axis=0)
+            high = bands_ref[(k - 1) * 128 : k * 128, :]
             if t == 0:
-                band = jnp.concatenate([strip_ref[0, k - 1], strip_ref[1, k - 1]], axis=0)
+                band = jnp.concatenate([high, bands_ref[896 + k * 128 : 1024 + k * 128, :]], axis=0)
                 term = dot(both, band, LAST)
                 a = term[:, 0:128] + term[:, 128:256]
             else:
-                a = a + dot(both, strip_ref[0, k - 1], LAST)
+                a = a + dot(both, high, LAST)
         finish(
             k,
             lambda c: jnp.concatenate(
@@ -485,27 +521,28 @@
 
 VM = pl.BlockSpec(memory_space=pltpu.VMEM)
 SM = pl.BlockSpec(memory_space=pltpu.SMEM)
-
-
-def call(kernel, out_shape, scratch, flops, moved, *args, scalars=0):
+HB = pl.BlockSpec(memory_space=pltpu.HBM)
+
+
+def call(kernel, out_shape, scratch, flops, moved, *args, scalars=0, result=VM):
     return pl.pallas_call(
         kernel,
         out_shape=out_shape,
         in_specs=[SM] * scalars + [VM] * (len(args) - scalars),
-        out_specs=jax.tree.map(lambda _: VM, out_shape),
+        out_specs=jax.tree.map(lambda _: result, out_shape),
         scratch_shapes=scratch,
         compiler_params=pltpu.CompilerParams(vmem_limit_bytes=VMEM_LIMIT),
         cost_estimate=pl.CostEstimate(flops=flops, bytes_accessed=moved, transcendentals=0),
     )(*args)
 
 
-def frames_call(thresholds, where, halves, base, dual, strip, down):
+def frames_call(thresholds, where, halves, base, dual, bands):
     channels = dual.shape[0]
     block = (channels, ROWS, COLS)
     return pl.pallas_call(
         frames_kernel,
         out_shape=(jax.ShapeDtypeStruct(block, F32), jax.ShapeDtypeStruct(dual.shape, BF)),
-        in_specs=[SM, SM, VM, VM, VM, VM, VM],
+        in_specs=[SM, SM, VM, VM, VM, VM],
         out_specs=(pl.BlockSpec(memory_space=pl.ANY), pl.BlockSpec(memory_space=pl.ANY)),
         scratch_shapes=[
             pltpu.VMEM(block, F32),
@@ -518,7 +555,7 @@
         ],
         compiler_params=pltpu.CompilerParams(vmem_limit_bytes=VMEM_LIMIT),
         cost_estimate=pl.CostEstimate(flops=1 << 31, bytes_accessed=3 << 20, transcendentals=0),
-    )(thresholds, where, halves, base, dual, strip, down)
+    )(thresholds, where, halves, base, dual, bands)
 
 
 def after(values, *events):
@@ -555,18 +592,11 @@
     )(pltpu.with_memory_space_constraint(sky_estimate, pltpu.HBM))
     lines = lax.all_to_all(sent, "fou", split_axis=0, concat_axis=0, tiled=True)
 
-    strip, down = call(
-        band_kernel,
-        (
-            jax.ShapeDtypeStruct((2, FRAMES, 128, 256), BF),
-            jax.ShapeDtypeStruct((FRAMES * ROWS, 256), BF),
-        ),
-        [],
-        1 << 20,
-        1 << 20,
-        jnp.pad(filters, ((0, 0), (0, 256 - filters.shape[1]))),
-    )
-    (ready_where,) = after((where,), strip)
+    taps = jnp.pad(filters, ((0, 0), (0, 256 - filters.shape[1])))
+    bands = call(
+        bands_kernel, jax.ShapeDtypeStruct((2560, 256), BF), [], 1 << 20, 1 << 20, taps
+    )
+    (ready_where,) = after((where,), bands)
     line = wave_table()
     held = call(hold_kernel, jax.ShapeDtypeStruct(line.shape, BF), [], 1 << 10, 1 << 20, line)
     packed = call(
@@ -584,7 +614,7 @@
 
     spread = call(
         tiles_kernel,
-        jax.ShapeDtypeStruct((640, 1536), BF),
+        jax.ShapeDtypeStruct((320, 1536), BF),
         [],
         1 << 23,
         1 << 20,
@@ -600,19 +630,27 @@
     ends = jax.ShapeDtypeStruct((2 * channels, 16, WIDE), BF)
     extended = jax.ShapeDtypeStruct((2 * channels, tile_rows + 16, WIDE), F32)
     (late_where,) = after((where,), packed)
-    base, head, tail = call(
+    base, head, tail = pl.pallas_call(
         synth_kernel,
-        (extended, ends, ends),
-        [pltpu.VMEM((channels, FRAMES * ROWS, WIDE), BF)],
-        1 << 31,
-        4 << 20,
+        out_shape=(extended, ends, ends),
+        in_specs=[SM, SM, HB, HB, HB, VM],
+        out_specs=(VM, VM, VM),
+        scratch_shapes=[
+            pltpu.VMEM((FRAMES + 1, channels, tile_rows, tile_cols), BF),
+            pltpu.VMEM(sky_estimate.shape, F32),
+            pltpu.VMEM(sky_estimate.shape, F32),
+            pltpu.VMEM((channels, FRAMES * ROWS, WIDE), BF),
+            pltpu.SemaphoreType.DMA((FRAMES + 1,)),
+            pltpu.SemaphoreType.DMA(()),
+            pltpu.SemaphoreType.DMA(()),
+        ],
+        compiler_params=pltpu.CompilerParams(vmem_limit_bytes=VMEM_LIMIT),
+        cost_estimate=pl.CostEstimate(flops=1 << 31, bytes_accessed=4 << 20, transcendentals=0),
+    )(
         late_where,
         facet_rows,
-        dual_coeffs,
-        sky_estimate,
-        dirty_image,
-        strip,
-        scalars=2,
+        *(pltpu.with_memory_space_constraint(a, pltpu.HBM) for a in (dual_coeffs, sky_estimate, dirty_image)),
+        bands,
     )
     (received,) = after((received,), head)
 
@@ -621,6 +659,8 @@
         pltpu.VMEM((64, 2048), BF),
         pltpu.VMEM((256, 1024), BF),
         pltpu.VMEM((64, 1024), BF),
+        pltpu.VMEM((2, 16, 40, 128), BF),
+        pltpu.SemaphoreType.DMA((2,)),
     ]
     weighted = call(
         gram_kernel,
@@ -630,6 +670,7 @@
         1 << 20,
         received,
         spread,
+        result=HB,
     )
     returned = lax.all_to_all(weighted, "img", split_axis=0, concat_axis=0, tiled=True)
 
@@ -661,7 +702,7 @@
     )
     halves = lax.all_to_all(blocks, "fou", split_axis=0, concat_axis=0, tiled=True)
 
-    return frames_call(thresholds, where, halves, base, dual_coeffs, strip, down)
+    return frames_call(thresholds, where, halves, base, dual_coeffs, bands)
 
 
 def solution(mesh):

time: 81.5 us -> 82.3 us (level)
    pallas_call x8 -> x7, Pallas kernels: 11.7 us -> 6.98 us  [call(): pl.pallas_call(kernel, out_shape=out_shape, in_specs=[SM] * scalars + [VM...]
    pallas_call x0 -> x1, Pallas kernels: none -> 4.59 us  [body(): pl.pallas_call(synth_kernel, out_shape=(extended, ends, ends), in_specs=[...]
    all_to_all x1, waiting for transfers between devices: 4.11 us -> 5.09 us  [body(): lines = lax.all_to_all(sent, 'fou', split_axis=0, concat_axis=0, tiled=True)]
    unnamed x39 -> x29, local copies, waits for them, and re-layouts: 5.05 us -> 4.88 us
  transfers between devices with their start and end apart: 5 -> 5, of which waited for: 4 -> 5; matrix products, arithmetic and copies ran while one was open for 0% -> 0% of each run, Pallas kernels for 7% -> 8%
where the time goes in v5:
time: 82.3 us; the launch traced here: 81.6 us
  starting transfers between devices  30 us (36%)
  Pallas kernels  16.7 us (20%)
  waiting for transfers between devices  16.7 us (20%)
  blocking collectives  11.8 us (14%)
  local copies, waits for them, and re-layouts  4.88 us (6%)
  between operations  1.48 us (2%)
    all_to_all x1, starting transfers between devices, body(): lax.all_to_all(packed, 'img', split_axis=0, concat_axis=0, tiled=True)  12.3 us
    all_to_all x1, blocking collectives, body(): lax.all_to_all(blocks, 'fou', split_axis=0, concat_axis=0, tiled=True)  11.8 us
    pallas_call x7, Pallas kernels, call(): pl.pallas_call(kernel, out_shape=out_shape, in_specs=[SM] * scalars + [VM...  6.98 us
    all_to_all x1, starting transfers between devices, body(): lines = lax.all_to_all(sent, 'fou', split_axis=0, concat_axis=0, tiled=True)  6.39 us
    all_to_all x1, starting transfers between devices, body(): lax.all_to_all(weighted, 'img', split_axis=0, concat_axis=0, tiled=True)  5.85 us
    ppermute x1, waiting for transfers between devices, body(): from_after = lax.ppermute(head, 'img', [(j, i) for i, j in steps])  5.37 us
    all_to_all x1, waiting for transfers between devices, body(): lines = lax.all_to_all(sent, 'fou', split_axis=0, concat_axis=0, tiled=True)  5.09 us
    unnamed x29, local copies, waits for them, and re-layouts  4.88 us
  transfers between devices with their start and end apart: 5, of which 5 were waited for; matrix products, arithmetic and copies ran while one was open for 0% of the time, Pallas kernels for 8%

profile of v5, /device:TPU:1, one launch (start us, length us, event | category | flops | bytes accessed | tf_op | source)
XLA Modules:
  0.0 81.6 jit_solution(2484663343400887272)
XLA Ops:
  0.6 0.0 copy-start
  0.6 0.0 copy-start.12
  0.7 1.7 %shard_map.132 = bf16[8,64,256]{2,1,0:T(8,128)(2,1)} custom-call(f32[4,64,256]{2,1,0:T(8,128)} %sky_hbm.1), custom_call_target="tpu_custom_call" | custom-call | tf_op jit(solution)/shard_map/pallas_call | solution.py:580
  2.4 6.4 %all-to-all-start = ((bf16[8,64,256]{2,1,0:T(8,128)(2,1)}), bf16[8,64,256]{2,1,0:T(8,128)(2,1)S(1)}, u32[]{:S(2)}, u32[]{:S(2)}) async-start(bf16[8,64,256]{2,1,0:T(8,128)(2,1)} %shard_map.132), calls=%async_computation | async-start | bytes 524288 | tf_op jit(solution)/shard_map/all_to_all | solution.py:593
  8.8 0.0 copy-done
  8.8 0.0 copy-done.12
  8.9 0.8 %shard_map.131.bands_ref = bf16[2560,256]{1,0:T(8,128)(2,1)S(1)} custom-call(f32[8,256]{1,0:T(8,128)S(1)} %pad.4.taps_ref), custom_call_target="tpu_custom_call" | custom-call | flops 1048576 | bytes 1048576 | tf_op jit(solution)/shard_map/pallas_call | solution.py:528
  9.7 0.1 pad_add_fusion.par_ref.where_ref
  9.8 0.0 copy-start.3
  9.8 0.0 copy-start.7
  9.8 5.1 %all-to-all-done.x_ref = bf16[8,64,256]{2,1,0:T(8,128)(2,1)S(1)} async-done(((bf16[8,64,256]{2,1,0:T(8,128)(2,1)}), bf16[8,64,256]{2,1,0:T(8,128)(2,1)S(1)}, u32[]{:S(2)}, u32[]{:S(2)}) %all-to-all-start) | async-done | bytes 262176 | tf_op jit(solution)/shard_map/all_to_all | solution.py:593
  14.9 1.1 %shard_map.134 = bf16[32,32,128]{2,1,0:T(8,128)(2,1)S(1)} custom-call(s32[4]{0:T(128)S(1)} %pad_add_fusion.par_ref.where_ref, bf16[8,64,256]{2,1,0:T(8,128)(2,1)S(1)} %all-to-all-done.x_ref, bf16[2,288,512]{2,1,0:T(8,128)(2,1)S(1)} %shard_map.133.line_ref), custom_call_target="tpu_custom_call" | custom-call | flops 536870912 | bytes 1048576 | tf_op jit(solution)/shard_map/pallas_call | solution.py:528
  16.0 0.0 copy-start.5
  16.0 0.7 copy-done.5
  16.7 12.3 %all-to-all-start.1 = ((bf16[32,32,128]{2,1,0:T(8,128)(2,1)}), bf16[32,32,128]{2,1,0:T(8,128)(2,1)S(1)}, u32[]{:S(2)}, u32[]{:S(2)}) async-start(bf16[32,32,128]{2,1,0:T(8,128)(2,1)} %copy-done.5), calls=%async_computation.1 | async-start | bytes 524288 | tf_op jit(solution)/shard_map/all_to_all | solution.py:613
  29.6 0.0 copy-done.13
  29.6 0.1 copy.14.count_ref
  29.7 0.0 copy-done.3
  29.7 0.0 copy-done.7
  29.7 0.0 copy-start.4
  29.8 1.0 %copy-done.4 = bf16[2,128,768]{2,1,0:T(8,128)(2,1)S(1)} copy-done((bf16[2,128,768]{2,1,0:T(8,128)(2,1)S(1)}, bf16[2,128,768]{2,1,0:T(8,128)(2,1)}, u32[]{:S(2)}) %copy-start.4) | copy-done | bytes 393240
  30.7 0.0 copy-start.6
  30.7 0.9 %copy-done.6 = bf16[64,1152]{1,0:T(8,128)(2,1)S(1)} copy-done((bf16[64,1152]{1,0:T(8,128)(2,1)S(1)}, bf16[64,1152]{1,0:T(8,128)(2,1)}, u32[]{:S(2)}) %copy-start.6) | copy-done | bytes 147480
  31.7 0.9 %shard_map.136.e_ref = bf16[320,1536]{1,0:T(8,128)(2,1)S(1)} custom-call(s32[4]{0:T(128)S(1)} %pad_add_fusion.par_ref.where_ref, s32[4,1,6]{2,1,0:T(1,128)S(1)} %copy-done.7, s32[4,1]{1,0:T(4,128)S(1)} %copy.14.count_ref, bf16[4,1,6,64,64]{4,3,2,1,0:T(8,128)(2,1)S(1)} %copy-done.3, bf16[2,128,768]{2,1,0:T(8,128)(2,1)S(1)} %copy-done.4, ...), custom_call_target="tpu_custom_call" | custom-call | flops 8388608 | bytes 1048576 | tf_op jit(solution)/shard_map/pallas_call | solution.py:528
  32.5 4.6 %shard_map.135 = (f32[8,80,384]{2,1,0:T(8,128)S(1)}, bf16[8,16,384]{2,1,0:T(8,128)(2,1)S(1)}, bf16[8,16,384]{2,1,0:T(8,128)(2,1)S(1)}) custom-call(s32[4]{0:T(128)S(1)} %pad_add_fusion.par_ref.where_ref, s32[1]{0:T(128)S(6)} %copy.15.live_ref, bf16[4,9,64,256]{3,2,1,0:T(8,128)(2,1)} %dual_ref.1, f32[4,64,256]{2,1,0:T(8,128)} %sky_hbm.1, ...), custom_call_target="tpu_custom_call" | custom-call | flops 2147483648 | bytes 4194304 | tf_op jit(solution)/shard_map/pallas_call | solution.py:633
  37.1 0.0 copy-start.1
  37.1 0.9 %copy-done.1 = f32[8,80,384]{2,1,0:T(8,128)} copy-done((f32[8,80,384]{2,1,0:T(8,128)}, f32[8,80,384]{2,1,0:T(8,128)S(1)}, u32[]{:S(2)}) %copy-start.1) | copy-done | bytes 983064
  38.1 0.0 copy-start.9
  38.1 0.0 copy-start.10
  38.1 3.9 %all-to-all-done.1.d_ref = bf16[32,32,128]{2,1,0:T(8,128)(2,1)S(1)} async-done(((bf16[32,32,128]{2,1,0:T(8,128)(2,1)}), bf16[32,32,128]{2,1,0:T(8,128)(2,1)S(1)}, u32[]{:S(2)}, u32[]{:S(2)}) %all-to-all-start.1) | async-done | bytes 262176 | tf_op jit(solution)/shard_map/all_to_all | solution.py:613
  42.0 2.5 %shard_map.137 = bf16[32,40,128]{2,1,0:T(8,128)(2,1)} custom-call(bf16[32,32,128]{2,1,0:T(8,128)(2,1)S(1)} %all-to-all-done.1.d_ref, bf16[320,1536]{1,0:T(8,128)(2,1)S(1)} %shard_map.136.e_ref), custom_call_target="tpu_custom_call" | custom-call | flops 536870912 | bytes 1048576 | tf_op jit(solution)/shard_map/pallas_call | solution.py:528
  44.6 0.0 copy-done.9
  44.6 0.0 copy-done.10
  44.6 5.9 %all-to-all-start.2 = ((bf16[32,40,128]{2,1,0:T(8,128)(2,1)}), bf16[32,40,128]{2,1,0:T(8,128)(2,1)S(1)}, u32[]{:S(2)}, u32[]{:S(2)}) async-start(bf16[32,40,128]{2,1,0:T(8,128)(2,1)} %shard_map.137), calls=%async_computation.2 | async-start | bytes 655360 | tf_op jit(solution)/shard_map/all_to_all | solution.py:675
  50.4 3.5 %collective-permute-start = (bf16[8,16,384]{2,1,0:T(8,128)(2,1)}, bf16[8,16,384]{2,1,0:T(8,128)(2,1)S(1)}, u32[]{:S(2)}, u32[]{:S(2)}) collective-permute-start(bf16[8,16,384]{2,1,0:T(8,128)(2,1)} %copy-done.10), channel_id=1, source_target_pairs={{0,8},{8,16},{16,24},{24,32},{32,40},{40,48},{48,56},{56,64},{64,7... | collective-permute-start | bytes 294920 | tf_op jit(solution)/shard_map/ppermute | solution.py:679
  54.0 1.9 %collective-permute-start.1 = (bf16[8,16,384]{2,1,0:T(8,128)(2,1)}, bf16[8,16,384]{2,1,0:T(8,128)(2,1)S(1)}, u32[]{:S(2)}, u32[]{:S(2)}) collective-permute-start(bf16[8,16,384]{2,1,0:T(8,128)(2,1)} %copy-done.9), channel_id=1, source_target_pairs={{8,0},{16,8},{24,16},{32,24},{40,32},{48,40},{56,48},{64,56},{72,6... | collective-permute-start | bytes 294920 | tf_op jit(solution)/shard_map/ppermute | solution.py:680
  55.9 0.2 collective-permute-done.before_ref
  56.2 5.4 %collective-permute-done.1.after_ref = bf16[8,16,384]{2,1,0:T(8,128)(2,1)S(1)} collective-permute-done((bf16[8,16,384]{2,1,0:T(8,128)(2,1)}, bf16[8,16,384]{2,1,0:T(8,128)(2,1)S(1)}, u32[]{:S(2)}, u32[]{:S(2)}) %collective-permute-start.1) | collective-permute-done | bytes 98336 | tf_op jit(solution)/shard_map/ppermute | solution.py:680
  61.5 0.0 copy-start.2
  61.5 1.2 %copy-done.2 = f32[8,80,384]{2,1,0:T(8,128)S(1)} copy-done((f32[8,80,384]{2,1,0:T(8,128)S(1)}, f32[8,80,384]{2,1,0:T(8,128)}, u32[]{:S(2)}) %copy-start.2) | copy-done | bytes 983064
  62.7 0.2 shard_map.138.base_ref
  63.0 0.0 copy-start.11
  63.0 2.1 %all-to-all-done.2.t_ref = bf16[32,40,128]{2,1,0:T(8,128)(2,1)S(1)} async-done(((bf16[32,40,128]{2,1,0:T(8,128)(2,1)}), bf16[32,40,128]{2,1,0:T(8,128)(2,1)S(1)}, u32[]{:S(2)}, u32[]{:S(2)}) %all-to-all-start.2) | async-done | bytes 327712 | tf_op jit(solution)/shard_map/all_to_all | solution.py:675
  65.1 1.3 %shard_map.139 = bf16[8,80,384]{2,1,0:T(8,128)(2,1)S(1)} custom-call(s32[4]{0:T(128)S(1)} %pad_add_fusion.par_ref.where_ref, bf16[32,40,128]{2,1,0:T(8,128)(2,1)S(1)} %all-to-all-done.2.t_ref, bf16[2,288,512]{2,1,0:T(8,128)(2,1)S(1)} %copy-done, f32[8,80,384]{2,1,0:T(8,128)S(1)} %shard_map.138.base_ref), custom_call_target="tpu_custom_call" | custom-call | flops 536870912 | bytes 1048576 | tf_op jit(solution)/shard_map/pallas_call | solution.py:528
  66.4 11.8 %all_to_all.20.half_ref = bf16[8,80,384]{2,1,0:T(8,128)(2,1)S(1)} all-to-all(bf16[8,80,384]{2,1,0:T(8,128)(2,1)S(1)} %shard_map.139), channel_id=1, replica_groups=mesh['img'=32,'fou'=8] {'fou'}, dimensions={0} | all-to-all | bytes 983040 | tf_op jit(solution)/shard_map/all_to_all | solution.py:703
  78.2 0.0 copy-done.11
  78.2 0.0 copy-done.8
  78.2 3.4 %shard_map.140 = (f32[4,64,256]{2,1,0:T(8,128)}, bf16[4,9,64,256]{3,2,1,0:T(8,128)(2,1)}) custom-call(f32[9]{0:T(128)S(1)} %copy-done.11, s32[4]{0:T(128)S(1)} %pad_add_fusion.par_ref.where_ref, bf16[8,80,384]{2,1,0:T(8,128)(2,1)S(1)} %all_to_all.20.half_ref, f32[8,80,384]{2,1,0:T(8,128)S(1)} %shard_map.138.base_ref, bf16[4,9,64,256]{3,2,1,0:T(8,128)(2,1)S(1)} %copy-done.8, ...), custom_call_target="tpu_custom_call" | custom-call | flops 2147483648 | bytes 3145728 | tf_op jit(solution)/shard_map/pallas_call | solution.py:542
  (4 shorter events, 0.0 us)
Async XLA Ops:
  0.6 8.1 %copy-start = (bf16[2,288,512]{2,1,0:T(8,128)(2,1)S(1)}, bf16[2,288,512]{2,1,0:T(8,128)(2,1)}, u32[]{:S(2)}) copy-start(bf16[2,288,512]{2,1,0:T(8,128)(2,1)} %constant.20.clone.table_ref.line_ref) | copy-start | bytes 1769476
  0.6 8.2 %copy-start.12 = (f32[8,17]{1,0:T(8,128)S(1)}, f32[8,17]{1,0:T(8,128)}, u32[]{:S(2)}) copy-start(f32[8,17]{1,0:T(8,128)} %param.15) | copy-start | bytes 1636
  2.4 12.5 %all-to-all-start = ((bf16[8,64,256]{2,1,0:T(8,128)(2,1)}), bf16[8,64,256]{2,1,0:T(8,128)(2,1)S(1)}, u32[]{:S(2)}, u32[]{:S(2)}) async-start(bf16[8,64,256]{2,1,0:T(8,128)(2,1)} %shard_map.132), calls=%async_computation | async-start | bytes 524288 | tf_op jit(solution)/shard_map/all_to_all | solution.py:593
  9.8 19.9 %copy-start.13 = (s32[4,1]{0,1:T(1,128)S(1)}, s32[4,1]{0,1:T(1,128)}, u32[]{:S(2)}) copy-start(s32[4,1]{0,1:T(1,128)} %param.19) | copy-start | bytes 52
  9.8 20.0 %copy-start.3 = (bf16[4,1,6,64,64]{4,3,2,1,0:T(8,128)(2,1)S(1)}, bf16[4,1,6,64,64]{4,3,2,1,0:T(8,128)(2,1)}, u32[]{:S(2)}) copy-start(bf16[4,1,6,64,64]{4,3,2,1,0:T(8,128)(2,1)} %tiles_ref.1) | copy-start | bytes 589828
  9.8 20.0 %copy-start.7 = (s32[4,1,6]{2,1,0:T(1,128)S(1)}, s32[4,1,6]{2,1,0:T(1,128)}, u32[]{:S(2)}) copy-start(s32[4,1,6]{2,1,0:T(1,128)} %slots_ref.1) | copy-start | bytes 292
  16.0 0.7 copy-start.5
  16.7 25.3 %all-to-all-start.1 = ((bf16[32,32,128]{2,1,0:T(8,128)(2,1)}), bf16[32,32,128]{2,1,0:T(8,128)(2,1)S(1)}, u32[]{:S(2)}, u32[]{:S(2)}) async-start(bf16[32,32,128]{2,1,0:T(8,128)(2,1)} %copy-done.5), calls=%async_computation.1 | async-start | bytes 524288 | tf_op jit(solution)/shard_map/all_to_all | solution.py:613
  29.7 1.0 %copy-start.4 = (bf16[2,128,768]{2,1,0:T(8,128)(2,1)S(1)}, bf16[2,128,768]{2,1,0:T(8,128)(2,1)}, u32[]{:S(2)}) copy-start(bf16[2,128,768]{2,1,0:T(8,128)(2,1)} %constant.21.clone.table_ref) | copy-start | bytes 1179652
  30.7 0.9 %copy-start.6 = (bf16[64,1152]{1,0:T(8,128)(2,1)S(1)}, bf16[64,1152]{1,0:T(8,128)(2,1)}, u32[]{:S(2)}) copy-start(bf16[64,1152]{1,0:T(8,128)(2,1)} %constant.22.clone.fixed_ref) | copy-start | bytes 442372
  37.1 0.9 %copy-start.1 = (f32[8,80,384]{2,1,0:T(8,128)}, f32[8,80,384]{2,1,0:T(8,128)S(1)}, u32[]{:S(2)}) copy-start(f32[8,80,384]{2,1,0:T(8,128)S(1)} %get-tuple-element.14.base_ref) | copy-start | bytes 2949124
  38.1 6.5 %copy-start.9 = (bf16[8,16,384]{2,1,0:T(8,128)(2,1)}, bf16[8,16,384]{2,1,0:T(8,128)(2,1)S(1)}, u32[]{:S(2)}) copy-start(bf16[8,16,384]{2,1,0:T(8,128)(2,1)S(1)} %get-tuple-element.17) | copy-start | bytes 294916
  38.1 6.5 %copy-start.10 = (bf16[8,16,384]{2,1,0:T(8,128)(2,1)}, bf16[8,16,384]{2,1,0:T(8,128)(2,1)S(1)}, u32[]{:S(2)}) copy-start(bf16[8,16,384]{2,1,0:T(8,128)(2,1)S(1)} %get-tuple-element.16) | copy-start | bytes 294916
  44.6 20.5 %all-to-all-start.2 = ((bf16[32,40,128]{2,1,0:T(8,128)(2,1)}), bf16[32,40,128]{2,1,0:T(8,128)(2,1)S(1)}, u32[]{:S(2)}, u32[]{:S(2)}) async-start(bf16[32,40,128]{2,1,0:T(8,128)(2,1)} %shard_map.137), calls=%async_computation.2 | async-start | bytes 655360 | tf_op jit(solution)/shard_map/all_to_all | solution.py:675
  50.4 5.7 %collective-permute-start = (bf16[8,16,384]{2,1,0:T(8,128)(2,1)}, bf16[8,16,384]{2,1,0:T(8,128)(2,1)S(1)}, u32[]{:S(2)}, u32[]{:S(2)}) collective-permute-start(bf16[8,16,384]{2,1,0:T(8,128)(2,1)} %copy-done.10), channel_id=1, source_target_pairs={{0,8},{8,16},{16,24},{24,32},{32,40},{40,48},{48,56},{56,64},{64,7... | collective-permute-start | bytes 294920 | tf_op jit(solution)/shard_map/ppermute | solution.py:679
  54.0 7.5 %collective-permute-start.1 = (bf16[8,16,384]{2,1,0:T(8,128)(2,1)}, bf16[8,16,384]{2,1,0:T(8,128)(2,1)S(1)}, u32[]{:S(2)}, u32[]{:S(2)}) collective-permute-start(bf16[8,16,384]{2,1,0:T(8,128)(2,1)} %copy-done.9), channel_id=1, source_target_pairs={{8,0},{16,8},{24,16},{32,24},{40,32},{48,40},{56,48},{64,56},{72,6... | collective-permute-start | bytes 294920 | tf_op jit(solution)/shard_map/ppermute | solution.py:680
  61.5 1.2 %copy-start.2 = (f32[8,80,384]{2,1,0:T(8,128)S(1)}, f32[8,80,384]{2,1,0:T(8,128)}, u32[]{:S(2)}) copy-start(f32[8,80,384]{2,1,0:T(8,128)} %copy-done.1) | copy-start | bytes 2949124
  63.0 15.2 %copy-start.11 = (f32[9]{0:T(128)S(1)}, f32[9]{0:T(128)}, u32[]{:S(2)}) copy-start(f32[9]{0:T(128)} %bound_ref.1) | copy-start | bytes 112
  65.1 13.2 %copy-start.8 = (bf16[4,9,64,256]{3,2,1,0:T(8,128)(2,1)S(1)}, bf16[4,9,64,256]{3,2,1,0:T(8,128)(2,1)}, u32[]{:S(2)}) copy-start(bf16[4,9,64,256]{3,2,1,0:T(8,128)(2,1)} %dual_ref.1) | copy-start | bytes 3538948

commit v6 on v5

--- a/solution.py
+++ b/solution.py
@@ -71,6 +71,13 @@
 def fixed_table():
     turns = [np.concatenate(np.split(t, 4), axis=1) for t in turn_table()]
     return np.concatenate([*block_table(), *turns], axis=1)
+
+
+def sampled_table():
+    fixed = fixed_table()
+    rest = np.zeros((64, 768), fixed.dtype)
+    rest[:, 0:384] = fixed[:, 768:1152]
+    return np.concatenate([*tile_table(), fixed[:, 0:768], rest], axis=0)
 
 
 def tile_table():
@@ -209,7 +216,7 @@
         o_ref[f, :, 256:384] = jnp.where(lane < 16, line[:, 256:384], pack).astype(BF)
 
 
-def tiles_kernel(where_ref, slots_ref, count_ref, tiles_ref, table_ref, fixed_ref, o_ref):
+def tiles_kernel(where_ref, slots_ref, count_ref, tiles_ref, table_ref, o_ref):
     channel = where_ref[0]
     left = lax.broadcasted_iota(jnp.int32, (32, 128), 0)
     right = lax.broadcasted_iota(jnp.int32, (32, 128), 1)
@@ -223,9 +230,10 @@
     for k in range(0, SLOTS, 2):
         pair = [tiles_ref[channel, 0, k + n].astype(F32).T for n in range(2)]
         o_ref[256:320, k * 64 : k * 64 + 128] = jnp.concatenate(pair, axis=1).astype(BF)
-    o_ref[256:320, 384:1536] = fixed_ref[...]
+    o_ref[256:320, 384:1152] = table_ref[256:320, :]
+    o_ref[256:320, 1152:1536] = table_ref[320:384, 0:384]
     for t in range(2):
-        row = dot(pick, table_ref[t]).astype(BF)
+        row = dot(pick, table_ref[t * 128 : t * 128 + 128, :]).astype(BF)
         for j in range(2):
             for chi in range(2):
                 p = 2 * j + chi
@@ -329,29 +337,20 @@
 def synth_kernel(
     where_ref,
     live_ref,
-    dual_hbm,
+    dual_ref,
     sky_hbm,
     dirty_hbm,
     bands_ref,
     o_ref,
     head_ref,
     tail_ref,
-    dual_ref,
     sky_ref,
     dirty_ref,
     across,
-    dual_sem,
     sky_sem,
     dirty_sem,
 ):
     channels = sky_ref.shape[0]
-    copies = [
-        pltpu.make_async_copy(dual_hbm.at[:, k], dual_ref.at[k], dual_sem.at[k])
-        for k in range(FRAMES + 1)
-    ]
-    for k in range(1, FRAMES + 1):
-        copies[k].start()
-    copies[0].start()
     sky_copy = pltpu.make_async_copy(sky_hbm, sky_ref, sky_sem)
     sky_copy.start()
     dirty_copy = pltpu.make_async_copy(dirty_hbm, dirty_ref, dirty_sem)
@@ -361,8 +360,7 @@
     col = lane + where_ref[3] * COLS - RADIUS
     inside = (row >= 0) & (row < PIXELS) & (col >= 0) & (col < PIXELS)
     for k in range(FRAMES):
-        copies[k + 1].wait()
-        p = dual_ref[k + 1].reshape(channels * ROWS, COLS)
+        p = dual_ref[:, k + 1].reshape(channels * ROWS, COLS)
         both = jnp.concatenate([p[:, 0:128], p[:, 128:256]], axis=0)
         both = jnp.concatenate([both, both], axis=1)
         at = k * 128
@@ -375,7 +373,6 @@
         out = jnp.concatenate([a0[:, 0:128], a0[:, 128:256] + a1[:, 0:128], a1[:, 128:256]], axis=1)
         for c in range(channels):
             across[c, k * ROWS : (k + 1) * ROWS, :] = out[c * ROWS : (c + 1) * ROWS].astype(BF)
-    copies[0].wait()
     sky_copy.wait()
     dirty_copy.wait()
     live = lax.broadcasted_iota(jnp.int32, (ROWS, COLS), 0) < live_ref[0]
@@ -385,7 +382,7 @@
         total = dot(bands_ref[2048:2560, :], across[c], FIRST)
         total = total[0:80] + total[160:240]
         sky = sky_ref[c]
-        own = sky + STEP_PRIMAL * dirty_ref[c] - STEP_PRIMAL * dual_ref[0, c].astype(F32)
+        own = sky + STEP_PRIMAL * dirty_ref[c] - STEP_PRIMAL * dual_ref[c, 0].astype(F32)
         own = jnp.where(live, own, OUTSIDE)
         own = pltpu.roll(jnp.concatenate([own, none], axis=1), 8, 1)
         sky = pltpu.roll(jnp.concatenate([sky, none], axis=1), 8, 1)
@@ -622,8 +619,7 @@
         tile_slots,
         tile_count,
         gram_tiles,
-        np.stack(tile_table()),
-        fixed_table(),
+        sampled_table(),
         scalars=3,
     )
 
@@ -633,14 +629,12 @@
     base, head, tail = pl.pallas_call(
         synth_kernel,
         out_shape=(extended, ends, ends),
-        in_specs=[SM, SM, HB, HB, HB, VM],
+        in_specs=[SM, SM, VM, HB, HB, VM],
         out_specs=(VM, VM, VM),
         scratch_shapes=[
-            pltpu.VMEM((FRAMES + 1, channels, tile_rows, tile_cols), BF),
             pltpu.VMEM(sky_estimate.shape, F32),
             pltpu.VMEM(sky_estimate.shape, F32),
             pltpu.VMEM((channels, FRAMES * ROWS, WIDE), BF),
-            pltpu.SemaphoreType.DMA((FRAMES + 1,)),
             pltpu.SemaphoreType.DMA(()),
             pltpu.SemaphoreType.DMA(()),
         ],
@@ -649,7 +643,9 @@
     )(
         late_where,
         facet_rows,
-        *(pltpu.with_memory_space_constraint(a, pltpu.HBM) for a in (dual_coeffs, sky_estimate, dirty_image)),
+        dual_coeffs,
+        pltpu.with_memory_space_constraint(sky_estimate, pltpu.HBM),
+        pltpu.with_memory_space_constraint(dirty_image, pltpu.HBM),
         bands,
     )
     (received,) = after((received,), head)

time: 82.3 us -> 81.7 us (level)
  waiting for transfers between devices: 16.7 us -> 19 us
  starting transfers between devices: 30 us -> 28.7 us
  Pallas kernels: 16.7 us -> 15.4 us
    all_to_all x1, waiting for transfers between devices: 3.95 us -> 6.71 us  [body(): lax.all_to_all(packed, 'img', split_axis=0, concat_axis=0, tiled=True)]
    pallas_call x1, Pallas kernels: 4.59 us -> 2.37 us  [body(): pl.pallas_call(synth_kernel, out_shape=(extended, ends, ends), in_specs=[...]
    all_to_all x1, starting transfers between devices: 5.85 us -> 4.5 us  [body(): lax.all_to_all(weighted, 'img', split_axis=0, concat_axis=0, tiled=True)]
    pallas_call x7, Pallas kernels: 6.98 us -> 7.94 us  [call(): pl.pallas_call(kernel, out_shape=out_shape, in_specs=[SM] * scalars + [VM...]
    unnamed x29 -> x25, local copies, waits for them, and re-layouts: 4.88 us -> 4.38 us
  transfers between devices with their start and end apart: 5 -> 5, of which waited for: 5 -> 4; matrix products, arithmetic and copies ran while one was open for 0% -> 0% of each run, Pallas kernels for 8% -> 5%
where the time goes in v6:
time: 81.7 us; the launch traced here: 80.9 us
  starting transfers between devices  28.7 us (35%)
  waiting for transfers between devices  19 us (23%)
  Pallas kernels  15.4 us (19%)
  blocking collectives  11.8 us (14%)
  local copies, waits for them, and re-layouts  4.38 us (5%)
  between operations  1.47 us (2%)
    all_to_all x1, starting transfers between devices, body(): lax.all_to_all(packed, 'img', split_axis=0, concat_axis=0, tiled=True)  12.3 us
    all_to_all x1, blocking collectives, body(): lax.all_to_all(blocks, 'fou', split_axis=0, concat_axis=0, tiled=True)  11.8 us
    pallas_call x7, Pallas kernels, call(): pl.pallas_call(kernel, out_shape=out_shape, in_specs=[SM] * scalars + [VM...  7.94 us
    all_to_all x1, waiting for transfers between devices, body(): lax.all_to_all(packed, 'img', split_axis=0, concat_axis=0, tiled=True)  6.71 us
    all_to_all x1, starting transfers between devices, body(): lines = lax.all_to_all(sent, 'fou', split_axis=0, concat_axis=0, tiled=True)  6.39 us
    ppermute x1, waiting for transfers between devices, body(): from_after = lax.ppermute(head, 'img', [(j, i) for i, j in steps])  5.44 us
    all_to_all x1, waiting for transfers between devices, body(): lines = lax.all_to_all(sent, 'fou', split_axis=0, concat_axis=0, tiled=True)  5.09 us
    all_to_all x1, starting transfers between devices, body(): lax.all_to_all(weighted, 'img', split_axis=0, concat_axis=0, tiled=True)  4.5 us
  transfers between devices with their start and end apart: 5, of which 4 were waited for; matrix products, arithmetic and copies ran while one was open for 0% of the time, Pallas kernels for 5%

profile of v6, /device:TPU:1, one launch (start us, length us, event | category | flops | bytes accessed | tf_op | source)
XLA Modules:
  0.0 80.9 jit_solution(13986017926520228837)
XLA Ops:
  0.6 0.0 copy-start
  0.6 0.0 copy-start.10
  0.7 1.7 %shard_map.123 = bf16[8,64,256]{2,1,0:T(8,128)(2,1)} custom-call(f32[4,64,256]{2,1,0:T(8,128)} %sky_hbm.1), custom_call_target="tpu_custom_call" | custom-call | tf_op jit(solution)/shard_map/pallas_call | solution.py:577
  2.4 6.4 %all-to-all-start = ((bf16[8,64,256]{2,1,0:T(8,128)(2,1)}), bf16[8,64,256]{2,1,0:T(8,128)(2,1)S(1)}, u32[]{:S(2)}, u32[]{:S(2)}) async-start(bf16[8,64,256]{2,1,0:T(8,128)(2,1)} %shard_map.123), calls=%async_computation | async-start | bytes 524288 | tf_op jit(solution)/shard_map/all_to_all | solution.py:590
  8.8 0.0 copy-done
  8.8 0.0 copy-done.10
  8.9 0.8 %shard_map.122.bands_ref = bf16[2560,256]{1,0:T(8,128)(2,1)S(1)} custom-call(f32[8,256]{1,0:T(8,128)S(1)} %pad.4.taps_ref), custom_call_target="tpu_custom_call" | custom-call | flops 1048576 | bytes 1048576 | tf_op jit(solution)/shard_map/pallas_call | solution.py:525
  9.7 0.1 pad_add_fusion.par_ref.where_ref
  9.8 0.0 copy-start.11
  9.8 0.0 copy-start.3
  9.8 0.0 copy-start.6
  9.8 5.1 %all-to-all-done.x_ref = bf16[8,64,256]{2,1,0:T(8,128)(2,1)S(1)} async-done(((bf16[8,64,256]{2,1,0:T(8,128)(2,1)}), bf16[8,64,256]{2,1,0:T(8,128)(2,1)S(1)}, u32[]{:S(2)}, u32[]{:S(2)}) %all-to-all-start) | async-done | bytes 262176 | tf_op jit(solution)/shard_map/all_to_all | solution.py:590
  14.9 1.1 %shard_map.125 = bf16[32,32,128]{2,1,0:T(8,128)(2,1)S(1)} custom-call(s32[4]{0:T(128)S(1)} %pad_add_fusion.par_ref.where_ref, bf16[8,64,256]{2,1,0:T(8,128)(2,1)S(1)} %all-to-all-done.x_ref, bf16[2,288,512]{2,1,0:T(8,128)(2,1)S(1)} %shard_map.124.line_ref), custom_call_target="tpu_custom_call" | custom-call | flops 536870912 | bytes 1048576 | tf_op jit(solution)/shard_map/pallas_call | solution.py:525
  16.0 0.0 copy-start.5
  16.0 0.7 copy-done.5
  16.7 12.3 %all-to-all-start.1 = ((bf16[32,32,128]{2,1,0:T(8,128)(2,1)}), bf16[32,32,128]{2,1,0:T(8,128)(2,1)}, u32[]{:S(2)}, u32[]{:S(2)}) async-start(bf16[32,32,128]{2,1,0:T(8,128)(2,1)} %copy-done.5), calls=%async_computation.1 | async-start | bytes 524288 | tf_op jit(solution)/shard_map/all_to_all | solution.py:610
  29.7 0.0 copy-done.11
  29.7 0.1 copy.13.count_ref
  29.8 0.0 copy-done.3
  29.8 0.0 copy-done.6
  29.8 0.0 copy-start.4
  29.8 1.0 %copy-done.4 = bf16[4,1,6,64,64]{4,3,2,1,0:T(8,128)(2,1)S(1)} copy-done((bf16[4,1,6,64,64]{4,3,2,1,0:T(8,128)(2,1)S(1)}, bf16[4,1,6,64,64]{4,3,2,1,0:T(8,128)(2,1)}, u32[]{:S(2)}) %copy-start.4) | copy-done | bytes 196632
  30.8 0.0 copy-start.7
  30.8 0.8 %shard_map.127.e_ref = bf16[320,1536]{1,0:T(8,128)(2,1)S(1)} custom-call(s32[4]{0:T(128)S(1)} %pad_add_fusion.par_ref.where_ref, s32[4,1,6]{2,1,0:T(1,128)S(1)} %copy-done.6, s32[4,1]{1,0:T(4,128)S(1)} %copy.13.count_ref, bf16[4,1,6,64,64]{4,3,2,1,0:T(8,128)(2,1)S(1)} %copy-done.4, bf16[384,768]{1,0:T(8,128)(2,1)S(1)} %copy-done.3), custom_call_target="tpu_custom_call" | custom-call | flops 8388608 | bytes 1048576 | tf_op jit(solution)/shard_map/pallas_call | solution.py:525
  31.7 0.4 copy-done.7
  32.1 2.4 %shard_map.126 = (f32[8,80,384]{2,1,0:T(8,128)S(1)}, bf16[8,16,384]{2,1,0:T(8,128)(2,1)S(1)}, bf16[8,16,384]{2,1,0:T(8,128)(2,1)S(1)}) custom-call(s32[4]{0:T(128)S(1)} %pad_add_fusion.par_ref.where_ref, s32[1]{0:T(128)S(6)} %copy.14.live_ref, bf16[4,9,64,256]{3,2,1,0:T(8,128)(2,1)S(1)} %copy-done.7, f32[4,64,256]{2,1,0:T(8,128)} %sky_hbm.1, ...), custom_call_target="tpu_custom_call" | custom-call | flops 2147483648 | bytes 4194304 | tf_op jit(solution)/shard_map/pallas_call | solution.py:629
  34.5 0.0 copy-start.1
  34.5 0.9 %copy-done.1 = f32[8,80,384]{2,1,0:T(8,128)} copy-done((f32[8,80,384]{2,1,0:T(8,128)}, f32[8,80,384]{2,1,0:T(8,128)S(1)}, u32[]{:S(2)}) %copy-start.1) | copy-done | bytes 983064
  35.4 6.7 %all-to-all-done.1.d_ref = bf16[32,32,128]{2,1,0:T(8,128)(2,1)} async-done(((bf16[32,32,128]{2,1,0:T(8,128)(2,1)}), bf16[32,32,128]{2,1,0:T(8,128)(2,1)}, u32[]{:S(2)}, u32[]{:S(2)}) %all-to-all-start.1) | async-done | bytes 262176 | tf_op jit(solution)/shard_map/all_to_all | solution.py:610
  42.1 3.5 %shard_map.128 = bf16[32,40,128]{2,1,0:T(8,128)(2,1)} custom-call(bf16[32,32,128]{2,1,0:T(8,128)(2,1)} %all-to-all-done.1.d_ref, bf16[320,1536]{1,0:T(8,128)(2,1)S(1)} %shard_map.127.e_ref), custom_call_target="tpu_custom_call" | custom-call | flops 536870912 | bytes 1048576 | tf_op jit(solution)/shard_map/pallas_call | solution.py:525
  45.6 4.5 %all-to-all-start.2 = ((bf16[32,40,128]{2,1,0:T(8,128)(2,1)}), bf16[32,40,128]{2,1,0:T(8,128)(2,1)S(1)}, u32[]{:S(2)}, u32[]{:S(2)}) async-start(bf16[32,40,128]{2,1,0:T(8,128)(2,1)} %shard_map.128), calls=%async_computation.2 | async-start | bytes 655360 | tf_op jit(solution)/shard_map/all_to_all | solution.py:671
  50.1 3.5 %collective-permute-start = (bf16[8,16,384]{2,1,0:T(8,128)(2,1)S(1)}, bf16[8,16,384]{2,1,0:T(8,128)(2,1)S(1)}, u32[]{:S(2)}, u32[]{:S(2)}) collective-permute-start(bf16[8,16,384]{2,1,0:T(8,128)(2,1)S(1)} %get-tuple-element.16), channel_id=1, source_target_pairs={{0,8},{8,16},{16,24},{24,32},{32,40},{40,48},{48,56},{56,64},{64,7... | collective-permute-start | bytes 294920 | tf_op jit(solution)/shard_map/ppermute | solution.py:675
  53.7 1.9 %collective-permute-start.1 = (bf16[8,16,384]{2,1,0:T(8,128)(2,1)S(1)}, bf16[8,16,384]{2,1,0:T(8,128)(2,1)S(1)}, u32[]{:S(2)}, u32[]{:S(2)}) collective-permute-start(bf16[8,16,384]{2,1,0:T(8,128)(2,1)S(1)} %get-tuple-element.17), channel_id=1, source_target_pairs={{8,0},{16,8},{24,16},{32,24},{40,32},{48,40},{56,48},{64,56},{72,6... | collective-permute-start | bytes 294920 | tf_op jit(solution)/shard_map/ppermute | solution.py:676
  55.6 0.0 collective-permute-done.before_ref
  55.6 5.4 %collective-permute-done.1.after_ref = bf16[8,16,384]{2,1,0:T(8,128)(2,1)S(1)} collective-permute-done((bf16[8,16,384]{2,1,0:T(8,128)(2,1)S(1)}, bf16[8,16,384]{2,1,0:T(8,128)(2,1)S(1)}, u32[]{:S(2)}, u32[]{:S(2)}) %collective-permute-start.1) | collective-permute-done | bytes 98336 | tf_op jit(solution)/shard_map/ppermute | solution.py:676
  61.1 0.0 copy-start.2
  61.1 1.2 %copy-done.2 = f32[8,80,384]{2,1,0:T(8,128)S(1)} copy-done((f32[8,80,384]{2,1,0:T(8,128)S(1)}, f32[8,80,384]{2,1,0:T(8,128)}, u32[]{:S(2)}) %copy-start.2) | copy-done | bytes 983064
  62.3 0.2 shard_map.129.base_ref
  62.5 0.0 copy-start.9
  62.5 1.8 %all-to-all-done.2.t_ref = bf16[32,40,128]{2,1,0:T(8,128)(2,1)S(1)} async-done(((bf16[32,40,128]{2,1,0:T(8,128)(2,1)}), bf16[32,40,128]{2,1,0:T(8,128)(2,1)S(1)}, u32[]{:S(2)}, u32[]{:S(2)}) %all-to-all-start.2) | async-done | bytes 327712 | tf_op jit(solution)/shard_map/all_to_all | solution.py:671
  64.3 0.0 copy-start.8
  64.3 1.3 %shard_map.130 = bf16[8,80,384]{2,1,0:T(8,128)(2,1)S(1)} custom-call(s32[4]{0:T(128)S(1)} %pad_add_fusion.par_ref.where_ref, bf16[32,40,128]{2,1,0:T(8,128)(2,1)S(1)} %all-to-all-done.2.t_ref, bf16[2,288,512]{2,1,0:T(8,128)(2,1)S(1)} %copy-done, f32[8,80,384]{2,1,0:T(8,128)S(1)} %shard_map.129.base_ref), custom_call_target="tpu_custom_call" | custom-call | flops 536870912 | bytes 1048576 | tf_op jit(solution)/shard_map/pallas_call | solution.py:525
  65.6 11.8 %all_to_all.20.half_ref = bf16[8,80,384]{2,1,0:T(8,128)(2,1)S(1)} all-to-all(bf16[8,80,384]{2,1,0:T(8,128)(2,1)S(1)} %shard_map.130), channel_id=1, replica_groups=mesh['img'=32,'fou'=8] {'fou'}, dimensions={0} | all-to-all | bytes 983040 | tf_op jit(solution)/shard_map/all_to_all | solution.py:699
  77.5 0.0 copy-done.9
  77.5 0.0 copy-done.8
  77.5 3.4 %shard_map.131 = (f32[4,64,256]{2,1,0:T(8,128)}, bf16[4,9,64,256]{3,2,1,0:T(8,128)(2,1)}) custom-call(f32[9]{0:T(128)S(1)} %copy-done.9, s32[4]{0:T(128)S(1)} %pad_add_fusion.par_ref.where_ref, bf16[8,80,384]{2,1,0:T(8,128)(2,1)S(1)} %all_to_all.20.half_ref, f32[8,80,384]{2,1,0:T(8,128)S(1)} %shard_map.129.base_ref, bf16[4,9,64,256]{3,2,1,0:T(8,128)(2,1)S(1)} %copy-done.8, ...), custom_call_target="tpu_custom_call" | custom-call | flops 2147483648 | bytes 3145728 | tf_op jit(solution)/shard_map/pallas_call | solution.py:539
  (2 shorter events, 0.0 us)
Async XLA Ops:
  0.6 8.1 %copy-start = (bf16[2,288,512]{2,1,0:T(8,128)(2,1)S(1)}, bf16[2,288,512]{2,1,0:T(8,128)(2,1)}, u32[]{:S(2)}) copy-start(bf16[2,288,512]{2,1,0:T(8,128)(2,1)} %constant.18.clone.table_ref.line_ref) | copy-start | bytes 1769476
  0.6 8.2 %copy-start.10 = (f32[8,17]{1,0:T(8,128)S(1)}, f32[8,17]{1,0:T(8,128)}, u32[]{:S(2)}) copy-start(f32[8,17]{1,0:T(8,128)} %param.14) | copy-start | bytes 1636
  2.4 12.5 %all-to-all-start = ((bf16[8,64,256]{2,1,0:T(8,128)(2,1)}), bf16[8,64,256]{2,1,0:T(8,128)(2,1)S(1)}, u32[]{:S(2)}, u32[]{:S(2)}) async-start(bf16[8,64,256]{2,1,0:T(8,128)(2,1)} %shard_map.123), calls=%async_computation | async-start | bytes 524288 | tf_op jit(solution)/shard_map/all_to_all | solution.py:590
  9.8 19.9 %copy-start.11 = (s32[4,1]{0,1:T(1,128)S(1)}, s32[4,1]{0,1:T(1,128)}, u32[]{:S(2)}) copy-start(s32[4,1]{0,1:T(1,128)} %param.18) | copy-start | bytes 52
  9.8 20.0 %copy-start.3 = (bf16[384,768]{1,0:T(8,128)(2,1)S(1)}, bf16[384,768]{1,0:T(8,128)(2,1)}, u32[]{:S(2)}) copy-start(bf16[384,768]{1,0:T(8,128)(2,1)} %constant.19.clone.table_ref) | copy-start | bytes 1769476
  9.8 20.0 %copy-start.6 = (s32[4,1,6]{2,1,0:T(1,128)S(1)}, s32[4,1,6]{2,1,0:T(1,128)}, u32[]{:S(2)}) copy-start(s32[4,1,6]{2,1,0:T(1,128)} %slots_ref.1) | copy-start | bytes 292
  16.0 0.7 copy-start.5
  16.7 25.4 %all-to-all-start.1 = ((bf16[32,32,128]{2,1,0:T(8,128)(2,1)}), bf16[32,32,128]{2,1,0:T(8,128)(2,1)}, u32[]{:S(2)}, u32[]{:S(2)}) async-start(bf16[32,32,128]{2,1,0:T(8,128)(2,1)} %copy-done.5), calls=%async_computation.1 | async-start | bytes 524288 | tf_op jit(solution)/shard_map/all_to_all | solution.py:610
  29.8 1.0 %copy-start.4 = (bf16[4,1,6,64,64]{4,3,2,1,0:T(8,128)(2,1)S(1)}, bf16[4,1,6,64,64]{4,3,2,1,0:T(8,128)(2,1)}, u32[]{:S(2)}) copy-start(bf16[4,1,6,64,64]{4,3,2,1,0:T(8,128)(2,1)} %tiles_ref.1) | copy-start | bytes 589828
  30.8 1.3 %copy-start.7 = (bf16[4,9,64,256]{3,2,1,0:T(8,128)(2,1)S(1)}, bf16[4,9,64,256]{3,2,1,0:T(8,128)(2,1)}, u32[]{:S(2)}) copy-start(bf16[4,9,64,256]{3,2,1,0:T(8,128)(2,1)} %dual_ref.3) | copy-start | bytes 3538948
  34.5 0.9 %copy-start.1 = (f32[8,80,384]{2,1,0:T(8,128)}, f32[8,80,384]{2,1,0:T(8,128)S(1)}, u32[]{:S(2)}) copy-start(f32[8,80,384]{2,1,0:T(8,128)S(1)} %get-tuple-element.14.base_ref) | copy-start | bytes 2949124
  45.6 18.7 %all-to-all-start.2 = ((bf16[32,40,128]{2,1,0:T(8,128)(2,1)}), bf16[32,40,128]{2,1,0:T(8,128)(2,1)S(1)}, u32[]{:S(2)}, u32[]{:S(2)}) async-start(bf16[32,40,128]{2,1,0:T(8,128)(2,1)} %shard_map.128), calls=%async_computation.2 | async-start | bytes 655360 | tf_op jit(solution)/shard_map/all_to_all | solution.py:671
  50.1 5.5 %collective-permute-start = (bf16[8,16,384]{2,1,0:T(8,128)(2,1)S(1)}, bf16[8,16,384]{2,1,0:T(8,128)(2,1)S(1)}, u32[]{:S(2)}, u32[]{:S(2)}) collective-permute-start(bf16[8,16,384]{2,1,0:T(8,128)(2,1)S(1)} %get-tuple-element.16), channel_id=1, source_target_pairs={{0,8},{8,16},{16,24},{24,32},{32,40},{40,48},{48,56},{56,64},{64,7... | collective-permute-start | bytes 294920 | tf_op jit(solution)/shard_map/ppermute | solution.py:675
  53.7 7.4 %collective-permute-start.1 = (bf16[8,16,384]{2,1,0:T(8,128)(2,1)S(1)}, bf16[8,16,384]{2,1,0:T(8,128)(2,1)S(1)}, u32[]{:S(2)}, u32[]{:S(2)}) collective-permute-start(bf16[8,16,384]{2,1,0:T(8,128)(2,1)S(1)} %get-tuple-element.17), channel_id=1, source_target_pairs={{8,0},{16,8},{24,16},{32,24},{40,32},{48,40},{56,48},{64,56},{72,6... | collective-permute-start | bytes 294920 | tf_op jit(solution)/shard_map/ppermute | solution.py:676
  61.1 1.2 %copy-start.2 = (f32[8,80,384]{2,1,0:T(8,128)S(1)}, f32[8,80,384]{2,1,0:T(8,128)}, u32[]{:S(2)}) copy-start(f32[8,80,384]{2,1,0:T(8,128)} %copy-done.1) | copy-start | bytes 2949124
  62.5 14.9 %copy-start.9 = (f32[9]{0:T(128)S(1)}, f32[9]{0:T(128)}, u32[]{:S(2)}) copy-start(f32[9]{0:T(128)} %bound_ref.1) | copy-start | bytes 112
  64.3 13.1 %copy-start.8 = (bf16[4,9,64,256]{3,2,1,0:T(8,128)(2,1)S(1)}, bf16[4,9,64,256]{3,2,1,0:T(8,128)(2,1)}, u32[]{:S(2)}) copy-start(bf16[4,9,64,256]{3,2,1,0:T(8,128)(2,1)} %dual_ref.3) | copy-start | bytes 3538948

commit v7 on v6

--- a/solution.py
+++ b/solution.py
@@ -146,7 +146,7 @@
             place(c, h).wait()
 
 
-def forward_kernel(par_ref, x_ref, line_ref, o_ref):
+def forward_kernel(par_ref, x_ref, line_ref, o_ref, out, sem):
     par = par_ref[1]
     folds = fold_rows(line_ref, par)
     sign = (1 - 2 * par).astype(F32)
@@ -162,12 +162,18 @@
             yi = yi + xe[f] * sin[f : f + 1]
         rows[0].append(jnp.concatenate([yr, -yi], axis=1).astype(BF))
         rows[1].append(jnp.concatenate([-yi, -yr], axis=1).astype(BF))
+    def leave(part):
+        to = o_ref.at[:, pl.ds(part * 16, 16), :]
+        return pltpu.make_async_copy(out.at[part], to, sem.at[part])
+
     for part in range(2):
         r = jnp.concatenate(rows[part], axis=0)
-        out = dot(line_ref[0, 0:256], r, LAST) + dot(line_ref[1, 0:256], r, LAST)
-        both = [out[:, chi * 128 : chi * 128 + 128].reshape(32, 8, 128) for chi in range(2)]
-        both = jnp.concatenate(both, axis=1)
-        o_ref[:, part * 16 : (part + 1) * 16, :] = both.astype(BF)
+        wave = dot(line_ref[0, 0:256], r, LAST) + dot(line_ref[1, 0:256], r, LAST)
+        both = [wave[:, chi * 128 : chi * 128 + 128].reshape(32, 8, 128) for chi in range(2)]
+        out[part] = jnp.concatenate(both, axis=1).astype(BF)
+        leave(part).start()
+    for part in range(2):
+        leave(part).wait()
 
 
 def inverse_kernel(par_ref, t_ref, line_ref, base_ref, o_ref):
@@ -599,29 +605,17 @@
     packed = call(
         forward_kernel,
         jax.ShapeDtypeStruct((PEERS_IMG, 32, 128), BF),
-        [],
+        [pltpu.VMEM((2, PEERS_IMG, 16, 128), BF), pltpu.SemaphoreType.DMA((2,))],
         1 << 29,
         1 << 20,
         ready_where,
         lines,
         held,
         scalars=1,
+        result=HB,
     )
     received = lax.all_to_all(packed, "img", split_axis=0, concat_axis=0, tiled=True)
 
-    spread = call(
-        tiles_kernel,
-        jax.ShapeDtypeStruct((320, 1536), BF),
-        [],
-        1 << 23,
-        1 << 20,
-        where,
-        tile_slots,
-        tile_count,
-        gram_tiles,
-        sampled_table(),
-        scalars=3,
-    )
 
     ends = jax.ShapeDtypeStruct((2 * channels, 16, WIDE), BF)
     extended = jax.ShapeDtypeStruct((2 * channels, tile_rows + 16, WIDE), F32)
@@ -648,6 +642,20 @@
         pltpu.with_memory_space_constraint(dirty_image, pltpu.HBM),
         bands,
     )
+    (tiles_where,) = after((where,), head)
+    spread = call(
+        tiles_kernel,
+        jax.ShapeDtypeStruct((320, 1536), BF),
+        [],
+        1 << 23,
+        1 << 20,
+        tiles_where,
+        tile_slots,
+        tile_count,
+        gram_tiles,
+        sampled_table(),
+        scalars=3,
+    )
     (received,) = after((received,), head)
 
     scratch = [

time: 81.7 us -> 80.6 us (0.987)
  local copies, waits for them, and re-layouts: 4.38 us -> 3.55 us
    unnamed x25 -> x23, local copies, waits for them, and re-layouts: 4.38 us -> 3.54 us
where the time goes in v7:
time: 80.6 us; the launch traced here: 79.8 us
  starting transfers between devices  28.6 us (35%)
  waiting for transfers between devices  19.1 us (24%)
  Pallas kernels  15.2 us (19%)
  blocking collectives  11.8 us (15%)
  local copies, waits for them, and re-layouts  3.55 us (4%)
  between operations  1.46 us (2%)
    all_to_all x1, starting transfers between devices, body(): lax.all_to_all(packed, 'img', split_axis=0, concat_axis=0, tiled=True)  12.3 us
    all_to_all x1, blocking collectives, body(): lax.all_to_all(blocks, 'fou', split_axis=0, concat_axis=0, tiled=True)  11.8 us
    pallas_call x7, Pallas kernels, call(): pl.pallas_call(kernel, out_shape=out_shape, in_specs=[SM] * scalars + [VM...  7.69 us
    all_to_all x1, waiting for transfers between devices, body(): lax.all_to_all(packed, 'img', split_axis=0, concat_axis=0, tiled=True)  6.8 us
    all_to_all x1, starting transfers between devices, body(): lines = lax.all_to_all(sent, 'fou', split_axis=0, concat_axis=0, tiled=True)  6.39 us
    ppermute x1, waiting for transfers between devices, body(): from_after = lax.ppermute(head, 'img', [(j, i) for i, j in steps])  5.44 us
    all_to_all x1, waiting for transfers between devices, body(): lines = lax.all_to_all(sent, 'fou', split_axis=0, concat_axis=0, tiled=True)  5.09 us
    all_to_all x1, starting transfers between devices, body(): lax.all_to_all(weighted, 'img', split_axis=0, concat_axis=0, tiled=True)  4.5 us
  transfers between devices with their start and end apart: 5, of which 4 were waited for; matrix products, arithmetic and copies ran while one was open for 0% of the time, Pallas kernels for 5%

profile of v7, /device:TPU:1, one launch (start us, length us, event | category | flops | bytes accessed | tf_op | source)
XLA Modules:
  0.0 79.8 jit_solution(8686055074672474500)
XLA Ops:
  0.6 0.0 copy-start
  0.6 0.0 copy-start.9
  0.7 1.7 %shard_map.123 = bf16[8,64,256]{2,1,0:T(8,128)(2,1)} custom-call(f32[4,64,256]{2,1,0:T(8,128)} %sky_hbm.1), custom_call_target="tpu_custom_call" | custom-call | tf_op jit(solution)/shard_map/pallas_call | solution.py:583
  2.4 6.4 %all-to-all-start = ((bf16[8,64,256]{2,1,0:T(8,128)(2,1)}), bf16[8,64,256]{2,1,0:T(8,128)(2,1)S(1)}, u32[]{:S(2)}, u32[]{:S(2)}) async-start(bf16[8,64,256]{2,1,0:T(8,128)(2,1)} %shard_map.123), calls=%async_computation | async-start | bytes 524288 | tf_op jit(solution)/shard_map/all_to_all | solution.py:596
  8.8 0.0 copy-done
  8.8 0.0 copy-done.9
  8.9 0.8 %shard_map.122.bands_ref = bf16[2560,256]{1,0:T(8,128)(2,1)S(1)} custom-call(f32[8,256]{1,0:T(8,128)S(1)} %pad.4.taps_ref), custom_call_target="tpu_custom_call" | custom-call | flops 1048576 | bytes 1048576 | tf_op jit(solution)/shard_map/pallas_call | solution.py:531
  9.7 0.1 pad_add_fusion.par_ref.where_ref
  9.8 0.0 copy-start.10
  9.8 5.1 %all-to-all-done.x_ref = bf16[8,64,256]{2,1,0:T(8,128)(2,1)S(1)} async-done(((bf16[8,64,256]{2,1,0:T(8,128)(2,1)}), bf16[8,64,256]{2,1,0:T(8,128)(2,1)S(1)}, u32[]{:S(2)}, u32[]{:S(2)}) %all-to-all-start) | async-done | bytes 262176 | tf_op jit(solution)/shard_map/all_to_all | solution.py:596
  14.9 1.8 %shard_map.125 = bf16[32,32,128]{2,1,0:T(8,128)(2,1)} custom-call(s32[4]{0:T(128)S(1)} %pad_add_fusion.par_ref.where_ref, bf16[8,64,256]{2,1,0:T(8,128)(2,1)S(1)} %all-to-all-done.x_ref, bf16[2,288,512]{2,1,0:T(8,128)(2,1)S(1)} %shard_map.124.line_ref), custom_call_target="tpu_custom_call" | custom-call | flops 536870912 | bytes 1048576 | tf_op jit(solution)/shard_map/pallas_call | solution.py:531
  16.7 12.3 %all-to-all-start.1 = ((bf16[32,32,128]{2,1,0:T(8,128)(2,1)}), bf16[32,32,128]{2,1,0:T(8,128)(2,1)S(1)}, u32[]{:S(2)}, u32[]{:S(2)}) async-start(bf16[32,32,128]{2,1,0:T(8,128)(2,1)} %shard_map.125), calls=%async_computation.1 | async-start | bytes 524288 | tf_op jit(solution)/shard_map/all_to_all | solution.py:617
  29.7 0.0 copy-done.10
  29.7 0.1 copy.13.count_ref
  29.8 0.0 copy-start.6
  29.8 1.3 %copy-done.6 = bf16[4,9,64,256]{3,2,1,0:T(8,128)(2,1)S(1)} copy-done((bf16[4,9,64,256]{3,2,1,0:T(8,128)(2,1)S(1)}, bf16[4,9,64,256]{3,2,1,0:T(8,128)(2,1)}, u32[]{:S(2)}) %copy-start.6) | copy-done | bytes 1179672
  31.0 0.0 copy-start.3
  31.0 0.0 copy-start.4
  31.0 0.0 copy-start.5
  31.0 2.4 %shard_map.126 = (f32[8,80,384]{2,1,0:T(8,128)S(1)}, bf16[8,16,384]{2,1,0:T(8,128)(2,1)S(1)}, bf16[8,16,384]{2,1,0:T(8,128)(2,1)S(1)}) custom-call(s32[4]{0:T(128)S(1)} %pad_add_fusion.par_ref.where_ref, s32[1]{0:T(128)S(6)} %copy.14.live_ref, bf16[4,9,64,256]{3,2,1,0:T(8,128)(2,1)S(1)} %copy-done.6, f32[4,64,256]{2,1,0:T(8,128)} %sky_hbm.1, ...), custom_call_target="tpu_custom_call" | custom-call | flops 2147483648 | bytes 4194304 | tf_op jit(solution)/shard_map/pallas_call | solution.py:623
  33.4 0.0 copy-start.1
  33.4 0.9 %copy-done.1 = f32[8,80,384]{2,1,0:T(8,128)} copy-done((f32[8,80,384]{2,1,0:T(8,128)}, f32[8,80,384]{2,1,0:T(8,128)S(1)}, u32[]{:S(2)}) %copy-start.1) | copy-done | bytes 983064
  34.4 0.0 copy-done.3
  34.4 0.0 copy-done.4
  34.4 0.0 copy-done.5
  34.4 0.8 %shard_map.127.e_ref = bf16[320,1536]{1,0:T(8,128)(2,1)S(1)} custom-call(s32[4]{0:T(128)S(1)} %pad_add_fusion.par_ref.where_ref, s32[4,1,6]{2,1,0:T(1,128)S(1)} %copy-done.5, s32[4,1]{1,0:T(4,128)S(1)} %copy.13.count_ref, bf16[4,1,6,64,64]{4,3,2,1,0:T(8,128)(2,1)S(1)} %copy-done.4, bf16[384,768]{1,0:T(8,128)(2,1)S(1)} %copy-done.3), custom_call_target="tpu_custom_call" | custom-call | flops 8388608 | bytes 1048576 | tf_op jit(solution)/shard_map/pallas_call | solution.py:531
  35.2 6.8 %all-to-all-done.1.d_ref = bf16[32,32,128]{2,1,0:T(8,128)(2,1)S(1)} async-done(((bf16[32,32,128]{2,1,0:T(8,128)(2,1)}), bf16[32,32,128]{2,1,0:T(8,128)(2,1)S(1)}, u32[]{:S(2)}, u32[]{:S(2)}) %all-to-all-start.1) | async-done | bytes 262176 | tf_op jit(solution)/shard_map/all_to_all | solution.py:617
  42.0 2.6 %shard_map.128 = bf16[32,40,128]{2,1,0:T(8,128)(2,1)} custom-call(bf16[32,32,128]{2,1,0:T(8,128)(2,1)S(1)} %all-to-all-done.1.d_ref, bf16[320,1536]{1,0:T(8,128)(2,1)S(1)} %shard_map.127.e_ref), custom_call_target="tpu_custom_call" | custom-call | flops 536870912 | bytes 1048576 | tf_op jit(solution)/shard_map/pallas_call | solution.py:531
  44.6 4.5 %all-to-all-start.2 = ((bf16[32,40,128]{2,1,0:T(8,128)(2,1)}), bf16[32,40,128]{2,1,0:T(8,128)(2,1)S(1)}, u32[]{:S(2)}, u32[]{:S(2)}) async-start(bf16[32,40,128]{2,1,0:T(8,128)(2,1)} %shard_map.128), calls=%async_computation.2 | async-start | bytes 655360 | tf_op jit(solution)/shard_map/all_to_all | solution.py:679
  49.1 3.5 %collective-permute-start = (bf16[8,16,384]{2,1,0:T(8,128)(2,1)S(1)}, bf16[8,16,384]{2,1,0:T(8,128)(2,1)S(1)}, u32[]{:S(2)}, u32[]{:S(2)}) collective-permute-start(bf16[8,16,384]{2,1,0:T(8,128)(2,1)S(1)} %get-tuple-element.18), channel_id=1, source_target_pairs={{0,8},{8,16},{16,24},{24,32},{32,40},{40,48},{48,56},{56,64},{64,7... | collective-permute-start | bytes 294920 | tf_op jit(solution)/shard_map/ppermute | solution.py:683
  52.6 1.9 %collective-permute-start.1 = (bf16[8,16,384]{2,1,0:T(8,128)(2,1)S(1)}, bf16[8,16,384]{2,1,0:T(8,128)(2,1)S(1)}, u32[]{:S(2)}, u32[]{:S(2)}) collective-permute-start(bf16[8,16,384]{2,1,0:T(8,128)(2,1)S(1)} %get-tuple-element.19), channel_id=1, source_target_pairs={{8,0},{16,8},{24,16},{32,24},{40,32},{48,40},{56,48},{64,56},{72,6... | collective-permute-start | bytes 294920 | tf_op jit(solution)/shard_map/ppermute | solution.py:684
  54.6 0.0 collective-permute-done.before_ref
  54.6 5.4 %collective-permute-done.1.after_ref = bf16[8,16,384]{2,1,0:T(8,128)(2,1)S(1)} collective-permute-done((bf16[8,16,384]{2,1,0:T(8,128)(2,1)S(1)}, bf16[8,16,384]{2,1,0:T(8,128)(2,1)S(1)}, u32[]{:S(2)}, u32[]{:S(2)}) %collective-permute-start.1) | collective-permute-done | bytes 98336 | tf_op jit(solution)/shard_map/ppermute | solution.py:684
  60.0 0.0 copy-start.2
  60.0 1.2 %copy-done.2 = f32[8,80,384]{2,1,0:T(8,128)S(1)} copy-done((f32[8,80,384]{2,1,0:T(8,128)S(1)}, f32[8,80,384]{2,1,0:T(8,128)}, u32[]{:S(2)}) %copy-start.2) | copy-done | bytes 983064
  61.2 0.2 shard_map.129.base_ref
  61.5 0.0 copy-start.8
  61.5 1.8 %all-to-all-done.2.t_ref = bf16[32,40,128]{2,1,0:T(8,128)(2,1)S(1)} async-done(((bf16[32,40,128]{2,1,0:T(8,128)(2,1)}), bf16[32,40,128]{2,1,0:T(8,128)(2,1)S(1)}, u32[]{:S(2)}, u32[]{:S(2)}) %all-to-all-start.2) | async-done | bytes 327712 | tf_op jit(solution)/shard_map/all_to_all | solution.py:679
  63.3 0.0 copy-start.7
  63.3 1.3 %shard_map.130 = bf16[8,80,384]{2,1,0:T(8,128)(2,1)S(1)} custom-call(s32[4]{0:T(128)S(1)} %pad_add_fusion.par_ref.where_ref, bf16[32,40,128]{2,1,0:T(8,128)(2,1)S(1)} %all-to-all-done.2.t_ref, bf16[2,288,512]{2,1,0:T(8,128)(2,1)S(1)} %copy-done, f32[8,80,384]{2,1,0:T(8,128)S(1)} %shard_map.129.base_ref), custom_call_target="tpu_custom_call" | custom-call | flops 536870912 | bytes 1048576 | tf_op jit(solution)/shard_map/pallas_call | solution.py:531
  64.6 11.8 %all_to_all.20.half_ref = bf16[8,80,384]{2,1,0:T(8,128)(2,1)S(1)} all-to-all(bf16[8,80,384]{2,1,0:T(8,128)(2,1)S(1)} %shard_map.130), channel_id=1, replica_groups=mesh['img'=32,'fou'=8] {'fou'}, dimensions={0} | all-to-all | bytes 983040 | tf_op jit(solution)/shard_map/all_to_all | solution.py:707
  76.4 0.0 copy-done.8
  76.4 0.0 copy-done.7
  76.4 3.4 %shard_map.131 = (f32[4,64,256]{2,1,0:T(8,128)}, bf16[4,9,64,256]{3,2,1,0:T(8,128)(2,1)}) custom-call(f32[9]{0:T(128)S(1)} %copy-done.8, s32[4]{0:T(128)S(1)} %pad_add_fusion.par_ref.where_ref, bf16[8,80,384]{2,1,0:T(8,128)(2,1)S(1)} %all_to_all.20.half_ref, f32[8,80,384]{2,1,0:T(8,128)S(1)} %shard_map.129.base_ref, bf16[4,9,64,256]{3,2,1,0:T(8,128)(2,1)S(1)} %copy-done.7, ...), custom_call_target="tpu_custom_call" | custom-call | flops 2147483648 | bytes 3145728 | tf_op jit(solution)/shard_map/pallas_call | solution.py:545
  (2 shorter events, 0.0 us)
Async XLA Ops:
  0.6 8.1 %copy-start = (bf16[2,288,512]{2,1,0:T(8,128)(2,1)S(1)}, bf16[2,288,512]{2,1,0:T(8,128)(2,1)}, u32[]{:S(2)}) copy-start(bf16[2,288,512]{2,1,0:T(8,128)(2,1)} %constant.18.clone.table_ref.line_ref) | copy-start | bytes 1769476
  0.6 8.2 %copy-start.9 = (f32[8,17]{1,0:T(8,128)S(1)}, f32[8,17]{1,0:T(8,128)}, u32[]{:S(2)}) copy-start(f32[8,17]{1,0:T(8,128)} %param.14) | copy-start | bytes 1636
  2.4 12.5 %all-to-all-start = ((bf16[8,64,256]{2,1,0:T(8,128)(2,1)}), bf16[8,64,256]{2,1,0:T(8,128)(2,1)S(1)}, u32[]{:S(2)}, u32[]{:S(2)}) async-start(bf16[8,64,256]{2,1,0:T(8,128)(2,1)} %shard_map.123), calls=%async_computation | async-start | bytes 524288 | tf_op jit(solution)/shard_map/all_to_all | solution.py:596
  9.8 19.9 %copy-start.10 = (s32[4,1]{0,1:T(1,128)S(1)}, s32[4,1]{0,1:T(1,128)}, u32[]{:S(2)}) copy-start(s32[4,1]{0,1:T(1,128)} %param.18) | copy-start | bytes 52
  16.7 25.3 %all-to-all-start.1 = ((bf16[32,32,128]{2,1,0:T(8,128)(2,1)}), bf16[32,32,128]{2,1,0:T(8,128)(2,1)S(1)}, u32[]{:S(2)}, u32[]{:S(2)}) async-start(bf16[32,32,128]{2,1,0:T(8,128)(2,1)} %shard_map.125), calls=%async_computation.1 | async-start | bytes 524288 | tf_op jit(solution)/shard_map/all_to_all | solution.py:617
  29.8 1.3 %copy-start.6 = (bf16[4,9,64,256]{3,2,1,0:T(8,128)(2,1)S(1)}, bf16[4,9,64,256]{3,2,1,0:T(8,128)(2,1)}, u32[]{:S(2)}) copy-start(bf16[4,9,64,256]{3,2,1,0:T(8,128)(2,1)} %dual_ref.3) | copy-start | bytes 3538948
  31.0 3.3 %copy-start.3 = (bf16[384,768]{1,0:T(8,128)(2,1)S(1)}, bf16[384,768]{1,0:T(8,128)(2,1)}, u32[]{:S(2)}) copy-start(bf16[384,768]{1,0:T(8,128)(2,1)} %constant.19.clone.table_ref) | copy-start | bytes 1769476
  31.0 3.3 %copy-start.4 = (bf16[4,1,6,64,64]{4,3,2,1,0:T(8,128)(2,1)S(1)}, bf16[4,1,6,64,64]{4,3,2,1,0:T(8,128)(2,1)}, u32[]{:S(2)}) copy-start(bf16[4,1,6,64,64]{4,3,2,1,0:T(8,128)(2,1)} %tiles_ref.1) | copy-start | bytes 589828
  31.0 3.3 %copy-start.5 = (s32[4,1,6]{2,1,0:T(1,128)S(1)}, s32[4,1,6]{2,1,0:T(1,128)}, u32[]{:S(2)}) copy-start(s32[4,1,6]{2,1,0:T(1,128)} %slots_ref.1) | copy-start | bytes 292
  33.4 0.9 %copy-start.1 = (f32[8,80,384]{2,1,0:T(8,128)}, f32[8,80,384]{2,1,0:T(8,128)S(1)}, u32[]{:S(2)}) copy-start(f32[8,80,384]{2,1,0:T(8,128)S(1)} %get-tuple-element.16.base_ref) | copy-start | bytes 2949124
  44.6 18.7 %all-to-all-start.2 = ((bf16[32,40,128]{2,1,0:T(8,128)(2,1)}), bf16[32,40,128]{2,1,0:T(8,128)(2,1)S(1)}, u32[]{:S(2)}, u32[]{:S(2)}) async-start(bf16[32,40,128]{2,1,0:T(8,128)(2,1)} %shard_map.128), calls=%async_computation.2 | async-start | bytes 655360 | tf_op jit(solution)/shard_map/all_to_all | solution.py:679
  49.1 5.5 %collective-permute-start = (bf16[8,16,384]{2,1,0:T(8,128)(2,1)S(1)}, bf16[8,16,384]{2,1,0:T(8,128)(2,1)S(1)}, u32[]{:S(2)}, u32[]{:S(2)}) collective-permute-start(bf16[8,16,384]{2,1,0:T(8,128)(2,1)S(1)} %get-tuple-element.18), channel_id=1, source_target_pairs={{0,8},{8,16},{16,24},{24,32},{32,40},{40,48},{48,56},{56,64},{64,7... | collective-permute-start | bytes 294920 | tf_op jit(solution)/shard_map/ppermute | solution.py:683
  52.6 7.4 %collective-permute-start.1 = (bf16[8,16,384]{2,1,0:T(8,128)(2,1)S(1)}, bf16[8,16,384]{2,1,0:T(8,128)(2,1)S(1)}, u32[]{:S(2)}, u32[]{:S(2)}) collective-permute-start(bf16[8,16,384]{2,1,0:T(8,128)(2,1)S(1)} %get-tuple-element.19), channel_id=1, source_target_pairs={{8,0},{16,8},{24,16},{32,24},{40,32},{48,40},{56,48},{64,56},{72,6... | collective-permute-start | bytes 294920 | tf_op jit(solution)/shard_map/ppermute | solution.py:684
  60.0 1.2 %copy-start.2 = (f32[8,80,384]{2,1,0:T(8,128)S(1)}, f32[8,80,384]{2,1,0:T(8,128)}, u32[]{:S(2)}) copy-start(f32[8,80,384]{2,1,0:T(8,128)} %copy-done.1) | copy-start | bytes 2949124
  61.5 14.9 %copy-start.8 = (f32[9]{0:T(128)S(1)}, f32[9]{0:T(128)}, u32[]{:S(2)}) copy-start(f32[9]{0:T(128)} %bound_ref.1) | copy-start | bytes 112
  63.3 13.1 %copy-start.7 = (bf16[4,9,64,256]{3,2,1,0:T(8,128)(2,1)S(1)}, bf16[4,9,64,256]{3,2,1,0:T(8,128)(2,1)}, u32[]{:S(2)}) copy-start(bf16[4,9,64,256]{3,2,1,0:T(8,128)(2,1)} %dual_ref.3) | copy-start | bytes 3538948

commit v8 on v7

--- a/solution.py
+++ b/solution.py
@@ -678,6 +678,11 @@
     )
     returned = lax.all_to_all(weighted, "img", split_axis=0, concat_axis=0, tiled=True)
 
+    (late_taps,) = after((taps,), weighted)
+    late_bands = call(
+        bands_kernel, jax.ShapeDtypeStruct((2560, 256), BF), [], 1 << 20, 1 << 20, late_taps
+    )
+    (last_where,) = after((where,), late_bands)
     head, tail = after((head, tail), weighted)
     steps = [(i, i + 1) for i in range(PEERS_IMG - 1)]
     from_before = lax.ppermute(tail, "img", steps)
@@ -698,7 +703,7 @@
         [],
         1 << 29,
         1 << 20,
-        where,
+        last_where,
         returned,
         line,
         base,
@@ -706,7 +711,7 @@
     )
     halves = lax.all_to_all(blocks, "fou", split_axis=0, concat_axis=0, tiled=True)
 
-    return frames_call(thresholds, where, halves, base, dual_coeffs, bands)
+    return frames_call(thresholds, where, halves, base, dual_coeffs, late_bands)
 
 
 def solution(mesh):

time: 80.6 us -> 80.3 us (level)
  local copies, waits for them, and re-layouts: 3.55 us -> 2.35 us
    unnamed x23, local copies, waits for them, and re-layouts: 3.54 us -> 2.35 us
    all_to_all x1, waiting for transfers between devices: 1.79 us -> 2.87 us  [body(): lax.all_to_all(weighted, 'img', split_axis=0, concat_axis=0, tiled=True)]
    ppermute x1, waiting for transfers between devices: 5.44 us -> 4.55 us  [body(): from_after = lax.ppermute(head, 'img', [(j, i) for i, j in steps])]
    pallas_call x7 -> x8, Pallas kernels: 7.69 us -> 8.55 us  [call(): pl.pallas_call(kernel, out_shape=out_shape, in_specs=[SM] * scalars + [VM...]
  transfers between devices with their start and end apart: 5 -> 5, of which waited for: 4 -> 4; matrix products, arithmetic and copies ran while one was open for 0% -> 0% of each run, Pallas kernels for 5% -> 7%
where the time goes in v8:
time: 80.3 us; the launch traced here: 79.8 us
  starting transfers between devices  28.7 us (36%)
  waiting for transfers between devices  19.3 us (24%)
  Pallas kernels  16 us (20%)
  blocking collectives  11.8 us (15%)
  local copies, waits for them, and re-layouts  2.35 us (3%)
  between operations  1.48 us (2%)
    all_to_all x1, starting transfers between devices, body(): lax.all_to_all(packed, 'img', split_axis=0, concat_axis=0, tiled=True)  12.3 us
    all_to_all x1, blocking collectives, body(): lax.all_to_all(blocks, 'fou', split_axis=0, concat_axis=0, tiled=True)  11.8 us
    pallas_call x8, Pallas kernels, call(): pl.pallas_call(kernel, out_shape=out_shape, in_specs=[SM] * scalars + [VM...  8.55 us
    all_to_all x1, waiting for transfers between devices, body(): lax.all_to_all(packed, 'img', split_axis=0, concat_axis=0, tiled=True)  6.8 us
    all_to_all x1, starting transfers between devices, body(): lines = lax.all_to_all(sent, 'fou', split_axis=0, concat_axis=0, tiled=True)  6.39 us
    all_to_all x1, waiting for transfers between devices, body(): lines = lax.all_to_all(sent, 'fou', split_axis=0, concat_axis=0, tiled=True)  5.08 us
    ppermute x1, waiting for transfers between devices, body(): from_after = lax.ppermute(head, 'img', [(j, i) for i, j in steps])  4.55 us
    all_to_all x1, starting transfers between devices, body(): lax.all_to_all(weighted, 'img', split_axis=0, concat_axis=0, tiled=True)  4.5 us
  transfers between devices with their start and end apart: 5, of which 4 were waited for; matrix products, arithmetic and copies ran while one was open for 0% of the time, Pallas kernels for 7%

profile of v8, /device:TPU:1, one launch (start us, length us, event | category | flops | bytes accessed | tf_op | source)
XLA Modules:
  0.0 79.8 jit_solution(6447127702781312903)
XLA Ops:
  0.6 0.0 copy-start
  0.6 0.0 copy-start.9
  0.7 1.7 %shard_map.123 = bf16[8,64,256]{2,1,0:T(8,128)(2,1)} custom-call(f32[4,64,256]{2,1,0:T(8,128)} %sky_hbm.1), custom_call_target="tpu_custom_call" | custom-call | tf_op jit(solution)/shard_map/pallas_call | solution.py:583
  2.4 6.4 %all-to-all-start = ((bf16[8,64,256]{2,1,0:T(8,128)(2,1)}), bf16[8,64,256]{2,1,0:T(8,128)(2,1)S(1)}, u32[]{:S(2)}, u32[]{:S(2)}) async-start(bf16[8,64,256]{2,1,0:T(8,128)(2,1)} %shard_map.123), calls=%async_computation | async-start | bytes 524288 | tf_op jit(solution)/shard_map/all_to_all | solution.py:596
  8.8 0.0 copy-done
  8.8 0.0 copy-done.9
  8.9 0.8 %shard_map.122.bands_ref = bf16[2560,256]{1,0:T(8,128)(2,1)S(1)} custom-call(f32[8,256]{1,0:T(8,128)S(1)} %pad.4.taps_ref), custom_call_target="tpu_custom_call" | custom-call | flops 1048576 | bytes 1048576 | tf_op jit(solution)/shard_map/pallas_call | solution.py:531
  9.7 0.0 copy-start.10
  9.7 0.1 pad_add_fusion.par_ref.where_ref
  9.8 5.1 %all-to-all-done.x_ref = bf16[8,64,256]{2,1,0:T(8,128)(2,1)S(1)} async-done(((bf16[8,64,256]{2,1,0:T(8,128)(2,1)}), bf16[8,64,256]{2,1,0:T(8,128)(2,1)S(1)}, u32[]{:S(2)}, u32[]{:S(2)}) %all-to-all-start) | async-done | bytes 262176 | tf_op jit(solution)/shard_map/all_to_all | solution.py:596
  14.9 1.8 %shard_map.125 = bf16[32,32,128]{2,1,0:T(8,128)(2,1)} custom-call(s32[4]{0:T(128)S(1)} %pad_add_fusion.par_ref.where_ref, bf16[8,64,256]{2,1,0:T(8,128)(2,1)S(1)} %all-to-all-done.x_ref, bf16[2,288,512]{2,1,0:T(8,128)(2,1)S(1)} %shard_map.124.line_ref), custom_call_target="tpu_custom_call" | custom-call | flops 536870912 | bytes 1048576 | tf_op jit(solution)/shard_map/pallas_call | solution.py:531
  16.7 12.3 %all-to-all-start.1 = ((bf16[32,32,128]{2,1,0:T(8,128)(2,1)}), bf16[32,32,128]{2,1,0:T(8,128)(2,1)S(1)}, u32[]{:S(2)}, u32[]{:S(2)}) async-start(bf16[32,32,128]{2,1,0:T(8,128)(2,1)} %shard_map.125), calls=%async_computation.1 | async-start | bytes 524288 | tf_op jit(solution)/shard_map/all_to_all | solution.py:617
  29.7 0.0 copy-done.10
  29.7 0.1 copy.13.count_ref
  29.8 0.0 copy-start.6
  29.8 1.3 %copy-done.6 = bf16[4,9,64,256]{3,2,1,0:T(8,128)(2,1)S(1)} copy-done((bf16[4,9,64,256]{3,2,1,0:T(8,128)(2,1)S(1)}, bf16[4,9,64,256]{3,2,1,0:T(8,128)(2,1)}, u32[]{:S(2)}) %copy-start.6) | copy-done | bytes 1179672
  31.0 0.0 copy-start.3
  31.0 0.0 copy-start.4
  31.0 0.0 copy-start.5
  31.0 2.4 %shard_map.126 = (f32[8,80,384]{2,1,0:T(8,128)S(1)}, bf16[8,16,384]{2,1,0:T(8,128)(2,1)S(1)}, bf16[8,16,384]{2,1,0:T(8,128)(2,1)S(1)}) custom-call(s32[4]{0:T(128)S(1)} %pad_add_fusion.par_ref.where_ref, s32[1]{0:T(128)S(6)} %copy.14.live_ref, bf16[4,9,64,256]{3,2,1,0:T(8,128)(2,1)S(1)} %copy-done.6, f32[4,64,256]{2,1,0:T(8,128)} %sky_hbm.1, ...), custom_call_target="tpu_custom_call" | custom-call | flops 2147483648 | bytes 4194304 | tf_op jit(solution)/shard_map/pallas_call | solution.py:623
  33.4 0.0 copy-start.1
  33.4 0.9 %copy-done.1 = f32[8,80,384]{2,1,0:T(8,128)} copy-done((f32[8,80,384]{2,1,0:T(8,128)}, f32[8,80,384]{2,1,0:T(8,128)S(1)}, u32[]{:S(2)}) %copy-start.1) | copy-done | bytes 983064
  34.4 0.0 copy-done.3
  34.4 0.0 copy-done.4
  34.4 0.0 copy-done.5
  34.4 0.8 %shard_map.127.e_ref = bf16[320,1536]{1,0:T(8,128)(2,1)S(1)} custom-call(s32[4]{0:T(128)S(1)} %pad_add_fusion.par_ref.where_ref, s32[4,1,6]{2,1,0:T(1,128)S(1)} %copy-done.5, s32[4,1]{1,0:T(4,128)S(1)} %copy.13.count_ref, bf16[4,1,6,64,64]{4,3,2,1,0:T(8,128)(2,1)S(1)} %copy-done.4, bf16[384,768]{1,0:T(8,128)(2,1)S(1)} %copy-done.3), custom_call_target="tpu_custom_call" | custom-call | flops 8388608 | bytes 1048576 | tf_op jit(solution)/shard_map/pallas_call | solution.py:531
  35.2 6.8 %all-to-all-done.1.d_ref = bf16[32,32,128]{2,1,0:T(8,128)(2,1)S(1)} async-done(((bf16[32,32,128]{2,1,0:T(8,128)(2,1)}), bf16[32,32,128]{2,1,0:T(8,128)(2,1)S(1)}, u32[]{:S(2)}, u32[]{:S(2)}) %all-to-all-start.1) | async-done | bytes 262176 | tf_op jit(solution)/shard_map/all_to_all | solution.py:617
  42.0 2.6 %shard_map.128 = bf16[32,40,128]{2,1,0:T(8,128)(2,1)} custom-call(bf16[32,32,128]{2,1,0:T(8,128)(2,1)S(1)} %all-to-all-done.1.d_ref, bf16[320,1536]{1,0:T(8,128)(2,1)S(1)} %shard_map.127.e_ref), custom_call_target="tpu_custom_call" | custom-call | flops 536870912 | bytes 1048576 | tf_op jit(solution)/shard_map/pallas_call | solution.py:531
  44.6 4.5 %all-to-all-start.2 = ((bf16[32,40,128]{2,1,0:T(8,128)(2,1)}), bf16[32,40,128]{2,1,0:T(8,128)(2,1)S(1)}, u32[]{:S(2)}, u32[]{:S(2)}) async-start(bf16[32,40,128]{2,1,0:T(8,128)(2,1)} %shard_map.128), calls=%async_computation.2 | async-start | bytes 655360 | tf_op jit(solution)/shard_map/all_to_all | solution.py:679
  49.1 0.0 copy-start.2
  49.1 3.7 %collective-permute-start = (bf16[8,16,384]{2,1,0:T(8,128)(2,1)S(1)}, bf16[8,16,384]{2,1,0:T(8,128)(2,1)S(1)}, u32[]{:S(2)}, u32[]{:S(2)}) collective-permute-start(bf16[8,16,384]{2,1,0:T(8,128)(2,1)S(1)} %get-tuple-element.22), channel_id=1, source_target_pairs={{0,8},{8,16},{16,24},{24,32},{32,40},{40,48},{48,56},{56,64},{64,7... | collective-permute-start | bytes 294920 | tf_op jit(solution)/shard_map/ppermute | solution.py:688
  52.8 1.9 %collective-permute-start.1 = (bf16[8,16,384]{2,1,0:T(8,128)(2,1)S(1)}, bf16[8,16,384]{2,1,0:T(8,128)(2,1)S(1)}, u32[]{:S(2)}, u32[]{:S(2)}) collective-permute-start(bf16[8,16,384]{2,1,0:T(8,128)(2,1)S(1)} %get-tuple-element.23), channel_id=1, source_target_pairs={{8,0},{16,8},{24,16},{32,24},{40,32},{48,40},{56,48},{64,56},{72,6... | collective-permute-start | bytes 294920 | tf_op jit(solution)/shard_map/ppermute | solution.py:689
  54.7 0.8 %shard_map.129.bands_ref = bf16[2560,256]{1,0:T(8,128)(2,1)S(1)} custom-call(f32[8,256]{1,0:T(8,128)S(1)} %pad.4.taps_ref), custom_call_target="tpu_custom_call" | custom-call | flops 1048576 | bytes 1048576 | tf_op jit(solution)/shard_map/pallas_call | solution.py:531
  55.6 0.0 collective-permute-done.before_ref
  55.6 4.5 %collective-permute-done.1.after_ref = bf16[8,16,384]{2,1,0:T(8,128)(2,1)S(1)} collective-permute-done((bf16[8,16,384]{2,1,0:T(8,128)(2,1)S(1)}, bf16[8,16,384]{2,1,0:T(8,128)(2,1)S(1)}, u32[]{:S(2)}, u32[]{:S(2)}) %collective-permute-start.1) | collective-permute-done | bytes 98336 | tf_op jit(solution)/shard_map/ppermute | solution.py:689
  60.1 0.0 copy-done.2
  60.1 0.3 shard_map.130.base_ref
  60.4 0.0 copy-start.8
  60.4 2.9 %all-to-all-done.2.t_ref = bf16[32,40,128]{2,1,0:T(8,128)(2,1)S(1)} async-done(((bf16[32,40,128]{2,1,0:T(8,128)(2,1)}), bf16[32,40,128]{2,1,0:T(8,128)(2,1)S(1)}, u32[]{:S(2)}, u32[]{:S(2)}) %all-to-all-start.2) | async-done | bytes 327712 | tf_op jit(solution)/shard_map/all_to_all | solution.py:679
  63.3 0.0 copy-start.7
  63.3 1.3 %shard_map.131 = bf16[8,80,384]{2,1,0:T(8,128)(2,1)S(1)} custom-call(s32[4]{0:T(128)S(1)} %pad_add_fusion.par_ref.where_ref, bf16[32,40,128]{2,1,0:T(8,128)(2,1)S(1)} %all-to-all-done.2.t_ref, bf16[2,288,512]{2,1,0:T(8,128)(2,1)S(1)} %copy-done, f32[8,80,384]{2,1,0:T(8,128)S(1)} %shard_map.130.base_ref), custom_call_target="tpu_custom_call" | custom-call | flops 536870912 | bytes 1048576 | tf_op jit(solution)/shard_map/pallas_call | solution.py:531
  64.6 11.8 %all_to_all.20.half_ref = bf16[8,80,384]{2,1,0:T(8,128)(2,1)S(1)} all-to-all(bf16[8,80,384]{2,1,0:T(8,128)(2,1)S(1)} %shard_map.131), channel_id=1, replica_groups=mesh['img'=32,'fou'=8] {'fou'}, dimensions={0} | all-to-all | bytes 983040 | tf_op jit(solution)/shard_map/all_to_all | solution.py:712
  76.4 0.0 copy-done.8
  76.4 0.0 copy-done.7
  76.4 3.4 %shard_map.132 = (f32[4,64,256]{2,1,0:T(8,128)}, bf16[4,9,64,256]{3,2,1,0:T(8,128)(2,1)}) custom-call(f32[9]{0:T(128)S(1)} %copy-done.8, s32[4]{0:T(128)S(1)} %pad_add_fusion.par_ref.where_ref, bf16[8,80,384]{2,1,0:T(8,128)(2,1)S(1)} %all_to_all.20.half_ref, f32[8,80,384]{2,1,0:T(8,128)S(1)} %shard_map.130.base_ref, bf16[4,9,64,256]{3,2,1,0:T(8,128)(2,1)S(1)} %copy-done.7, ...), custom_call_target="tpu_custom_call" | custom-call | flops 2147483648 | bytes 3145728 | tf_op jit(solution)/shard_map/pallas_call | solution.py:545
  (2 shorter events, 0.0 us)
Async XLA Ops:
  0.6 8.1 %copy-start = (bf16[2,288,512]{2,1,0:T(8,128)(2,1)S(1)}, bf16[2,288,512]{2,1,0:T(8,128)(2,1)}, u32[]{:S(2)}) copy-start(bf16[2,288,512]{2,1,0:T(8,128)(2,1)} %constant.18.clone.table_ref.line_ref) | copy-start | bytes 1769476
  0.6 8.2 %copy-start.9 = (f32[8,17]{1,0:T(8,128)S(1)}, f32[8,17]{1,0:T(8,128)}, u32[]{:S(2)}) copy-start(f32[8,17]{1,0:T(8,128)} %param.14) | copy-start | bytes 1636
  2.4 12.5 %all-to-all-start = ((bf16[8,64,256]{2,1,0:T(8,128)(2,1)}), bf16[8,64,256]{2,1,0:T(8,128)(2,1)S(1)}, u32[]{:S(2)}, u32[]{:S(2)}) async-start(bf16[8,64,256]{2,1,0:T(8,128)(2,1)} %shard_map.123), calls=%async_computation | async-start | bytes 524288 | tf_op jit(solution)/shard_map/all_to_all | solution.py:596
  9.7 20.0 %copy-start.10 = (s32[4,1]{0,1:T(1,128)S(1)}, s32[4,1]{0,1:T(1,128)}, u32[]{:S(2)}) copy-start(s32[4,1]{0,1:T(1,128)} %param.18) | copy-start | bytes 52
  16.7 25.3 %all-to-all-start.1 = ((bf16[32,32,128]{2,1,0:T(8,128)(2,1)}), bf16[32,32,128]{2,1,0:T(8,128)(2,1)S(1)}, u32[]{:S(2)}, u32[]{:S(2)}) async-start(bf16[32,32,128]{2,1,0:T(8,128)(2,1)} %shard_map.125), calls=%async_computation.1 | async-start | bytes 524288 | tf_op jit(solution)/shard_map/all_to_all | solution.py:617
  29.8 1.3 %copy-start.6 = (bf16[4,9,64,256]{3,2,1,0:T(8,128)(2,1)S(1)}, bf16[4,9,64,256]{3,2,1,0:T(8,128)(2,1)}, u32[]{:S(2)}) copy-start(bf16[4,9,64,256]{3,2,1,0:T(8,128)(2,1)} %dual_ref.3) | copy-start | bytes 3538948
  31.0 3.3 %copy-start.3 = (bf16[384,768]{1,0:T(8,128)(2,1)S(1)}, bf16[384,768]{1,0:T(8,128)(2,1)}, u32[]{:S(2)}) copy-start(bf16[384,768]{1,0:T(8,128)(2,1)} %constant.19.clone.table_ref) | copy-start | bytes 1769476
  31.0 3.3 %copy-start.4 = (bf16[4,1,6,64,64]{4,3,2,1,0:T(8,128)(2,1)S(1)}, bf16[4,1,6,64,64]{4,3,2,1,0:T(8,128)(2,1)}, u32[]{:S(2)}) copy-start(bf16[4,1,6,64,64]{4,3,2,1,0:T(8,128)(2,1)} %tiles_ref.1) | copy-start | bytes 589828
  31.0 3.3 %copy-start.5 = (s32[4,1,6]{2,1,0:T(1,128)S(1)}, s32[4,1,6]{2,1,0:T(1,128)}, u32[]{:S(2)}) copy-start(s32[4,1,6]{2,1,0:T(1,128)} %slots_ref.1) | copy-start | bytes 292
  33.4 0.9 %copy-start.1 = (f32[8,80,384]{2,1,0:T(8,128)}, f32[8,80,384]{2,1,0:T(8,128)S(1)}, u32[]{:S(2)}) copy-start(f32[8,80,384]{2,1,0:T(8,128)S(1)} %get-tuple-element.20.base_ref) | copy-start | bytes 2949124
  44.6 18.7 %all-to-all-start.2 = ((bf16[32,40,128]{2,1,0:T(8,128)(2,1)}), bf16[32,40,128]{2,1,0:T(8,128)(2,1)S(1)}, u32[]{:S(2)}, u32[]{:S(2)}) async-start(bf16[32,40,128]{2,1,0:T(8,128)(2,1)} %shard_map.128), calls=%async_computation.2 | async-start | bytes 655360 | tf_op jit(solution)/shard_map/all_to_all | solution.py:679
  49.1 11.0 %copy-start.2 = (f32[8,80,384]{2,1,0:T(8,128)S(1)}, f32[8,80,384]{2,1,0:T(8,128)}, u32[]{:S(2)}) copy-start(f32[8,80,384]{2,1,0:T(8,128)} %copy-done.1) | copy-start | bytes 2949124
  49.1 6.5 %collective-permute-start = (bf16[8,16,384]{2,1,0:T(8,128)(2,1)S(1)}, bf16[8,16,384]{2,1,0:T(8,128)(2,1)S(1)}, u32[]{:S(2)}, u32[]{:S(2)}) collective-permute-start(bf16[8,16,384]{2,1,0:T(8,128)(2,1)S(1)} %get-tuple-element.22), channel_id=1, source_target_pairs={{0,8},{8,16},{16,24},{24,32},{32,40},{40,48},{48,56},{56,64},{64,7... | collective-permute-start | bytes 294920 | tf_op jit(solution)/shard_map/ppermute | solution.py:688
  52.8 7.3 %collective-permute-start.1 = (bf16[8,16,384]{2,1,0:T(8,128)(2,1)S(1)}, bf16[8,16,384]{2,1,0:T(8,128)(2,1)S(1)}, u32[]{:S(2)}, u32[]{:S(2)}) collective-permute-start(bf16[8,16,384]{2,1,0:T(8,128)(2,1)S(1)} %get-tuple-element.23), channel_id=1, source_target_pairs={{8,0},{16,8},{24,16},{32,24},{40,32},{48,40},{56,48},{64,56},{72,6... | collective-permute-start | bytes 294920 | tf_op jit(solution)/shard_map/ppermute | solution.py:689
  60.4 16.0 %copy-start.8 = (f32[9]{0:T(128)S(1)}, f32[9]{0:T(128)}, u32[]{:S(2)}) copy-start(f32[9]{0:T(128)} %bound_ref.1) | copy-start | bytes 112
  63.3 13.1 %copy-start.7 = (bf16[4,9,64,256]{3,2,1,0:T(8,128)(2,1)S(1)}, bf16[4,9,64,256]{3,2,1,0:T(8,128)(2,1)}, u32[]{:S(2)}) copy-start(bf16[4,9,64,256]{3,2,1,0:T(8,128)(2,1)} %dual_ref.3) | copy-start | bytes 3538948

commit v9 on v8

--- a/solution.py
+++ b/solution.py
@@ -251,8 +251,15 @@
                     o_ref[rows, to : to + 128] = row[:, at : at + 128]
 
 
-def gram_kernel(d_ref, e_ref, o_ref, rows, rhs, mid, edge, out, sem):
-    rows[0:1024, :] = d_ref[...].reshape(1024, 128).astype(F32)
+def gram_kernel(d_hbm, e_ref, o_ref, taken, rows, rhs, mid, edge, out, in_sem, sem):
+    fetch = [
+        pltpu.make_async_copy(d_hbm.at[pl.ds(n * 8, 8)], taken.at[n], in_sem.at[n]) for n in range(4)
+    ]
+    for move in fetch:
+        move.start()
+    for n in range(4):
+        fetch[n].wait()
+        rows[n * 256 : n * 256 + 256, :] = taken[n].reshape(256, 128).astype(F32)
     for p in range(16):
         lanes = slice(p * 128, p * 128 + 128)
         at = (p % 2) * 8 + p // 2
@@ -527,11 +534,11 @@
 HB = pl.BlockSpec(memory_space=pltpu.HBM)
 
 
-def call(kernel, out_shape, scratch, flops, moved, *args, scalars=0, result=VM):
+def call(kernel, out_shape, scratch, flops, moved, *args, scalars=0, sources=0, result=VM):
     return pl.pallas_call(
         kernel,
         out_shape=out_shape,
-        in_specs=[SM] * scalars + [VM] * (len(args) - scalars),
+        in_specs=[SM] * scalars + [HB] * sources + [VM] * (len(args) - scalars - sources),
         out_specs=jax.tree.map(lambda _: result, out_shape),
         scratch_shapes=scratch,
         compiler_params=pltpu.CompilerParams(vmem_limit_bytes=VMEM_LIMIT),
@@ -656,14 +663,18 @@
         sampled_table(),
         scalars=3,
     )
-    (received,) = after((received,), head)
+    steps = [(i, i + 1) for i in range(PEERS_IMG - 1)]
+    from_after = lax.ppermute(head, "img", [(j, i) for i, j in steps])
+    (received,) = after((received,), from_after)
 
     scratch = [
+        pltpu.VMEM((4, 8, 32, 128), BF),
         pltpu.VMEM((1280, 128), F32),
         pltpu.VMEM((64, 2048), BF),
         pltpu.VMEM((256, 1024), BF),
         pltpu.VMEM((64, 1024), BF),
         pltpu.VMEM((2, 16, 40, 128), BF),
+        pltpu.SemaphoreType.DMA((4,)),
         pltpu.SemaphoreType.DMA((2,)),
     ]
     weighted = call(
@@ -672,9 +683,10 @@
         scratch,
         1 << 29,
         1 << 20,
-        received,
+        pltpu.with_memory_space_constraint(received, pltpu.HBM),
         spread,
         result=HB,
+        sources=1,
     )
     returned = lax.all_to_all(weighted, "img", split_axis=0, concat_axis=0, tiled=True)
 
@@ -683,10 +695,8 @@
         bands_kernel, jax.ShapeDtypeStruct((2560, 256), BF), [], 1 << 20, 1 << 20, late_taps
     )
     (last_where,) = after((where,), late_bands)
-    head, tail = after((head, tail), weighted)
-    steps = [(i, i + 1) for i in range(PEERS_IMG - 1)]
+    (tail,) = after((tail,), weighted)
     from_before = lax.ppermute(tail, "img", steps)
-    from_after = lax.ppermute(head, "img", [(j, i) for i, j in steps])
     base = call(
         edge_kernel,
         extended,

time: 80.3 us -> 88.9 us (1.11)
  starting transfers between devices: 28.7 us -> 37.5 us
  waiting for transfers between devices: 19.3 us -> 16.4 us
  local copies, waits for them, and re-layouts: 2.35 us -> 3.98 us
  Pallas kernels: 16 us -> 17.6 us
    all_to_all x1, starting transfers between devices: 4.5 us -> 12.9 us  [body(): lax.all_to_all(weighted, 'img', split_axis=0, concat_axis=0, tiled=True)]
    all_to_all x1, waiting for transfers between devices: 6.8 us -> 0.37 us  [body(): lax.all_to_all(packed, 'img', split_axis=0, concat_axis=0, tiled=True)]
    all_to_all x1, waiting for transfers between devices: 2.87 us -> 8.19 us  [body(): lax.all_to_all(weighted, 'img', split_axis=0, concat_axis=0, tiled=True)]
    ppermute x1, waiting for transfers between devices: 4.55 us -> 2.02 us  [body(): from_after = lax.ppermute(head, 'img', [(j, i) for i, j in steps])]
    unnamed x23 -> x31, local copies, waits for them, and re-layouts: 2.35 us -> 3.98 us
    pallas_call x8, Pallas kernels: 8.55 us -> 9.48 us  [call(): pl.pallas_call(kernel, out_shape=out_shape, in_specs=[SM] * scalars + [HB...]
  transfers between devices with their start and end apart: 5 -> 5, of which waited for: 4 -> 5; matrix products, arithmetic and copies ran while one was open for 0% -> 0% of each run, Pallas kernels for 7% -> 7%
where the time goes in v9:
time: 88.9 us; the launch traced here: 88.3 us
  starting transfers between devices  37.5 us (42%)
  Pallas kernels  17.6 us (20%)
  waiting for transfers between devices  16.4 us (18%)
  blocking collectives  11.2 us (13%)
  local copies, waits for them, and re-layouts  3.98 us (4%)
  between operations  1.51 us (2%)
    all_to_all x1, starting transfers between devices, body(): lax.all_to_all(weighted, 'img', split_axis=0, concat_axis=0, tiled=True)  12.9 us
    all_to_all x1, starting transfers between devices, body(): lax.all_to_all(packed, 'img', split_axis=0, concat_axis=0, tiled=True)  12.3 us
    all_to_all x1, blocking collectives, body(): lax.all_to_all(blocks, 'fou', split_axis=0, concat_axis=0, tiled=True)  11.2 us
    pallas_call x8, Pallas kernels, call(): pl.pallas_call(kernel, out_shape=out_shape, in_specs=[SM] * scalars + [HB...  9.48 us
    all_to_all x1, waiting for transfers between devices, body(): lax.all_to_all(weighted, 'img', split_axis=0, concat_axis=0, tiled=True)  8.19 us
    all_to_all x1, starting transfers between devices, body(): lines = lax.all_to_all(sent, 'fou', split_axis=0, concat_axis=0, tiled=True)  6.39 us
    all_to_all x1, waiting for transfers between devices, body(): lines = lax.all_to_all(sent, 'fou', split_axis=0, concat_axis=0, tiled=True)  5.09 us
    unnamed x31, local copies, waits for them, and re-layouts  3.98 us
  transfers between devices with their start and end apart: 5, of which 5 were waited for; matrix products, arithmetic and copies ran while one was open for 0% of the time, Pallas kernels for 7%

profile of v9, /device:TPU:1, one launch (start us, length us, event | category | flops | bytes accessed | tf_op | source)
XLA Modules:
  0.0 88.3 jit_solution(10659787888617659200)
XLA Ops:
  0.6 0.0 copy-start
  0.6 0.0 copy-start.13
  0.7 1.7 %shard_map.123 = bf16[8,64,256]{2,1,0:T(8,128)(2,1)} custom-call(f32[4,64,256]{2,1,0:T(8,128)} %sky_hbm.1), custom_call_target="tpu_custom_call" | custom-call | tf_op jit(solution)/shard_map/pallas_call | solution.py:590
  2.4 6.4 %all-to-all-start = ((bf16[8,64,256]{2,1,0:T(8,128)(2,1)}), bf16[8,64,256]{2,1,0:T(8,128)(2,1)S(1)}, u32[]{:S(2)}, u32[]{:S(2)}) async-start(bf16[8,64,256]{2,1,0:T(8,128)(2,1)} %shard_map.123), calls=%async_computation | async-start | bytes 524288 | tf_op jit(solution)/shard_map/all_to_all | solution.py:603
  8.8 0.0 copy-done
  8.8 0.0 copy-done.13
  8.9 0.8 shard_map.122.bands_ref
  9.7 0.1 pad_add_fusion.par_ref.where_ref
  9.8 5.1 %all-to-all-done.x_ref = bf16[8,64,256]{2,1,0:T(8,128)(2,1)S(1)} async-done(((bf16[8,64,256]{2,1,0:T(8,128)(2,1)}), bf16[8,64,256]{2,1,0:T(8,128)(2,1)S(1)}, u32[]{:S(2)}, u32[]{:S(2)}) %all-to-all-start) | async-done | bytes 262176 | tf_op jit(solution)/shard_map/all_to_all | solution.py:603
  14.9 1.8 %shard_map.125 = bf16[32,32,128]{2,1,0:T(8,128)(2,1)} custom-call(s32[4]{0:T(128)S(1)} %pad_add_fusion.par_ref.where_ref, bf16[8,64,256]{2,1,0:T(8,128)(2,1)S(1)} %all-to-all-done.x_ref, bf16[2,288,512]{2,1,0:T(8,128)(2,1)S(1)} %shard_map.124.line_ref), custom_call_target="tpu_custom_call" | custom-call | flops 536870912 | bytes 1048576 | tf_op jit(solution)/shard_map/pallas_call | solution.py:538
  16.7 12.3 %all-to-all-start.1 = ((bf16[32,32,128]{2,1,0:T(8,128)(2,1)}), bf16[32,32,128]{2,1,0:T(8,128)(2,1)}, u32[]{:S(2)}, u32[]{:S(2)}) async-start(bf16[32,32,128]{2,1,0:T(8,128)(2,1)} %shard_map.125), calls=%async_computation.1 | async-start | bytes 524288 | tf_op jit(solution)/shard_map/all_to_all | solution.py:624
  29.7 0.0 copy-start.8
  29.7 1.3 %copy-done.8 = bf16[4,9,64,256]{3,2,1,0:T(8,128)(2,1)S(1)} copy-done((bf16[4,9,64,256]{3,2,1,0:T(8,128)(2,1)S(1)}, bf16[4,9,64,256]{3,2,1,0:T(8,128)(2,1)}, u32[]{:S(2)}) %copy-start.8) | copy-done | bytes 1179672
  31.0 0.0 copy-start.14
  31.0 0.0 copy-start.3
  31.0 3.0 %shard_map.126 = (f32[8,80,384]{2,1,0:T(8,128)S(1)}, bf16[8,16,384]{2,1,0:T(8,128)(2,1)}, bf16[8,16,384]{2,1,0:T(8,128)(2,1)S(1)}) custom-call(s32[4]{0:T(128)S(1)} %pad_add_fusion.par_ref.where_ref, s32[1]{0:T(128)S(6)} %copy.14.live_ref, bf16[4,9,64,256]{3,2,1,0:T(8,128)(2,1)S(1)} %copy-done.8, f32[4,64,256]{2,1,0:T(8,128)} %sky_hbm.1, ...), custom_call_target="tpu_custom_call" | custom-call | flops 2147483648 | bytes 4194304 | tf_op jit(solution)/shard_map/pallas_call | solution.py:630
  34.0 0.0 copy-start.1
  34.0 0.9 %copy-done.1 = f32[8,80,384]{2,1,0:T(8,128)} copy-done((f32[8,80,384]{2,1,0:T(8,128)}, f32[8,80,384]{2,1,0:T(8,128)S(1)}, u32[]{:S(2)}) %copy-start.1) | copy-done | bytes 983064
  34.9 0.6 copy-done.10
  35.6 2.2 %collective-permute-start = (bf16[8,16,384]{2,1,0:T(8,128)(2,1)}, bf16[8,16,384]{2,1,0:T(8,128)(2,1)S(1)}, u32[]{:S(2)}, u32[]{:S(2)}) collective-permute-start(bf16[8,16,384]{2,1,0:T(8,128)(2,1)} %get-tuple-element.14), channel_id=1, source_target_pairs={{8,0},{16,8},{24,16},{32,24},{40,32},{48,40},{56,48},{64,56},{72,6... | collective-permute-start | bytes 294920 | tf_op jit(solution)/shard_map/ppermute | solution.py:667
  37.8 0.0 copy-done.14
  37.8 0.1 copy.13.count_ref
  37.9 0.0 copy-done.3
  37.9 0.0 copy-done.7
  37.9 1.0 %copy-done.4 = bf16[4,1,6,64,64]{4,3,2,1,0:T(8,128)(2,1)S(1)} copy-done((bf16[4,1,6,64,64]{4,3,2,1,0:T(8,128)(2,1)S(1)}, bf16[4,1,6,64,64]{4,3,2,1,0:T(8,128)(2,1)}, u32[]{:S(2)}) %copy-start.4) | copy-done | bytes 196632
  38.9 0.8 shard_map.127.e_ref
  39.7 0.0 copy-start.11
  39.7 2.0 %collective-permute-done.after_ref = bf16[8,16,384]{2,1,0:T(8,128)(2,1)S(1)} collective-permute-done((bf16[8,16,384]{2,1,0:T(8,128)(2,1)}, bf16[8,16,384]{2,1,0:T(8,128)(2,1)S(1)}, u32[]{:S(2)}, u32[]{:S(2)}) %collective-permute-start) | collective-permute-done | bytes 98336 | tf_op jit(solution)/shard_map/ppermute | solution.py:667
  41.8 0.4 all-to-all-done.1.d_hbm
  42.1 3.5 %shard_map.128 = bf16[32,40,128]{2,1,0:T(8,128)(2,1)} custom-call(bf16[32,32,128]{2,1,0:T(8,128)(2,1)} %all-to-all-done.1.d_hbm, bf16[320,1536]{1,0:T(8,128)(2,1)S(1)} %shard_map.127.e_ref), custom_call_target="tpu_custom_call" | custom-call | flops 536870912 | bytes 1048576 | tf_op jit(solution)/shard_map/pallas_call | solution.py:538
  45.6 0.0 copy-done.5
  45.6 12.9 %all-to-all-start.2 = ((bf16[32,40,128]{2,1,0:T(8,128)(2,1)}), bf16[32,40,128]{2,1,0:T(8,128)(2,1)S(1)}, u32[]{:S(2)}, u32[]{:S(2)}) async-start(bf16[32,40,128]{2,1,0:T(8,128)(2,1)} %shard_map.128), calls=%async_computation.2 | async-start | bytes 655360 | tf_op jit(solution)/shard_map/all_to_all | solution.py:691
  58.6 0.0 copy-start.2
  58.6 0.0 copy-start.6
  58.6 0.0 copy-done.11
  58.6 3.7 %collective-permute-start.1 = (bf16[8,16,384]{2,1,0:T(8,128)(2,1)S(1)}, bf16[8,16,384]{2,1,0:T(8,128)(2,1)S(1)}, u32[]{:S(2)}, u32[]{:S(2)}) collective-permute-start(bf16[8,16,384]{2,1,0:T(8,128)(2,1)S(1)} %copy-done.11), channel_id=1, source_target_pairs={{0,8},{8,16},{16,24},{24,32},{32,40},{40,48},{48,56},{56,64},{64,7... | collective-permute-start | bytes 294920 | tf_op jit(solution)/shard_map/ppermute | solution.py:699
  62.3 0.8 shard_map.129.bands_ref
  63.1 0.8 collective-permute-done.1.before_ref
  63.9 0.0 copy-done.2
  63.9 0.0 copy-done.6
  63.9 0.3 shard_map.130.base_ref
  64.2 0.0 copy-start.12
  64.2 8.2 %all-to-all-done.2.t_ref = bf16[32,40,128]{2,1,0:T(8,128)(2,1)S(1)} async-done(((bf16[32,40,128]{2,1,0:T(8,128)(2,1)}), bf16[32,40,128]{2,1,0:T(8,128)(2,1)S(1)}, u32[]{:S(2)}, u32[]{:S(2)}) %all-to-all-start.2) | async-done | bytes 327712 | tf_op jit(solution)/shard_map/all_to_all | solution.py:691
  72.4 1.3 %shard_map.131 = bf16[8,80,384]{2,1,0:T(8,128)(2,1)S(1)} custom-call(s32[4]{0:T(128)S(1)} %pad_add_fusion.par_ref.where_ref, bf16[32,40,128]{2,1,0:T(8,128)(2,1)S(1)} %all-to-all-done.2.t_ref, bf16[2,288,512]{2,1,0:T(8,128)(2,1)S(1)} %copy-done, f32[8,80,384]{2,1,0:T(8,128)S(1)} %shard_map.130.base_ref), custom_call_target="tpu_custom_call" | custom-call | flops 536870912 | bytes 1048576 | tf_op jit(solution)/shard_map/pallas_call | solution.py:538
  73.7 11.2 %all_to_all.20.half_ref = bf16[8,80,384]{2,1,0:T(8,128)(2,1)S(1)} all-to-all(bf16[8,80,384]{2,1,0:T(8,128)(2,1)S(1)} %shard_map.131), channel_id=1, replica_groups=mesh['img'=32,'fou'=8] {'fou'}, dimensions={0} | all-to-all | bytes 983040 | tf_op jit(solution)/shard_map/all_to_all | solution.py:722
  84.9 0.0 copy-done.12
  84.9 0.0 copy-done.9
  84.9 3.4 %shard_map.132 = (f32[4,64,256]{2,1,0:T(8,128)}, bf16[4,9,64,256]{3,2,1,0:T(8,128)(2,1)}) custom-call(f32[9]{0:T(128)S(1)} %copy-done.12, s32[4]{0:T(128)S(1)} %pad_add_fusion.par_ref.where_ref, bf16[8,80,384]{2,1,0:T(8,128)(2,1)S(1)} %all_to_all.20.half_ref, f32[8,80,384]{2,1,0:T(8,128)S(1)} %shard_map.130.base_ref, bf16[4,9,64,256]{3,2,1,0:T(8,128)(2,1)S(1)} %copy-done.9, ...), custom_call_target="tpu_custom_call" | custom-call | flops 2147483648 | bytes 3145728 | tf_op jit(solution)/shard_map/pallas_call | solution.py:552
  (7 shorter events, 0.1 us)
Async XLA Ops:
  0.6 8.1 %copy-start = (bf16[2,288,512]{2,1,0:T(8,128)(2,1)S(1)}, bf16[2,288,512]{2,1,0:T(8,128)(2,1)}, u32[]{:S(2)}) copy-start(bf16[2,288,512]{2,1,0:T(8,128)(2,1)} %constant.18.clone.table_ref.line_ref) | copy-start | bytes 1769476
  0.6 8.2 %copy-start.13 = (f32[8,17]{1,0:T(8,128)S(1)}, f32[8,17]{1,0:T(8,128)}, u32[]{:S(2)}) copy-start(f32[8,17]{1,0:T(8,128)} %param.14) | copy-start | bytes 1636
  2.4 12.5 %all-to-all-start = ((bf16[8,64,256]{2,1,0:T(8,128)(2,1)}), bf16[8,64,256]{2,1,0:T(8,128)(2,1)S(1)}, u32[]{:S(2)}, u32[]{:S(2)}) async-start(bf16[8,64,256]{2,1,0:T(8,128)(2,1)} %shard_map.123), calls=%async_computation | async-start | bytes 524288 | tf_op jit(solution)/shard_map/all_to_all | solution.py:603
  16.7 25.4 %all-to-all-start.1 = ((bf16[32,32,128]{2,1,0:T(8,128)(2,1)}), bf16[32,32,128]{2,1,0:T(8,128)(2,1)}, u32[]{:S(2)}, u32[]{:S(2)}) async-start(bf16[32,32,128]{2,1,0:T(8,128)(2,1)} %shard_map.125), calls=%async_computation.1 | async-start | bytes 524288 | tf_op jit(solution)/shard_map/all_to_all | solution.py:624
  29.7 1.3 %copy-start.8 = (bf16[4,9,64,256]{3,2,1,0:T(8,128)(2,1)S(1)}, bf16[4,9,64,256]{3,2,1,0:T(8,128)(2,1)}, u32[]{:S(2)}) copy-start(bf16[4,9,64,256]{3,2,1,0:T(8,128)(2,1)} %dual_ref.3) | copy-start | bytes 3538948
  31.0 6.8 %copy-start.14 = (s32[4,1]{0,1:T(1,128)S(1)}, s32[4,1]{0,1:T(1,128)}, u32[]{:S(2)}) copy-start(s32[4,1]{0,1:T(1,128)} %param.18) | copy-start | bytes 52
  31.0 6.9 %copy-start.3 = (bf16[384,768]{1,0:T(8,128)(2,1)S(1)}, bf16[384,768]{1,0:T(8,128)(2,1)}, u32[]{:S(2)}) copy-start(bf16[384,768]{1,0:T(8,128)(2,1)} %constant.19.clone.table_ref) | copy-start | bytes 1769476
  31.0 6.9 %copy-start.7 = (s32[4,1,6]{2,1,0:T(1,128)S(1)}, s32[4,1,6]{2,1,0:T(1,128)}, u32[]{:S(2)}) copy-start(s32[4,1,6]{2,1,0:T(1,128)} %slots_ref.1) | copy-start | bytes 292
  34.0 0.9 %copy-start.1 = (f32[8,80,384]{2,1,0:T(8,128)}, f32[8,80,384]{2,1,0:T(8,128)S(1)}, u32[]{:S(2)}) copy-start(f32[8,80,384]{2,1,0:T(8,128)S(1)} %get-tuple-element.19.base_ref) | copy-start | bytes 2949124
  34.9 0.6 copy-start.10
  35.6 6.2 %collective-permute-start = (bf16[8,16,384]{2,1,0:T(8,128)(2,1)}, bf16[8,16,384]{2,1,0:T(8,128)(2,1)S(1)}, u32[]{:S(2)}, u32[]{:S(2)}) collective-permute-start(bf16[8,16,384]{2,1,0:T(8,128)(2,1)} %get-tuple-element.14), channel_id=1, source_target_pairs={{8,0},{16,8},{24,16},{32,24},{40,32},{48,40},{56,48},{64,56},{72,6... | collective-permute-start | bytes 294920 | tf_op jit(solution)/shard_map/ppermute | solution.py:667
  37.9 1.0 %copy-start.4 = (bf16[4,1,6,64,64]{4,3,2,1,0:T(8,128)(2,1)S(1)}, bf16[4,1,6,64,64]{4,3,2,1,0:T(8,128)(2,1)}, u32[]{:S(2)}) copy-start(bf16[4,1,6,64,64]{4,3,2,1,0:T(8,128)(2,1)} %tiles_ref.1) | copy-start | bytes 589828
  39.7 18.9 %copy-start.11 = (bf16[8,16,384]{2,1,0:T(8,128)(2,1)S(1)}, bf16[8,16,384]{2,1,0:T(8,128)(2,1)}, u32[]{:S(2)}) copy-start(bf16[8,16,384]{2,1,0:T(8,128)(2,1)} %copy-done.10) | copy-start | bytes 294916
  41.8 3.9 %copy-start.5 = (bf16[8,16,384]{2,1,0:T(8,128)(2,1)}, bf16[8,16,384]{2,1,0:T(8,128)(2,1)S(1)}, u32[]{:S(2)}) copy-start(bf16[8,16,384]{2,1,0:T(8,128)(2,1)S(1)} %collective-permute-done.after_ref) | copy-start | bytes 294916
  45.6 26.7 %all-to-all-start.2 = ((bf16[32,40,128]{2,1,0:T(8,128)(2,1)}), bf16[32,40,128]{2,1,0:T(8,128)(2,1)S(1)}, u32[]{:S(2)}, u32[]{:S(2)}) async-start(bf16[32,40,128]{2,1,0:T(8,128)(2,1)} %shard_map.128), calls=%async_computation.2 | async-start | bytes 655360 | tf_op jit(solution)/shard_map/all_to_all | solution.py:691
  58.6 5.3 %copy-start.2 = (f32[8,80,384]{2,1,0:T(8,128)S(1)}, f32[8,80,384]{2,1,0:T(8,128)}, u32[]{:S(2)}) copy-start(f32[8,80,384]{2,1,0:T(8,128)} %copy-done.1) | copy-start | bytes 2949124
  58.6 5.3 %copy-start.6 = (bf16[8,16,384]{2,1,0:T(8,128)(2,1)S(1)}, bf16[8,16,384]{2,1,0:T(8,128)(2,1)}, u32[]{:S(2)}) copy-start(bf16[8,16,384]{2,1,0:T(8,128)(2,1)} %copy-done.5) | copy-start | bytes 294916
  58.6 5.3 %collective-permute-start.1 = (bf16[8,16,384]{2,1,0:T(8,128)(2,1)S(1)}, bf16[8,16,384]{2,1,0:T(8,128)(2,1)S(1)}, u32[]{:S(2)}, u32[]{:S(2)}) collective-permute-start(bf16[8,16,384]{2,1,0:T(8,128)(2,1)S(1)} %copy-done.11), channel_id=1, source_target_pairs={{0,8},{8,16},{16,24},{24,32},{32,40},{40,48},{48,56},{56,64},{64,7... | collective-permute-start | bytes 294920 | tf_op jit(solution)/shard_map/ppermute | solution.py:699
  64.2 20.7 %copy-start.12 = (f32[9]{0:T(128)S(1)}, f32[9]{0:T(128)}, u32[]{:S(2)}) copy-start(f32[9]{0:T(128)} %bound_ref.1) | copy-start | bytes 112
  72.4 12.5 %copy-start.9 = (bf16[4,9,64,256]{3,2,1,0:T(8,128)(2,1)S(1)}, bf16[4,9,64,256]{3,2,1,0:T(8,128)(2,1)}, u32[]{:S(2)}) copy-start(bf16[4,9,64,256]{3,2,1,0:T(8,128)(2,1)} %dual_ref.3) | copy-start | bytes 3538948

commit v10 on v8

--- a/solution.py
+++ b/solution.py
@@ -162,18 +162,21 @@
             yi = yi + xe[f] * sin[f : f + 1]
         rows[0].append(jnp.concatenate([yr, -yi], axis=1).astype(BF))
         rows[1].append(jnp.concatenate([-yi, -yr], axis=1).astype(BF))
-    def leave(part):
-        to = o_ref.at[:, pl.ds(part * 16, 16), :]
-        return pltpu.make_async_copy(out.at[part], to, sem.at[part])
-
+    def leave(n):
+        return pltpu.make_async_copy(out.at[n], o_ref.at[pl.ds(n * 8, 8)], sem.at[n])
+
+    parts = []
     for part in range(2):
         r = jnp.concatenate(rows[part], axis=0)
         wave = dot(line_ref[0, 0:256], r, LAST) + dot(line_ref[1, 0:256], r, LAST)
         both = [wave[:, chi * 128 : chi * 128 + 128].reshape(32, 8, 128) for chi in range(2)]
-        out[part] = jnp.concatenate(both, axis=1).astype(BF)
-        leave(part).start()
-    for part in range(2):
-        leave(part).wait()
+        parts.append(jnp.concatenate(both, axis=1))
+    for n in range(4):
+        piece = [part[n * 8 : n * 8 + 8] for part in parts]
+        out[n] = jnp.concatenate(piece, axis=1).astype(BF)
+        leave(n).start()
+    for n in range(4):
+        leave(n).wait()
 
 
 def inverse_kernel(par_ref, t_ref, line_ref, base_ref, o_ref):
@@ -605,7 +608,7 @@
     packed = call(
         forward_kernel,
         jax.ShapeDtypeStruct((PEERS_IMG, 32, 128), BF),
-        [pltpu.VMEM((2, PEERS_IMG, 16, 128), BF), pltpu.SemaphoreType.DMA((2,))],
+        [pltpu.VMEM((4, 8, 32, 128), BF), pltpu.SemaphoreType.DMA((4,))],
         1 << 29,
         1 << 20,
         ready_where,
@@ -683,7 +686,7 @@
         bands_kernel, jax.ShapeDtypeStruct((2560, 256), BF), [], 1 << 20, 1 << 20, late_taps
     )
     (last_where,) = after((where,), late_bands)
-    head, tail = after((head, tail), weighted)
+    (tail,) = after((tail,), weighted)
     steps = [(i, i + 1) for i in range(PEERS_IMG - 1)]
     from_before = lax.ppermute(tail, "img", steps)
     from_after = lax.ppermute(head, "img", [(j, i) for i, j in steps])

time: 80.3 us -> 80.3 us (level)
    ppermute x1, waiting for transfers between devices: 4.55 us -> 0.03 us  [body(): from_after = lax.ppermute(head, 'img', [(j, i) for i, j in steps])]
    all_to_all x1, waiting for transfers between devices: 2.87 us -> 6 us  [body(): lax.all_to_all(weighted, 'img', split_axis=0, concat_axis=0, tiled=True)]
    ppermute x1, waiting for transfers between devices: 0.01 us -> 1.31 us  [body(): from_before = lax.ppermute(tail, 'img', steps)]
where the time goes in v10:
time: 80.3 us; the launch traced here: 79.8 us
  starting transfers between devices  28.8 us (36%)
  waiting for transfers between devices  19.2 us (24%)
  Pallas kernels  16 us (20%)
  blocking collectives  11.8 us (15%)
  local copies, waits for them, and re-layouts  2.35 us (3%)
  between operations  1.47 us (2%)
    all_to_all x1, starting transfers between devices, body(): lax.all_to_all(packed, 'img', split_axis=0, concat_axis=0, tiled=True)  12.3 us
    all_to_all x1, blocking collectives, body(): lax.all_to_all(blocks, 'fou', split_axis=0, concat_axis=0, tiled=True)  11.8 us
    pallas_call x8, Pallas kernels, call(): pl.pallas_call(kernel, out_shape=out_shape, in_specs=[SM] * scalars + [VM...  8.51 us
    all_to_all x1, waiting for transfers between devices, body(): lax.all_to_all(packed, 'img', split_axis=0, concat_axis=0, tiled=True)  6.8 us
    all_to_all x1, starting transfers between devices, body(): lines = lax.all_to_all(sent, 'fou', split_axis=0, concat_axis=0, tiled=True)  6.39 us
    all_to_all x1, waiting for transfers between devices, body(): lax.all_to_all(weighted, 'img', split_axis=0, concat_axis=0, tiled=True)  6 us
    all_to_all x1, waiting for transfers between devices, body(): lines = lax.all_to_all(sent, 'fou', split_axis=0, concat_axis=0, tiled=True)  5.08 us
    all_to_all x1, starting transfers between devices, body(): lax.all_to_all(weighted, 'img', split_axis=0, concat_axis=0, tiled=True)  4.5 us
  transfers between devices with their start and end apart: 5, of which 4 were waited for; matrix products, arithmetic and copies ran while one was open for 0% of the time, Pallas kernels for 7%

profile of v10, /device:TPU:1, one launch (start us, length us, event | category | flops | bytes accessed | tf_op | source)
XLA Modules:
  0.0 79.8 jit_solution(504130767365806065)
XLA Ops:
  0.6 0.0 copy-start
  0.6 0.0 copy-start.9
  0.7 1.7 %shard_map.123 = bf16[8,64,256]{2,1,0:T(8,128)(2,1)} custom-call(f32[4,64,256]{2,1,0:T(8,128)} %sky_hbm.1), custom_call_target="tpu_custom_call" | custom-call | tf_op jit(solution)/shard_map/pallas_call | solution.py:586
  2.4 6.4 %all-to-all-start = ((bf16[8,64,256]{2,1,0:T(8,128)(2,1)}), bf16[8,64,256]{2,1,0:T(8,128)(2,1)S(1)}, u32[]{:S(2)}, u32[]{:S(2)}) async-start(bf16[8,64,256]{2,1,0:T(8,128)(2,1)} %shard_map.123), calls=%async_computation | async-start | bytes 524288 | tf_op jit(solution)/shard_map/all_to_all | solution.py:599
  8.8 0.0 copy-done
  8.8 0.0 copy-done.9
  8.9 0.8 %shard_map.122.bands_ref = bf16[2560,256]{1,0:T(8,128)(2,1)S(1)} custom-call(f32[8,256]{1,0:T(8,128)S(1)} %pad.4.taps_ref), custom_call_target="tpu_custom_call" | custom-call | flops 1048576 | bytes 1048576 | tf_op jit(solution)/shard_map/pallas_call | solution.py:534
  9.7 0.0 copy-start.10
  9.7 0.1 pad_add_fusion.par_ref.where_ref
  9.8 5.1 %all-to-all-done.x_ref = bf16[8,64,256]{2,1,0:T(8,128)(2,1)S(1)} async-done(((bf16[8,64,256]{2,1,0:T(8,128)(2,1)}), bf16[8,64,256]{2,1,0:T(8,128)(2,1)S(1)}, u32[]{:S(2)}, u32[]{:S(2)}) %all-to-all-start) | async-done | bytes 262176 | tf_op jit(solution)/shard_map/all_to_all | solution.py:599
  14.9 1.8 %shard_map.125 = bf16[32,32,128]{2,1,0:T(8,128)(2,1)} custom-call(s32[4]{0:T(128)S(1)} %pad_add_fusion.par_ref.where_ref, bf16[8,64,256]{2,1,0:T(8,128)(2,1)S(1)} %all-to-all-done.x_ref, bf16[2,288,512]{2,1,0:T(8,128)(2,1)S(1)} %shard_map.124.line_ref), custom_call_target="tpu_custom_call" | custom-call | flops 536870912 | bytes 1048576 | tf_op jit(solution)/shard_map/pallas_call | solution.py:534
  16.7 12.3 %all-to-all-start.1 = ((bf16[32,32,128]{2,1,0:T(8,128)(2,1)}), bf16[32,32,128]{2,1,0:T(8,128)(2,1)S(1)}, u32[]{:S(2)}, u32[]{:S(2)}) async-start(bf16[32,32,128]{2,1,0:T(8,128)(2,1)} %shard_map.125), calls=%async_computation.1 | async-start | bytes 524288 | tf_op jit(solution)/shard_map/all_to_all | solution.py:620
  29.6 0.0 copy-done.10
  29.6 0.1 copy.13.count_ref
  29.7 0.0 copy-start.6
  29.7 1.3 %copy-done.6 = bf16[4,9,64,256]{3,2,1,0:T(8,128)(2,1)S(1)} copy-done((bf16[4,9,64,256]{3,2,1,0:T(8,128)(2,1)S(1)}, bf16[4,9,64,256]{3,2,1,0:T(8,128)(2,1)}, u32[]{:S(2)}) %copy-start.6) | copy-done | bytes 1179672
  31.0 0.0 copy-start.3
  31.0 0.0 copy-start.4
  31.0 0.0 copy-start.5
  31.0 2.4 %shard_map.126 = (f32[8,80,384]{2,1,0:T(8,128)S(1)}, bf16[8,16,384]{2,1,0:T(8,128)(2,1)S(1)}, bf16[8,16,384]{2,1,0:T(8,128)(2,1)S(1)}) custom-call(s32[4]{0:T(128)S(1)} %pad_add_fusion.par_ref.where_ref, s32[1]{0:T(128)S(6)} %copy.14.live_ref, bf16[4,9,64,256]{3,2,1,0:T(8,128)(2,1)S(1)} %copy-done.6, f32[4,64,256]{2,1,0:T(8,128)} %sky_hbm.1, ...), custom_call_target="tpu_custom_call" | custom-call | flops 2147483648 | bytes 4194304 | tf_op jit(solution)/shard_map/pallas_call | solution.py:626
  33.4 0.0 copy-start.1
  33.4 0.9 %copy-done.1 = f32[8,80,384]{2,1,0:T(8,128)} copy-done((f32[8,80,384]{2,1,0:T(8,128)}, f32[8,80,384]{2,1,0:T(8,128)S(1)}, u32[]{:S(2)}) %copy-start.1) | copy-done | bytes 983064
  34.3 0.0 copy-done.3
  34.3 0.0 copy-done.4
  34.3 0.0 copy-done.5
  34.3 0.8 %shard_map.127.e_ref = bf16[320,1536]{1,0:T(8,128)(2,1)S(1)} custom-call(s32[4]{0:T(128)S(1)} %pad_add_fusion.par_ref.where_ref, s32[4,1,6]{2,1,0:T(1,128)S(1)} %copy-done.5, s32[4,1]{1,0:T(4,128)S(1)} %copy.13.count_ref, bf16[4,1,6,64,64]{4,3,2,1,0:T(8,128)(2,1)S(1)} %copy-done.4, bf16[384,768]{1,0:T(8,128)(2,1)S(1)} %copy-done.3), custom_call_target="tpu_custom_call" | custom-call | flops 8388608 | bytes 1048576 | tf_op jit(solution)/shard_map/pallas_call | solution.py:534
  35.2 6.8 %all-to-all-done.1.d_ref = bf16[32,32,128]{2,1,0:T(8,128)(2,1)S(1)} async-done(((bf16[32,32,128]{2,1,0:T(8,128)(2,1)}), bf16[32,32,128]{2,1,0:T(8,128)(2,1)S(1)}, u32[]{:S(2)}, u32[]{:S(2)}) %all-to-all-start.1) | async-done | bytes 262176 | tf_op jit(solution)/shard_map/all_to_all | solution.py:620
  42.0 2.6 %shard_map.128 = bf16[32,40,128]{2,1,0:T(8,128)(2,1)} custom-call(bf16[32,32,128]{2,1,0:T(8,128)(2,1)S(1)} %all-to-all-done.1.d_ref, bf16[320,1536]{1,0:T(8,128)(2,1)S(1)} %shard_map.127.e_ref), custom_call_target="tpu_custom_call" | custom-call | flops 536870912 | bytes 1048576 | tf_op jit(solution)/shard_map/pallas_call | solution.py:534
  44.6 4.5 %all-to-all-start.2 = ((bf16[32,40,128]{2,1,0:T(8,128)(2,1)}), bf16[32,40,128]{2,1,0:T(8,128)(2,1)S(1)}, u32[]{:S(2)}, u32[]{:S(2)}) async-start(bf16[32,40,128]{2,1,0:T(8,128)(2,1)} %shard_map.128), calls=%async_computation.2 | async-start | bytes 655360 | tf_op jit(solution)/shard_map/all_to_all | solution.py:682
  49.1 0.0 copy-start.2
  49.1 2.3 %collective-permute-start.1 = (bf16[8,16,384]{2,1,0:T(8,128)(2,1)S(1)}, bf16[8,16,384]{2,1,0:T(8,128)(2,1)S(1)}, u32[]{:S(2)}, u32[]{:S(2)}) collective-permute-start(bf16[8,16,384]{2,1,0:T(8,128)(2,1)S(1)} %get-tuple-element.14), channel_id=1, source_target_pairs={{8,0},{16,8},{24,16},{32,24},{40,32},{48,40},{56,48},{64,56},{72,6... | collective-permute-start | bytes 294920 | tf_op jit(solution)/shard_map/ppermute | solution.py:692
  51.4 3.4 %collective-permute-start = (bf16[8,16,384]{2,1,0:T(8,128)(2,1)S(1)}, bf16[8,16,384]{2,1,0:T(8,128)(2,1)S(1)}, u32[]{:S(2)}, u32[]{:S(2)}) collective-permute-start(bf16[8,16,384]{2,1,0:T(8,128)(2,1)S(1)} %get-tuple-element.21), channel_id=1, source_target_pairs={{0,8},{8,16},{16,24},{24,32},{32,40},{40,48},{48,56},{56,64},{64,7... | collective-permute-start | bytes 294920 | tf_op jit(solution)/shard_map/ppermute | solution.py:691
  54.8 0.8 %shard_map.129.bands_ref = bf16[2560,256]{1,0:T(8,128)(2,1)S(1)} custom-call(f32[8,256]{1,0:T(8,128)S(1)} %pad.4.taps_ref), custom_call_target="tpu_custom_call" | custom-call | flops 1048576 | bytes 1048576 | tf_op jit(solution)/shard_map/pallas_call | solution.py:534
  55.6 0.0 collective-permute-done.1.after_ref
  55.7 1.3 %collective-permute-done.before_ref = bf16[8,16,384]{2,1,0:T(8,128)(2,1)S(1)} collective-permute-done((bf16[8,16,384]{2,1,0:T(8,128)(2,1)S(1)}, bf16[8,16,384]{2,1,0:T(8,128)(2,1)S(1)}, u32[]{:S(2)}, u32[]{:S(2)}) %collective-permute-start) | collective-permute-done | bytes 98336 | tf_op jit(solution)/shard_map/ppermute | solution.py:691
  57.0 0.0 copy-done.2
  57.0 0.3 shard_map.130.base_ref
  57.2 0.0 copy-start.8
  57.3 6.0 %all-to-all-done.2.t_ref = bf16[32,40,128]{2,1,0:T(8,128)(2,1)S(1)} async-done(((bf16[32,40,128]{2,1,0:T(8,128)(2,1)}), bf16[32,40,128]{2,1,0:T(8,128)(2,1)S(1)}, u32[]{:S(2)}, u32[]{:S(2)}) %all-to-all-start.2) | async-done | bytes 327712 | tf_op jit(solution)/shard_map/all_to_all | solution.py:682
  63.2 0.0 copy-start.7
  63.2 1.3 %shard_map.131 = bf16[8,80,384]{2,1,0:T(8,128)(2,1)S(1)} custom-call(s32[4]{0:T(128)S(1)} %pad_add_fusion.par_ref.where_ref, bf16[32,40,128]{2,1,0:T(8,128)(2,1)S(1)} %all-to-all-done.2.t_ref, bf16[2,288,512]{2,1,0:T(8,128)(2,1)S(1)} %copy-done, f32[8,80,384]{2,1,0:T(8,128)S(1)} %shard_map.130.base_ref), custom_call_target="tpu_custom_call" | custom-call | flops 536870912 | bytes 1048576 | tf_op jit(solution)/shard_map/pallas_call | solution.py:534
  64.6 11.8 %all_to_all.20.half_ref = bf16[8,80,384]{2,1,0:T(8,128)(2,1)S(1)} all-to-all(bf16[8,80,384]{2,1,0:T(8,128)(2,1)S(1)} %shard_map.131), channel_id=1, replica_groups=mesh['img'=32,'fou'=8] {'fou'}, dimensions={0} | all-to-all | bytes 983040 | tf_op jit(solution)/shard_map/all_to_all | solution.py:715
  76.4 0.0 copy-done.8
  76.4 0.0 copy-done.7
  76.4 3.4 %shard_map.132 = (f32[4,64,256]{2,1,0:T(8,128)}, bf16[4,9,64,256]{3,2,1,0:T(8,128)(2,1)}) custom-call(f32[9]{0:T(128)S(1)} %copy-done.8, s32[4]{0:T(128)S(1)} %pad_add_fusion.par_ref.where_ref, bf16[8,80,384]{2,1,0:T(8,128)(2,1)S(1)} %all_to_all.20.half_ref, f32[8,80,384]{2,1,0:T(8,128)S(1)} %shard_map.130.base_ref, bf16[4,9,64,256]{3,2,1,0:T(8,128)(2,1)S(1)} %copy-done.7, ...), custom_call_target="tpu_custom_call" | custom-call | flops 2147483648 | bytes 3145728 | tf_op jit(solution)/shard_map/pallas_call | solution.py:548
  (2 shorter events, 0.0 us)
Async XLA Ops:
  0.6 8.1 %copy-start = (bf16[2,288,512]{2,1,0:T(8,128)(2,1)S(1)}, bf16[2,288,512]{2,1,0:T(8,128)(2,1)}, u32[]{:S(2)}) copy-start(bf16[2,288,512]{2,1,0:T(8,128)(2,1)} %constant.18.clone.table_ref.line_ref) | copy-start | bytes 1769476
  0.6 8.2 %copy-start.9 = (f32[8,17]{1,0:T(8,128)S(1)}, f32[8,17]{1,0:T(8,128)}, u32[]{:S(2)}) copy-start(f32[8,17]{1,0:T(8,128)} %param.14) | copy-start | bytes 1636
  2.4 12.5 %all-to-all-start = ((bf16[8,64,256]{2,1,0:T(8,128)(2,1)}), bf16[8,64,256]{2,1,0:T(8,128)(2,1)S(1)}, u32[]{:S(2)}, u32[]{:S(2)}) async-start(bf16[8,64,256]{2,1,0:T(8,128)(2,1)} %shard_map.123), calls=%async_computation | async-start | bytes 524288 | tf_op jit(solution)/shard_map/all_to_all | solution.py:599
  9.7 19.9 %copy-start.10 = (s32[4,1]{0,1:T(1,128)S(1)}, s32[4,1]{0,1:T(1,128)}, u32[]{:S(2)}) copy-start(s32[4,1]{0,1:T(1,128)} %param.18) | copy-start | bytes 52
  16.7 25.3 %all-to-all-start.1 = ((bf16[32,32,128]{2,1,0:T(8,128)(2,1)}), bf16[32,32,128]{2,1,0:T(8,128)(2,1)S(1)}, u32[]{:S(2)}, u32[]{:S(2)}) async-start(bf16[32,32,128]{2,1,0:T(8,128)(2,1)} %shard_map.125), calls=%async_computation.1 | async-start | bytes 524288 | tf_op jit(solution)/shard_map/all_to_all | solution.py:620
  29.7 1.3 %copy-start.6 = (bf16[4,9,64,256]{3,2,1,0:T(8,128)(2,1)S(1)}, bf16[4,9,64,256]{3,2,1,0:T(8,128)(2,1)}, u32[]{:S(2)}) copy-start(bf16[4,9,64,256]{3,2,1,0:T(8,128)(2,1)} %dual_ref.3) | copy-start | bytes 3538948
  31.0 3.3 %copy-start.3 = (bf16[384,768]{1,0:T(8,128)(2,1)S(1)}, bf16[384,768]{1,0:T(8,128)(2,1)}, u32[]{:S(2)}) copy-start(bf16[384,768]{1,0:T(8,128)(2,1)} %constant.19.clone.table_ref) | copy-start | bytes 1769476
  31.0 3.3 %copy-start.4 = (bf16[4,1,6,64,64]{4,3,2,1,0:T(8,128)(2,1)S(1)}, bf16[4,1,6,64,64]{4,3,2,1,0:T(8,128)(2,1)}, u32[]{:S(2)}) copy-start(bf16[4,1,6,64,64]{4,3,2,1,0:T(8,128)(2,1)} %tiles_ref.1) | copy-start | bytes 589828
  31.0 3.3 %copy-start.5 = (s32[4,1,6]{2,1,0:T(1,128)S(1)}, s32[4,1,6]{2,1,0:T(1,128)}, u32[]{:S(2)}) copy-start(s32[4,1,6]{2,1,0:T(1,128)} %slots_ref.1) | copy-start | bytes 292
  33.4 0.9 %copy-start.1 = (f32[8,80,384]{2,1,0:T(8,128)}, f32[8,80,384]{2,1,0:T(8,128)S(1)}, u32[]{:S(2)}) copy-start(f32[8,80,384]{2,1,0:T(8,128)S(1)} %get-tuple-element.19.base_ref) | copy-start | bytes 2949124
  44.6 18.7 %all-to-all-start.2 = ((bf16[32,40,128]{2,1,0:T(8,128)(2,1)}), bf16[32,40,128]{2,1,0:T(8,128)(2,1)S(1)}, u32[]{:S(2)}, u32[]{:S(2)}) async-start(bf16[32,40,128]{2,1,0:T(8,128)(2,1)} %shard_map.128), calls=%async_computation.2 | async-start | bytes 655360 | tf_op jit(solution)/shard_map/all_to_all | solution.py:682
  49.1 7.9 %copy-start.2 = (f32[8,80,384]{2,1,0:T(8,128)S(1)}, f32[8,80,384]{2,1,0:T(8,128)}, u32[]{:S(2)}) copy-start(f32[8,80,384]{2,1,0:T(8,128)} %copy-done.1) | copy-start | bytes 2949124
  49.1 6.6 %collective-permute-start.1 = (bf16[8,16,384]{2,1,0:T(8,128)(2,1)S(1)}, bf16[8,16,384]{2,1,0:T(8,128)(2,1)S(1)}, u32[]{:S(2)}, u32[]{:S(2)}) collective-permute-start(bf16[8,16,384]{2,1,0:T(8,128)(2,1)S(1)} %get-tuple-element.14), channel_id=1, source_target_pairs={{8,0},{16,8},{24,16},{32,24},{40,32},{48,40},{56,48},{64,56},{72,6... | collective-permute-start | bytes 294920 | tf_op jit(solution)/shard_map/ppermute | solution.py:692
  51.4 5.6 %collective-permute-start = (bf16[8,16,384]{2,1,0:T(8,128)(2,1)S(1)}, bf16[8,16,384]{2,1,0:T(8,128)(2,1)S(1)}, u32[]{:S(2)}, u32[]{:S(2)}) collective-permute-start(bf16[8,16,384]{2,1,0:T(8,128)(2,1)S(1)} %get-tuple-element.21), channel_id=1, source_target_pairs={{0,8},{8,16},{16,24},{24,32},{32,40},{40,48},{48,56},{56,64},{64,7... | collective-permute-start | bytes 294920 | tf_op jit(solution)/shard_map/ppermute | solution.py:691
  57.2 19.2 %copy-start.8 = (f32[9]{0:T(128)S(1)}, f32[9]{0:T(128)}, u32[]{:S(2)}) copy-start(f32[9]{0:T(128)} %bound_ref.1) | copy-start | bytes 112
  63.2 13.1 %copy-start.7 = (bf16[4,9,64,256]{3,2,1,0:T(8,128)(2,1)S(1)}, bf16[4,9,64,256]{3,2,1,0:T(8,128)(2,1)}, u32[]{:S(2)}) copy-start(bf16[4,9,64,256]{3,2,1,0:T(8,128)(2,1)} %dual_ref.3) | copy-start | bytes 3538948
